TPU v7x, 32 devices: a whole 2x2x4 slice. The times are simulated.
32 devices in a mesh: dp: 16 (over z, x, core), seq: 2 (over y).
Axes of the slice: x: 2, y: 2, z: 4, core: 2. Of those that a mesh axis runs over, the one named last changes fastest.
Arguments:
- block_input: bfloat16 [16, 2048, 768], P('dp', 'seq'), may hold values from -6 to 6
- cotangent: bfloat16 [16, 2048, 768], P('dp', 'seq'), may hold values from -6 to 6
- in_weight: float32 [768, 3328], P('dp'), may hold values from -0.21875 to 0.21875
- dt_weight: float32 [768, 24], P('dp'), may hold values from -0.21875 to 0.21875
- out_weight: float32 [1536, 768], P('dp'), may hold values from -0.15625 to 0.15625
- norm_gain: float32 [768], replicated, may hold values from 0.5 to 1.5
- conv_weight: float32 [4, 1792], replicated, may hold values from -3 to 3
- conv_bias: float32 [1792], replicated, may hold values from -1.5 to 1.5
- dt_bias: float32 [24], replicated, may hold values from -6.9 to -2.25
- decay_log: float32 [24], replicated, may hold values from 0 to 2.5
- skip_gain: float32 [24], replicated, may hold values from 0.5 to 1.5
- gate_gain: float32 [1536], replicated, may hold values from 0.5 to 1.5
- in_left: float32 [32, 26, 24, 24], P('dp'), as said below
- in_right: float32 [32, 26, 128, 128], P('dp'), as said below
- in_left_root: float32 [32, 26, 24, 24], P('dp'), as said below
- in_right_root: float32 [32, 26, 128, 128], P('dp'), as said below
- dt_left: float32 [32, 24, 24], P('dp'), as said below
- dt_right: float32 [32, 24, 24], P('dp'), as said below
- dt_left_root: float32 [32, 24, 24], P('dp'), as said below
- dt_right_root: float32 [32, 24, 24], P('dp'), as said below
- out_left: float32 [64, 6, 24, 24], P('dp'), as said below
- out_right: float32 [64, 6, 128, 128], P('dp'), as said below
- out_left_root: float32 [64, 6, 24, 24], P('dp'), as said below
- out_right_root: float32 [64, 6, 128, 128], P('dp'), as said below
- vector_moment: float32 [11336], replicated, may hold values from 1638.4 to 65536
Outputs:
- block_output: bfloat16 [16, 2048, 768], P('dp', 'seq')
- input_grad: float32 [16, 2048, 768], P('dp', 'seq')
- in_grad: float32 [768, 3328], P('dp')
- dt_grad: float32 [768, 24], P('dp')
- out_grad: float32 [1536, 768], P('dp')
- in_update: float32 [768, 3328], P('dp')
- dt_update: float32 [768, 24], P('dp')
- out_update: float32 [1536, 768], P('dp')
- in_left_new: float32 [32, 26, 24, 24], P('dp')
- in_right_new: float32 [32, 26, 128, 128], P('dp')
- dt_left_new: float32 [32, 24, 24], P('dp')
- dt_right_new: float32 [32, 24, 24], P('dp')
- out_left_new: float32 [64, 6, 24, 24], P('dp')
- out_right_new: float32 [64, 6, 128, 128], P('dp')
- vector_grad: float32 [11336], replicated
- vector_moment_new: float32 [11336], replicated
- vector_update: float32 [11336], replicated
Inputs may be any that keep to these rules, and one draw needn't show every extreme that they name: `in_left`: every block of the statistics and of the given roots is symmetric. `in_right`: every block is symmetric. `in_left_root`: every block is symmetric. `in_right_root`: every block is symmetric. `dt_left`: every block is symmetric. `dt_right`: every block is symmetric. `dt_left_root`: every block is symmetric. `dt_right_root`: every block is symmetric. `out_left`: every block is symmetric. `out_right`: every block is symmetric. `out_left_root`: every block is symmetric. `out_right_root`: every block is symmetric.
All inputs are finite; a program needn't handle non-finite values.
Results may differ from a plain program's by a relative error of at most 0.0033.
The roundings to bfloat16 on the way count: a program that leaves them out, or rounds other values in their place, can miss the bound.
Values may be sent and summed in bfloat16 or wider, within the bound.
No kernel may reach another device: no remote copies, remote signals or barrier semaphores. Data moves between devices by JAX's collectives and lax.ppermute only.
A program may use at most 256 MiB of HBM per device.

v0:
```python
import jax
import jax.numpy as jnp
from jax import lax
from jax.sharding import PartitionSpec as P

D = 768
HEADS = 24
HEADDIM = 64
DSTATE = 128
KCONV = 4
BLOCK_LEN = 256
DI = 1536


EPS = 1e-05
LR = 0.25
LR_VEC = 0.02
HIGH = lax.Precision.HIGHEST
ROWS_CONTRACT = (((0,), (0,)), ((), ()))
COLS_CONTRACT = (((1,), (1,)), ((), ()))


def causal_conv(signal, kernel, offset):
    length = signal.shape[-2]
    widths = [(0, 0)] * (signal.ndim - 2) + [(KCONV - 1, 0), (0, 0)]
    padded = jnp.pad(signal, widths)
    running = offset + kernel[0] * padded[..., 0:length, :]
    for tap_index in range(1, KCONV):
        running = running + kernel[tap_index] * padded[..., tap_index : tap_index + length, :]
    return jax.nn.silu(running)


def carry_step(carried, scanned):
    new_state, factor = scanned
    return (carried * factor[:, None, None] + new_state, carried)


def state_space(values, step_sizes, decay_rates, inputs_b, inputs_c, skip_gain):
    length, head_count, head_size = values.shape
    block_count = length // BLOCK_LEN
    blocks_x = values.reshape(block_count, BLOCK_LEN, head_count, head_size)
    blocks_dt = step_sizes.reshape(block_count, BLOCK_LEN, head_count)
    blocks_b = inputs_b.reshape(block_count, BLOCK_LEN, -1)
    blocks_c = inputs_c.reshape(block_count, BLOCK_LEN, -1)
    cumulative = jnp.cumsum(blocks_dt * decay_rates, axis=1)
    row_index = lax.broadcasted_iota(jnp.int32, (BLOCK_LEN, BLOCK_LEN), 0)
    earlier = lax.broadcasted_iota(jnp.int32, (BLOCK_LEN, BLOCK_LEN), 1)
    causal = (row_index >= earlier)[None, :, :, None]
    spread = cumulative[:, :, None, :] - cumulative[:, None, :, :]
    kernel = jnp.where(causal, jnp.exp(jnp.where(causal, spread, 0.0)), 0.0)
    scores = jnp.einsum("cqn,csn->cqs", blocks_c, blocks_b, precision=HIGH)
    mixing = scores[..., None] * kernel * blocks_dt[:, None, :, :]
    inner_part = jnp.einsum("cqsh,cshp->cqhp", mixing, blocks_x, precision=HIGH)
    weights = jnp.exp(cumulative[:, -1:, :] - cumulative) * blocks_dt
    fresh_state = jnp.einsum(
        "csn,cshp->chnp", blocks_b, weights[..., None] * blocks_x, precision=HIGH
    )
    factor = jnp.exp(cumulative[:, -1, :])
    initial = jnp.zeros((head_count, blocks_b.shape[-1], head_size), jnp.float32)
    last_state, entering = lax.scan(jax.checkpoint(carry_step), initial, (fresh_state, factor))
    outer_part = (
        jnp.einsum("cqn,chnp->cqhp", blocks_c, entering, precision=HIGH)
        * jnp.exp(cumulative)[..., None]
    )
    combined = inner_part + outer_part + skip_gain[None, None, :, None] * blocks_x
    return combined.reshape(length, head_count, head_size)


def norm_piece(incoming, norm_gain):
    inv_rms = lax.rsqrt(jnp.mean(incoming * incoming, axis=-1, keepdims=True) + EPS)
    return incoming * inv_rms * norm_gain


def gate_piece(states, gate_part, gate_gain):
    gated_out = states * jax.nn.silu(gate_part)
    norm_gate = lax.rsqrt(jnp.mean(gated_out * gated_out, axis=-1, keepdims=True) + EPS)
    return gated_out * norm_gate * gate_gain


def kron_update(gradient, left_stat, right_stat, left_root, right_root):
    row_tiles, col_tiles = (left_stat.shape[0], left_stat.shape[1])
    row_size, col_size = (left_stat.shape[-1], right_stat.shape[-1])
    grad_tiles = gradient.reshape(row_tiles, row_size, col_tiles, col_size).transpose(0, 2, 1, 3)
    left_new = 0.5 * left_stat + 0.5 * jnp.einsum(
        "abij,abkj->abik", grad_tiles, grad_tiles, precision=HIGH
    )
    right_new = 0.5 * right_stat + 0.5 * jnp.einsum(
        "abji,abjk->abik", grad_tiles, grad_tiles, precision=HIGH
    )
    shaped = jnp.einsum("abij,abjk->abik", left_root, grad_tiles, precision=HIGH)
    shaped = jnp.einsum("abij,abjk->abik", shaped, right_root, precision=HIGH)
    update = (-LR * shaped).transpose(0, 2, 1, 3).reshape(gradient.shape)
    return (update, left_new, right_new)


def body(
    block_input,
    cotangent,
    in_weight,
    dt_weight,
    out_weight,
    norm_gain,
    conv_weight,
    conv_bias,
    dt_bias,
    decay_log,
    skip_gain,
    gate_gain,
    in_left,
    in_right,
    in_left_root,
    in_right_root,
    dt_left,
    dt_right,
    dt_left_root,
    dt_right_root,
    out_left,
    out_right,
    out_left_root,
    out_right_root,
    vector_moment,
):
    seq_count = block_input.shape[0]
    local_len = block_input.shape[1]
    seq_devices = lax.axis_size("seq")
    head_local = HEADS // seq_devices
    width_local = head_local * HEADDIM
    row_count = seq_count * local_len
    whole_len = local_len * seq_devices
    in_full, dt_full, out_full = (
        lax.all_gather(in_weight.astype(jnp.bfloat16), "dp", axis=0, tiled=True),
        lax.all_gather(dt_weight.astype(jnp.bfloat16), "dp", axis=0, tiled=True),
        lax.all_gather(out_weight.astype(jnp.bfloat16), "dp", axis=0, tiled=True),
    )
    incoming = block_input.reshape(row_count, D).astype(jnp.float32)
    normed, norm_back = jax.vjp(norm_piece, incoming, norm_gain)
    normed_low = normed.astype(jnp.bfloat16)
    projected = jnp.dot(normed_low, in_full, preferred_element_type=jnp.float32)
    dt_raw = jnp.dot(normed_low, dt_full, preferred_element_type=jnp.float32).astype(jnp.bfloat16)
    gate_part = projected[:, :DI]
    values_out = (
        projected[:, DI : 2 * DI]
        .astype(jnp.bfloat16)
        .reshape(seq_count, local_len, seq_devices, width_local)
    )
    dt_out = dt_raw.reshape(seq_count, local_len, seq_devices, head_local)
    values_in, dt_in = (
        lax.all_to_all(values_out, "seq", split_axis=2, concat_axis=1, tiled=True),
        lax.all_to_all(dt_out, "seq", split_axis=2, concat_axis=1, tiled=True),
    )
    bc_local = projected[:, 2 * DI :].astype(jnp.bfloat16).reshape(seq_count, local_len, 2 * DSTATE)
    bc_whole = lax.all_gather(bc_local, "seq", axis=1, tiled=True)
    first_head = lax.axis_index("seq") * head_local

    def head_piece(
        values, step_raw, bc_values, conv_weight, conv_bias, dt_bias, decay_log, skip_gain
    ):
        kernel = jnp.concatenate(
            [
                lax.dynamic_slice_in_dim(conv_weight, first_head * HEADDIM, width_local, 1),
                conv_weight[:, DI:],
            ],
            axis=1,
        )
        offset = jnp.concatenate(
            [
                lax.dynamic_slice_in_dim(conv_bias, first_head * HEADDIM, width_local, 0),
                conv_bias[DI:],
            ]
        )
        convolved = causal_conv(jnp.concatenate([values, bc_values], axis=-1), kernel, offset)
        head_values = convolved[..., :width_local].reshape(
            seq_count, whole_len, head_local, HEADDIM
        )
        inputs_b = convolved[..., width_local : width_local + DSTATE]
        inputs_c = convolved[..., width_local + DSTATE :]
        step_sizes = jax.nn.softplus(
            step_raw + lax.dynamic_slice_in_dim(dt_bias, first_head, head_local, 0)
        )
        decay_rates = -jnp.exp(lax.dynamic_slice_in_dim(decay_log, first_head, head_local, 0))
        skip_local = lax.dynamic_slice_in_dim(skip_gain, first_head, head_local, 0)
        result = jax.vmap(state_space, in_axes=(0, 0, None, 0, 0, None))(
            head_values, step_sizes, decay_rates, inputs_b, inputs_c, skip_local
        )
        return result.reshape(seq_count, whole_len, width_local)

    head_states, head_back = jax.vjp(
        head_piece,
        values_in.reshape(seq_count, whole_len, width_local).astype(jnp.float32),
        dt_in.reshape(seq_count, whole_len, head_local).astype(jnp.float32),
        bc_whole.astype(jnp.float32),
        conv_weight,
        conv_bias,
        dt_bias,
        decay_log,
        skip_gain,
    )
    states_out = head_states.astype(jnp.bfloat16).reshape(
        seq_count, seq_devices, local_len, width_local
    )
    states_in = lax.all_to_all(states_out, "seq", split_axis=1, concat_axis=3, tiled=True).reshape(
        row_count, DI
    )
    branch, gate_back = jax.vjp(gate_piece, states_in.astype(jnp.float32), gate_part, gate_gain)
    branch_low = branch.astype(jnp.bfloat16)
    output = incoming + jnp.dot(branch_low, out_full, preferred_element_type=jnp.float32)
    block_output = output.astype(jnp.bfloat16).reshape(block_input.shape)
    upstream = cotangent.reshape(row_count, D)
    branch_grad = lax.dot_general(
        upstream, out_full, COLS_CONTRACT, preferred_element_type=jnp.float32
    )
    states_grad, gate_grad, gate_gain_grad = gate_back(branch_grad)
    grad_heads = lax.all_to_all(
        states_grad.astype(jnp.bfloat16).reshape(seq_count, local_len, seq_devices, width_local),
        "seq",
        split_axis=2,
        concat_axis=1,
        tiled=True,
    )
    head_grads = head_back(
        grad_heads.reshape(seq_count, whole_len, width_local).astype(jnp.float32)
    )
    (
        values_grad,
        step_grad,
        bc_grad,
        conv_weight_grad,
        conv_bias_grad,
        dt_bias_grad,
        decay_grad,
        skip_grad,
    ) = head_grads
    values_send = values_grad.astype(jnp.bfloat16).reshape(
        seq_count, seq_devices, local_len, width_local
    )
    steps_send = step_grad.astype(jnp.bfloat16).reshape(
        seq_count, seq_devices, local_len, head_local
    )
    values_back, steps_back = (
        lax.all_to_all(values_send, "seq", split_axis=1, concat_axis=3, tiled=True),
        lax.all_to_all(steps_send, "seq", split_axis=1, concat_axis=3, tiled=True),
    )
    bc_back = lax.psum_scatter(
        bc_grad.astype(jnp.bfloat16), "seq", scatter_dimension=1, tiled=True
    ).astype(jnp.float32)
    proj_grad = jnp.concatenate(
        [
            gate_grad.astype(jnp.bfloat16),
            values_back.reshape(row_count, DI),
            bc_back.reshape(row_count, 2 * DSTATE).astype(jnp.bfloat16),
        ],
        axis=1,
    )
    step_rows = steps_back.reshape(row_count, HEADS)
    normed_grad = lax.dot_general(
        proj_grad, in_full, COLS_CONTRACT, preferred_element_type=jnp.float32
    )
    normed_grad = normed_grad + lax.dot_general(
        step_rows, dt_full, COLS_CONTRACT, preferred_element_type=jnp.float32
    )
    input_part, norm_gain_grad = norm_back(normed_grad)
    input_grad = (input_part + upstream.astype(jnp.float32)).reshape(block_input.shape)
    in_partial = lax.dot_general(
        normed_low, proj_grad, ROWS_CONTRACT, preferred_element_type=jnp.float32
    )
    dt_partial = lax.dot_general(
        normed_low, step_rows, ROWS_CONTRACT, preferred_element_type=jnp.float32
    )
    out_partial = lax.dot_general(
        branch_low, upstream, ROWS_CONTRACT, preferred_element_type=jnp.float32
    )
    in_owned, dt_owned, out_owned = (
        lax.psum_scatter(in_partial, "dp", scatter_dimension=0, tiled=True),
        lax.psum_scatter(dt_partial, "dp", scatter_dimension=0, tiled=True),
        lax.psum_scatter(out_partial, "dp", scatter_dimension=0, tiled=True),
    )
    in_grad, dt_grad, out_grad = lax.psum((in_owned, dt_owned, out_owned), "seq")
    vector_local = jnp.concatenate(
        [
            norm_gain_grad,
            gate_gain_grad,
            conv_weight_grad.reshape(-1),
            conv_bias_grad,
            dt_bias_grad,
            decay_grad,
            skip_grad,
        ]
    )
    vector_grad = lax.psum(vector_local, ("dp", "seq"))
    in_update, in_left_new, in_right_new = kron_update(
        in_grad, in_left, in_right, in_left_root, in_right_root
    )
    dt_update, dt_left_wide, dt_right_wide = kron_update(
        dt_grad, dt_left[:, None], dt_right[:, None], dt_left_root[:, None], dt_right_root[:, None]
    )
    out_update, out_left_new, out_right_new = kron_update(
        out_grad, out_left, out_right, out_left_root, out_right_root
    )
    vector_moment_new = 0.5 * vector_moment + 0.5 * vector_grad * vector_grad
    vector_update = -LR_VEC * vector_grad * lax.rsqrt(vector_moment_new)
    return (
        block_output,
        input_grad,
        in_grad,
        dt_grad,
        out_grad,
        in_update,
        dt_update,
        out_update,
        in_left_new,
        in_right_new,
        dt_left_wide[:, 0],
        dt_right_wide[:, 0],
        out_left_new,
        out_right_new,
        vector_grad,
        vector_moment_new,
        vector_update,
    )


def solution(mesh):
    placed = (
        P("dp", "seq", None),
        P("dp", "seq", None),
        P("dp", None),
        P("dp", None),
        P("dp", None),
        P(),
        P(),
        P(),
        P(),
        P(),
        P(),
        P(),
        P("dp", None, None, None),
        P("dp", None, None, None),
        P("dp", None, None, None),
        P("dp", None, None, None),
        P("dp", None, None),
        P("dp", None, None),
        P("dp", None, None),
        P("dp", None, None),
        P("dp", None, None, None),
        P("dp", None, None, None),
        P("dp", None, None, None),
        P("dp", None, None, None),
        P(),
    )
    return jax.shard_map(
        body,
        mesh=mesh,
        in_specs=placed,
        out_specs=(
            P("dp", "seq", None),
            P("dp", "seq", None),
            P("dp", None),
            P("dp", None),
            P("dp", None),
            P("dp", None),
            P("dp", None),
            P("dp", None),
            P("dp", None, None, None),
            P("dp", None, None, None),
            P("dp", None, None),
            P("dp", None, None),
            P("dp", None, None, None),
            P("dp", None, None, None),
            P(),
            P(),
            P(),
        ),
        check_vma=False,
    )
```

profile of v0, /device:TPU:0, one launch (start us, length us, event | category | flops | bytes accessed | tf_op | source)
XLA Modules:
  0.0 1251.5 jit_solution(8939775388463713640)
XLA Ops:
  11.7 56.9 %all-gather.6.cloned.1.call-done = bf16[768,3328]{1,0:T(8,128)(2,1)} async-done(((bf16[48,3328]{1,0:T(8,128)(2,1)}), bf16[768,3328]{1,0:T(8,128)(2,1)}) %all-gather.6.cloned.1.call-update) | async-done | bytes 5111824 | tf_op jit(solution)/shard_map/all_gather | solution.py:131
  68.7 11.5 fusion.166
  83.7 19.3 %all-gather.1 = bf16[16,48,24]{1,2,0:T(8,128)(2,1)S(1)} all-gather(bf16[1,48,24]{1,2,0:T(8,128)(2,1)S(1)} %convert_bitcast_fusion.1), channel_id=1, replica_groups=mesh['dp'=16,'seq'=2] {'dp'}, dimensions={0}, use_global_device_ids=true | all-gather | bytes 39168 | tf_op jit(solution)/shard_map/all_gather | solution.py:132
  121.8 9.4 reduce-window.14
  139.2 7.5 reshape.946
  170.1 22.9 %all-to-all-done = bf16[1,1024,2,768]{3,1,0,2:T(8,128)(2,1)} async-done(((bf16[1,1024,2,768]{3,1,0,2:T(8,128)(2,1)}), bf16[1,1024,2,768]{3,1,0,2:T(8,128)(2,1)}, u32[]{:S(2)}, u32[]{:S(2)}) %all-to-all-start) | async-done | bytes 3145760 | tf_op jit(solution)/shard_map/all_to_all | solution.py:148
  195.4 7.9 pad_maximum_fusion
  203.4 18.7 %fusion.22 = (f32[1,2048,1024]{2,1,0:T(8,128)}, f32[1,2048,1024]{2,1,0:T(8,128)}) fusion(f32[1,2048,1024]{2,1,0:T(8,128)} %pad_maximum_fusion, f32[1024]{0:T(1024)S(1)} %bitcast.521, f32[1024]{0:T(1024)S(1)} %bitcast.523, f32[1024]{0:T(1024)S(1)} %bitcast.519, f32[1024]{0:T(1024)S(1)} %bitcast.517, f32[1024]{0:T(1024)S(1)} %copy-done.70), kind=kLoop, calls=%fused_computation.50 | loop fusion | flops 25165824 | bytes 25186304 | tf_op jit(solution)/shard_map/jvp(jit(silu))/mul | solution.py:30
  230.9 6.7 copy.372
  246.1 8.7 fusion.73
  258.3 71.2 %while.32 = (s32[]{:T(128)}, f32[1,12,128,64]{3,2,1,0:T(8,128)}, f32[8,1,12,128,64]{4,3,2,1,0:T(8,128)}, f32[8,1,12]{2,1,0:T(1,128)}, f32[8,1,12,128,64]{3,4,2,0,1:T(8,128)}, /*index=5*/s32[]{:T(128)}, s32[]{:T(128)}) while((s32[]{:T(128)}, f32[1,12,128,64]{3,2,1,0:T(8,128)}, f32[8,1,12,128,64]{4,3,2,1,0:T(8,128)}, ...), condition=%wide.region_4.5_spmd.clone, body=%wide.region_3.4_spmd.clone.sunk | while | flops 393219 | bytes 4325628 | solution.py:60
  335.6 7.2 fusion.168
  344.7 35.0 %fusion.27 = bf16[1,8,256,12,64]{2,4,3,1,0:T(8,128)(2,1)S(1)} fusion(f32[8,256,12,64]{1,3,2,0:T(8,128)S(1)} %bitcast.491, f32[1,8,256,12,64]{2,1,4,3,0:T(8,128)} %bitcast.478, f32[12]{0:T(128)S(1)} %copy-done.81, f32[8,256,12]{1,2,0:T(8,128)S(1)} %copy-done.27, f32[8,256,12]{1,2,0:T(8,128)S(1)} %copy-done.41, f32[8,256,12]{1,2,0:T(8,128)S(1)} %copy-done.43, ...), kind=kOutput, calls=%fused_computation.61 | convolution fusion | flops 4871159808 | bytes 24477744 | tf_op jit(solution)/shard_map/jvp(vmap(cqsh,cshp->cqhp))/dot_general | solution.py:53
  392.1 38.7 %all_to_all.72 = bf16[1,2,1024,768]{2,3,0,1:T(8,128)(2,1)S(1)} all-to-all(bf16[1,2,1024,768]{2,3,0,1:T(8,128)(2,1)S(1)} %copy.395), channel_id=1, replica_groups=mesh['dp'=16,'seq'=2] {'seq'}, dimensions={1} | all-to-all | bytes 6291456 | tf_op jit(solution)/shard_map/all_to_all | solution.py:201
  434.2 6.5 copy.462
  440.7 7.5 multiply_reduce_fusion.9
  448.2 10.3 multiply_reduce_fusion.6
  458.5 9.6 fusion.25
  481.4 31.9 %all-to-all-done.3 = bf16[1,1024,2,768]{1,3,0,2:T(8,128)(2,1)} async-done(((bf16[1,1024,2,768]{1,3,0,2:T(8,128)(2,1)}), bf16[1,1024,2,768]{1,3,0,2:T(8,128)(2,1)}, u32[]{:S(2)}, u32[]{:S(2)}) %all-to-all-start.3) | async-done | bytes 3145760 | tf_op jit(solution)/shard_map/all_to_all | solution.py:213
  518.6 10.3 copy.398
  528.9 9.0 reshape.991
  537.9 11.4 fusion.72
  552.7 108.1 %while.33 = (s32[]{:T(128)}, f32[1,12,128,64]{3,2,1,0:T(8,128)}, f32[8,1,12,128,64]{4,3,2,1,0:T(8,128)}, f32[8,1,12]{2,1,0:T(1,128)S(1)}, f32[8,1,12,128,64]{4,3...) while((s32[]{:T(128)}, f32[1,12,128,64]{3,2,1,0:T(8,128)}, ...), condition=%wide.region_10.11_spmd.clone, body=%wide.region_8.10_spmd.clone.sunk | while | flops 491512 | bytes 6292823 | solution.py:60
  660.8 18.1 %fusion.30 = (f32[8,256,12]{1,2,0:T(8,128)}, f32[8,12,64,256]{3,2,1,0:T(8,128)}) fusion(f32[1,8,256,12,64]{2,1,4,3,0:T(8,128)} %bitcast.479, f32[8,256,128,1]{2,1,3,0:T(8,128)} %bitcast.483, f32[8,1,12,128,64]{4,3,2,1,0:T(8,128)} %get-tuple-element.191), kind=kOutput, calls=%fused_computation.67 | convolution fusion | flops 2419040256 | bytes 16875520 | tf_op jit(solution)/shard_map/transpose(jvp(vmap(csn,cshp->chnp)))/dot_general | solution.py:55
  678.9 10.3 fusion.87
  689.2 23.7 %fusion.86 = f32[8,256,128]{2,1,0:T(8,128)} fusion(f32[8,256,12,64]{1,0,3,2:T(8,128)} %reshape.991, f32[8,256,12]{1,2,0:T(8,128)S(1)} %copy-done.27, f32[8,1,12,128,64]{4,3,2,1,0:T(8,128)S(1)} %copy-done.1), kind=kOutput, calls=%fused_computation.138 | convolution fusion | flops 2417491968 | bytes 10584064 | tf_op jit(solution)/shard_map/transpose(jvp(vmap(cqn,chnp->cqhp)))/dot_general | solution.py:62
  712.9 6.8 copy.401
  725.5 34.2 %fusion.7 = (f32[8,256,12]{1,2,0:T(8,128)}, f32[8,256,12]{1,2,0:T(8,128)}, f32[8,256,12]{1,2,0:T(8,128)}, f32[8,256,256]{2,1,0:T(8,128)}) fusion(f32[8,256,256]{2,1,0:T(8,128)} %copy-done.23, f32[8,256,12]{1,2,0:T(8,128)} %copy.380, f32[8,256,12]{1,2,0:T(8,128)S(1)} %copy-done.42, pred[256,256]{1,0:T(8,128)(4,1)} %iota_compare_fusion, ...), kind=kOutput, calls=%fused_computation.25 | convolution fusion | flops 4925612032 | bytes 14188544 | tf_op jit(solution)/shard_map/transpose(jvp(vmap(cqsh,cshp->cqhp)))/dot_general | solution.py:53
  759.8 20.6 %bitcast_add_fusion.1 = f32[1,8,256,12,64]{2,4,3,1,0:T(8,128)S(1)} fusion(f32[8,12,64,256]{3,2,1,0:T(8,128)} %get-tuple-element.484, f32[8,256,12]{1,2,0:T(8,128)S(1)} %copy-done.45, f32[12]{0:T(128)S(1)} %copy-done.82, f32[8,256,12]{1,2,0:T(8,128)S(1)} %copy-done.42, f32[8,256,12]{1,2,0:T(8,128)S(1)} %copy-done.44, f32[8,256,256]{2,1,0:T(8,128)S(1)} %copy-done.24, ...), kind=kOutput, calls=%fused_computation.58 | convolution fusion | flops 4871159808 | bytes 18186288 | tf_op jit(solution)/shard_map/transpose(jvp(vmap(cqsh,cshp->cqhp)))/dot_general | solution.py:53
  780.4 7.0 copy.417
  787.4 7.0 reshape.967
  794.4 6.7 copy.418
  813.2 21.8 %multiply_reduce_fusion.4 = (f32[1024]{0:T(1024)S(1)}, f32[1024]{0:T(1024)S(1)}, f32[1024]{0:T(1024)S(1)}, f32[1024]{0:T(1024)}, f32[1024]{0:T(1024)S(1)}, /*index=5*/f32[1,2048,1024]{2,1,0:T(8,128)}) fusion(f32[1,2048,1024]{2,1,0:T(8,128)} %pad_maximum_fusion, f32[1,2048,256]{2,1,0:T(8,128)S(1)} %copy-done.13, f32[1,2048,768]{2,1,0:T(8,128)} %bitcast.482, ...), kind=kLoop, calls=%fused_computation.47 | loop fusion | flops 44035072 | bytes 41963520 | tf_op jit(solution)/shard_map/transpose(jvp())/reduce_sum | solution.py:29
  835.0 11.4 broadcast_multiply_fusion
  858.7 7.5 multiply_reduce_fusion.7
  867.3 21.3 %reduce-window.16 = f32[1,8,12,2,128]{4,2,3,1,0:T(8,128)} reduce-window(f32[1,8,12,2,128]{4,2,3,1,0:T(8,128)} %copy.431, f32[]{:T(128)} %constant.116.clone.1), window={size=1x1x1x1x128 pad=0_0x0_0x0_0x0_0x0_127}, to_apply=%region_18.19 | reduce-window | flops 3121152 | bytes 196612 | tf_op jit(solution)/shard_map/reduce-window.2
  894.8 6.5 all_to_all.73
  904.4 8.2 fusion.79
  912.7 13.0 %add_convert_fusion = bf16[1,2051,1024]{2,1,0:T(8,128)(2,1)S(1)} fusion(f32[1,2048,1024]{2,1,0:T(8,128)} %get-tuple-element.469, f32[1,2048,1024]{2,1,0:T(8,128)} %get-tuple-element.470, f32[1,2048,1024]{2,1,0:T(8,128)} %get-tuple-element.471, f32[1,2048,1024]{2,1,0:T(8,128)} %copy-done.2), kind=kLoop, calls=%fused_computation.41 | loop fusion | flops 8400896 | bytes 37754880 | tf_op jit(solution)/shard_map/convert.22
  926.5 36.4 %all_to_all.74 = bf16[1,2,1024,768]{3,2,0,1:T(8,128)(2,1)S(1)} all-to-all(bf16[1,2,1024,768]{3,2,0,1:T(8,128)(2,1)S(1)} %bitcast.496), channel_id=1, replica_groups=mesh['dp'=16,'seq'=2] {'seq'}, dimensions={1} | all-to-all | bytes 6291456 | tf_op jit(solution)/shard_map/all_to_all | solution.py:240
  968.5 13.5 %fusion.66 = f32[768,3328]{1,0:T(8,128)} fusion(bf16[1024,256]{1,0:T(8,128)(2,1)} %bitcast.540, bf16[1024,1536]{1,0:T(8,128)(2,1)} %bitcast.502, bf16[1024,1536]{1,0:T(8,128)(2,1)} %get-tuple-element.466, bf16[1,1024,768]{2,1,0:T(8,128)(2,1)} %param.29, f32[768]{0:T(1024)S(1)} %copy-done.65, f32[1024]{0:T(1024)S(1)} %copy-done.51), kind=kOutput, calls=%fused_computation.120 | convolution fusion | flops 5258084352 | bytes 18619392 | tf_op jit(solution)/shard_map/dot_general | solution.py:263
  986.6 8.3 fusion.85
  994.9 6.7 copy.448
  1009.1 6.7 psum.29
  1023.5 9.3 fusion.67
  1036.4 119.3 %reduce-scatter.9.cloned.1.call-done = f32[48,3328]{1,0:T(8,128)} async-done(((f32[768,3328]{1,0:T(8,128)}), f32[48,3328]{1,0:T(8,128)}) %reduce-scatter.9.cloned.1.call-update) | async-done | bytes 638992 | tf_op jit(solution)/shard_map/reduce_scatter | solution.py:273
  1156.6 41.2 %psum.31 = f32[11336]{0:T(1024)S(1)} all-reduce(f32[11336]{0:T(1024)S(1)} %concatenate.27), channel_id=1, replica_groups=mesh['dp'=16,'seq'=2] {'dp','seq'}, use_global_device_ids=true, to_apply=%region_38.39 | all-reduce | flops 11336 | bytes 90688 | tf_op jit(solution)/shard_map/psum | solution.py:289
  1227.4 10.3 add_multiply_fusion
  (434 shorter events, 412.5 us)
Async XLA Ops:
  7.2 1202.3 %copy-start = (f32[2,26,128,128]{3,2,1,0:T(8,128)S(1)}, f32[2,26,128,128]{3,2,1,0:T(8,128)}, u32[]{:S(2)}) copy-start(f32[2,26,128,128]{3,2,1,0:T(8,128)} %param.44) | copy-start | bytes 10223620
  7.2 61.5 %all-gather.6.cloned.1.call-start = ((), (), s32[]{:S(2)}) async-start(), calls=%async_computation.10 | async-start | bytes 5431296 | tf_op jit(solution)/shard_map/all_gather | solution.py:131
  9.3 158.1 %all-gather.10.cloned.1.call-start = ((), (), s32[]{:S(2)}) async-start(), calls=%async_computation.15 | async-start | bytes 1572864 | tf_op jit(solution)/shard_map/all_gather | solution.py:152
  11.7 91.4 %copy-start.50 = (f32[1024]{0:T(1024)}, f32[1024]{0:T(1024)S(1)}, u32[]{:S(2)}) copy-start(f32[1024]{0:T(1024)S(1)} %fusion.145) | copy-start | bytes 12292
  11.7 72.0 %copy-start.71 = (f32[48,24]{0,1:T(8,128)S(1)}, f32[48,24]{0,1:T(8,128)}, u32[]{:S(2)}) copy-start(f32[48,24]{0,1:T(8,128)} %param.32) | copy-start | bytes 13828
  11.7 91.4 %copy-start.64 = (f32[768]{0:T(1024)S(1)}, f32[768]{0:T(1024)}, u32[]{:S(2)}) copy-start(f32[768]{0:T(1024)} %param.34) | copy-start | bytes 9220
  11.7 102.0 %slice-start = ((f32[4,1792]{1,0:T(4,128)}), f32[4,256]{1,0:T(4,128)S(1)}, s32[]{:S(2)}) async-start(f32[4,1792]{1,0:T(4,128)} %param.35), calls=%async_computation.18 | async-start | bytes 8192 | tf_op jit(solution)/shard_map/jvp()/slice | solution.py:161
  103.2 43.5 %copy-start.37 = (bf16[768,24]{0,1:T(8,128)(2,1)}, bf16[768,24]{0,1:T(8,128)(2,1)S(1)}, u32[]{:S(2)}) copy-start(bf16[768,24]{0,1:T(8,128)(2,1)S(1)} %reshape.1002) | copy-start | bytes 110596
  105.8 11.8 all-to-all-start.1
  109.1 339.0 %all-gather.8.cloned.1.call-start = ((), (), s32[]{:S(2)}) async-start(), calls=%async_computation.11 | async-start | bytes 2506752 | tf_op jit(solution)/shard_map/all_gather | solution.py:133
  115.6 15.6 %copy-start.74 = (f32[12]{0:T(128)}, f32[12]{0:T(128)S(1)}, u32[]{:S(2)}) copy-start(f32[12]{0:T(128)S(1)} %fusion.147) | copy-start | bytes 148
  116.4 14.9 %copy-start.62 = (f32[12]{0:T(128)}, f32[12]{0:T(128)S(1)}, u32[]{:S(2)}) copy-start(f32[12]{0:T(128)S(1)} %dynamic_slice.52) | copy-start | bytes 148
  119.3 46.4 %copy-start.16 = (f32[1,8,256,12]{2,1,3,0:T(8,128)}, f32[1,8,256,12]{2,1,3,0:T(8,128)S(1)}, u32[]{:S(2)}) copy-start(f32[1,8,256,12]{2,1,3,0:T(8,128)S(1)} %reshape.988) | copy-start | bytes 294916
  135.4 20.6 %copy-start.46 = (f32[8,12,2]{0,2,1:T(2,128)}, f32[8,12,2]{0,2,1:T(2,128)S(1)}, u32[]{:S(2)}) copy-start(f32[8,12,2]{0,2,1:T(2,128)S(1)} %copy.379) | copy-start | bytes 2308
  150.6 42.3 %all-to-all-start = ((bf16[1,1024,2,768]{3,1,0,2:T(8,128)(2,1)}), bf16[1,1024,2,768]{3,1,0,2:T(8,128)(2,1)}, u32[]{:S(2)}, u32[]{:S(2)}) async-start(bf16[1,1024,2,768]{3,1,0,2:T(8,128)(2,1)} %copy.371), calls=%async_computation | async-start | bytes 6291456 | tf_op jit(solution)/shard_map/all_to_all | solution.py:148
  160.7 34.7 %copy-start.32 = (f32[1,8,1,12]{1,3,0,2:T(8,128)}, f32[1,8,1,12]{1,3,0,2:T(8,128)S(1)}, u32[]{:S(2)}) copy-start(f32[1,8,1,12]{1,3,0,2:T(8,128)S(1)} %copy.461) | copy-start | bytes 1156
  246.1 12.2 copy-start.5
  342.8 37.0 %copy-start.12 = (f32[8,256,768]{1,2,0}, f32[8,256,768]{1,2,0:S(1)}, u32[]{:S(2)}) copy-start(f32[8,256,768]{1,2,0:S(1)} %fusion.168) | copy-start | bytes 18874372
  344.7 35.1 %copy-start.23 = (f32[8,256,256]{2,1,0:T(8,128)}, f32[8,256,256]{2,1,0:T(8,128)S(1)}, u32[]{:S(2)}) copy-start(f32[8,256,256]{2,1,0:T(8,128)S(1)} %fusion.167) | copy-start | bytes 6291460
  448.2 10.3 copy-start.68
  448.2 10.3 copy-start.6
  448.2 10.3 copy-start.11
  472.8 40.5 %all-to-all-start.3 = ((bf16[1,1024,2,768]{1,3,0,2:T(8,128)(2,1)}), bf16[1,1024,2,768]{1,3,0,2:T(8,128)(2,1)}, u32[]{:S(2)}, u32[]{:S(2)}) async-start(bf16[1,1024,2,768]{1,3,0,2:T(8,128)(2,1)} %bitcast.495), calls=%async_computation.3 | async-start | bytes 6291456 | tf_op jit(solution)/shard_map/all_to_all | solution.py:213
  478.1 490.4 %reduce-scatter.7.cloned.1.call-start = ((), (), s32[]{:S(2)}) async-start(), calls=%async_computation.12 | async-start | bytes 1572864 | tf_op jit(solution)/shard_map/reduce_scatter | solution.py:243
  660.8 18.1 %copy-start.4 = (f32[8,1,12,128,64]{4,3,2,1,0:T(8,128)S(1)}, f32[8,1,12,128,64]{4,3,2,1,0:T(8,128)}, u32[]{:S(2)}) copy-start(f32[8,1,12,128,64]{4,3,2,1,0:T(8,128)} %get-tuple-element.191) | copy-start | bytes 9437188
  712.9 12.6 %copy-start.42 = (f32[8,256,12]{1,2,0:T(8,128)S(1)}, f32[8,256,12]{1,2,0:T(8,128)}, u32[]{:S(2)}) copy-start(f32[8,256,12]{1,2,0:T(8,128)} %copy.382) | copy-start | bytes 294916
  725.5 34.3 %copy-start.20 = (bf16[1,8,256,12,64]{2,1,4,3,0:T(8,128)(2,1)S(1)}, bf16[1,8,256,12,64]{2,1,4,3,0:T(8,128)(2,1)}, u32[]{:S(2)}) copy-start(bf16[1,8,256,12,64]{2,1,4,3,0:T(8,128)(2,1)} %reshape.962) | copy-start | bytes 9437188
  725.5 34.3 %copy-start.24 = (f32[8,256,256]{2,1,0:T(8,128)S(1)}, f32[8,256,256]{2,1,0:T(8,128)}, u32[]{:S(2)}) copy-start(f32[8,256,256]{2,1,0:T(8,128)} %copy-done.23) | copy-start | bytes 6291460
  725.5 34.3 %copy-start.44 = (f32[8,256,12]{1,2,0:T(8,128)S(1)}, f32[8,256,12]{1,2,0:T(8,128)}, u32[]{:S(2)}) copy-start(f32[8,256,12]{1,2,0:T(8,128)} %copy.380) | copy-start | bytes 294916
  725.5 34.3 %copy-start.45 = (f32[8,256,12]{1,2,0:T(8,128)S(1)}, f32[8,256,12]{1,2,0:T(8,128)}, u32[]{:S(2)}) copy-start(f32[8,256,12]{1,2,0:T(8,128)} %copy.415) | copy-start | bytes 294916
  725.5 34.3 %copy-start.48 = (pred[256,256]{1,0:T(8,128)(4,1)S(1)}, pred[256,256]{1,0:T(8,128)(4,1)}, u32[]{:S(2)}) copy-start(pred[256,256]{1,0:T(8,128)(4,1)} %iota_compare_fusion) | copy-start | bytes 196612
  725.5 34.3 %copy-start.82 = (f32[12]{0:T(128)S(1)}, f32[12]{0:T(128)}, u32[]{:S(2)}) copy-start(f32[12]{0:T(128)} %dynamic_slice.54) | copy-start | bytes 148
  813.1 21.8 %copy-start.53 = (f32[1,1024]{1,0:T(1,128)S(1)}, f32[1,1024]{1,0:T(1,128)}, u32[]{:S(2)}) copy-start(f32[1,1024]{1,0:T(1,128)} %get-tuple-element.476) | copy-start | bytes 12292
  813.1 21.8 %copy-start.55 = (f32[1,1024]{1,0:T(1,128)S(1)}, f32[1,1024]{1,0:T(1,128)}, u32[]{:S(2)}) copy-start(f32[1,1024]{1,0:T(1,128)} %get-tuple-element.477) | copy-start | bytes 12292
  813.2 21.8 %copy-start.57 = (f32[1,1024]{1,0:T(1,128)S(1)}, f32[1,1024]{1,0:T(1,128)}, u32[]{:S(2)}) copy-start(f32[1,1024]{1,0:T(1,128)} %get-tuple-element.478) | copy-start | bytes 12292
  813.2 21.8 %copy-start.59 = (f32[1,1024]{1,0:T(1,128)S(1)}, f32[1,1024]{1,0:T(1,128)}, u32[]{:S(2)}) copy-start(f32[1,1024]{1,0:T(1,128)} %get-tuple-element.479) | copy-start | bytes 12292
  854.4 154.0 %reduce-scatter.13.cloned.1.call-start = ((), (), s32[]{:S(2)}) async-start(), calls=%async_computation.16 | async-start | bytes 417792
  858.7 42.6 %copy-start.51 = (f32[1024]{0:T(1024)S(1)}, f32[1024]{0:T(1024)}, u32[]{:S(2)}) copy-start(f32[1024]{0:T(1024)} %copy-done.50) | copy-start | bytes 12292
  904.3 132.1 %reduce-scatter.11.cloned.1.call-start = ((), (), s32[]{:S(2)}) async-start(), calls=%async_computation.14 | async-start | bytes 5013504 | tf_op jit(solution)/shard_map/reduce_scatter | solution.py:275
  912.6 243.1 %reduce-scatter.9.cloned.1.call-start = ((), (), s32[]{:S(2)}) async-start(), calls=%async_computation.13 | async-start | bytes 10862592 | tf_op jit(solution)/shard_map/reduce_scatter | solution.py:273
  982.0 222.6 %all-reduce.19.cloned.1.call-start = ((), (), s32[]{:S(2)}) async-start(), calls=%async_computation.17 | async-start | bytes 1867776 | tf_op jit(solution)/shard_map/psum | solution.py:277
  1032.9 122.8 %copy-start.61 = (f32[1024]{0:T(1024)S(1)}, f32[1024]{0:T(1024)}, u32[]{:S(2)}) copy-start(f32[1024]{0:T(1024)} %copy-done.60) | copy-start | bytes 12292
  1197.8 11.7 copy-start.36
  1227.4 10.4 copy-start.15
  1227.4 10.4 copy-start.31
  1227.4 11.7 copy-start.26
  1227.4 15.5 %copy-start.21 = (f32[48,3328]{1,0:T(8,128)S(1)}, f32[48,3328]{1,0:T(8,128)}, u32[]{:S(2)}) copy-start(f32[48,3328]{1,0:T(8,128)} %get-tuple-element.625) | copy-start | bytes 1916932
  1227.4 16.3 %copy-start.28 = (f32[96,768]{1,0:T(8,128)S(1)}, f32[96,768]{1,0:T(8,128)}, u32[]{:S(2)}) copy-start(f32[96,768]{1,0:T(8,128)} %get-tuple-element.627) | copy-start | bytes 884740
  (47 other events, 286.7 us)
Sparse Core Ops, SparseCore 0:
  10.9 57.7 all-gather.5
  83.8 19.8 all-gather.9
  112.8 40.0 all-gather.7
  854.5 16.4 reduce-scatter.6
  904.4 52.1 reduce-scatter.12
  960.4 74.6 reduce-scatter.10
  1039.2 116.4 reduce-scatter.8
  1158.0 37.8 all-reduce.18
where the time goes:
time: 1260 us; the launch traced here: 1250 us
  local copies, waits for them, and re-layouts  302 us (24%)
  matrix products  286 us (23%)
  other arithmetic  254 us (20%)
  waiting for transfers between devices  231 us (18%)
  blocking collectives  149 us (12%)
  between operations  15.5 us (1%)
  starting transfers between devices  14.4 us (1%)
    reduce_scatter x1, waiting for transfers between devices, body(): lax.psum_scatter(in_partial, 'dp', scatter_dimension=0, tiled=True)  119 us
    dot_general x3, matrix products, state_space(): inner_part = jnp.einsum('cqsh,cshp->cqhp', mixing, blocks_x, precision=HIGH)  89.9 us
    dynamic_slice x32, local copies, waits for them, and re-layouts, state_space(): lax.scan(jax.checkpoint(carry_step), initial, (fresh_state, factor))  62.9 us
    all_gather x1, waiting for transfers between devices, body(): lax.all_gather(in_weight.astype(jnp.bfloat16), 'dp', axis=0, tiled=True)  56.9 us
    another operation x6, other arithmetic  44.2 us
    psum x1, blocking collectives, body(): vector_grad = lax.psum(vector_local, ('dp', 'seq'))  41.2 us
    all_to_all x1, blocking collectives, body(): lax.all_to_all(states_out, 'seq', split_axis=1, concat_axis=3, tiled=True)  38.7 us
    dot_general x3, matrix products, state_space(): jnp.einsum('csn,cshp->chnp', blocks_b, weights[..., None] * blocks_x, pre...  37.1 us
  transfers between devices with their start and end apart: 11, of which 4 were waited for; matrix products, arithmetic and copies ran while one was open for 33% of the time, Pallas kernels for 0%

commit v1 on v0

v1 whole, which is shorter than its diff:
```python
import functools

import jax
import jax.numpy as jnp
from jax import lax
from jax.experimental import pallas as pl
from jax.experimental.pallas import tpu as pltpu
from jax.sharding import PartitionSpec as P

D = 768
HEADS = 24
HEADDIM = 64
DSTATE = 128
KCONV = 4
DI = 1536
CONVCH = 1792
INCOLS = 3328

BL = 128
PAIRS = HEADS // 2
ROWS = 16

AXES = ("z", "x", "core")

EPS = 1e-05
LR = 0.25
LR_VEC = 0.02
NEG = -1e30
BF = jnp.bfloat16
F32 = jnp.float32
HIGH = lax.Precision.HIGHEST
NN = (((1,), (0,)), ((), ()))
NT = (((1,), (1,)), ((), ()))
TN = (((0,), (0,)), ((), ()))


def dot(a, b, dims=NN):
    return lax.dot_general(a, b, dims, preferred_element_type=F32)


def split2(v):
    high = v.astype(BF)
    return high, (v - high.astype(F32)).astype(BF)


def dot3(a, b, dims=NN):
    ah, al = split2(a)
    bh, bl = split2(b)
    return dot(ah, bh, dims) + dot(al, bh, dims) + dot(ah, bl, dims)


def pack(v):
    high = v.astype(BF).astype(F32)
    rest = v - high
    mid = rest.astype(BF).astype(F32)
    low = rest - mid
    return (high + pltpu.roll(mid, 32, 1) + pltpu.roll(low, 64, 1)).astype(BF)


def head_lanes(shape):
    return lax.broadcasted_iota(jnp.int32, shape, 1) < HEADS


def prefix(tri, v):
    parts = dot(tri, pack(v))
    total = parts + pltpu.roll(parts, 96, 1) + pltpu.roll(parts, 64, 1)
    return jnp.where(head_lanes(total.shape), total, 0.0)


def expand(v, emat):
    return dot(pack(v), emat)


def head_sum(v, gather):
    high, low = split2(v)
    return dot(high, gather) + dot(low, gather)


def tri_mask(lower):
    rows = lax.broadcasted_iota(jnp.int32, (BL, BL), 0)
    cols = lax.broadcasted_iota(jnp.int32, (BL, BL), 1)
    return (rows >= cols) if lower else (cols >= rows)


def softplus(v):
    return jnp.maximum(v, 0.0) + jnp.log1p(jnp.exp(-jnp.abs(v)))


def sigmoid(v):
    return 1.0 / (1.0 + jnp.exp(-v))


def rates(alog_ref):
    rate = -jnp.exp(alog_ref[0:1, :])
    return jnp.where(head_lanes(rate.shape), rate, 0.0)


def pair_blocks(v):
    left = lax.broadcasted_iota(jnp.int32, v.shape, 1) < HEADDIM
    return jnp.concatenate([jnp.where(left, v, 0.0), jnp.where(left, 0.0, v)], axis=0).astype(BF)


def norm_rows(u, gain):
    inv = lax.rsqrt(jnp.mean(u * u, axis=-1, keepdims=True) + EPS)
    return u * inv * gain


def first_kernel(
    u_ref, halo_ref, gain_ref, wm_ref, wdt_ref, cw_ref, cb_ref, dtb_ref, alog_ref, emat_ref,
    normed_ref, mixed_ref, pre_ref, z_ref, state_ref, total_ref,
    tail, full,
):
    step_index = pl.program_id(1)
    tile = u_ref.shape[1]
    gain = gain_ref[0:1, :]

    @pl.when(step_index == 0)
    def _():
        near = norm_rows(halo_ref[0].astype(F32), gain).astype(BF)
        tail[...] = dot(near, wm_ref[...]).astype(BF).astype(F32)
        state_ref[...] = jnp.zeros_like(state_ref)
        total_ref[...] = jnp.zeros_like(total_ref)

    normed = norm_rows(u_ref[0].astype(F32), gain).astype(BF)
    normed_ref[0] = normed
    mixed_low = dot(normed, wm_ref[...]).astype(BF)
    mixed_ref[0] = mixed_low
    mixed = mixed_low.astype(F32)
    z = dot(normed, wdt_ref[...]).astype(BF).astype(F32) + dtb_ref[0:1, :]
    z_ref[0] = z
    full[0:8, :] = tail[...]
    full[8:, :] = mixed
    tail[...] = mixed[tile - 8 :, :]
    pre = cb_ref[0:1, :] + cw_ref[KCONV - 1 : KCONV, :] * mixed
    for tap in range(KCONV - 1):
        pre = pre + cw_ref[tap : tap + 1, :] * full[5 + tap : 5 + tap + tile, :]
    pre_ref[0] = pre
    conv = pre * sigmoid(pre)
    step_all = softplus(z)
    rate = rates(alog_ref)
    tri = jnp.where(tri_mask(True), 1.0, 0.0).astype(BF)
    emat = emat_ref[...]
    for part in range(tile // BL):
        rows = slice(part * BL, (part + 1) * BL)
        step = step_all[rows]
        cum = prefix(tri, step * rate)
        last = cum[BL - 1 : BL, :]
        weights = expand(jnp.exp(last - cum) * step, emat)
        decay = expand(
            jnp.where(head_lanes((8, 128)), jnp.broadcast_to(jnp.exp(last), (8, 128)), 0.0), emat
        )[0:1, :]
        inputs_b = conv[rows, DI : DI + DSTATE]
        fresh = dot3(inputs_b.T, weights * conv[rows, :DI])
        state_ref[0] = state_ref[0] * decay + fresh
        total_ref[0] = total_ref[0] + jnp.broadcast_to(last, (8, 128))


def second_kernel(
    pre_ref, z_ref, gate_ref, bgrad_ref, u_ref, enter_ref, wo_ref, skip_ref, ggain_ref, alog_ref,
    emat_ref, gmat_ref,
    out_ref, branch_ref, dy_ref, ggrad_ref, state_ref, rdot_ref, dstate_ref, gain_acc, skip_acc,
    state, running, xs, ys, es,
):
    step_index = pl.program_id(1)
    tile = pre_ref.shape[1]
    parts = tile // BL

    @pl.when(step_index == 0)
    def _():
        state[...] = enter_ref[0]
        running[...] = jnp.ones_like(running)
        dstate_ref[...] = jnp.zeros_like(dstate_ref)

    @pl.when((step_index == 0) & (pl.program_id(0) == 0))
    def _():
        gain_acc[...] = jnp.zeros_like(gain_acc)
        skip_acc[...] = jnp.zeros_like(skip_acc)

    rate = rates(alog_ref)
    mask = tri_mask(True)
    tri = jnp.where(mask, 1.0, 0.0).astype(BF)
    emat = emat_ref[...]
    cts = []
    for part in range(parts):
        rows = slice(part * BL, (part + 1) * BL)
        pre = pre_ref[0, rows, :]
        conv = pre * sigmoid(pre)
        x = conv[:, :DI]
        inputs_b = conv[:, DI : DI + DSTATE]
        inputs_c = conv[:, DI + DSTATE :]
        step = softplus(z_ref[0, rows, :])
        cum = prefix(tri, step * rate)
        cum_t = cum.T
        last = cum[BL - 1 : BL, :]
        lanes = head_lanes(cum.shape)
        wide = expand(
            jnp.concatenate(
                [step, jnp.where(lanes, jnp.exp(cum), 0.0), jnp.exp(last - cum) * step], axis=0
            ),
            emat,
        )
        grown = wide[BL : 2 * BL]
        decay = grown[BL - 1 : BL, :]
        scaled = wide[:BL] * x
        scores = dot3(inputs_c, inputs_b, NT)
        held = state[...]
        state_ref[0, part] = held
        outer = grown * dot3(inputs_c, held)
        state[...] = held * decay + dot3(inputs_b.T, wide[2 * BL :] * x)
        for pair in range(PAIRS):
            cols = slice(pair * 128, (pair + 1) * 128)
            mixing = []
            for h in (2 * pair, 2 * pair + 1):
                spread = jnp.where(mask, cum[:, h : h + 1] - cum_t[h : h + 1, :], NEG)
                mixing.append(scores * jnp.exp(spread))
            mh, ml = split2(jnp.concatenate(mixing, axis=1))
            piece = scaled[:, cols]
            high = piece.astype(BF).astype(F32)
            rh, rl = pair_blocks(high), pair_blocks(piece - high)
            inner = dot(mh, rh) + dot(ml, rh) + dot(mh, rl)
            ys[rows, cols] = inner + outer[:, cols]
        xs[rows, :] = x
        es[rows, :] = grown * running[0:1, :]
        running[...] = running[...] * decay
        cts.append(inputs_c.T)

    gain = ggain_ref[0:1, :]
    skip = skip_ref[0:1, :]

    def rows_step(r, carry):
        rows = pl.ds(pl.multiple_of(r * ROWS, ROWS), ROWS)
        x = xs[rows, :]
        yhat = ys[rows, :]
        states = (yhat + skip * x).astype(BF).astype(F32)
        gate = gate_ref[rows, :]
        sg = sigmoid(gate)
        sl = gate * sg
        gated = states * sl
        inv = lax.rsqrt(jnp.mean(gated * gated, axis=-1, keepdims=True) + EPS)
        norm = gated * inv
        branch_ref[rows, :] = (norm * gain).astype(BF)
        bg = bgrad_ref[rows, :]
        tg = bg * gain
        gain_acc[...] += bg * norm
        dot_row = jnp.mean(tg * norm, axis=-1, keepdims=True)
        dgated = inv * (tg - norm * dot_row)
        dy_low = (dgated * sl).astype(BF)
        dy_ref[rows, :] = dy_low
        ggrad_ref[rows, :] = (dgated * states * (sg * (1.0 + gate * (1.0 - sg)))).astype(BF)
        dy = dy_low.astype(F32)
        skip_acc[...] += dy * x
        ys[rows, :] = dy * yhat
        es[rows, :] = es[rows, :] * dy
        return carry

    lax.fori_loop(0, tile // ROWS, rows_step, 0)
    out_ref[0] = (u_ref[0].astype(F32) + dot(branch_ref[...], wo_ref[...])).astype(BF)
    rdot_ref[0] = head_sum(ys[...], gmat_ref[...])
    for part in range(parts):
        rows = slice(part * BL, (part + 1) * BL)
        dstate_ref[0] = dstate_ref[0] + dot3(cts[part], es[rows, :])


def third_kernel(
    pre_ref, mixed_ref, z_ref, dy_ref, state_ref, rdot_ref, leave_ref, cw_ref, skip_ref, alog_ref,
    emat_ref, gmat_ref,
    mgrad_ref, dz_ref, last_ref, first_ref, cw_acc, cb_acc, dtb_acc, rate_acc,
    dstate, tail, full,
):
    step_index = pl.program_id(1)

    @pl.when(step_index == 0)
    def _():
        dstate[...] = leave_ref[0]
        tail[...] = jnp.zeros_like(tail)

    @pl.when((step_index == 0) & (pl.program_id(0) == 0))
    def _():
        for ref in (cw_acc, cb_acc, dtb_acc, rate_acc):
            ref[...] = jnp.zeros_like(ref)

    rate = rates(alog_ref)
    mask = tri_mask(False)
    low_tri = jnp.where(tri_mask(True), 1.0, 0.0).astype(BF)
    high_tri = jnp.where(mask, 1.0, 0.0).astype(BF)
    emat = emat_ref[...]
    gmat = gmat_ref[...]
    skip = skip_ref[0:1, :]
    pre = pre_ref[0]
    sg = sigmoid(pre)
    conv = pre * sg
    x = conv[:, :DI]
    inputs_b = conv[:, DI : DI + DSTATE]
    inputs_c = conv[:, DI + DSTATE :]
    z = z_ref[0]
    step = softplus(z)
    cum = prefix(low_tri, step * rate)
    cum_t = cum.T
    last = cum[BL - 1 : BL, :]
    lanes = head_lanes(cum.shape)
    wide = expand(
        jnp.concatenate(
            [
                step,
                jnp.where(lanes, jnp.exp(cum), 0.0),
                jnp.where(lanes, jnp.exp(last - cum), 0.0),
            ],
            axis=0,
        ),
        emat,
    )
    dt_wide, grown, shrink = wide[:BL], wide[BL : 2 * BL], wide[2 * BL :]
    decay = grown[BL - 1 : BL, :]
    scaled = dt_wide * x
    dy = dy_ref[...].astype(F32)
    held = state_ref[0, 0]
    ds = dstate[...]
    scores_t = dot3(inputs_b, inputs_c, NT)
    dscaled_state = shrink * dot3(inputs_b, ds)
    dscores_t = jnp.zeros((BL, BL), F32)
    pieces = []
    for pair in range(PAIRS):
        cols = slice(pair * 128, (pair + 1) * 128)
        kernels = []
        for h in (2 * pair, 2 * pair + 1):
            spread = jnp.where(mask, cum_t[h : h + 1, :] - cum[:, h : h + 1], NEG)
            kernels.append(jnp.exp(spread))
        mh, ml = split2(jnp.concatenate([scores_t * k for k in kernels], axis=1))
        dyb = pair_blocks(dy[:, cols])
        pieces.append(dot(mh, dyb) + dot(ml, dyb))
        sh, sl = split2(scaled[:, cols])
        dmix = dot(sh, dyb, NT) + dot(sl, dyb, NT)
        dscores_t = dscores_t + dmix[:, :BL] * kernels[0] + dmix[:, BL:] * kernels[1]
    dscaled = jnp.concatenate(pieces, axis=1) + dscaled_state
    dx = dt_wide * dscaled + skip * dy
    grown_dy = grown * dy
    ends = jnp.sum(scaled * dscaled_state, axis=0, keepdims=True) + decay * jnp.sum(
        held * ds, axis=0, keepdims=True
    )
    sums = head_sum(
        jnp.concatenate([x * dscaled, jnp.broadcast_to(ends, (8, DI))], axis=0), gmat
    )
    direct = sums[:BL]
    is_last = lax.broadcasted_iota(jnp.int32, (BL, 128), 0) == BL - 1
    dcum = rdot_ref[0] - step * direct + jnp.where(is_last, sums[BL : BL + 1, :], 0.0)
    dcum = jnp.where(lanes, dcum, 0.0)
    drate = prefix(high_tri, dcum)
    dz = (rate * drate + direct) * sigmoid(z)
    dz_ref[0] = dz.astype(BF)
    dtb_acc[...] += jnp.sum(dz.reshape(BL // 8, 8, 128), axis=0)
    rate_acc[...] += jnp.sum((step * drate).reshape(BL // 8, 8, 128), axis=0)
    db = dot3(dscores_t, inputs_c) + dot3(shrink * scaled, ds, NT)
    dc = dot3(dscores_t.T, inputs_b) + dot3(grown_dy, held, NT)
    dstate[...] = decay * ds + dot3(inputs_c.T, grown_dy)
    dpre = jnp.concatenate([dx, db, dc], axis=1) * (sg * (1.0 + pre * (1.0 - sg)))
    full[0:BL, :] = dpre
    full[BL:, :] = tail[...]
    tail[...] = dpre[0:8, :]
    first_ref[0] = dpre[0:8, :]
    mixed = mixed_ref[0].astype(F32)
    cb_acc[...] += jnp.sum(dpre.reshape(BL // 8, 8, CONVCH), axis=0)
    mgrad = jnp.zeros_like(dpre)
    for tap in range(KCONV):
        moved = full[KCONV - 1 - tap : KCONV - 1 - tap + BL, :]
        mgrad = mgrad + cw_ref[tap : tap + 1, :] * moved
        cw_acc[tap] += jnp.sum((moved * mixed).reshape(BL // 8, 8, CONVCH), axis=0)
    mgrad_ref[0] = mgrad.astype(BF)

    @pl.when(step_index == 0)
    def _():
        last_ref[0] = mgrad[BL - 8 :, :]


PARAMS = dict(vmem_limit_bytes=60 * 1024 * 1024)


def whole(shape):
    zeros = (0,) * len(shape)
    return pl.BlockSpec(shape, lambda b, i: zeros)


def run_first(u, halo, gain, wm, wdt, cw, cb, dtb, alog, emat):
    seqs, length, _ = u.shape
    tile = min(256, length)
    grid = (seqs, length // tile)
    tok = lambda width: pl.BlockSpec((1, tile, width), lambda b, i: (b, i, 0))
    per = lambda *shape: pl.BlockSpec((1,) + shape, lambda b, i: (b,) + (0,) * len(shape))
    return pl.pallas_call(
        first_kernel,
        grid=grid,
        in_specs=[
            tok(D), per(8, D), whole(gain.shape), whole(wm.shape), whole(wdt.shape),
            whole(cw.shape), whole(cb.shape), whole(dtb.shape), whole(alog.shape), whole(emat.shape),
        ],
        out_specs=[
            tok(D), tok(CONVCH), tok(CONVCH), tok(128), per(DSTATE, DI), per(8, 128),
        ],
        out_shape=[
            jax.ShapeDtypeStruct((seqs, length, D), BF),
            jax.ShapeDtypeStruct((seqs, length, CONVCH), BF),
            jax.ShapeDtypeStruct((seqs, length, CONVCH), F32),
            jax.ShapeDtypeStruct((seqs, length, 128), F32),
            jax.ShapeDtypeStruct((seqs, DSTATE, DI), F32),
            jax.ShapeDtypeStruct((seqs, 8, 128), F32),
        ],
        scratch_shapes=[pltpu.VMEM((8, CONVCH), F32), pltpu.VMEM((tile + 8, CONVCH), F32)],
        compiler_params=pltpu.CompilerParams(**PARAMS),
        name="first",
    )(u, halo, gain, wm, wdt, cw, cb, dtb, alog, emat)


def run_second(pre, z, gate, bgrad, u, enter, wo, skip, ggain, alog, emat, gmat):
    seqs, length, _ = u.shape
    tile = min(256, length)
    steps = length // tile
    parts = tile // BL
    grid = (seqs, steps)
    tok = lambda width: pl.BlockSpec((1, tile, width), lambda b, i: (b, i, 0))
    flat = lambda width: pl.BlockSpec((tile, width), lambda b, i: (b * steps + i, 0))
    per = lambda *shape: pl.BlockSpec((1,) + shape, lambda b, i: (b,) + (0,) * len(shape))
    rows = seqs * length
    return pl.pallas_call(
        second_kernel,
        grid=grid,
        in_specs=[
            tok(CONVCH), tok(128), flat(DI), flat(DI), tok(D), per(DSTATE, DI), whole(wo.shape),
            whole(skip.shape), whole(ggain.shape), whole(alog.shape), whole(emat.shape),
            whole(gmat.shape),
        ],
        out_specs=[
            tok(D), flat(DI), flat(DI), flat(DI),
            pl.BlockSpec((1, parts, DSTATE, DI), lambda b, i: (b, i, 0, 0)),
            tok(128), per(DSTATE, DI), whole((ROWS, DI)), whole((ROWS, DI)),
        ],
        out_shape=[
            jax.ShapeDtypeStruct((seqs, length, D), BF),
            jax.ShapeDtypeStruct((rows, DI), BF),
            jax.ShapeDtypeStruct((rows, DI), BF),
            jax.ShapeDtypeStruct((rows, DI), BF),
            jax.ShapeDtypeStruct((seqs, length // BL, DSTATE, DI), F32),
            jax.ShapeDtypeStruct((seqs, length, 128), F32),
            jax.ShapeDtypeStruct((seqs, DSTATE, DI), F32),
            jax.ShapeDtypeStruct((ROWS, DI), F32),
            jax.ShapeDtypeStruct((ROWS, DI), F32),
        ],
        scratch_shapes=[
            pltpu.VMEM((DSTATE, DI), F32), pltpu.VMEM((8, DI), F32), pltpu.VMEM((tile, DI), F32),
            pltpu.VMEM((tile, DI), F32), pltpu.VMEM((tile, DI), F32),
        ],
        compiler_params=pltpu.CompilerParams(**PARAMS),
        name="second",
    )(pre, z, gate, bgrad, u, enter, wo, skip, ggain, alog, emat, gmat)


def run_third(pre, mixed, z, dy, states, rdot, leave, cw, skip, alog, emat, gmat):
    seqs, length, _ = pre.shape
    steps = length // BL
    grid = (seqs, steps)
    tok = lambda width: pl.BlockSpec((1, BL, width), lambda b, i: (b, steps - 1 - i, 0))
    per = lambda *shape: pl.BlockSpec((1,) + shape, lambda b, i: (b,) + (0,) * len(shape))
    return pl.pallas_call(
        third_kernel,
        grid=grid,
        in_specs=[
            tok(CONVCH), tok(CONVCH), tok(128),
            pl.BlockSpec((BL, DI), lambda b, i: (b * steps + steps - 1 - i, 0)),
            pl.BlockSpec((1, 1, DSTATE, DI), lambda b, i: (b, steps - 1 - i, 0, 0)),
            tok(128), per(DSTATE, DI), whole(cw.shape), whole(skip.shape), whole(alog.shape),
            whole(emat.shape), whole(gmat.shape),
        ],
        out_specs=[
            tok(CONVCH), tok(128), per(8, CONVCH), per(8, CONVCH), whole((KCONV, 8, CONVCH)),
            whole((8, CONVCH)), whole((8, 128)), whole((8, 128)),
        ],
        out_shape=[
            jax.ShapeDtypeStruct((seqs, length, CONVCH), BF),
            jax.ShapeDtypeStruct((seqs, length, 128), BF),
            jax.ShapeDtypeStruct((seqs, 8, CONVCH), F32),
            jax.ShapeDtypeStruct((seqs, 8, CONVCH), F32),
            jax.ShapeDtypeStruct((KCONV, 8, CONVCH), F32),
            jax.ShapeDtypeStruct((8, CONVCH), F32),
            jax.ShapeDtypeStruct((8, 128), F32),
            jax.ShapeDtypeStruct((8, 128), F32),
        ],
        scratch_shapes=[
            pltpu.VMEM((DSTATE, DI), F32), pltpu.VMEM((8, CONVCH), F32),
            pltpu.VMEM((BL + 8, CONVCH), F32),
        ],
        compiler_params=pltpu.CompilerParams(**PARAMS),
        name="third",
    )(pre, mixed, z, dy, states, rdot, leave, cw, skip, alog, emat, gmat)


def norm_piece(incoming, norm_gain):
    inv_rms = lax.rsqrt(jnp.mean(incoming * incoming, axis=-1, keepdims=True) + EPS)
    return incoming * inv_rms * norm_gain


def kron_update(gradient, left_stat, right_stat, left_root, right_root):
    row_tiles, col_tiles = (left_stat.shape[0], left_stat.shape[1])
    row_size, col_size = (left_stat.shape[-1], right_stat.shape[-1])
    grad_tiles = gradient.reshape(row_tiles, row_size, col_tiles, col_size).transpose(0, 2, 1, 3)
    left_new = 0.5 * left_stat + 0.5 * jnp.einsum(
        "abij,abkj->abik", grad_tiles, grad_tiles, precision=HIGH
    )
    right_new = 0.5 * right_stat + 0.5 * jnp.einsum(
        "abji,abjk->abik", grad_tiles, grad_tiles, precision=HIGH
    )
    shaped = jnp.einsum("abij,abjk->abik", left_root, grad_tiles, precision=HIGH)
    shaped = jnp.einsum("abij,abjk->abik", shaped, right_root, precision=HIGH)
    update = (-LR * shaped).transpose(0, 2, 1, 3).reshape(gradient.shape)
    return (update, left_new, right_new)


def swapped(v, axis, size, offset):
    return lax.ppermute(v, axis, [(i, (i + offset) % size) for i in range(size)])


def pick(v, index):
    return lax.dynamic_index_in_dim(v, index, 0, keepdims=False)


def scatter_stage(v, axis, kind=BF):
    size = lax.axis_size(axis)
    here = lax.axis_index(axis)
    total = pick(v, here)
    for offset in range(1, size):
        sent = pick(v, lax.rem(here + offset, size)).astype(kind)
        total = total + swapped(sent, axis, size, offset).astype(F32)
    return total


def gather_stage(v, axis):
    size = lax.axis_size(axis)
    here = lax.axis_index(axis)
    out = jnp.zeros((size,) + v.shape, v.dtype)
    out = lax.dynamic_update_index_in_dim(out, v, here, 0)
    for offset in range(1, size):
        got = swapped(v, axis, size, offset)
        out = lax.dynamic_update_index_in_dim(out, got, lax.rem(here - offset + size, size), 0)
    return out


def core_sum(partial):
    z, x, core = (lax.axis_size(a) for a in ("z", "x", "core"))
    rows, cols = partial.shape
    blocks = partial.reshape(z, x, core, rows // (z * x * core), cols)
    return scatter_stage(jnp.moveaxis(blocks, 2, 0), "core", F32)


def across(v):
    return scatter_stage(scatter_stage(jnp.moveaxis(v, 1, 0), "x"), "z")


def reduce_plain(v):
    owned = across(v)
    total = owned
    size = lax.axis_size("seq")
    if size > 2:
        return lax.psum(owned, "seq")
    for offset in range(1, size):
        total = total + swapped(owned, "seq", size, offset)
    return total


def reduce_split(v):
    size = lax.axis_size("seq")
    z, x, rows, cols = v.shape
    if cols % (128 * size):
        return reduce_plain(v)
    v = jnp.moveaxis(v.reshape(z, x, rows, size, cols // size), 3, 0)
    owned = across(scatter_stage(v, "seq"))
    return jnp.moveaxis(gather_stage(owned, "seq"), 0, 1).reshape(rows, cols)


def row8(v, width=None):
    v = v.reshape(1, -1)
    if width is not None:
        v = jnp.pad(v, ((0, 0), (0, width - v.shape[1])))
    return jnp.broadcast_to(v, (8, v.shape[1]))


def body(
    block_input,
    cotangent,
    in_weight,
    dt_weight,
    out_weight,
    norm_gain,
    conv_weight,
    conv_bias,
    dt_bias,
    decay_log,
    skip_gain,
    gate_gain,
    in_left,
    in_right,
    in_left_root,
    in_right_root,
    dt_left,
    dt_right,
    dt_left_root,
    dt_right_root,
    out_left,
    out_right,
    out_left_root,
    out_right_root,
    vector_moment,
):
    seq_count, local_len, _ = block_input.shape
    seq_devices = lax.axis_size("seq")
    row_count = seq_count * local_len
    up = [(i, i + 1) for i in range(seq_devices - 1)]
    down = [(i + 1, i) for i in range(seq_devices - 1)]

    in_low = in_weight.astype(BF)
    dt_low = jnp.pad(dt_weight.astype(BF), ((0, 0), (0, 128 - HEADS)))
    main = lax.all_gather(
        jnp.concatenate([in_low[:, DI:], dt_low], axis=1), AXES, axis=0, tiled=True
    )
    wg = lax.all_gather(in_low[:, :DI], AXES, axis=0, tiled=True)
    wo = lax.all_gather(out_weight.astype(BF), AXES, axis=0, tiled=True)
    wm, wdt = main[:, :CONVCH], main[:, CONVCH:]
    halo = lax.ppermute(block_input[:, local_len - 8 :, :], "seq", up)

    part = jnp.arange(128)
    channel = jnp.arange(DI)
    emat = (
        ((part[:, None] % 32) == (channel[None, :] // HEADDIM)) & (part[:, None] < 96)
    ).astype(BF)
    gmat = ((channel[:, None] // HEADDIM) == part[None, :]).astype(BF)
    skip_wide = row8(jnp.repeat(skip_gain, HEADDIM))
    alog = row8(decay_log, 128)
    dtb = row8(jnp.concatenate([dt_bias, jnp.full((128 - HEADS,), -1e4, F32)]))
    cw8 = jnp.pad(conv_weight, ((0, 4), (0, 0)))

    normed, mixed, pre, z, local_state, total = run_first(
        block_input, halo, row8(norm_gain), wm, wdt, cw8, row8(conv_bias), dtb, alog, emat
    )
    span = jnp.repeat(jnp.exp(total[:, 0:1, :HEADS]), HEADDIM, axis=2)
    enter = lax.ppermute(local_state, "seq", up)
    for _ in range(seq_devices - 2):
        enter = lax.ppermute(local_state + span * enter, "seq", up)

    normed_rows = normed.reshape(row_count, D)
    upstream = cotangent.reshape(row_count, D)
    gate_part = dot(normed_rows, wg)
    branch_grad = dot(upstream, wo, NT)
    (
        block_output, branch, states_grad, gate_grad, states, rdot, local_dstate, gain_acc, skip_acc,
    ) = run_second(
        pre, z, gate_part, branch_grad, block_input, enter, wo, skip_wide, row8(gate_gain), alog,
        emat, gmat,
    )
    leave = lax.ppermute(local_dstate, "seq", down)
    for _ in range(seq_devices - 2):
        leave = lax.ppermute(local_dstate + span * leave, "seq", down)

    out_grad = reduce_split(core_sum(dot(branch, upstream, TN)))
    gate_sum = reduce_plain(core_sum(dot(normed_rows, gate_grad, TN)))

    mgrad, dz, last8, first8, cw_acc, cb_acc, dtb_acc, rate_acc = run_third(
        pre, mixed, z, states_grad, states, rdot, leave, cw8, skip_wide, alog, emat, gmat
    )
    near = lax.ppermute(first8, "seq", down)
    ends = mixed[:, local_len - 8 :, :].astype(F32)
    extra = jnp.stack(
        [
            sum(conv_weight[k] * near[:, j - k, :] for k in range(j + 1))
            for j in range(KCONV - 1)
        ],
        axis=1,
    )
    last8 = last8 + jnp.pad(extra, ((0, 0), (8 - (KCONV - 1), 0), (0, 0)))
    mgrad = lax.dynamic_update_slice(mgrad, last8.astype(BF), (0, local_len - 8, 0))
    cw_extra = jnp.stack(
        [
            sum(
                (near[:, j - k, :] * ends[:, 8 - (KCONV - 1) + j, :] for j in range(k, KCONV - 1)),
                jnp.zeros((seq_count, CONVCH), F32),
            ).sum(0)
            for k in range(KCONV)
        ]
    )
    conv_weight_grad = cw_acc.sum(1) + cw_extra
    conv_bias_grad = cb_acc.sum(0)

    mgrad_rows = mgrad.reshape(row_count, CONVCH)
    dz_rows = dz.reshape(row_count, 128)
    mixed_local = jnp.concatenate(
        [
            dot(normed_rows, mgrad_rows, TN),
            dot(normed_rows, dz_rows, TN),
        ],
        axis=1,
    )
    mixed_chip = core_sum(mixed_local)
    third_cols = mixed_chip.shape[3] // 3
    mixed_sum = jnp.concatenate(
        [
            reduce_plain(mixed_chip[..., :third_cols]),
            reduce_split(mixed_chip[..., third_cols:]),
        ],
        axis=1,
    )
    normed_grad = (
        dot(gate_grad, wg, NT) + dot(mgrad_rows, wm, NT) + dot(dz_rows, wdt, NT)
    )
    incoming = block_input.reshape(row_count, D).astype(F32)
    _, norm_back = jax.vjp(norm_piece, incoming, norm_gain)
    input_part, norm_gain_grad = norm_back(normed_grad)
    input_grad = (input_part + upstream.astype(F32)).reshape(block_input.shape)

    vector_local = jnp.concatenate(
        [
            norm_gain_grad,
            gain_acc.sum(0),
            conv_weight_grad.reshape(-1),
            conv_bias_grad,
            dtb_acc.sum(0)[:HEADS],
            -jnp.exp(decay_log) * rate_acc.sum(0)[:HEADS],
            skip_acc.sum(0).reshape(HEADS, HEADDIM).sum(1),
        ]
    )
    vector_grad = lax.psum(vector_local, AXES + ("seq",))

    in_grad = jnp.concatenate([gate_sum, mixed_sum[:, :CONVCH]], axis=1)
    dt_grad = mixed_sum[:, CONVCH : CONVCH + HEADS]

    in_update, in_left_new, in_right_new = kron_update(
        in_grad, in_left, in_right, in_left_root, in_right_root
    )
    dt_update, dt_left_wide, dt_right_wide = kron_update(
        dt_grad, dt_left[:, None], dt_right[:, None], dt_left_root[:, None], dt_right_root[:, None]
    )
    out_update, out_left_new, out_right_new = kron_update(
        out_grad, out_left, out_right, out_left_root, out_right_root
    )
    vector_moment_new = 0.5 * vector_moment + 0.5 * vector_grad * vector_grad
    vector_update = -LR_VEC * vector_grad * lax.rsqrt(vector_moment_new)
    return (
        block_output,
        input_grad,
        in_grad,
        dt_grad,
        out_grad,
        in_update,
        dt_update,
        out_update,
        in_left_new,
        in_right_new,
        dt_left_wide[:, 0],
        dt_right_wide[:, 0],
        out_left_new,
        out_right_new,
        vector_grad,
        vector_moment_new,
        vector_update,
    )


def solution(mesh):
    dp, seq = mesh.shape["dp"], mesh.shape["seq"]
    split = (4, dp // 8, 2)
    torus = jax.sharding.Mesh(mesh.devices.reshape(split + (seq,)), AXES + ("seq",))
    tokens = P(AXES, "seq", None)
    rows = P(AXES, None)
    tri = P(AXES, None, None)
    quad = P(AXES, None, None, None)
    placed = (
        (tokens, tokens, rows, rows, rows) + (P(),) * 7 + (quad,) * 4 + (tri,) * 4 + (quad,) * 4 + (P(),)
    )
    return jax.shard_map(
        body,
        mesh=torus,
        in_specs=placed,
        out_specs=(tokens, tokens)
        + (rows,) * 6
        + (quad, quad, tri, tri, quad, quad)
        + (P(), P(), P()),
        check_vma=False,
    )
```

time: 1260 us -> 522 us (0.41)
  matrix products: 286 us -> 69 us
  other arithmetic: 254 us -> 40.6 us
  local copies, waits for them, and re-layouts: 302 us -> 92.4 us
  waiting for transfers between devices: 231 us -> 86.9 us
  Pallas kernels: 0 us -> 112 us
  blocking collectives: 149 us -> 46.9 us
  starting transfers between devices: 14.4 us -> 51.7 us
    dot_general x19 -> x9, matrix products: 240 us -> 39.6 us  [dot(): return lax.dot_general(a, b, dims, preferred_element_type=F32)]
    reduce_scatter x3 -> x0, waiting for transfers between devices: 119 us -> none  [the longest x1 119 us: body(): lax.psum_scatter(in_partial, 'dp', scatter_dimension=0, tiled=True)]
    pallas_call x0 -> x3, Pallas kernels: none -> 112 us  [the longest x1 49.1 us: run_second(): pl.pallas_call(second_kernel, grid=grid, in_specs=[tok(CONVCH), tok(128),...]
    all_to_all x3 -> x0, blocking collectives: 81.6 us -> none  [the longest x1 38.7 us: body(): lax.all_to_all(states_out, 'seq', split_axis=1, concat_axis=3, tiled=True)]
    dynamic_slice x36 -> x0, local copies, waits for them, and re-layouts: 66.3 us -> none  [the longest x32 62.9 us: state_space(): lax.scan(jax.checkpoint(carry_step), initial, (fresh_state, factor))]
    reduce_sum x15 -> x7, other arithmetic: 68.2 us -> 6.22 us  [the longest x2 1.55 us: body(): skip_acc.sum(0).reshape(HEADS, HEADDIM).sum(1)]
    another operation x14 -> x1, other arithmetic: 59.8 us -> 0.97 us  [body(): jnp.stack([sum((conv_weight[k] * near[:, j - k, :] for k in range(j + 1))...]
    all_to_all x3 -> x0, waiting for transfers between devices: 54.8 us -> none  [the longest x1 31.9 us: body(): lax.all_to_all(states_grad.astype(jnp.bfloat16).reshape(seq_count, local_...]
  transfers between devices with their start and end apart: 11 -> 32, of which waited for: 4 -> 12; matrix products, arithmetic and copies ran while one was open for 33% -> 28% of each run, Pallas kernels for 0% -> 12%
where the time goes in v1:
time: 522 us; the launch traced here: 514 us
  Pallas kernels  112 us (21%)
  local copies, waits for them, and re-layouts  92.4 us (18%)
  waiting for transfers between devices  86.9 us (17%)
  matrix products  69 us (13%)
  starting transfers between devices  51.7 us (10%)
  blocking collectives  46.9 us (9%)
  other arithmetic  40.6 us (8%)
  between operations  14.8 us (3%)
    pallas_call x1, Pallas kernels, run_second(): pl.pallas_call(second_kernel, grid=grid, in_specs=[tok(CONVCH), tok(128),...  49.1 us
    psum x1, blocking collectives, body(): vector_grad = lax.psum(vector_local, AXES + ('seq',))  46.9 us
    pallas_call x1, Pallas kernels, run_third(): pl.pallas_call(third_kernel, grid=grid, in_specs=[tok(CONVCH), tok(CONVCH...  45.4 us
    dot_general x9, matrix products, dot(): return lax.dot_general(a, b, dims, preferred_element_type=F32)  39.6 us
    ppermute x25, starting transfers between devices, swapped(): lax.ppermute(v, axis, [(i, (i + offset) % size) for i in range(size)])  39 us
    all_gather x1, waiting for transfers between devices, body(): lax.all_gather(jnp.concatenate([in_low[:, DI:], dt_low], axis=1), AXES, a...  38.5 us
    unnamed x111, local copies, waits for them, and re-layouts  26 us
    all_gather x1, waiting for transfers between devices, body(): wo = lax.all_gather(out_weight.astype(BF), AXES, axis=0, tiled=True)  24.8 us
  transfers between devices with their start and end apart: 32, of which 12 were waited for; matrix products, arithmetic and copies ran while one was open for 28% of the time, Pallas kernels for 12%

profile of v1, /device:TPU:0, one launch (start us, length us, event | category | flops | bytes accessed | tf_op | source)
XLA Modules:
  0.0 513.9 jit_solution(16729670989162754915)
XLA Ops:
  16.5 4.9 collective-permute-start
  21.6 2.3 copy.206
  23.9 2.3 copy.213
  31.2 24.8 %all-gather.8.cloned.1.call-done.wo_ref = bf16[1536,768]{1,0:T(8,128)(2,1)} async-done(((bf16[96,768]{1,0:T(8,128)(2,1)}), bf16[1536,768]{1,0:T(8,128)(2,1)}) %all-gather.8.cloned.1.call-update) | async-done | bytes 2359312 | tf_op jit(solution)/shard_map/all_gather | solution.py:622
  56.0 7.3 %fusion.10.bgrad_ref = f32[1024,1536]{1,0:T(8,128)} fusion(bf16[1536,768]{1,0:T(8,128)(2,1)} %all-gather.8.cloned.1.call-done.wo_ref, bf16[1,1024,768]{2,1,0:T(8,128)(2,1)} %param.26), kind=kOutput, calls=%fused_computation.24 | convolution fusion | flops 2415919104 | bytes 10223616 | tf_op jit(solution)/shard_map/dot_general | solution.py:38
  63.3 38.5 %all-gather.4.cloned.1.call-done = bf16[768,1920]{1,0:T(8,128)(2,1)} async-done(((bf16[48,1920]{1,0:T(8,128)(2,1)}), bf16[768,1920]{1,0:T(8,128)(2,1)}) %all-gather.4.cloned.1.call-update) | async-done | bytes 2949136 | tf_op jit(solution)/shard_map/all_gather | solution.py:618
  101.8 3.5 slice.100.wm_ref
  109.3 17.1 %first.1 = (bf16[1,1024,768]{2,1,0:T(8,128)(2,1)}, bf16[1,1024,1792]{2,1,0:T(8,128)(2,1)}, f32[1,1024,1792]{2,1,0:T(8,128)}, f32[1,1024,128]{2,1,0:T(8,128)}, f3...) custom-call(bf16[1,1024,768]{2,1,0:T(8,128)(2,1)} %u_ref.3, bf16[1,8,768]{2,1,0:T(8,128)(2,1)} %copy-done.36, ...), custom_call_target="tpu_custom_call" | custom-call | tf_op jit(solution)/shard_map/first/pallas_call | solution.py:388
  126.4 4.4 collective-permute-start.1
  131.6 2.6 copy.197
  134.2 11.3 %all-gather.6.cloned.1.call-done = bf16[768,1536]{1,0:T(8,128)(2,1)} async-done(((bf16[48,1536]{1,0:T(8,128)(2,1)}), bf16[768,1536]{1,0:T(8,128)(2,1)}) %all-gather.6.cloned.1.call-update) | async-done | bytes 2359312 | tf_op jit(solution)/shard_map/all_gather | solution.py:621
  145.5 7.4 %fusion.16.gate_ref = f32[1024,1536]{1,0:T(8,128)} fusion(bf16[768,1536]{1,0:T(8,128)(2,1)} %all-gather.6.cloned.1.call-done, bf16[1,1024,768]{2,1,0:T(8,128)(2,1)} %get-tuple-element.41), kind=kOutput, calls=%fused_computation.30 | convolution fusion | flops 2415919104 | bytes 10223616 | tf_op jit(solution)/shard_map/dot_general | solution.py:38
  154.2 49.1 %second.1 = (bf16[1,1024,768]{2,1,0:T(8,128)(2,1)}, bf16[1024,1536]{1,0:T(8,128)(2,1)}, bf16[1024,1536]{1,0:T(8,128)(2,1)}, bf16[1024,1536]{1,0:T(8,128)(2,1)}, ...) custom-call(f32[1,1024,1792]{2,1,0:T(8,128)} %get-tuple-element.39.p, ...), custom_call_target="tpu_custom_call" | custom-call | tf_op jit(solution)/shard_map/second/pallas_call | solution.py:422
  207.4 4.6 copy.202
  212.0 5.0 fusion.8
  221.9 2.6 fusion.6
  229.1 4.3 fusion.85
  233.4 45.4 %third.1 = (bf16[1,1024,1792]{2,1,0:T(8,128)(2,1)}, bf16[1,1024,128]{2,1,0:T(8,128)(2,1)}, f32[1,8,1792]{2,1,0:T(8,128)}, f32[1,8,1792]{2,1,0:T(8,128)}, f32[4,8...) custom-call(f32[1,1024,1792]{2,1,0:T(8,128)} %get-tuple-element.39.pre_ref, ...), custom_call_target="tpu_custom_call" | custom-call | tf_op jit(solution)/shard_map/third/pallas_call | solution.py:461
  281.3 2.8 fusion.14
  290.1 5.7 %fusion.12 = f32[768,1792]{1,0:T(8,128)S(1)} fusion(bf16[1024,1792]{1,0:T(8,128)(2,1)} %bitcast_dynamic-update-slice_fusion.1, bf16[1,1024,768]{2,1,0:T(8,128)(2,1)} %get-tuple-element.41), kind=kOutput, calls=%fused_computation.26 | convolution fusion | flops 2818572288 | bytes 10747904 | tf_op jit(solution)/shard_map/dot_general | solution.py:38
  298.1 2.6 copy-done.2
  301.9 3.0 fusion.81
  308.0 2.6 fusion.1
  310.6 3.5 bitcast_add_fusion.1
  314.1 3.9 reshape.462
  318.0 2.7 dynamic-slice_convert_fusion
  321.6 4.2 collective-permute-start.23
  325.8 2.8 bitcast_add_fusion.2
  331.7 46.9 %psum.7 = f32[11336]{0:T(1024)} all-reduce(f32[11336]{0:T(1024)S(1)} %concatenate.23), channel_id=1, replica_groups=mesh['z'=4,'x'=2,'core'=2,'seq'=2] {'z','x','core','seq'}, use_global_device_ids=true, to_apply=%region_10.11 | all-reduce | flops 11336 | bytes 90688 | tf_op jit(solution)/shard_map/psum | solution.py:725
  378.6 3.0 constant_dynamic-slice_fusion
  382.9 2.3 collective-permute-start.24
  391.9 3.3 collective-permute-done.6
  395.2 5.9 %collective-permute-start.26 = (bf16[96,384]{1,0:T(8,128)(2,1)S(1)}, bf16[96,384]{1,0:T(8,128)(2,1)S(1)}, u32[]{:S(2)}, u32[]{:S(2)}) collective-permute-start(bf16[96,384]{1,0:T(8,128)(2,1)S(1)} %get-tuple-element.191), channel_id=1, source_target_pairs={{0,16},{8,24},{16,0},{24,8},{1,17},{9,25},{17,1},{25,9},{2,18},{10... | collective-permute-start | bytes 221192 | tf_op jit(solution)/shard_map/ppermute | solution.py:516
  401.0 4.2 collective-permute-start.27
  410.4 4.1 dynamic_update_slice.21
  417.4 4.1 dynamic_update_slice.22
  423.5 2.4 fusion.49
  425.9 5.4 %add_multiply_fusion.1 = f32[4,6,128,128]{3,2,1,0:T(8,128)} fusion(f32[4,6,128,128]{3,2,1,0:T(8,128)} %param.46, f32[4,6,24,128]{3,1,2,0:T(8,128)} %bitcast.265), kind=kOutput, calls=%fused_computation.32 | convolution fusion | flops 114032640 | bytes 3440640 | tf_op jit(solution)/shard_map/abji,abjk->abik/dot_general | solution.py:506
  431.3 3.0 bitcast_add_fusion
  437.5 3.2 reshape.460
  440.7 2.6 constant_dynamic-slice_fusion.1
  449.3 4.7 collective-permute-done.16
  457.9 2.6 collective-permute-start.13
  474.7 3.6 dynamic_update_slice.20
  483.2 10.1 %add_multiply_fusion = f32[2,26,128,128]{3,2,1,0:T(8,128)} fusion(f32[2,26,128,128]{3,2,1,0:T(8,128)} %param.38, f32[2,24,26,128]{3,2,1,0:T(8,128)} %reshape.464), kind=kOutput, calls=%fused_computation.6 | convolution fusion | flops 247070720 | bytes 7454720 | tf_op jit(solution)/shard_map/abji,abjk->abik/dot_general | solution.py:506
  494.8 3.0 fusion.19
  499.2 2.3 fusion.18
  501.5 2.2 copy.224
  (256 shorter events, 108.8 us)
Async XLA Ops:
  7.2 487.6 %copy-start = (f32[2,26,128,128]{3,2,1,0:T(8,128)S(1)}, f32[2,26,128,128]{3,2,1,0:T(8,128)}, u32[]{:S(2)}) copy-start(f32[2,26,128,128]{3,2,1,0:T(8,128)} %param.40) | copy-start | bytes 10223620
  7.2 14.2 %copy-start.43 = (f32[24]{0:T(128)S(1)}, f32[24]{0:T(128)}, u32[]{:S(2)}) copy-start(f32[24]{0:T(128)} %param.35) | copy-start | bytes 292
  7.2 18.9 %copy-start.26 = (f32[4,1792]{1,0:T(4,128)S(1)}, f32[4,1792]{1,0:T(4,128)}, u32[]{:S(2)}) copy-start(f32[4,1792]{1,0:T(4,128)} %param.31) | copy-start | bytes 86020
  7.2 19.6 %copy-start.46 = (f32[24]{0:T(128)S(1)}, f32[24]{0:T(128)}, u32[]{:S(2)}) copy-start(f32[24]{0:T(128)} %param.33) | copy-start | bytes 292
  7.2 20.1 %copy-start.47 = (f32[24]{0:T(128)S(1)}, f32[24]{0:T(128)}, u32[]{:S(2)}) copy-start(f32[24]{0:T(128)} %param.34) | copy-start | bytes 292
  7.2 48.7 %all-gather.8.cloned.1.call-start = ((), (), s32[]{:S(2)}) async-start(), calls=%async_computation.2 | async-start | bytes 2506752 | tf_op jit(solution)/shard_map/all_gather | solution.py:622
  9.1 92.7 %all-gather.4.cloned.1.call-start = ((), (), s32[]{:S(2)}) async-start(), calls=%async_computation | async-start | bytes 3133440 | tf_op jit(solution)/shard_map/all_gather | solution.py:618
  14.1 131.4 %all-gather.6.cloned.1.call-start = ((), (), s32[]{:S(2)}) async-start(), calls=%async_computation.1 | async-start | bytes 2506752 | tf_op jit(solution)/shard_map/all_gather | solution.py:621
  16.5 90.4 %collective-permute-start = (bf16[1,8,768]{2,1,0:T(8,128)(2,1)S(1)}, bf16[1,8,768]{2,1,0:T(8,128)(2,1)S(1)}, u32[]{:S(2)}, u32[]{:S(2)}) collective-permute-start(bf16[1,8,768]{2,1,0:T(8,128)(2,1)S(1)} %slice.78), channel_id=1, source_target_pairs={{0,1},{2,3},{4,5},{6,7},{8,9},{10,11},{12,13},{14,15},{16,17},{18,... | collective-permute-start | bytes 36872 | tf_op jit(solution)/shard_map/ppermute | solution.py:624
  63.3 44.2 %copy-start.38 = (f32[1792]{0:T(1024)S(1)}, f32[1792]{0:T(1024)}, u32[]{:S(2)}) copy-start(f32[1792]{0:T(1024)} %param.32) | copy-start | bytes 21508
  63.3 44.8 %copy-start.28 = (f32[768]{0:T(1024)S(1)}, f32[768]{0:T(1024)}, u32[]{:S(2)}) copy-start(f32[768]{0:T(1024)} %param.30) | copy-start | bytes 9220
  126.4 26.5 %collective-permute-start.1 = (f32[1,128,1536]{2,1,0:T(8,128)}, f32[1,128,1536]{2,1,0:T(8,128)}, u32[]{:S(2)}, u32[]{:S(2)}) collective-permute-start(f32[1,128,1536]{2,1,0:T(8,128)} %get-tuple-element.42), channel_id=1, source_target_pairs={{0,1},{2,3},{4,5},{6,7},{8,9},{10,11},{12,13},{14,15},{16,17},{18,... | collective-permute-start | bytes 2359304 | tf_op jit(solution)/shard_map/ppermute | solution.py:641
  134.2 19.4 %copy-start.37 = (f32[1536]{0:T(1024)S(1)}, f32[1536]{0:T(1024)}, u32[]{:S(2)}) copy-start(f32[1536]{0:T(1024)} %param.36) | copy-start | bytes 18436
  203.3 30.1 %collective-permute-start.2 = (f32[1,128,1536]{2,1,0:T(8,128)}, f32[1,128,1536]{2,1,0:T(8,128)}, u32[]{:S(2)}, u32[]{:S(2)}) collective-permute-start(f32[1,128,1536]{2,1,0:T(8,128)} %get-tuple-element.49), channel_id=1, source_target_pairs={{1,0},{3,2},{5,4},{7,6},{9,8},{11,10},{13,12},{15,14},{17,16},{19,... | collective-permute-start | bytes 2359304 | tf_op jit(solution)/shard_map/ppermute | solution.py:655
  218.7 91.8 %collective-permute-start.22 = (f32[4,2,96,768]{3,2,1,0:T(8,128)}, f32[4,2,96,768]{3,2,1,0:T(8,128)}, u32[]{:S(2)}, u32[]{:S(2)}) collective-permute-start(f32[4,2,96,768]{3,2,1,0:T(8,128)} %dynamic-slice_bitcast_fusion.1), channel_id=1, source_target_pairs={{0,2},{2,0},{1,3},{3,1},{4,6},{6,4},{5,7},{7,5},{8,10},{10,8},{9,1... | collective-permute-start | bytes 7077896 | tf_op jit(solution)/shard_map/ppermute | solution.py:516
  228.2 97.6 %collective-permute-start.4 = (f32[4,2,48,1536]{3,2,1,0:T(8,128)}, f32[4,2,48,1536]{3,2,1,0:T(8,128)}, u32[]{:S(2)}, u32[]{:S(2)}) collective-permute-start(f32[4,2,48,1536]{3,2,1,0:T(8,128)} %dynamic-slice_bitcast_fusion.2), channel_id=1, source_target_pairs={{0,2},{2,0},{1,3},{3,1},{4,6},{6,4},{5,7},{7,5},{8,10},{10,8},{9,1... | collective-permute-start | bytes 7077896 | tf_op jit(solution)/shard_map/ppermute | solution.py:516
  278.8 8.8 %collective-permute-start.3 = (f32[1,8,1792]{2,1,0:T(8,128)}, f32[1,8,1792]{2,1,0:T(8,128)}, u32[]{:S(2)}, u32[]{:S(2)}) collective-permute-start(f32[1,8,1792]{2,1,0:T(8,128)} %get-tuple-element.52), channel_id=1, source_target_pairs={{1,0},{3,2},{5,4},{7,6},{9,8},{11,10},{13,12},{15,14},{17,16},{19,... | collective-permute-start | bytes 172040 | tf_op jit(solution)/shard_map/ppermute | solution.py:665
  296.2 14.3 %slice-start = ((s8[4718592]{0:T(1024)(128)(4,1)}), s8[4194304]{0:T(1024)(128)(4,1)S(1)}, s32[]{:S(2)}) async-start(s8[4718592]{0:T(1024)(128)(4,1)} %bitcast.262), calls=%async_computation.3 | async-start | bytes 8388608
  300.6 130.7 %collective-permute-start.10 = (f32[4,2,48,1920]{3,2,1,0:T(8,128)}, f32[4,2,48,1920]{3,2,1,0:T(8,128)}, u32[]{:S(2)}, u32[]{:S(2)}) collective-permute-start(f32[4,2,48,1920]{3,2,1,0:T(8,128)} %dynamic-slice_bitcast_fusion), channel_id=1, source_target_pairs={{0,2},{2,0},{1,3},{3,1},{4,6},{6,4},{5,7},{7,5},{8,10},{10,8},{9,1... | collective-permute-start | bytes 8847368 | tf_op jit(solution)/shard_map/ppermute | solution.py:516
  321.6 60.0 %collective-permute-start.23 = (bf16[4,2,96,384]{3,2,1,0:T(8,128)(2,1)}, bf16[4,2,96,384]{3,2,1,0:T(8,128)(2,1)}, u32[]{:S(2)}, u32[]{:S(2)}) collective-permute-start(bf16[4,2,96,384]{3,2,1,0:T(8,128)(2,1)} %bitcast.255), channel_id=1, source_target_pairs={{0,1},{1,0},{2,3},{3,2},{4,5},{5,4},{6,7},{7,6},{8,9},{9,8},{10,11... | collective-permute-start | bytes 1769480 | tf_op jit(solution)/shard_map/ppermute | solution.py:516
  330.9 54.3 %collective-permute-start.5 = (bf16[4,48,1536]{2,1,0:T(8,128)(2,1)}, bf16[4,48,1536]{2,1,0:T(8,128)(2,1)}, u32[]{:S(2)}, u32[]{:S(2)}) collective-permute-start(bf16[4,48,1536]{2,1,0:T(8,128)(2,1)} %fusion.30), channel_id=1, source_target_pairs={{0,4},{4,0},{1,5},{5,1},{2,6},{6,2},{3,7},{7,3},{8,12},{12,8},{9,1... | collective-permute-start | bytes 1769480 | tf_op jit(solution)/shard_map/ppermute | solution.py:516
  382.9 25.3 %copy-start.25 = (f32[11336]{0:T(1024)S(1)}, f32[11336]{0:T(1024)}, u32[]{:S(2)}) copy-start(f32[11336]{0:T(1024)} %psum.7) | copy-start | bytes 136036
  382.9 25.3 %copy-start.27 = (f32[11336]{0:T(1024)S(1)}, f32[11336]{0:T(1024)}, u32[]{:S(2)}) copy-start(f32[11336]{0:T(1024)} %param.49) | copy-start | bytes 136036
  382.9 8.4 %collective-permute-start.24 = (bf16[4,96,384]{2,1,0:T(8,128)(2,1)S(1)}, bf16[4,96,384]{2,1,0:T(8,128)(2,1)S(1)}, u32[]{:S(2)}, u32[]{:S(2)}) collective-permute-start(bf16[4,96,384]{2,1,0:T(8,128)(2,1)S(1)} %fusion.36), channel_id=1, source_target_pairs={{0,4},{4,0},{1,5},{5,1},{2,6},{6,2},{3,7},{7,3},{8,12},{12,8},{9,1... | collective-permute-start | bytes 884744 | tf_op jit(solution)/shard_map/ppermute | solution.py:516
  386.5 8.6 %collective-permute-start.6 = (bf16[48,1536]{1,0:T(8,128)(2,1)S(1)}, bf16[48,1536]{1,0:T(8,128)(2,1)S(1)}, u32[]{:S(2)}, u32[]{:S(2)}) collective-permute-start(bf16[48,1536]{1,0:T(8,128)(2,1)S(1)} %get-tuple-element.186), channel_id=1, source_target_pairs={{0,8},{8,16},{16,24},{24,0},{1,9},{9,17},{17,25},{25,1},{2,10},{10... | collective-permute-start | bytes 442376 | tf_op jit(solution)/shard_map/ppermute | solution.py:516
  387.0 14.1 %collective-permute-start.7 = (bf16[48,1536]{1,0:T(8,128)(2,1)S(1)}, bf16[48,1536]{1,0:T(8,128)(2,1)S(1)}, u32[]{:S(2)}, u32[]{:S(2)}) collective-permute-start(bf16[48,1536]{1,0:T(8,128)(2,1)S(1)} %get-tuple-element.188), channel_id=1, source_target_pairs={{0,16},{8,24},{16,0},{24,8},{1,17},{9,25},{17,1},{25,9},{2,18},{10... | collective-permute-start | bytes 442376 | tf_op jit(solution)/shard_map/ppermute | solution.py:516
  388.9 16.3 %collective-permute-start.8 = (bf16[48,1536]{1,0:T(8,128)(2,1)S(1)}, bf16[48,1536]{1,0:T(8,128)(2,1)S(1)}, u32[]{:S(2)}, u32[]{:S(2)}) collective-permute-start(bf16[48,1536]{1,0:T(8,128)(2,1)S(1)} %get-tuple-element.187), channel_id=1, source_target_pairs={{0,24},{8,0},{16,8},{24,16},{1,25},{9,1},{17,9},{25,17},{2,26},{10... | collective-permute-start | bytes 442376 | tf_op jit(solution)/shard_map/ppermute | solution.py:516
  391.5 15.3 %collective-permute-start.25 = (bf16[96,384]{1,0:T(8,128)(2,1)S(1)}, bf16[96,384]{1,0:T(8,128)(2,1)S(1)}, u32[]{:S(2)}, u32[]{:S(2)}) collective-permute-start(bf16[96,384]{1,0:T(8,128)(2,1)S(1)} %get-tuple-element.189), channel_id=1, source_target_pairs={{0,8},{8,16},{16,24},{24,0},{1,9},{9,17},{17,25},{25,1},{2,10},{10... | collective-permute-start | bytes 221192 | tf_op jit(solution)/shard_map/ppermute | solution.py:516
  395.2 11.9 %collective-permute-start.26 = (bf16[96,384]{1,0:T(8,128)(2,1)S(1)}, bf16[96,384]{1,0:T(8,128)(2,1)S(1)}, u32[]{:S(2)}, u32[]{:S(2)}) collective-permute-start(bf16[96,384]{1,0:T(8,128)(2,1)S(1)} %get-tuple-element.191), channel_id=1, source_target_pairs={{0,16},{8,24},{16,0},{24,8},{1,17},{9,25},{17,1},{25,9},{2,18},{10... | collective-permute-start | bytes 221192 | tf_op jit(solution)/shard_map/ppermute | solution.py:516
  401.0 6.2 %collective-permute-start.27 = (bf16[96,384]{1,0:T(8,128)(2,1)S(1)}, bf16[96,384]{1,0:T(8,128)(2,1)S(1)}, u32[]{:S(2)}, u32[]{:S(2)}) collective-permute-start(bf16[96,384]{1,0:T(8,128)(2,1)S(1)} %get-tuple-element.190), channel_id=1, source_target_pairs={{0,24},{8,0},{16,8},{24,16},{1,25},{9,1},{17,9},{25,17},{2,26},{10... | collective-permute-start | bytes 221192 | tf_op jit(solution)/shard_map/ppermute | solution.py:516
  406.0 8.5 %collective-permute-start.9 = (f32[48,1536]{1,0:T(8,128)}, f32[48,1536]{1,0:T(8,128)}, u32[]{:S(2)}, u32[]{:S(2)}) collective-permute-start(f32[48,1536]{1,0:T(8,128)} %fusion.38), channel_id=1, source_target_pairs={{0,1},{1,0},{2,3},{3,2},{4,5},{5,4},{6,7},{7,6},{8,9},{9,8},{10,11... | collective-permute-start | bytes 884744 | tf_op jit(solution)/shard_map/ppermute | solution.py:516
  407.3 9.1 %collective-permute-start.28 = (f32[96,384]{1,0:T(8,128)S(1)}, f32[96,384]{1,0:T(8,128)}, u32[]{:S(2)}, u32[]{:S(2)}) collective-permute-start(f32[96,384]{1,0:T(8,128)S(1)} %fusion.55), channel_id=1, source_target_pairs={{0,1},{1,0},{2,3},{3,2},{4,5},{5,4},{6,7},{7,6},{8,9},{9,8},{10,11... | collective-permute-start | bytes 442376 | tf_op jit(solution)/shard_map/ppermute | solution.py:516
  443.4 10.7 %collective-permute-start.16 = (bf16[4,2,48,640]{3,2,1,0:T(8,128)(2,1)S(1)}, bf16[4,2,48,640]{3,2,1,0:T(8,128)(2,1)S(1)}, u32[]{:S(2)}, u32[]{:S(2)}) collective-permute-start(bf16[4,2,48,640]{3,2,1,0:T(8,128)(2,1)S(1)} %bitcast.283), channel_id=1, source_target_pairs={{0,1},{1,0},{2,3},{3,2},{4,5},{5,4},{6,7},{7,6},{8,9},{9,8},{10,11... | collective-permute-start | bytes 1474568 | tf_op jit(solution)/shard_map/ppermute | solution.py:516
  447.3 8.3 %collective-permute-start.11 = (bf16[4,48,640]{2,1,0:T(8,128)(2,1)S(1)}, bf16[4,48,640]{2,1,0:T(8,128)(2,1)S(1)}, u32[]{:S(2)}, u32[]{:S(2)}) collective-permute-start(bf16[4,48,640]{2,1,0:T(8,128)(2,1)S(1)} %fusion.44), channel_id=1, source_target_pairs={{0,4},{4,0},{1,5},{5,1},{2,6},{6,2},{3,7},{7,3},{8,12},{12,8},{9,1... | collective-permute-start | bytes 737288 | tf_op jit(solution)/shard_map/ppermute | solution.py:516
  454.1 16.1 %copy-start.10 = (f32[4,24,6,128]{3,2,1,0:T(8,128)S(1)}, f32[4,24,6,128]{3,2,1,0:T(8,128)}, u32[]{:S(2)}) copy-start(f32[4,24,6,128]{3,2,1,0:T(8,128)} %reshape_reshape.4) | copy-start | bytes 884740
  454.1 16.0 %copy-start.24 = (f32[4,6,24,24]{3,2,1,0:T(8,128)S(1)}, f32[4,6,24,24]{3,2,1,0:T(8,128)}, u32[]{:S(2)}) copy-start(f32[4,6,24,24]{3,2,1,0:T(8,128)} %param.45) | copy-start | bytes 165892
  454.2 6.4 %collective-permute-start.17 = (bf16[4,48,640]{2,1,0:T(8,128)(2,1)S(1)}, bf16[4,48,640]{2,1,0:T(8,128)(2,1)S(1)}, u32[]{:S(2)}, u32[]{:S(2)}) collective-permute-start(bf16[4,48,640]{2,1,0:T(8,128)(2,1)S(1)} %fusion.45), channel_id=1, source_target_pairs={{0,4},{4,0},{1,5},{5,1},{2,6},{6,2},{3,7},{7,3},{8,12},{12,8},{9,1... | collective-permute-start | bytes 737288 | tf_op jit(solution)/shard_map/ppermute | solution.py:516
  455.7 16.7 %copy-start.14 = (f32[2,96,384]{2,0,1:T(2,128)S(1)}, f32[2,96,384]{2,0,1:T(2,128)}, u32[]{:S(2)}) copy-start(f32[2,96,384]{2,0,1:T(2,128)} %dynamic_update_slice.22) | copy-start | bytes 884740
  455.7 7.8 %collective-permute-start.12 = (bf16[48,640]{1,0:T(8,128)(2,1)S(1)}, bf16[48,640]{1,0:T(8,128)(2,1)S(1)}, u32[]{:S(2)}, u32[]{:S(2)}) collective-permute-start(bf16[48,640]{1,0:T(8,128)(2,1)S(1)} %get-tuple-element.192), channel_id=1, source_target_pairs={{0,8},{8,16},{16,24},{24,0},{1,9},{9,17},{17,25},{25,1},{2,10},{10... | collective-permute-start | bytes 184328 | tf_op jit(solution)/shard_map/ppermute | solution.py:516
  457.9 7.7 %collective-permute-start.13 = (bf16[48,640]{1,0:T(8,128)(2,1)S(1)}, bf16[48,640]{1,0:T(8,128)(2,1)S(1)}, u32[]{:S(2)}, u32[]{:S(2)}) collective-permute-start(bf16[48,640]{1,0:T(8,128)(2,1)S(1)} %get-tuple-element.194), channel_id=1, source_target_pairs={{0,16},{8,24},{16,0},{24,8},{1,17},{9,25},{17,1},{25,9},{2,18},{10... | collective-permute-start | bytes 184328 | tf_op jit(solution)/shard_map/ppermute | solution.py:516
  460.6 5.4 %collective-permute-start.14 = (bf16[48,640]{1,0:T(8,128)(2,1)S(1)}, bf16[48,640]{1,0:T(8,128)(2,1)S(1)}, u32[]{:S(2)}, u32[]{:S(2)}) collective-permute-start(bf16[48,640]{1,0:T(8,128)(2,1)S(1)} %get-tuple-element.193), channel_id=1, source_target_pairs={{0,24},{8,0},{16,8},{24,16},{1,25},{9,1},{17,9},{25,17},{2,26},{10... | collective-permute-start | bytes 184328 | tf_op jit(solution)/shard_map/ppermute | solution.py:516
  460.7 6.2 %collective-permute-start.18 = (bf16[48,640]{1,0:T(8,128)(2,1)S(1)}, bf16[48,640]{1,0:T(8,128)(2,1)S(1)}, u32[]{:S(2)}, u32[]{:S(2)}) collective-permute-start(bf16[48,640]{1,0:T(8,128)(2,1)S(1)} %get-tuple-element.195), channel_id=1, source_target_pairs={{0,8},{8,16},{16,24},{24,0},{1,9},{9,17},{17,25},{25,1},{2,10},{10... | collective-permute-start | bytes 184328 | tf_op jit(solution)/shard_map/ppermute | solution.py:516
  462.7 6.1 %collective-permute-start.19 = (bf16[48,640]{1,0:T(8,128)(2,1)S(1)}, bf16[48,640]{1,0:T(8,128)(2,1)S(1)}, u32[]{:S(2)}, u32[]{:S(2)}) collective-permute-start(bf16[48,640]{1,0:T(8,128)(2,1)S(1)} %get-tuple-element.197), channel_id=1, source_target_pairs={{0,16},{8,24},{16,0},{24,8},{1,17},{9,25},{17,1},{25,9},{2,18},{10... | collective-permute-start | bytes 184328 | tf_op jit(solution)/shard_map/ppermute | solution.py:516
  463.5 5.3 %collective-permute-start.20 = (bf16[48,640]{1,0:T(8,128)(2,1)S(1)}, bf16[48,640]{1,0:T(8,128)(2,1)S(1)}, u32[]{:S(2)}, u32[]{:S(2)}) collective-permute-start(bf16[48,640]{1,0:T(8,128)(2,1)S(1)} %get-tuple-element.196), channel_id=1, source_target_pairs={{0,24},{8,0},{16,8},{24,16},{1,25},{9,1},{17,9},{25,17},{2,26},{10... | collective-permute-start | bytes 184328 | tf_op jit(solution)/shard_map/ppermute | solution.py:516
  466.0 7.1 %collective-permute-start.15 = (f32[48,640]{1,0:T(8,128)S(1)}, f32[48,640]{1,0:T(8,128)S(1)}, u32[]{:S(2)}, u32[]{:S(2)}) collective-permute-start(f32[48,640]{1,0:T(8,128)S(1)} %fusion.59), channel_id=1, source_target_pairs={{0,1},{1,0},{2,3},{3,2},{4,5},{5,4},{6,7},{7,6},{8,9},{9,8},{10,11... | collective-permute-start | bytes 368648 | tf_op jit(solution)/shard_map/ppermute | solution.py:516
  468.9 5.0 collective-permute-start.21
  483.2 10.1 %copy-start.4 = (f32[2,24,26,128]{3,2,1,0:T(8,128)S(1)}, f32[2,24,26,128]{3,2,1,0:T(8,128)}, u32[]{:S(2)}) copy-start(f32[2,24,26,128]{3,2,1,0:T(8,128)} %reshape.464) | copy-start | bytes 1916932
  483.2 10.1 %copy-start.16 = (f32[2,26,24,24]{3,2,1,0:T(8,128)S(1)}, f32[2,26,24,24]{3,2,1,0:T(8,128)}, u32[]{:S(2)}) copy-start(f32[2,26,24,24]{3,2,1,0:T(8,128)} %copy.206) | copy-start | bytes 359428
  (34 other events, 192.7 us)
Sparse Core Ops, SparseCore 0:
  10.9 45.0 all-gather.7
  58.7 43.0 all-gather.3
  104.7 40.8 all-gather.5

commit v2 on v1

--- a/solution.py
+++ b/solution.py
@@ -6,6 +6,7 @@
 from jax.experimental import pallas as pl
 from jax.experimental.pallas import tpu as pltpu
 from jax.sharding import PartitionSpec as P
+
 
 D = 768
 HEADS = 24
@@ -14,7 +15,6 @@
 KCONV = 4
 DI = 1536
 CONVCH = 1792
-INCOLS = 3328
 
 BL = 128
 PAIRS = HEADS // 2
@@ -28,7 +28,6 @@
 NEG = -1e30
 BF = jnp.bfloat16
 F32 = jnp.float32
-HIGH = lax.Precision.HIGHEST
 NN = (((1,), (0,)), ((), ()))
 NT = (((1,), (1,)), ((), ()))
 TN = (((0,), (0,)), ((), ()))
@@ -501,13 +500,13 @@
     row_size, col_size = (left_stat.shape[-1], right_stat.shape[-1])
     grad_tiles = gradient.reshape(row_tiles, row_size, col_tiles, col_size).transpose(0, 2, 1, 3)
     left_new = 0.5 * left_stat + 0.5 * jnp.einsum(
-        "abij,abkj->abik", grad_tiles, grad_tiles, precision=HIGH
+        "abij,abkj->abik", grad_tiles, grad_tiles, precision=lax.Precision.HIGH
     )
     right_new = 0.5 * right_stat + 0.5 * jnp.einsum(
-        "abji,abjk->abik", grad_tiles, grad_tiles, precision=HIGH
-    )
-    shaped = jnp.einsum("abij,abjk->abik", left_root, grad_tiles, precision=HIGH)
-    shaped = jnp.einsum("abij,abjk->abik", shaped, right_root, precision=HIGH)
+        "abji,abjk->abik", grad_tiles, grad_tiles, precision=lax.Precision.HIGH
+    )
+    shaped = jnp.einsum("abij,abjk->abik", left_root, grad_tiles, precision=lax.Precision.HIGH)
+    shaped = jnp.einsum("abij,abjk->abik", shaped, right_root, precision=lax.Precision.HIGH)
     update = (-LR * shaped).transpose(0, 2, 1, 3).reshape(gradient.shape)
     return (update, left_new, right_new)
 
@@ -571,6 +570,175 @@
     v = jnp.moveaxis(v.reshape(z, x, rows, size, cols // size), 3, 0)
     owned = across(scatter_stage(v, "seq"))
     return jnp.moveaxis(gather_stage(owned, "seq"), 0, 1).reshape(rows, cols)
+
+
+def xor_sum(v, axis):
+    size = lax.axis_size(axis)
+    bit = 1
+    while bit < size:
+        v = v + lax.ppermute(v, axis, [(i, i ^ bit) for i in range(size)])
+        bit *= 2
+    return v
+
+
+def fold_kernel(kinds, widths, idx, *refs):
+    refs = list(refs)
+    counts = {"split": (2, 4), "xz": (2, 2), "yx": (2, 2), "z": (2, 1), "plain": (2, 2), "halves": (2, 2)}
+    n_in = sum(counts[k][0] for k in kinds)
+    ins, outs = refs[:n_in], refs[n_in:]
+    at = pl.program_id(0)
+    z, x, y = idx[0], idx[1], idx[3]
+    for kind, (low, width, half) in zip(kinds, widths):
+        a, b = ins[0], ins[1]
+        ins = ins[2:]
+        mine, outs = outs[: counts[kind][1]], outs[counts[kind][1] :]
+        if kind in ("split", "plain"):
+            keep, send = mine[0], mine[1]
+            cols = slice(low, low + width)
+            keep[0] = a[0, x, 0, :, cols] + b[0, x, :, cols]
+            send[0] = (a[0, 1 - x, 0, :, cols] + b[0, 1 - x, :, cols]).astype(BF)
+        if kind in ("split", "halves"):
+            keep, send = mine[-2], mine[-1]
+            base = low + (width if kind == "split" else 0)
+            own = pl.ds(pl.multiple_of(base + y * half, 128), half)
+            other = pl.ds(pl.multiple_of(base + (1 - y) * half, 128), half)
+            for i in range(2):
+                keep[0, i] = a[0, i, 0, :, own] + b[0, i, :, own]
+                send[0, i] = (a[0, i, 0, :, other] + b[0, i, :, other]).astype(BF)
+        if kind == "xz":
+            own, send = mine
+            total = a[0] + b[0].astype(F32)
+            send[0] = total.astype(BF)
+
+            @pl.when(at == z)
+            def _(own=own, total=total):
+                own[...] = total
+
+        if kind == "yx":
+            keep, send = mine
+            keep[0] = a[0, x] + b[0, x].astype(F32)
+            send[0] = (a[0, 1 - x] + b[0, 1 - x].astype(F32)).astype(BF)
+        if kind == "z":
+            out = mine[0]
+
+            @pl.when(at == 0)
+            def _(out=out, a=a):
+                out[...] = a[...]
+
+            @pl.when(at != z)
+            def _(out=out, b=b):
+                out[...] += b[0].astype(F32)
+
+
+def fold(idx, jobs):
+    ins, in_specs, outs, out_specs = [], [], [], []
+
+    def step(*shape):
+        zeros = (0,) * len(shape)
+        return pl.BlockSpec((1,) + shape, lambda i, idx: (i,) + zeros)
+
+    def add_out(lead, rows, width, kind, spec=None):
+        outs.append(jax.ShapeDtypeStruct(lead + (rows, width), kind))
+        out_specs.append(spec or step(*(lead[1:] + (rows, width))))
+
+    for kind, first, second, low, width, half in jobs:
+        rows, cols = first.shape[-2:]
+        ins += [first, second]
+        if kind in ("split", "plain", "halves"):
+            in_specs.append(
+                pl.BlockSpec((1, 2, 1, rows, cols), lambda i, idx: (i, 0, idx[2], 0, 0))
+            )
+            in_specs.append(step(2, rows, cols))
+            if kind in ("split", "plain"):
+                add_out((4,), rows, width, F32)
+                add_out((4,), rows, width, BF)
+            if kind in ("split", "halves"):
+                add_out((4, 2), rows, half, F32)
+                add_out((4, 2), rows, half, BF)
+        if kind == "xz":
+            in_specs += [step(rows, cols)] * 2
+            add_out((), rows, cols, F32, pl.BlockSpec((rows, cols), lambda i, idx: (0, 0)))
+            add_out((4,), rows, cols, BF)
+        if kind == "yx":
+            in_specs += [step(2, rows, cols)] * 2
+            add_out((4,), rows, cols, F32)
+            add_out((4,), rows, cols, BF)
+        if kind == "z":
+            in_specs += [pl.BlockSpec((rows, cols), lambda i, idx: (0, 0)), step(rows, cols)]
+            add_out((), rows, cols, F32, pl.BlockSpec((rows, cols), lambda i, idx: (0, 0)))
+    return pl.pallas_call(
+        functools.partial(fold_kernel, [j[0] for j in jobs], [j[3:] for j in jobs]),
+        grid_spec=pltpu.PrefetchScalarGridSpec(
+            num_scalar_prefetch=1, grid=(4,), in_specs=in_specs, out_specs=out_specs
+        ),
+        out_shape=outs,
+        compiler_params=pltpu.CompilerParams(**PARAMS),
+        name="fold",
+    )(idx, *ins)
+
+
+def core_exchange(partial, core):
+    rows, cols = partial.shape
+    blocks = partial.reshape(4, 2, 2, rows // 16, cols)
+    sent = lax.dynamic_index_in_dim(blocks, 1 - core, 2, keepdims=False)
+    return blocks, swapped(sent, "core", 2, 1)
+
+
+def z_blocks(send):
+    return lax.all_to_all(send, "z", split_axis=0, concat_axis=0, tiled=True)
+
+
+def z_permutes(own, send, z):
+    total = own
+    for offset in range(1, 4):
+        total = total + swapped(pick(send, lax.rem(z + offset, 4)), "z", 4, offset).astype(F32)
+    return total
+
+
+def around(v, axis):
+    size = lax.axis_size(axis)
+    return jnp.stack([v] + [swapped(v, axis, size, offset) for offset in range(1, size)])
+
+
+def assemble_kernel(idx, near_ref, far_ref, out_ref, sems, *, order):
+    sizes = {"z": 4, "x": 2, "seq": 2}
+    here = {"z": idx[0], "x": idx[1], "core": idx[2], "seq": idx[3]}
+    copies = []
+    for a in range(near_ref.shape[0]):
+        for b in range(near_ref.shape[1]):
+            for c in range(near_ref.shape[2]):
+                at = dict(
+                    (axis, lax.rem(here[axis] - back + sizes[axis], sizes[axis]))
+                    for axis, back in zip(order[::-1], (a, b, c))
+                )
+                for ref, core in ((near_ref, here["core"]), (far_ref, 1 - here["core"])):
+                    block = ((at["z"] * 2 + at["x"]) * 2 + core) * 2 + at["seq"]
+                    copies.append(
+                        pltpu.make_async_copy(
+                            ref.at[a, b, c], out_ref.at[block], sems.at[len(copies)]
+                        )
+                    )
+    for copy in copies:
+        copy.start()
+    for copy in copies:
+        copy.wait()
+
+
+def assemble(idx, near, far, order):
+    rows, cols = near.shape[-2:]
+    out = pl.pallas_call(
+        functools.partial(assemble_kernel, order=order),
+        grid_spec=pltpu.PrefetchScalarGridSpec(
+            num_scalar_prefetch=1,
+            grid=(1,),
+            in_specs=[pl.BlockSpec(memory_space=pl.ANY)] * 2,
+            out_specs=pl.BlockSpec(memory_space=pl.ANY),
+            scratch_shapes=[pltpu.SemaphoreType.DMA((32,))],
+        ),
+        out_shape=jax.ShapeDtypeStruct((32, rows, cols), near.dtype),
+        name="assemble",
+    )(idx, near, far)
+    return out.reshape(32 * rows, cols)
 
 
 def row8(v, width=None):
@@ -618,8 +786,22 @@
     main = lax.all_gather(
         jnp.concatenate([in_low[:, DI:], dt_low], axis=1), AXES, axis=0, tiled=True
     )
-    wg = lax.all_gather(in_low[:, :DI], AXES, axis=0, tiled=True)
-    wo = lax.all_gather(out_weight.astype(BF), AXES, axis=0, tiled=True)
+    torus_sizes = tuple(lax.axis_size(a) for a in ("z", "x", "core", "seq"))
+    direct = torus_sizes == (4, 2, 2, 2)
+    idx = jnp.stack([lax.axis_index(a) for a in ("z", "x", "core", "seq")]).astype(jnp.int32)
+    gate_low, out_low = in_low[:, :DI], out_weight.astype(BF)
+    if direct:
+        order = ("z", "x", "seq")
+        gate_near = pick(gate_low.reshape(2, -1, DI), idx[3])
+        out_near = pick(out_low.reshape(2, -1, D), idx[3])
+        gate_near = around(around(gate_near, "z"), "x")
+        out_near = around(around(out_near, "z"), "x")
+        main, _, _ = lax.optimization_barrier((main, gate_near, out_near))
+        gate_near = around(gate_near, "seq")
+        out_near = around(out_near, "seq")
+    else:
+        wg = lax.all_gather(gate_low, AXES, axis=0, tiled=True)
+        wo = lax.all_gather(out_low, AXES, axis=0, tiled=True)
     wm, wdt = main[:, :CONVCH], main[:, CONVCH:]
     halo = lax.ppermute(block_input[:, local_len - 8 :, :], "seq", up)
 
@@ -642,6 +824,11 @@
     for _ in range(seq_devices - 2):
         enter = lax.ppermute(local_state + span * enter, "seq", up)
 
+    if direct:
+        out_far = swapped(out_near, "core", 2, 1)
+        gate_far = swapped(gate_near, "core", 2, 1)
+        wo = assemble(idx, out_near, out_far, order)
+        wg = assemble(idx, gate_near, gate_far, order)
     normed_rows = normed.reshape(row_count, D)
     upstream = cotangent.reshape(row_count, D)
     gate_part = dot(normed_rows, wg)
@@ -656,12 +843,42 @@
     for _ in range(seq_devices - 2):
         leave = lax.ppermute(local_dstate + span * leave, "seq", down)
 
-    out_grad = reduce_split(core_sum(dot(branch, upstream, TN)))
-    gate_sum = reduce_plain(core_sum(dot(normed_rows, gate_grad, TN)))
+    out_partial = dot(branch, upstream, TN)
+    gate_partial = dot(normed_rows, gate_grad, TN)
+    if direct:
+        out_half = D // 2
+        gate_blocks, gate_got = core_exchange(gate_partial, idx[2])
+        out_blocks, out_got = core_exchange(out_partial, idx[2])
+        gate_keep, gate_send, out_keep, out_send = fold(
+            idx,
+            [
+                ("plain", gate_blocks, gate_got, 0, DI, 0),
+                ("halves", out_blocks, out_got, 0, 0, out_half),
+            ],
+        )
+        states_grad, gate_send, out_send = lax.optimization_barrier(
+            (states_grad, gate_send, out_send)
+        )
+        gate_got = swapped(gate_send, "x", 2, 1)
+        out_got = swapped(out_send, "seq", 2, 1)
 
     mgrad, dz, last8, first8, cw_acc, cb_acc, dtb_acc, rate_acc = run_third(
         pre, mixed, z, states_grad, states, rdot, leave, cw8, skip_wide, alog, emat, gmat
     )
+    if direct:
+        gate_own, gate_send, out_keep, out_send = fold(
+            idx,
+            [
+                ("xz", gate_keep, gate_got, 0, 0, 0),
+                ("yx", out_keep, out_got, 0, 0, 0),
+            ],
+        )
+        mgrad, _, _ = lax.optimization_barrier((mgrad, gate_send, out_send))
+        out_got = swapped(out_send, "x", 2, 1)
+        gate_own = z_permutes(gate_own, gate_send, idx[0])
+    else:
+        gate_sum = reduce_plain(core_sum(gate_partial))
+        out_grad = reduce_split(core_sum(out_partial))
     near = lax.ppermute(first8, "seq", down)
     ends = mixed[:, local_len - 8 :, :].astype(F32)
     extra = jnp.stack(
@@ -694,15 +911,6 @@
         ],
         axis=1,
     )
-    mixed_chip = core_sum(mixed_local)
-    third_cols = mixed_chip.shape[3] // 3
-    mixed_sum = jnp.concatenate(
-        [
-            reduce_plain(mixed_chip[..., :third_cols]),
-            reduce_split(mixed_chip[..., third_cols:]),
-        ],
-        axis=1,
-    )
     normed_grad = (
         dot(gate_grad, wg, NT) + dot(mgrad_rows, wm, NT) + dot(dz_rows, wdt, NT)
     )
@@ -722,7 +930,57 @@
             skip_acc.sum(0).reshape(HEADS, HEADDIM).sum(1),
         ]
     )
-    vector_grad = lax.psum(vector_local, AXES + ("seq",))
+    if direct:
+        side = (CONVCH + 128) // 3
+        blocks, got = core_exchange(mixed_local, idx[2])
+        plain_keep, plain_send, half_keep, half_send = fold(
+            idx, [("split", blocks, got, 0, side, side)]
+        )
+        out_got, vector_local, _, _ = lax.optimization_barrier(
+            (out_got, vector_local, plain_send, half_send)
+        )
+        half_got = swapped(half_send, "seq", 2, 1)
+        plain_got = swapped(plain_send, "x", 2, 1)
+        out_own, out_send = fold(idx, [("xz", out_keep, out_got, 0, 0, 0)])
+        gate_sum = gate_own + swapped(gate_own, "seq", 2, 1)
+        out_own = z_permutes(out_own, out_send, idx[0])
+        out_grad = jnp.moveaxis(gather_stage(out_own, "seq"), 0, 1).reshape(-1, D)
+        plain_own, plain_send, half_keep, half_send = fold(
+            idx,
+            [
+                ("xz", plain_keep, plain_got, 0, 0, 0),
+                ("yx", half_keep, half_got, 0, 0, 0),
+            ],
+        )
+        half_got = swapped(half_send, "x", 2, 1)
+        plain_got = z_blocks(plain_send)
+        plain_own, half_own, half_send = fold(
+            idx,
+            [
+                ("z", plain_own, plain_got, 0, 0, 0),
+                ("xz", half_keep, half_got, 0, 0, 0),
+            ],
+        )
+        plain_got = swapped(plain_own, "seq", 2, 1)
+        half_got = z_blocks(half_send)
+        (half_own,) = fold(idx, [("z", half_own, half_got, 0, 0, 0)])
+        halves = gather_stage(half_own, "seq")
+        mixed_sum = jnp.concatenate([plain_own + plain_got, halves[0], halves[1]], axis=1)
+    else:
+        mixed_chip = core_sum(mixed_local)
+        third_cols = mixed_chip.shape[3] // 3
+        mixed_sum = jnp.concatenate(
+            [
+                reduce_plain(mixed_chip[..., :third_cols]),
+                reduce_split(mixed_chip[..., third_cols:]),
+            ],
+            axis=1,
+        )
+
+    vector_rows = jnp.pad(vector_local, (0, -vector_local.shape[0] % 1024)).reshape(-1, 128)
+    for axis in ("core", "seq", "x", "z"):
+        vector_rows = xor_sum(vector_rows, axis)
+    vector_grad = vector_rows.reshape(-1)[: vector_local.shape[0]]
 
     in_grad = jnp.concatenate([gate_sum, mixed_sum[:, :CONVCH]], axis=1)
     dt_grad = mixed_sum[:, CONVCH : CONVCH + HEADS]
@@ -770,6 +1028,7 @@
     placed = (
         (tokens, tokens, rows, rows, rows) + (P(),) * 7 + (quad,) * 4 + (tri,) * 4 + (quad,) * 4 + (P(),)
     )
+
     return jax.shard_map(
         body,
         mesh=torus,

time: 522 us -> 606 us (1.16)
  Pallas kernels: 112 us -> 291 us
  blocking collectives: 46.9 us -> 0 us
  local copies, waits for them, and re-layouts: 92.4 us -> 64.4 us
  waiting for transfers between devices: 86.9 us -> 66.3 us
  starting transfers between devices: 51.7 us -> 60.9 us
    pallas_call x0 -> x9, Pallas kernels: none -> 180 us  [the longest x2 147 us: assemble(): pl.pallas_call(functools.partial(assemble_kernel, order=order), grid_spec...]
    psum x1 -> x0, blocking collectives: 46.9 us -> none  [body(): vector_grad = lax.psum(vector_local, AXES + ('seq',))]
    all_gather x1, waiting for transfers between devices: 38.5 us -> 0.02 us  [body(): lax.all_gather(jnp.concatenate([in_low[:, DI:], dt_low], axis=1), AXES, a...]
    all_gather x2 -> x0, waiting for transfers between devices: 36.2 us -> none  [the longest x1 24.8 us: body(): wo = lax.all_gather(out_weight.astype(BF), AXES, axis=0, tiled=True)]
    ppermute x25 -> x31, waiting for transfers between devices: 12.2 us -> 43.5 us  [swapped(): lax.ppermute(v, axis, [(i, (i + offset) % size) for i in range(size)])]
    ppermute x1, waiting for transfers between devices: 0.01 us -> 11.6 us  [body(): leave = lax.ppermute(local_dstate, 'seq', down)]
    all_to_all x0 -> x2, waiting for transfers between devices: none -> 10.4 us  [z_blocks(): return lax.all_to_all(send, 'z', split_axis=0, concat_axis=0, tiled=True)]
    dot_general x12, matrix products: 29.5 us -> 19.8 us  [the longest x3 12.3 us: kron_update(): jnp.einsum('abji,abjk->abik', grad_tiles, grad_tiles, precision=lax.Preci...]
  transfers between devices with their start and end apart: 32 -> 43, of which waited for: 12 -> 18; matrix products, arithmetic and copies ran while one was open for 28% -> 18% of each run, Pallas kernels for 12% -> 31%
where the time goes in v2:
time: 606 us; the launch traced here: 598 us
  Pallas kernels  291 us (48%)
  waiting for transfers between devices  66.3 us (11%)
  local copies, waits for them, and re-layouts  64.4 us (11%)
  matrix products  64 us (11%)
  starting transfers between devices  60.9 us (10%)
  other arithmetic  36.7 us (6%)
  between operations  15 us (2%)
    pallas_call x2, Pallas kernels, assemble(): pl.pallas_call(functools.partial(assemble_kernel, order=order), grid_spec...  147 us
    pallas_call x1, Pallas kernels, run_second(): pl.pallas_call(second_kernel, grid=grid, in_specs=[tok(CONVCH), tok(128),...  49.1 us
    pallas_call x1, Pallas kernels, run_third(): pl.pallas_call(third_kernel, grid=grid, in_specs=[tok(CONVCH), tok(CONVCH...  45.4 us
    dot_general x9, matrix products, dot(): return lax.dot_general(a, b, dims, preferred_element_type=F32)  44.2 us
    ppermute x31, waiting for transfers between devices, swapped(): lax.ppermute(v, axis, [(i, (i + offset) % size) for i in range(size)])  43.5 us
    ppermute x31, starting transfers between devices, swapped(): lax.ppermute(v, axis, [(i, (i + offset) % size) for i in range(size)])  37.7 us
    pallas_call x7, Pallas kernels, fold(): pl.pallas_call(functools.partial(fold_kernel, [j[0] for j in jobs], [j[3:...  32.4 us
    unnamed x86, local copies, waits for them, and re-layouts  19.7 us
  transfers between devices with their start and end apart: 43, of which 18 were waited for; matrix products, arithmetic and copies ran while one was open for 18% of the time, Pallas kernels for 31%

profile of v2, /device:TPU:0, one launch (start us, length us, event | category | flops | bytes accessed | tf_op | source)
XLA Modules:
  0.0 598.1 jit_solution(11115148784303529545)
XLA Ops:
  13.4 4.1 collective-permute-start.6
  21.9 3.1 collective-permute-done.5
  29.0 2.7 collective-permute-start.3
  31.7 2.4 collective-permute-done.8
  35.8 2.6 collective-permute-done.2
  39.5 3.4 collective-permute-start
  43.0 3.0 collective-permute-done.4
  47.7 2.8 collective-permute-done.11
  52.6 8.7 %collective-permute-done.9 = bf16[2,4,24,1536]{3,2,1,0:T(8,128)(2,1)S(1)} collective-permute-done((bf16[2,4,24,1536]{3,2,1,0:T(8,128)(2,1)S(1)}, bf16[2,4,24,1536]{3,2,1,0:T(8,128)(2,1)S(1)}, u32[]{:S(2)}, u32[]{:S(2)}) %collective-permute-start.9) | collective-permute-done | bytes 589856 | tf_op jit(solution)/shard_map/ppermute | solution.py:515
  64.8 73.5 %assemble.3 = bf16[32,48,768]{2,1,0:T(8,128)(2,1)} custom-call(s32[4]{0:T(128)} %pad_add_fusion.idx, bf16[2,2,4,48,768]{4,3,2,1,0:T(8,128)(2,1)} %pad_maximum_fusion.2.near_ref, bf16[2,2,4,48,768]{4,3,2,1,0:T(8,128)(2,1)} %collective-permute-done.12.far_ref), custom_call_target="tpu_custom_call" | custom-call | tf_op jit(solution)/shard_map/assemble/pallas_call | solution.py:729
  138.4 3.5 slice.84.wm_ref
  146.0 17.0 %first.1 = (bf16[1,1024,768]{2,1,0:T(8,128)(2,1)}, bf16[1,1024,1792]{2,1,0:T(8,128)(2,1)}, f32[1,1024,1792]{2,1,0:T(8,128)}, f32[1,1024,128]{2,1,0:T(8,128)}, f3...) custom-call(bf16[1,1024,768]{2,1,0:T(8,128)(2,1)} %u_ref.3, bf16[1,8,768]{2,1,0:T(8,128)(2,1)} %copy-done.27, ...), custom_call_target="tpu_custom_call" | custom-call | tf_op jit(solution)/shard_map/first/pallas_call | solution.py:387
  162.9 4.7 collective-permute-start.13
  167.6 7.3 %convolution_bitcast_fusion.bgrad_ref = f32[1024,1536]{1,0:T(8,128)} fusion(bf16[1536,768]{1,0:T(8,128)(2,1)} %bitcast.231, bf16[1,1024,768]{2,1,0:T(8,128)(2,1)} %param.26), kind=kOutput, calls=%fused_computation.6 | convolution fusion | flops 2415919104 | bytes 10223616 | tf_op jit(solution)/shard_map/dot_general | solution.py:37
  175.0 73.5 %assemble.2 = bf16[32,24,1536]{2,1,0:T(8,128)(2,1)} custom-call(s32[4]{0:T(128)} %pad_add_fusion.idx, bf16[2,2,4,24,1536]{4,3,2,1,0:T(8,128)(2,1)} %pad_maximum_fusion.1.near_ref, bf16[2,2,4,24,1536]{4,3,2,1,0:T(8,128)(2,1)} %collective-permute-done.10.far_ref), custom_call_target="tpu_custom_call" | custom-call | tf_op jit(solution)/shard_map/assemble/pallas_call | solution.py:729
  248.5 2.6 copy.100
  251.1 7.4 %fusion.15.gate_ref = f32[1024,1536]{1,0:T(8,128)} fusion(bf16[768,1536]{1,0:T(8,128)(2,1)} %bitcast.242, bf16[1,1024,768]{2,1,0:T(8,128)(2,1)} %get-tuple-element.70), kind=kOutput, calls=%fused_computation.27 | convolution fusion | flops 2415919104 | bytes 10223616 | tf_op jit(solution)/shard_map/dot_general | solution.py:37
  259.8 49.1 %second.1 = (bf16[1,1024,768]{2,1,0:T(8,128)(2,1)}, bf16[1024,1536]{1,0:T(8,128)(2,1)}, bf16[1024,1536]{1,0:T(8,128)(2,1)}, bf16[1024,1536]{1,0:T(8,128)(2,1)}, ...) custom-call(f32[1,1024,1792]{2,1,0:T(8,128)} %get-tuple-element.68.p, ...), custom_call_target="tpu_custom_call" | custom-call | tf_op jit(solution)/shard_map/second/pallas_call | solution.py:421
  308.9 4.9 copy.101
  313.7 5.0 fusion.8.refs_2_
  323.6 2.6 fusion.6.refs_0_
  338.3 6.5 %fold.7 = (f32[4,48,1536]{2,1,0:T(8,128)}, bf16[4,48,1536]{2,1,0:T(8,128)(2,1)}, f32[4,2,96,384]{3,2,1,0:T(8,128)}, bf16[4,2,96,384]{3,2,1,0:T(8,128)(2,1)}) custom-call(s32[4]{0:T(128)} %pad_add_fusion.idx, f32[4,2,2,48,1536]{4,3,2,1,0:T(8,128)} %copy-done.4, f32[4,2,48,1536]{3,2,1,0:T(8,128)} %collective-permute-done.14.refs_1_, ...), custom_call_target="tpu_custom_call" | custom-call | tf_op jit(solution)/shard_map/fold/pallas_call | solution.py:669
  344.8 11.6 %collective-permute-done.16.leave_ref = f32[1,128,1536]{2,1,0:T(8,128)} collective-permute-done((f32[1,128,1536]{2,1,0:T(8,128)}, f32[1,128,1536]{2,1,0:T(8,128)}, u32[]{:S(2)}, u32[]{:S(2)}) %collective-permute-start.16) | collective-permute-done | bytes 786464 | tf_op jit(solution)/shard_map/ppermute | solution.py:842
  356.4 45.4 %third.1 = (bf16[1,1024,1792]{2,1,0:T(8,128)(2,1)}, bf16[1,1024,128]{2,1,0:T(8,128)(2,1)}, f32[1,8,1792]{2,1,0:T(8,128)}, f32[1,8,1792]{2,1,0:T(8,128)}, f32[4,8...) custom-call(f32[1,1024,1792]{2,1,0:T(8,128)} %get-tuple-element.68.pre_ref, ...), custom_call_target="tpu_custom_call" | custom-call | tf_op jit(solution)/shard_map/third/pallas_call | solution.py:460
  403.2 2.7 collective-permute-start.18
  408.8 9.4 %collective-permute-done.17.refs_1_ = bf16[4,48,1536]{2,1,0:T(8,128)(2,1)} collective-permute-done((bf16[4,48,1536]{2,1,0:T(8,128)(2,1)}, bf16[4,48,1536]{2,1,0:T(8,128)(2,1)}, u32[]{:S(2)}, u32[]{:S(2)}) %collective-permute-start.17) | collective-permute-done | bytes 589856 | tf_op jit(solution)/shard_map/ppermute | solution.py:515
  420.0 5.1 fold.8
  425.7 5.7 fusion.11
  435.2 2.4 copy-done.36
  437.5 4.3 fusion.63
  451.7 2.5 collective-permute-start.20
  457.9 6.1 %fusion.60 = f32[1024,768]{1,0:T(8,128)S(1)} fusion(bf16[1024,1792]{1,0:T(8,128)(2,1)} %bitcast_dynamic-update-slice_fusion.2, bf16[768,1920]{1,0:T(8,128)(2,1)} %all-gather.2.cloned.1.call-done), kind=kOutput, calls=%fused_computation.136 | convolution fusion | flops 2818572288 | bytes 9568256 | tf_op jit(solution)/shard_map/dot_general | solution.py:37
  464.0 3.8 fusion.5
  467.8 5.2 fold.9
  475.6 4.0 fold.13
  495.5 5.4 fusion.1
  506.2 4.3 dynamic_update_slice.21
  513.9 4.1 dynamic_update_slice.22
  519.9 4.3 add_multiply_fusion.1
  528.1 4.3 fold.10
  533.7 4.0 all-to-all-start
  539.2 5.3 all-to-all-done.refs_1_
  544.5 4.1 fold.11
  549.8 4.0 all-to-all-start.1
  555.5 5.1 all-to-all-done.1.refs_1_
  560.6 3.2 fold.12
  565.5 3.3 collective-permute-done.29
  572.8 7.2 %add_multiply_fusion = f32[2,26,128,128]{3,2,1,0:T(8,128)} fusion(f32[2,26,128,128]{3,2,1,0:T(8,128)} %param.38, f32[2,24,26,128]{3,2,1,0:T(8,128)} %reshape.421), kind=kOutput, calls=%fused_computation.7 | convolution fusion | flops 124387328 | bytes 7454720 | tf_op jit(solution)/shard_map/abji,abjk->abik/dot_general | solution.py:505
  (250 shorter events, 126.0 us)
Async XLA Ops:
  7.2 573.7 %copy-start = (f32[2,26,128,128]{3,2,1,0:T(8,128)S(1)}, f32[2,26,128,128]{3,2,1,0:T(8,128)}, u32[]{:S(2)}) copy-start(f32[2,26,128,128]{3,2,1,0:T(8,128)} %param.40) | copy-start | bytes 10223620
  7.2 131.2 %all-gather.2.cloned.1.call-start = ((), (), s32[]{:S(2)}) async-start(), calls=%async_computation.2 | async-start | bytes 3133440 | tf_op jit(solution)/shard_map/all_gather | solution.py:786
  13.4 7.7 %collective-permute-start.6 = (bf16[48,768]{1,0:T(8,128)(2,1)S(1)}, bf16[48,768]{1,0:T(8,128)(2,1)S(1)}, u32[]{:S(2)}, u32[]{:S(2)}) collective-permute-start(bf16[48,768]{1,0:T(8,128)(2,1)S(1)} %fusion.88), channel_id=1, source_target_pairs={{0,16},{8,24},{16,0},{24,8},{1,17},{9,25},{17,1},{25,9},{2,18},{10... | collective-permute-start | bytes 221192 | tf_op jit(solution)/shard_map/ppermute | solution.py:515
  17.5 4.4 collective-permute-start.7
  18.9 6.2 %collective-permute-start.5 = (bf16[48,768]{1,0:T(8,128)(2,1)S(1)}, bf16[48,768]{1,0:T(8,128)(2,1)S(1)}, u32[]{:S(2)}, u32[]{:S(2)}) collective-permute-start(bf16[48,768]{1,0:T(8,128)(2,1)S(1)} %fusion.88), channel_id=1, source_target_pairs={{0,8},{8,16},{16,24},{24,0},{1,9},{9,17},{17,25},{25,1},{2,10},{10... | collective-permute-start | bytes 221192 | tf_op jit(solution)/shard_map/ppermute | solution.py:515
  25.1 9.1 %collective-permute-start.8 = (bf16[4,48,768]{2,1,0:T(8,128)(2,1)S(1)}, bf16[4,48,768]{2,1,0:T(8,128)(2,1)S(1)}, u32[]{:S(2)}, u32[]{:S(2)}) collective-permute-start(bf16[4,48,768]{2,1,0:T(8,128)(2,1)S(1)} %get-tuple-element.201), channel_id=1, source_target_pairs={{0,4},{4,0},{1,5},{5,1},{2,6},{6,2},{3,7},{7,3},{8,12},{12,8},{9,1... | collective-permute-start | bytes 884744 | tf_op jit(solution)/shard_map/ppermute | solution.py:515
  26.6 9.1 %collective-permute-start.1 = (bf16[24,1536]{1,0:T(8,128)(2,1)S(1)}, bf16[24,1536]{1,0:T(8,128)(2,1)S(1)}, u32[]{:S(2)}, u32[]{:S(2)}) collective-permute-start(bf16[24,1536]{1,0:T(8,128)(2,1)S(1)} %fusion.89), channel_id=1, source_target_pairs={{0,8},{8,16},{16,24},{24,0},{1,9},{9,17},{17,25},{25,1},{2,10},{10... | collective-permute-start | bytes 221192 | tf_op jit(solution)/shard_map/ppermute | solution.py:515
  26.9 11.5 %collective-permute-start.2 = (bf16[24,1536]{1,0:T(8,128)(2,1)S(1)}, bf16[24,1536]{1,0:T(8,128)(2,1)S(1)}, u32[]{:S(2)}, u32[]{:S(2)}) collective-permute-start(bf16[24,1536]{1,0:T(8,128)(2,1)S(1)} %fusion.89), channel_id=1, source_target_pairs={{0,16},{8,24},{16,0},{24,8},{1,17},{9,25},{17,1},{25,9},{2,18},{10... | collective-permute-start | bytes 221192 | tf_op jit(solution)/shard_map/ppermute | solution.py:515
  29.0 9.3 %collective-permute-start.3 = (bf16[24,1536]{1,0:T(8,128)(2,1)S(1)}, bf16[24,1536]{1,0:T(8,128)(2,1)S(1)}, u32[]{:S(2)}, u32[]{:S(2)}) collective-permute-start(bf16[24,1536]{1,0:T(8,128)(2,1)S(1)} %fusion.89), channel_id=1, source_target_pairs={{0,24},{8,0},{16,8},{24,16},{1,25},{9,1},{17,9},{25,17},{2,26},{10... | collective-permute-start | bytes 221192 | tf_op jit(solution)/shard_map/ppermute | solution.py:515
  34.2 16.3 %collective-permute-start.11 = (bf16[2,4,48,768]{3,2,1,0:T(8,128)(2,1)S(1)}, bf16[2,4,48,768]{3,2,1,0:T(8,128)(2,1)S(1)}, u32[]{:S(2)}, u32[]{:S(2)}) collective-permute-start(bf16[2,4,48,768]{3,2,1,0:T(8,128)(2,1)S(1)} %get-tuple-element.194), channel_id=1, source_target_pairs={{0,1},{1,0},{2,3},{3,2},{4,5},{5,4},{6,7},{7,6},{8,9},{9,8},{10,11... | collective-permute-start | bytes 1769480 | tf_op jit(solution)/shard_map/ppermute | solution.py:515
  38.4 7.6 %collective-permute-start.4 = (bf16[4,24,1536]{2,1,0:T(8,128)(2,1)S(1)}, bf16[4,24,1536]{2,1,0:T(8,128)(2,1)S(1)}, u32[]{:S(2)}, u32[]{:S(2)}) collective-permute-start(bf16[4,24,1536]{2,1,0:T(8,128)(2,1)S(1)} %get-tuple-element.203), channel_id=1, source_target_pairs={{0,4},{4,0},{1,5},{5,1},{2,6},{6,2},{3,7},{7,3},{8,12},{12,8},{9,1... | collective-permute-start | bytes 884744 | tf_op jit(solution)/shard_map/ppermute | solution.py:515
  39.5 104.0 %collective-permute-start = (bf16[1,8,768]{2,1,0:T(8,128)(2,1)S(1)}, bf16[1,8,768]{2,1,0:T(8,128)(2,1)S(1)}, u32[]{:S(2)}, u32[]{:S(2)}) collective-permute-start(bf16[1,8,768]{2,1,0:T(8,128)(2,1)S(1)} %slice.81), channel_id=1, source_target_pairs={{0,1},{2,3},{4,5},{6,7},{8,9},{10,11},{12,13},{14,15},{16,17},{18,... | collective-permute-start | bytes 36872 | tf_op jit(solution)/shard_map/ppermute | solution.py:806
  46.1 18.7 %copy-start.37 = (f32[24]{0:T(128)S(1)}, f32[24]{0:T(128)}, u32[]{:S(2)}) copy-start(f32[24]{0:T(128)} %param.33) | copy-start | bytes 292
  46.1 15.3 %collective-permute-start.9 = (bf16[2,4,24,1536]{3,2,1,0:T(8,128)(2,1)S(1)}, bf16[2,4,24,1536]{3,2,1,0:T(8,128)(2,1)S(1)}, u32[]{:S(2)}, u32[]{:S(2)}) collective-permute-start(bf16[2,4,24,1536]{3,2,1,0:T(8,128)(2,1)S(1)} %get-tuple-element.196), channel_id=1, source_target_pairs={{0,1},{1,0},{2,3},{3,2},{4,5},{5,4},{6,7},{7,6},{8,9},{9,8},{10,11... | collective-permute-start | bytes 1769480 | tf_op jit(solution)/shard_map/ppermute | solution.py:515
  51.6 13.2 %collective-permute-start.12 = (bf16[2,2,4,48,768]{4,3,2,1,0:T(8,128)(2,1)}, bf16[2,2,4,48,768]{4,3,2,1,0:T(8,128)(2,1)}, u32[]{:S(2)}, u32[]{:S(2)}) collective-permute-start(bf16[2,2,4,48,768]{4,3,2,1,0:T(8,128)(2,1)} %pad_maximum_fusion.2.near_ref), channel_id=1, source_target_pairs={{0,2},{2,0},{1,3},{3,1},{4,6},{6,4},{5,7},{7,5},{8,10},{10,8},{9,1... | collective-permute-start | bytes 3538952 | tf_op jit(solution)/shard_map/ppermute | solution.py:515
  62.5 112.5 %collective-permute-start.10 = (bf16[2,2,4,24,1536]{4,3,2,1,0:T(8,128)(2,1)}, bf16[2,2,4,24,1536]{4,3,2,1,0:T(8,128)(2,1)}, u32[]{:S(2)}, u32[]{:S(2)}) collective-permute-start(bf16[2,2,4,24,1536]{4,3,2,1,0:T(8,128)(2,1)} %pad_maximum_fusion.1.near_ref), channel_id=1, source_target_pairs={{0,2},{2,0},{1,3},{3,1},{4,6},{6,4},{5,7},{7,5},{8,10},{10,8},{9,1... | collective-permute-start | bytes 3538952 | tf_op jit(solution)/shard_map/ppermute | solution.py:515
  162.9 95.6 %collective-permute-start.13 = (f32[1,128,1536]{2,1,0:T(8,128)}, f32[1,128,1536]{2,1,0:T(8,128)}, u32[]{:S(2)}, u32[]{:S(2)}) collective-permute-start(f32[1,128,1536]{2,1,0:T(8,128)} %get-tuple-element.71), channel_id=1, source_target_pairs={{0,1},{2,3},{4,5},{6,7},{8,9},{10,11},{12,13},{14,15},{16,17},{18,... | collective-permute-start | bytes 2359304 | tf_op jit(solution)/shard_map/ppermute | solution.py:823
  320.5 17.8 %collective-permute-start.15 = (f32[4,2,96,768]{3,2,1,0:T(8,128)}, f32[4,2,96,768]{3,2,1,0:T(8,128)}, u32[]{:S(2)}, u32[]{:S(2)}) collective-permute-start(f32[4,2,96,768]{3,2,1,0:T(8,128)} %dynamic-slice_bitcast_fusion.1), channel_id=1, source_target_pairs={{0,2},{2,0},{1,3},{3,1},{4,6},{6,4},{5,7},{7,5},{8,10},{10,8},{9,1... | collective-permute-start | bytes 7077896 | tf_op jit(solution)/shard_map/ppermute | solution.py:515
  329.1 9.2 %collective-permute-start.14 = (f32[4,2,48,1536]{3,2,1,0:T(8,128)}, f32[4,2,48,1536]{3,2,1,0:T(8,128)}, u32[]{:S(2)}, u32[]{:S(2)}) collective-permute-start(f32[4,2,48,1536]{3,2,1,0:T(8,128)} %dynamic-slice_bitcast_fusion.2), channel_id=1, source_target_pairs={{0,2},{2,0},{1,3},{3,1},{4,6},{6,4},{5,7},{7,5},{8,10},{10,8},{9,1... | collective-permute-start | bytes 7077896 | tf_op jit(solution)/shard_map/ppermute | solution.py:515
  334.4 21.9 %collective-permute-start.16 = (f32[1,128,1536]{2,1,0:T(8,128)}, f32[1,128,1536]{2,1,0:T(8,128)}, u32[]{:S(2)}, u32[]{:S(2)}) collective-permute-start(f32[1,128,1536]{2,1,0:T(8,128)} %get-tuple-element.82), channel_id=1, source_target_pairs={{1,0},{3,2},{5,4},{7,6},{9,8},{11,10},{13,12},{15,14},{17,16},{19,... | collective-permute-start | bytes 2359304 | tf_op jit(solution)/shard_map/ppermute | solution.py:842
  401.7 23.3 %copy-start.19 = (f32[1,8,1792]{2,1,0:T(8,128)S(1)}, f32[1,8,1792]{2,1,0:T(8,128)}, u32[]{:S(2)}) copy-start(f32[1,8,1792]{2,1,0:T(8,128)} %get-tuple-element.91) | copy-start | bytes 172036
  401.7 7.0 %collective-permute-start.19 = (f32[1,8,1792]{2,1,0:T(8,128)}, f32[1,8,1792]{2,1,0:T(8,128)S(1)}, u32[]{:S(2)}, u32[]{:S(2)}) collective-permute-start(f32[1,8,1792]{2,1,0:T(8,128)} %get-tuple-element.92), channel_id=1, source_target_pairs={{1,0},{3,2},{5,4},{7,6},{9,8},{11,10},{13,12},{15,14},{17,16},{19,... | collective-permute-start | bytes 172040 | tf_op jit(solution)/shard_map/ppermute | solution.py:882
  403.2 15.0 %collective-permute-start.17 = (bf16[4,48,1536]{2,1,0:T(8,128)(2,1)}, bf16[4,48,1536]{2,1,0:T(8,128)(2,1)}, u32[]{:S(2)}, u32[]{:S(2)}) collective-permute-start(bf16[4,48,1536]{2,1,0:T(8,128)(2,1)} %get-tuple-element.85), channel_id=1, source_target_pairs={{0,4},{4,0},{1,5},{5,1},{2,6},{6,2},{3,7},{7,3},{8,12},{12,8},{9,1... | collective-permute-start | bytes 1769480 | tf_op jit(solution)/shard_map/ppermute | solution.py:515
  403.2 16.7 %collective-permute-start.18 = (bf16[4,2,96,384]{3,2,1,0:T(8,128)(2,1)}, bf16[4,2,96,384]{3,2,1,0:T(8,128)(2,1)}, u32[]{:S(2)}, u32[]{:S(2)}) collective-permute-start(bf16[4,2,96,384]{3,2,1,0:T(8,128)(2,1)} %get-tuple-element.87), channel_id=1, source_target_pairs={{0,1},{1,0},{2,3},{3,2},{4,5},{5,4},{6,7},{7,6},{8,9},{9,8},{10,11... | collective-permute-start | bytes 1769480 | tf_op jit(solution)/shard_map/ppermute | solution.py:515
  408.8 22.6 %copy-start.22 = (f32[1,8,1792]{2,1,0:T(8,128)}, f32[1,8,1792]{2,1,0:T(8,128)S(1)}, u32[]{:S(2)}) copy-start(f32[1,8,1792]{2,1,0:T(8,128)S(1)} %collective-permute-done.19) | copy-start | bytes 172036
  433.6 34.2 %collective-permute-start.24 = (f32[4,2,48,1920]{3,2,1,0:T(8,128)}, f32[4,2,48,1920]{3,2,1,0:T(8,128)}, u32[]{:S(2)}, u32[]{:S(2)}) collective-permute-start(f32[4,2,48,1920]{3,2,1,0:T(8,128)} %dynamic-slice_bitcast_fusion), channel_id=1, source_target_pairs={{0,2},{2,0},{1,3},{3,1},{4,6},{6,4},{5,7},{7,5},{8,10},{10,8},{9,1... | collective-permute-start | bytes 8847368 | tf_op jit(solution)/shard_map/ppermute | solution.py:515
  449.2 23.9 %collective-permute-start.30 = (bf16[4,96,384]{2,1,0:T(8,128)(2,1)}, bf16[4,96,384]{2,1,0:T(8,128)(2,1)}, u32[]{:S(2)}, u32[]{:S(2)}) collective-permute-start(bf16[4,96,384]{2,1,0:T(8,128)(2,1)} %get-tuple-element.89), channel_id=1, source_target_pairs={{0,4},{4,0},{1,5},{5,1},{2,6},{6,2},{3,7},{7,3},{8,12},{12,8},{9,1... | collective-permute-start | bytes 884744 | tf_op jit(solution)/shard_map/ppermute | solution.py:515
  451.7 21.5 %collective-permute-start.20 = (bf16[48,1536]{1,0:T(8,128)(2,1)}, bf16[48,1536]{1,0:T(8,128)(2,1)}, u32[]{:S(2)}, u32[]{:S(2)}) collective-permute-start(bf16[48,1536]{1,0:T(8,128)(2,1)} %get-tuple-element.190), channel_id=1, source_target_pairs={{0,8},{8,16},{16,24},{24,0},{1,9},{9,17},{17,25},{25,1},{2,10},{10... | collective-permute-start | bytes 442376 | tf_op jit(solution)/shard_map/ppermute | solution.py:515
  454.2 19.0 %collective-permute-start.21 = (bf16[48,1536]{1,0:T(8,128)(2,1)}, bf16[48,1536]{1,0:T(8,128)(2,1)}, u32[]{:S(2)}, u32[]{:S(2)}) collective-permute-start(bf16[48,1536]{1,0:T(8,128)(2,1)} %get-tuple-element.192), channel_id=1, source_target_pairs={{0,16},{8,24},{16,0},{24,8},{1,17},{9,25},{17,1},{25,9},{2,18},{10... | collective-permute-start | bytes 442376 | tf_op jit(solution)/shard_map/ppermute | solution.py:515
  456.5 16.7 %collective-permute-start.22 = (bf16[48,1536]{1,0:T(8,128)(2,1)}, bf16[48,1536]{1,0:T(8,128)(2,1)}, u32[]{:S(2)}, u32[]{:S(2)}) collective-permute-start(bf16[48,1536]{1,0:T(8,128)(2,1)} %get-tuple-element.191), channel_id=1, source_target_pairs={{0,24},{8,0},{16,8},{24,16},{1,25},{9,1},{17,9},{25,17},{2,26},{10... | collective-permute-start | bytes 442376 | tf_op jit(solution)/shard_map/ppermute | solution.py:515
  473.1 6.5 %collective-permute-start.35 = (f32[96,128]{1,0:T(8,128)S(1)}, f32[96,128]{1,0:T(8,128)S(1)}, u32[]{:S(2)}, u32[]{:S(2)}) collective-permute-start(f32[96,128]{1,0:T(8,128)S(1)} %pad_bitcast_fusion), channel_id=1, source_target_pairs={{0,2},{2,0},{1,3},{3,1},{4,6},{6,4},{5,7},{7,5},{8,10},{10,8},{9,1... | collective-permute-start | bytes 147464 | tf_op jit(solution)/shard_map/ppermute | solution.py:579
  474.4 26.5 %collective-permute-start.23 = (f32[48,1536]{1,0:T(8,128)S(1)}, f32[48,1536]{1,0:T(8,128)}, u32[]{:S(2)}, u32[]{:S(2)}) collective-permute-start(f32[48,1536]{1,0:T(8,128)S(1)} %convert_add_fusion), channel_id=1, source_target_pairs={{0,1},{1,0},{2,3},{3,2},{4,5},{5,4},{6,7},{7,6},{8,9},{9,8},{10,11... | collective-permute-start | bytes 884744 | tf_op jit(solution)/shard_map/ppermute | solution.py:515
  479.6 5.8 collective-permute-start.36
  481.5 7.0 %collective-permute-start.31 = (bf16[96,384]{1,0:T(8,128)(2,1)S(1)}, bf16[96,384]{1,0:T(8,128)(2,1)S(1)}, u32[]{:S(2)}, u32[]{:S(2)}) collective-permute-start(bf16[96,384]{1,0:T(8,128)(2,1)S(1)} %get-tuple-element.197), channel_id=1, source_target_pairs={{0,8},{8,16},{16,24},{24,0},{1,9},{9,17},{17,25},{25,1},{2,10},{10... | collective-permute-start | bytes 221192 | tf_op jit(solution)/shard_map/ppermute | solution.py:515
  482.1 8.6 %collective-permute-start.32 = (bf16[96,384]{1,0:T(8,128)(2,1)S(1)}, bf16[96,384]{1,0:T(8,128)(2,1)S(1)}, u32[]{:S(2)}, u32[]{:S(2)}) collective-permute-start(bf16[96,384]{1,0:T(8,128)(2,1)S(1)} %get-tuple-element.199), channel_id=1, source_target_pairs={{0,16},{8,24},{16,0},{24,8},{1,17},{9,25},{17,1},{25,9},{2,18},{10... | collective-permute-start | bytes 221192 | tf_op jit(solution)/shard_map/ppermute | solution.py:515
  483.1 7.6 %collective-permute-start.33 = (bf16[96,384]{1,0:T(8,128)(2,1)S(1)}, bf16[96,384]{1,0:T(8,128)(2,1)S(1)}, u32[]{:S(2)}, u32[]{:S(2)}) collective-permute-start(bf16[96,384]{1,0:T(8,128)(2,1)S(1)} %get-tuple-element.198), channel_id=1, source_target_pairs={{0,24},{8,0},{16,8},{24,16},{1,25},{9,1},{17,9},{25,17},{2,26},{10... | collective-permute-start | bytes 221192 | tf_op jit(solution)/shard_map/ppermute | solution.py:515
  485.4 8.0 %collective-permute-start.37 = (f32[96,128]{1,0:T(8,128)S(1)}, f32[96,128]{1,0:T(8,128)S(1)}, u32[]{:S(2)}, u32[]{:S(2)}) collective-permute-start(f32[96,128]{1,0:T(8,128)S(1)} %fusion.87), channel_id=1, source_target_pairs={{0,4},{4,0},{1,5},{5,1},{2,6},{6,2},{3,7},{7,3},{8,12},{12,8},{9,1... | collective-permute-start | bytes 147464 | tf_op jit(solution)/shard_map/ppermute | solution.py:579
  492.4 20.4 %collective-permute-start.34 = (f32[96,384]{1,0:T(8,128)}, f32[96,384]{1,0:T(8,128)}, u32[]{:S(2)}, u32[]{:S(2)}) collective-permute-start(f32[96,384]{1,0:T(8,128)} %convert_add_fusion.1), channel_id=1, source_target_pairs={{0,1},{1,0},{2,3},{3,2},{4,5},{5,4},{6,7},{7,6},{8,9},{9,8},{10,11... | collective-permute-start | bytes 442376 | tf_op jit(solution)/shard_map/ppermute | solution.py:515
  494.1 16.3 %collective-permute-start.38 = (f32[96,128]{1,0:T(8,128)}, f32[96,128]{1,0:T(8,128)}, u32[]{:S(2)}, u32[]{:S(2)}) collective-permute-start(f32[96,128]{1,0:T(8,128)} %add.281), channel_id=1, source_target_pairs={{0,8},{8,0},{16,24},{24,16},{1,9},{9,1},{17,25},{25,17},{2,10},{10... | collective-permute-start | bytes 147464 | tf_op jit(solution)/shard_map/ppermute | solution.py:579
  502.6 25.5 %collective-permute-start.26 = (bf16[4,2,48,640]{3,2,1,0:T(8,128)(2,1)}, bf16[4,2,48,640]{3,2,1,0:T(8,128)(2,1)}, u32[]{:S(2)}, u32[]{:S(2)}) collective-permute-start(bf16[4,2,48,640]{3,2,1,0:T(8,128)(2,1)} %get-tuple-element.98), channel_id=1, source_target_pairs={{0,1},{1,0},{2,3},{3,2},{4,5},{5,4},{6,7},{7,6},{8,9},{9,8},{10,11... | collective-permute-start | bytes 1474568 | tf_op jit(solution)/shard_map/ppermute | solution.py:515
  503.5 24.6 %collective-permute-start.25 = (bf16[4,48,640]{2,1,0:T(8,128)(2,1)}, bf16[4,48,640]{2,1,0:T(8,128)(2,1)}, u32[]{:S(2)}, u32[]{:S(2)}) collective-permute-start(bf16[4,48,640]{2,1,0:T(8,128)(2,1)} %get-tuple-element.96), channel_id=1, source_target_pairs={{0,4},{4,0},{1,5},{5,1},{2,6},{6,2},{3,7},{7,3},{8,12},{12,8},{9,1... | collective-permute-start | bytes 737288 | tf_op jit(solution)/shard_map/ppermute | solution.py:515
  511.9 25.9 %collective-permute-start.39 = (f32[96,128]{1,0:T(8,128)}, f32[96,128]{1,0:T(8,128)}, u32[]{:S(2)}, u32[]{:S(2)}) collective-permute-start(f32[96,128]{1,0:T(8,128)} %add.282), channel_id=1, source_target_pairs={{0,16},{8,24},{16,0},{24,8},{1,17},{9,25},{17,1},{25,9},{2,18},{10... | collective-permute-start | bytes 147464 | tf_op jit(solution)/shard_map/ppermute | solution.py:579
  526.5 27.3 %copy-start.20 = (f32[11336]{0:T(1024)S(1)}, f32[11336]{0:T(1024)}, u32[]{:S(2)}) copy-start(f32[11336]{0:T(1024)} %param.49) | copy-start | bytes 136036
  532.5 6.7 %collective-permute-start.27 = (bf16[4,48,640]{2,1,0:T(8,128)(2,1)}, bf16[4,48,640]{2,1,0:T(8,128)(2,1)}, u32[]{:S(2)}, u32[]{:S(2)}) collective-permute-start(bf16[4,48,640]{2,1,0:T(8,128)(2,1)} %get-tuple-element.102), channel_id=1, source_target_pairs={{0,4},{4,0},{1,5},{5,1},{2,6},{6,2},{3,7},{7,3},{8,12},{12,8},{9,1... | collective-permute-start | bytes 737288 | tf_op jit(solution)/shard_map/ppermute | solution.py:515
  533.7 10.7 %all-to-all-start = ((bf16[4,48,640]{2,1,0:T(8,128)(2,1)}), bf16[4,48,640]{2,1,0:T(8,128)(2,1)}, u32[]{:S(2)}, u32[]{:S(2)}) async-start(bf16[4,48,640]{2,1,0:T(8,128)(2,1)} %get-tuple-element.100), calls=%async_computation | async-start | bytes 491520 | tf_op jit(solution)/shard_map/all_to_all | solution.py:688
  548.6 5.9 collective-permute-start.28
  549.8 10.8 %all-to-all-start.1 = ((bf16[4,48,640]{2,1,0:T(8,128)(2,1)}), bf16[4,48,640]{2,1,0:T(8,128)(2,1)}, u32[]{:S(2)}, u32[]{:S(2)}) async-start(bf16[4,48,640]{2,1,0:T(8,128)(2,1)} %get-tuple-element.105), calls=%async_computation.1 | async-start | bytes 491520 | tf_op jit(solution)/shard_map/all_to_all | solution.py:688
  563.7 5.1 collective-permute-start.29
  (34 other events, 234.3 us)
Sparse Core Ops, SparseCore 0:
  12.5 51.1 all-gather.1

commit v3 on v1

--- a/solution.py
+++ b/solution.py
@@ -6,6 +6,7 @@
 from jax.experimental import pallas as pl
 from jax.experimental.pallas import tpu as pltpu
 from jax.sharding import PartitionSpec as P
+
 
 D = 768
 HEADS = 24
@@ -14,7 +15,7 @@
 KCONV = 4
 DI = 1536
 CONVCH = 1792
-INCOLS = 3328
+WIDE = CONVCH + 128
 
 BL = 128
 PAIRS = HEADS // 2
@@ -28,7 +29,6 @@
 NEG = -1e30
 BF = jnp.bfloat16
 F32 = jnp.float32
-HIGH = lax.Precision.HIGHEST
 NN = (((1,), (0,)), ((), ()))
 NT = (((1,), (1,)), ((), ()))
 TN = (((0,), (0,)), ((), ()))
@@ -106,7 +106,7 @@
 
 
 def first_kernel(
-    u_ref, halo_ref, gain_ref, wm_ref, wdt_ref, cw_ref, cb_ref, dtb_ref, alog_ref, emat_ref,
+    u_ref, halo_ref, gain_ref, w_ref, cw_ref, cb_ref, dtb_ref, alog_ref, emat_ref,
     normed_ref, mixed_ref, pre_ref, z_ref, state_ref, total_ref,
     tail, full,
 ):
@@ -117,16 +117,17 @@
     @pl.when(step_index == 0)
     def _():
         near = norm_rows(halo_ref[0].astype(F32), gain).astype(BF)
-        tail[...] = dot(near, wm_ref[...]).astype(BF).astype(F32)
+        tail[...] = dot(near, w_ref[:, :CONVCH]).astype(BF).astype(F32)
         state_ref[...] = jnp.zeros_like(state_ref)
         total_ref[...] = jnp.zeros_like(total_ref)
 
     normed = norm_rows(u_ref[0].astype(F32), gain).astype(BF)
     normed_ref[0] = normed
-    mixed_low = dot(normed, wm_ref[...]).astype(BF)
+    projected = dot(normed, w_ref[...])
+    mixed_low = projected[:, :CONVCH].astype(BF)
     mixed_ref[0] = mixed_low
     mixed = mixed_low.astype(F32)
-    z = dot(normed, wdt_ref[...]).astype(BF).astype(F32) + dtb_ref[0:1, :]
+    z = projected[:, CONVCH:].astype(BF).astype(F32) + dtb_ref[0:1, :]
     z_ref[0] = z
     full[0:8, :] = tail[...]
     full[8:, :] = mixed
@@ -158,8 +159,8 @@
 def second_kernel(
     pre_ref, z_ref, gate_ref, bgrad_ref, u_ref, enter_ref, wo_ref, skip_ref, ggain_ref, alog_ref,
     emat_ref, gmat_ref,
-    out_ref, branch_ref, dy_ref, ggrad_ref, state_ref, rdot_ref, dstate_ref, gain_acc, skip_acc,
-    state, running, xs, ys, es,
+    out_ref, branch_ref, dy_ref, ggrad_ref, state_ref, rdot_ref, dstate_ref, sums_ref,
+    gain_acc, skip_acc, state, running, xs, ys, es,
 ):
     step_index = pl.program_id(1)
     tile = pre_ref.shape[1]
@@ -260,12 +261,17 @@
         rows = slice(part * BL, (part + 1) * BL)
         dstate_ref[0] = dstate_ref[0] + dot3(cts[part], es[rows, :])
 
+    @pl.when((step_index == pl.num_programs(1) - 1) & (pl.program_id(0) == pl.num_programs(0) - 1))
+    def _():
+        sums_ref[0:1, :] = jnp.sum(gain_acc[...], axis=0, keepdims=True)
+        sums_ref[1:2, :] = jnp.sum(skip_acc[...], axis=0, keepdims=True)
+
 
 def third_kernel(
     pre_ref, mixed_ref, z_ref, dy_ref, state_ref, rdot_ref, leave_ref, cw_ref, skip_ref, alog_ref,
     emat_ref, gmat_ref,
-    mgrad_ref, dz_ref, last_ref, first_ref, cw_acc, cb_acc, dtb_acc, rate_acc,
-    dstate, tail, full,
+    mgrad_ref, last_ref, first_ref, sums_ref,
+    cw_acc, cb_acc, dtb_acc, rate_acc, dstate, tail, full,
 ):
     step_index = pl.program_id(1)
 
@@ -346,7 +352,7 @@
     dcum = jnp.where(lanes, dcum, 0.0)
     drate = prefix(high_tri, dcum)
     dz = (rate * drate + direct) * sigmoid(z)
-    dz_ref[0] = dz.astype(BF)
+    mgrad_ref[0, :, CONVCH:] = dz.astype(BF)
     dtb_acc[...] += jnp.sum(dz.reshape(BL // 8, 8, 128), axis=0)
     rate_acc[...] += jnp.sum((step * drate).reshape(BL // 8, 8, 128), axis=0)
     db = dot3(dscores_t, inputs_c) + dot3(shrink * scaled, ds, NT)
@@ -364,12 +370,39 @@
         moved = full[KCONV - 1 - tap : KCONV - 1 - tap + BL, :]
         mgrad = mgrad + cw_ref[tap : tap + 1, :] * moved
         cw_acc[tap] += jnp.sum((moved * mixed).reshape(BL // 8, 8, CONVCH), axis=0)
-    mgrad_ref[0] = mgrad.astype(BF)
+    mgrad_ref[0, :, :CONVCH] = mgrad.astype(BF)
 
     @pl.when(step_index == 0)
     def _():
         last_ref[0] = mgrad[BL - 8 :, :]
 
+    @pl.when((step_index == pl.num_programs(1) - 1) & (pl.program_id(0) == pl.num_programs(0) - 1))
+    def _():
+        for tap in range(KCONV):
+            sums_ref[tap : tap + 1, :] = jnp.sum(cw_acc[tap], axis=0, keepdims=True)
+        sums_ref[4:5, :] = jnp.sum(cb_acc[...], axis=0, keepdims=True)
+        sums_ref[5:6, :128] = jnp.sum(dtb_acc[...], axis=0, keepdims=True)
+        sums_ref[6:7, :128] = jnp.sum(rate_acc[...], axis=0, keepdims=True)
+
+
+def patch_kernel(mgrad_ref, mixed_ref, last_ref, near_ref, cw_ref, out_ref, extra_ref):
+    @pl.when(pl.program_id(0) == 0)
+    def _():
+        extra_ref[...] = jnp.zeros_like(extra_ref)
+
+    rows = [last_ref[0, i : i + 1, :] for i in range(8)]
+    near = [near_ref[0, i : i + 1, :] for i in range(KCONV - 1)]
+    held = mixed_ref[0].astype(F32)
+    first = 8 - (KCONV - 1)
+    for k in range(KCONV - 1):
+        for j in range(k, KCONV - 1):
+            rows[first + j] = rows[first + j] + cw_ref[k : k + 1, :] * near[j - k]
+            extra_ref[k : k + 1, :] += near[j - k] * held[8 + first + j : 9 + first + j, :]
+    old = mgrad_ref[0].astype(F32)
+    patched = jnp.concatenate([old[:8, :CONVCH], jnp.concatenate(rows, axis=0)], axis=0)
+    out_ref[0, :, :CONVCH] = patched.astype(BF)
+    out_ref[0, :, CONVCH:] = mgrad_ref[0, :, CONVCH:]
+
 
 PARAMS = dict(vmem_limit_bytes=60 * 1024 * 1024)
 
@@ -379,7 +412,7 @@
     return pl.BlockSpec(shape, lambda b, i: zeros)
 
 
-def run_first(u, halo, gain, wm, wdt, cw, cb, dtb, alog, emat):
+def run_first(u, halo, gain, w, cw, cb, dtb, alog, emat):
     seqs, length, _ = u.shape
     tile = min(256, length)
     grid = (seqs, length // tile)
@@ -389,7 +422,7 @@
         first_kernel,
         grid=grid,
         in_specs=[
-            tok(D), per(8, D), whole(gain.shape), whole(wm.shape), whole(wdt.shape),
+            tok(D), per(8, D), whole(gain.shape), whole(w.shape),
             whole(cw.shape), whole(cb.shape), whole(dtb.shape), whole(alog.shape), whole(emat.shape),
         ],
         out_specs=[
@@ -406,7 +439,7 @@
         scratch_shapes=[pltpu.VMEM((8, CONVCH), F32), pltpu.VMEM((tile + 8, CONVCH), F32)],
         compiler_params=pltpu.CompilerParams(**PARAMS),
         name="first",
-    )(u, halo, gain, wm, wdt, cw, cb, dtb, alog, emat)
+    )(u, halo, gain, w, cw, cb, dtb, alog, emat)
 
 
 def run_second(pre, z, gate, bgrad, u, enter, wo, skip, ggain, alog, emat, gmat):
@@ -430,7 +463,7 @@
         out_specs=[
             tok(D), flat(DI), flat(DI), flat(DI),
             pl.BlockSpec((1, parts, DSTATE, DI), lambda b, i: (b, i, 0, 0)),
-            tok(128), per(DSTATE, DI), whole((ROWS, DI)), whole((ROWS, DI)),
+            tok(128), per(DSTATE, DI), whole((8, DI)),
         ],
         out_shape=[
             jax.ShapeDtypeStruct((seqs, length, D), BF),
@@ -440,10 +473,10 @@
             jax.ShapeDtypeStruct((seqs, length // BL, DSTATE, DI), F32),
             jax.ShapeDtypeStruct((seqs, length, 128), F32),
             jax.ShapeDtypeStruct((seqs, DSTATE, DI), F32),
-            jax.ShapeDtypeStruct((ROWS, DI), F32),
-            jax.ShapeDtypeStruct((ROWS, DI), F32),
+            jax.ShapeDtypeStruct((8, DI), F32),
         ],
         scratch_shapes=[
+            pltpu.VMEM((ROWS, DI), F32), pltpu.VMEM((ROWS, DI), F32),
             pltpu.VMEM((DSTATE, DI), F32), pltpu.VMEM((8, DI), F32), pltpu.VMEM((tile, DI), F32),
             pltpu.VMEM((tile, DI), F32), pltpu.VMEM((tile, DI), F32),
         ],
@@ -469,26 +502,43 @@
             whole(emat.shape), whole(gmat.shape),
         ],
         out_specs=[
-            tok(CONVCH), tok(128), per(8, CONVCH), per(8, CONVCH), whole((KCONV, 8, CONVCH)),
-            whole((8, CONVCH)), whole((8, 128)), whole((8, 128)),
+            tok(WIDE), per(8, CONVCH), per(8, CONVCH), whole((8, CONVCH)),
         ],
         out_shape=[
-            jax.ShapeDtypeStruct((seqs, length, CONVCH), BF),
-            jax.ShapeDtypeStruct((seqs, length, 128), BF),
+            jax.ShapeDtypeStruct((seqs, length, WIDE), BF),
             jax.ShapeDtypeStruct((seqs, 8, CONVCH), F32),
             jax.ShapeDtypeStruct((seqs, 8, CONVCH), F32),
-            jax.ShapeDtypeStruct((KCONV, 8, CONVCH), F32),
             jax.ShapeDtypeStruct((8, CONVCH), F32),
-            jax.ShapeDtypeStruct((8, 128), F32),
-            jax.ShapeDtypeStruct((8, 128), F32),
         ],
         scratch_shapes=[
+            pltpu.VMEM((KCONV, 8, CONVCH), F32), pltpu.VMEM((8, CONVCH), F32),
+            pltpu.VMEM((8, 128), F32), pltpu.VMEM((8, 128), F32),
             pltpu.VMEM((DSTATE, DI), F32), pltpu.VMEM((8, CONVCH), F32),
             pltpu.VMEM((BL + 8, CONVCH), F32),
         ],
         compiler_params=pltpu.CompilerParams(**PARAMS),
         name="third",
     )(pre, mixed, z, dy, states, rdot, leave, cw, skip, alog, emat, gmat)
+
+
+def run_patch(mgrad, mixed, last8, near, cw):
+    seqs, length, _ = mgrad.shape
+    end = length // 16 - 1
+    tok = lambda width: pl.BlockSpec((1, 16, width), lambda b: (b, end, 0))
+    per = pl.BlockSpec((1, 8, CONVCH), lambda b: (b, 0, 0))
+    row = pl.BlockSpec((8, CONVCH), lambda b: (0, 0))
+    return pl.pallas_call(
+        patch_kernel,
+        grid=(seqs,),
+        in_specs=[tok(WIDE), tok(CONVCH), per, per, row],
+        out_specs=[tok(WIDE), row],
+        out_shape=[
+            jax.ShapeDtypeStruct(mgrad.shape, BF),
+            jax.ShapeDtypeStruct((8, CONVCH), F32),
+        ],
+        input_output_aliases={0: 0},
+        name="patch",
+    )(mgrad, mixed, last8, near, cw)
 
 
 def norm_piece(incoming, norm_gain):
@@ -501,13 +551,13 @@
     row_size, col_size = (left_stat.shape[-1], right_stat.shape[-1])
     grad_tiles = gradient.reshape(row_tiles, row_size, col_tiles, col_size).transpose(0, 2, 1, 3)
     left_new = 0.5 * left_stat + 0.5 * jnp.einsum(
-        "abij,abkj->abik", grad_tiles, grad_tiles, precision=HIGH
+        "abij,abkj->abik", grad_tiles, grad_tiles, precision=lax.Precision.HIGH
     )
     right_new = 0.5 * right_stat + 0.5 * jnp.einsum(
-        "abji,abjk->abik", grad_tiles, grad_tiles, precision=HIGH
-    )
-    shaped = jnp.einsum("abij,abjk->abik", left_root, grad_tiles, precision=HIGH)
-    shaped = jnp.einsum("abij,abjk->abik", shaped, right_root, precision=HIGH)
+        "abji,abjk->abik", grad_tiles, grad_tiles, precision=lax.Precision.HIGH
+    )
+    shaped = jnp.einsum("abij,abjk->abik", left_root, grad_tiles, precision=lax.Precision.HIGH)
+    shaped = jnp.einsum("abij,abjk->abik", shaped, right_root, precision=lax.Precision.HIGH)
     update = (-LR * shaped).transpose(0, 2, 1, 3).reshape(gradient.shape)
     return (update, left_new, right_new)
 
@@ -571,6 +621,145 @@
     v = jnp.moveaxis(v.reshape(z, x, rows, size, cols // size), 3, 0)
     owned = across(scatter_stage(v, "seq"))
     return jnp.moveaxis(gather_stage(owned, "seq"), 0, 1).reshape(rows, cols)
+
+
+def xor_sum(v, axis):
+    size = lax.axis_size(axis)
+    bit = 1
+    while bit < size:
+        v = v + lax.ppermute(v, axis, [(i, i ^ bit) for i in range(size)])
+        bit *= 2
+    return v
+
+
+def chip_kernel(idx, *refs):
+    send_ref, own_ref = refs[-2:]
+    pieces = []
+    for part_ref, got_ref in zip(refs[:-2:2], refs[1:-2:2]):
+        total = part_ref[0, 0] + got_ref[0]
+        width = own_ref.shape[1]
+        rows = total.shape[0] * total.shape[1] // width
+        pieces += [
+            total[i * rows : (i + 1) * rows] for i in range(total.shape[0] // rows)
+        ]
+    mine = pl.program_id(0) == idx[0] * 2 + idx[1]
+    row = 0
+    col = 0
+    for piece in pieces:
+        rows, cols = piece.shape
+        at = (slice(row, row + rows), slice(col, col + cols))
+        send_ref[(0,) + at] = piece.astype(BF)
+
+        @pl.when(mine)
+        def _(at=at, piece=piece):
+            own_ref[at] = piece
+
+        col += cols
+        if col == own_ref.shape[1]:
+            row, col = row + rows, 0
+
+
+def chip_sum(idx, pairs):
+    in_specs, ins, total, width = [], [], 0, 0
+    for blocks, got in pairs:
+        _, _, rows, cols = blocks.shape
+        width = max(width, cols)
+        total += rows * cols
+        ins += [blocks, got]
+        in_specs += [
+            pl.BlockSpec((1, 1, rows, cols), lambda i, idx: (i, idx[2], 0, 0)),
+            pl.BlockSpec((1, rows, cols), lambda i, idx: (i, 0, 0)),
+        ]
+    rows = total // width
+    return pl.pallas_call(
+        chip_kernel,
+        grid_spec=pltpu.PrefetchScalarGridSpec(
+            num_scalar_prefetch=1,
+            grid=(8,),
+            in_specs=in_specs,
+            out_specs=[
+                pl.BlockSpec((1, rows, width), lambda i, idx: (i, 0, 0)),
+                pl.BlockSpec((rows, width), lambda i, idx: (0, 0)),
+            ],
+        ),
+        out_shape=[
+            jax.ShapeDtypeStruct((8, rows, width), BF),
+            jax.ShapeDtypeStruct((rows, width), F32),
+        ],
+        compiler_params=pltpu.CompilerParams(**PARAMS),
+        name="chip_sum",
+    )(idx, *ins)
+
+
+def owner_kernel(idx, own_ref, got_ref, out_ref):
+    mine = idx[0] * 2 + idx[1]
+    total = own_ref[...]
+    for i in range(8):
+        total = total + jnp.where(mine == i, 0.0, got_ref[i].astype(F32))
+    out_ref[...] = total
+
+
+def owner_sum(idx, own, got):
+    rows, width = own.shape
+    tile = 16
+    return pl.pallas_call(
+        owner_kernel,
+        grid_spec=pltpu.PrefetchScalarGridSpec(
+            num_scalar_prefetch=1,
+            grid=(rows // tile,),
+            in_specs=[
+                pl.BlockSpec((tile, width), lambda i, idx: (i, 0)),
+                pl.BlockSpec((8, tile, width), lambda i, idx: (0, i, 0)),
+            ],
+            out_specs=pl.BlockSpec((tile, width), lambda i, idx: (i, 0)),
+        ),
+        out_shape=jax.ShapeDtypeStruct((rows, width), F32),
+        name="owner_sum",
+    )(idx, own, got)
+
+
+def core_exchange(partial, core):
+    rows, cols = partial.shape
+    blocks = partial.reshape(8, 2, rows // 16, cols)
+    sent = lax.dynamic_index_in_dim(blocks, 1 - core, 1, keepdims=False)
+    return blocks, swapped(sent, "core", 2, 1)
+
+
+def around(v, axis):
+    size = lax.axis_size(axis)
+    return jnp.stack([v] + [swapped(v, axis, size, offset) for offset in range(1, size)])
+
+
+def assemble_kernel(idx, near_ref, far_ref, out_ref, *, order):
+    sizes = {"z": 4, "x": 2, "seq": 2}
+    here = {"z": idx[0], "x": idx[1], "core": idx[2], "seq": idx[3]}
+    for a in range(near_ref.shape[0]):
+        for b in range(near_ref.shape[1]):
+            for c in range(near_ref.shape[2]):
+                at = dict(
+                    (axis, lax.rem(here[axis] - back + sizes[axis], sizes[axis]))
+                    for axis, back in zip(order[::-1], (a, b, c))
+                )
+                for ref, core in ((near_ref, here["core"]), (far_ref, 1 - here["core"])):
+                    block = ((at["z"] * 2 + at["x"]) * 2 + core) * 2 + at["seq"]
+                    out_ref[block] = ref[a, b, c]
+
+
+def assemble(idx, near, far, order):
+    rows, cols = near.shape[-2:]
+    out = pl.pallas_call(
+        functools.partial(assemble_kernel, order=order),
+        grid_spec=pltpu.PrefetchScalarGridSpec(
+            num_scalar_prefetch=1,
+            grid=(1,),
+            in_specs=[pl.BlockSpec(near.shape, lambda i, idx: (0,) * 5)] * 2,
+            out_specs=pl.BlockSpec((32, rows, cols), lambda i, idx: (0, 0, 0)),
+        ),
+        out_shape=jax.ShapeDtypeStruct((32, rows, cols), near.dtype),
+        compiler_params=pltpu.CompilerParams(**PARAMS),
+        name="assemble",
+    )(idx, near, far)
+    return out.reshape(32 * rows, cols)
 
 
 def row8(v, width=None):
@@ -618,9 +807,22 @@
     main = lax.all_gather(
         jnp.concatenate([in_low[:, DI:], dt_low], axis=1), AXES, axis=0, tiled=True
     )
-    wg = lax.all_gather(in_low[:, :DI], AXES, axis=0, tiled=True)
-    wo = lax.all_gather(out_weight.astype(BF), AXES, axis=0, tiled=True)
-    wm, wdt = main[:, :CONVCH], main[:, CONVCH:]
+    torus_sizes = tuple(lax.axis_size(a) for a in ("z", "x", "core", "seq"))
+    direct = torus_sizes == (4, 2, 2, 2)
+    idx = jnp.stack([lax.axis_index(a) for a in ("z", "x", "core", "seq")]).astype(jnp.int32)
+    gate_low, out_low = in_low[:, :DI], out_weight.astype(BF)
+    if direct:
+        order = ("z", "x", "seq")
+        gate_near = pick(gate_low.reshape(2, -1, DI), idx[3])
+        out_near = pick(out_low.reshape(2, -1, D), idx[3])
+        gate_near = around(around(gate_near, "z"), "x")
+        out_near = around(around(out_near, "z"), "x")
+        main, _, _ = lax.optimization_barrier((main, gate_near, out_near))
+        gate_near = around(gate_near, "seq")
+        out_near = around(out_near, "seq")
+    else:
+        wg = lax.all_gather(gate_low, AXES, axis=0, tiled=True)
+        wo = lax.all_gather(out_low, AXES, axis=0, tiled=True)
     halo = lax.ppermute(block_input[:, local_len - 8 :, :], "seq", up)
 
     part = jnp.arange(128)
@@ -635,19 +837,24 @@
     cw8 = jnp.pad(conv_weight, ((0, 4), (0, 0)))
 
     normed, mixed, pre, z, local_state, total = run_first(
-        block_input, halo, row8(norm_gain), wm, wdt, cw8, row8(conv_bias), dtb, alog, emat
+        block_input, halo, row8(norm_gain), main, cw8, row8(conv_bias), dtb, alog, emat
     )
     span = jnp.repeat(jnp.exp(total[:, 0:1, :HEADS]), HEADDIM, axis=2)
     enter = lax.ppermute(local_state, "seq", up)
     for _ in range(seq_devices - 2):
         enter = lax.ppermute(local_state + span * enter, "seq", up)
 
+    if direct:
+        out_far = swapped(out_near, "core", 2, 1)
+        gate_far = swapped(gate_near, "core", 2, 1)
+        wo = assemble(idx, out_near, out_far, order)
+        wg = assemble(idx, gate_near, gate_far, order)
     normed_rows = normed.reshape(row_count, D)
     upstream = cotangent.reshape(row_count, D)
     gate_part = dot(normed_rows, wg)
     branch_grad = dot(upstream, wo, NT)
     (
-        block_output, branch, states_grad, gate_grad, states, rdot, local_dstate, gain_acc, skip_acc,
+        block_output, branch, states_grad, gate_grad, states, rdot, local_dstate, row_sums,
     ) = run_second(
         pre, z, gate_part, branch_grad, block_input, enter, wo, skip_wide, row8(gate_gain), alog,
         emat, gmat,
@@ -656,55 +863,27 @@
     for _ in range(seq_devices - 2):
         leave = lax.ppermute(local_dstate + span * leave, "seq", down)
 
-    out_grad = reduce_split(core_sum(dot(branch, upstream, TN)))
-    gate_sum = reduce_plain(core_sum(dot(normed_rows, gate_grad, TN)))
-
-    mgrad, dz, last8, first8, cw_acc, cb_acc, dtb_acc, rate_acc = run_third(
+    out_partial = dot(branch, upstream, TN)
+    gate_partial = dot(normed_rows, gate_grad, TN)
+    if direct:
+        early, early_own = chip_sum(
+            idx, [core_exchange(gate_partial, idx[2]), core_exchange(out_partial, idx[2])]
+        )
+        states_grad, early = lax.optimization_barrier((states_grad, early))
+        early = lax.all_to_all(early, ("z", "x"), split_axis=0, concat_axis=0, tiled=True)
+
+    mgrad, last8, first8, column_sums = run_third(
         pre, mixed, z, states_grad, states, rdot, leave, cw8, skip_wide, alog, emat, gmat
     )
     near = lax.ppermute(first8, "seq", down)
-    ends = mixed[:, local_len - 8 :, :].astype(F32)
-    extra = jnp.stack(
-        [
-            sum(conv_weight[k] * near[:, j - k, :] for k in range(j + 1))
-            for j in range(KCONV - 1)
-        ],
-        axis=1,
-    )
-    last8 = last8 + jnp.pad(extra, ((0, 0), (8 - (KCONV - 1), 0), (0, 0)))
-    mgrad = lax.dynamic_update_slice(mgrad, last8.astype(BF), (0, local_len - 8, 0))
-    cw_extra = jnp.stack(
-        [
-            sum(
-                (near[:, j - k, :] * ends[:, 8 - (KCONV - 1) + j, :] for j in range(k, KCONV - 1)),
-                jnp.zeros((seq_count, CONVCH), F32),
-            ).sum(0)
-            for k in range(KCONV)
-        ]
-    )
-    conv_weight_grad = cw_acc.sum(1) + cw_extra
-    conv_bias_grad = cb_acc.sum(0)
-
-    mgrad_rows = mgrad.reshape(row_count, CONVCH)
-    dz_rows = dz.reshape(row_count, 128)
-    mixed_local = jnp.concatenate(
-        [
-            dot(normed_rows, mgrad_rows, TN),
-            dot(normed_rows, dz_rows, TN),
-        ],
-        axis=1,
-    )
-    mixed_chip = core_sum(mixed_local)
-    third_cols = mixed_chip.shape[3] // 3
-    mixed_sum = jnp.concatenate(
-        [
-            reduce_plain(mixed_chip[..., :third_cols]),
-            reduce_split(mixed_chip[..., third_cols:]),
-        ],
-        axis=1,
-    )
+    mgrad, extra = run_patch(mgrad, mixed, last8, near, cw8)
+    conv_weight_grad = (column_sums + extra)[:KCONV]
+    conv_bias_grad = column_sums[KCONV]
+
+    mgrad_rows = mgrad.reshape(row_count, WIDE)
+    mixed_local = dot(normed_rows, mgrad_rows, TN)
     normed_grad = (
-        dot(gate_grad, wg, NT) + dot(mgrad_rows, wm, NT) + dot(dz_rows, wdt, NT)
+        dot(gate_grad, wg, NT) + dot(mgrad_rows, main, NT)
     )
     incoming = block_input.reshape(row_count, D).astype(F32)
     _, norm_back = jax.vjp(norm_piece, incoming, norm_gain)
@@ -714,15 +893,33 @@
     vector_local = jnp.concatenate(
         [
             norm_gain_grad,
-            gain_acc.sum(0),
+            row_sums[0],
             conv_weight_grad.reshape(-1),
             conv_bias_grad,
-            dtb_acc.sum(0)[:HEADS],
-            -jnp.exp(decay_log) * rate_acc.sum(0)[:HEADS],
-            skip_acc.sum(0).reshape(HEADS, HEADDIM).sum(1),
+            column_sums[5, :HEADS],
+            -jnp.exp(decay_log) * column_sums[6, :HEADS],
+            row_sums[1].reshape(HEADS, HEADDIM).sum(1),
         ]
     )
-    vector_grad = lax.psum(vector_local, AXES + ("seq",))
+    if direct:
+        late, late_own = chip_sum(idx, [core_exchange(mixed_local, idx[2])])
+        vector_local, early, late = lax.optimization_barrier((vector_local, early, late))
+        late = lax.all_to_all(late, ("z", "x"), split_axis=0, concat_axis=0, tiled=True)
+        early_own = owner_sum(idx, early_own, early)
+        early_own = early_own + swapped(early_own, "seq", 2, 1)
+        share = D // 16
+        gate_sum = early_own[:share]
+        out_grad = jnp.concatenate([early_own[share:, :D], early_own[share:, D:]], axis=0)
+        late_own = owner_sum(idx, late_own, late)
+        mixed_sum = late_own + swapped(late_own, "seq", 2, 1)
+    else:
+        gate_sum = reduce_plain(core_sum(gate_partial))
+        out_grad = reduce_split(core_sum(out_partial))
+        mixed_sum = reduce_plain(core_sum(mixed_local))
+    vector_rows = jnp.pad(vector_local, (0, -vector_local.shape[0] % 1024)).reshape(-1, 128)
+    for axis in ("core", "seq", "x", "z"):
+        vector_rows = xor_sum(vector_rows, axis)
+    vector_grad = vector_rows.reshape(-1)[: vector_local.shape[0]]
 
     in_grad = jnp.concatenate([gate_sum, mixed_sum[:, :CONVCH]], axis=1)
     dt_grad = mixed_sum[:, CONVCH : CONVCH + HEADS]
@@ -770,6 +967,7 @@
     placed = (
         (tokens, tokens, rows, rows, rows) + (P(),) * 7 + (quad,) * 4 + (tri,) * 4 + (quad,) * 4 + (P(),)
     )
+
     return jax.shard_map(
         body,
         mesh=torus,

time: 522 us -> 432 us (0.83)
  blocking collectives: 46.9 us -> 0 us
  local copies, waits for them, and re-layouts: 92.4 us -> 46 us
  Pallas kernels: 112 us -> 147 us
  other arithmetic: 40.6 us -> 23.5 us
    psum x1 -> x0, blocking collectives: 46.9 us -> none  [body(): vector_grad = lax.psum(vector_local, AXES + ('seq',))]
    all_gather x1, waiting for transfers between devices: 38.5 us -> 0.01 us  [body(): lax.all_gather(jnp.concatenate([in_low[:, DI:], dt_low], axis=1), AXES, a...]
    all_gather x2 -> x0, waiting for transfers between devices: 36.2 us -> none  [the longest x1 24.8 us: body(): wo = lax.all_gather(out_weight.astype(BF), AXES, axis=0, tiled=True)]
    pallas_call x0 -> x7, Pallas kernels: none -> 34.2 us  [the longest x2 15.3 us: chip_sum(): pl.pallas_call(chip_kernel, grid_spec=pltpu.PrefetchScalarGridSpec(num_sc...]
    ppermute x25 -> x17, waiting for transfers between devices: 12.2 us -> 39.3 us  [swapped(): lax.ppermute(v, axis, [(i, (i + offset) % size) for i in range(size)])]
    ppermute x25 -> x17, starting transfers between devices: 39 us -> 17.8 us  [swapped(): lax.ppermute(v, axis, [(i, (i + offset) % size) for i in range(size)])]
    ppermute x0 -> x5, waiting for transfers between devices: none -> 17.8 us  [xor_sum(): v = v + lax.ppermute(v, axis, [(i, i ^ bit) for i in range(size)])]
    all_to_all x0 -> x2, waiting for transfers between devices: none -> 15.7 us  [the longest x1 15.7 us: body(): lax.all_to_all(early, ('z', 'x'), split_axis=0, concat_axis=0, tiled=True)]
  transfers between devices with their start and end apart: 32 -> 29, of which waited for: 12 -> 16; matrix products, arithmetic and copies ran while one was open for 28% -> 20% of each run, Pallas kernels for 12% -> 11%
where the time goes in v3:
time: 432 us; the launch traced here: 425 us
  Pallas kernels  147 us (34%)
  waiting for transfers between devices  82.2 us (19%)
  matrix products  63.9 us (15%)
  starting transfers between devices  47.9 us (11%)
  local copies, waits for them, and re-layouts  46 us (11%)
  other arithmetic  23.5 us (5%)
  between operations  14.9 us (3%)
    pallas_call x1, Pallas kernels, run_second(): pl.pallas_call(second_kernel, grid=grid, in_specs=[tok(CONVCH), tok(128),...  50.2 us
    pallas_call x1, Pallas kernels, run_third(): pl.pallas_call(third_kernel, grid=grid, in_specs=[tok(CONVCH), tok(CONVCH...  45.3 us
    dot_general x7, matrix products, dot(): return lax.dot_general(a, b, dims, preferred_element_type=F32)  40.3 us
    ppermute x17, waiting for transfers between devices, swapped(): lax.ppermute(v, axis, [(i, (i + offset) % size) for i in range(size)])  39.3 us
    unnamed x73, local copies, waits for them, and re-layouts  21.8 us
    ppermute x5, waiting for transfers between devices, xor_sum(): v = v + lax.ppermute(v, axis, [(i, i ^ bit) for i in range(size)])  17.8 us
    ppermute x17, starting transfers between devices, swapped(): lax.ppermute(v, axis, [(i, (i + offset) % size) for i in range(size)])  17.8 us
    pallas_call x1, Pallas kernels, run_first(): pl.pallas_call(first_kernel, grid=grid, in_specs=[tok(D), per(8, D), whol...  16.8 us
  transfers between devices with their start and end apart: 29, of which 16 were waited for; matrix products, arithmetic and copies ran while one was open for 20% of the time, Pallas kernels for 11%

profile of v3, /device:TPU:0, one launch (start us, length us, event | category | flops | bytes accessed | tf_op | source)
XLA Modules:
  0.0 424.9 jit_solution(2009656832604835155)
XLA Ops:
  13.4 4.1 collective-permute-start.6
  21.9 3.1 collective-permute-done.5
  26.9 2.2 collective-permute-start.2
  29.0 2.7 collective-permute-start.3
  31.7 2.4 collective-permute-done.8
  35.8 2.6 collective-permute-done.2
  39.5 3.4 collective-permute-start
  43.0 3.0 collective-permute-done.4
  47.7 2.8 collective-permute-done.11
  52.6 8.7 %collective-permute-done.9 = bf16[2,4,24,1536]{3,2,1,0:T(8,128)(2,1)S(1)} collective-permute-done((bf16[2,4,24,1536]{3,2,1,0:T(8,128)(2,1)S(1)}, bf16[2,4,24,1536]{3,2,1,0:T(8,128)(2,1)S(1)}, u32[]{:S(2)}, u32[]{:S(2)}) %collective-permute-start.9) | collective-permute-done | bytes 589856 | tf_op jit(solution)/shard_map/ppermute | solution.py:566
  64.9 3.8 assemble.3
  71.2 16.8 %first.1 = (bf16[1,1024,768]{2,1,0:T(8,128)(2,1)}, bf16[1,1024,1792]{2,1,0:T(8,128)(2,1)}, f32[1,1024,1792]{2,1,0:T(8,128)}, f32[1,1024,128]{2,1,0:T(8,128)}, f3...) custom-call(bf16[1,1024,768]{2,1,0:T(8,128)(2,1)} %u_ref.3, bf16[1,8,768]{2,1,0:T(8,128)(2,1)} %copy-done.25, ...), custom_call_target="tpu_custom_call" | custom-call | tf_op jit(solution)/shard_map/first/pallas_call | solution.py:421
  88.0 4.7 %collective-permute-start.13 = (f32[1,128,1536]{2,1,0:T(8,128)}, f32[1,128,1536]{2,1,0:T(8,128)}, u32[]{:S(2)}, u32[]{:S(2)}) collective-permute-start(f32[1,128,1536]{2,1,0:T(8,128)} %get-tuple-element.50), channel_id=1, source_target_pairs={{0,1},{2,3},{4,5},{6,7},{8,9},{10,11},{12,13},{14,15},{16,17},{18,... | collective-permute-start | bytes 2359304 | tf_op jit(solution)/shard_map/ppermute | solution.py:843
  92.7 7.3 %convolution_bitcast_fusion.bgrad_ref = f32[1024,1536]{1,0:T(8,128)} fusion(bf16[1536,768]{1,0:T(8,128)(2,1)} %bitcast.145, bf16[1,1024,768]{2,1,0:T(8,128)(2,1)} %param.26), kind=kOutput, calls=%fused_computation.5 | convolution fusion | flops 2415919104 | bytes 10223616 | tf_op jit(solution)/shard_map/dot_general | solution.py:38
  100.1 3.9 assemble.2
  103.9 2.6 copy.70
  106.5 7.4 %fusion.15.gate_ref = f32[1024,1536]{1,0:T(8,128)} fusion(bf16[768,1536]{1,0:T(8,128)(2,1)} %bitcast.150, bf16[1,1024,768]{2,1,0:T(8,128)(2,1)} %get-tuple-element.49), kind=kOutput, calls=%fused_computation.26 | convolution fusion | flops 2415919104 | bytes 10223616 | tf_op jit(solution)/shard_map/dot_general | solution.py:38
  115.2 50.2 %second.1 = (bf16[1,1024,768]{2,1,0:T(8,128)(2,1)}, bf16[1024,1536]{1,0:T(8,128)(2,1)}, bf16[1024,1536]{1,0:T(8,128)(2,1)}, bf16[1024,1536]{1,0:T(8,128)(2,1)}, ...) custom-call(f32[1,1024,1792]{2,1,0:T(8,128)} %get-tuple-element.47.pre_ref, ...), custom_call_target="tpu_custom_call" | custom-call | tf_op jit(solution)/shard_map/second/pallas_call | solution.py:455
  165.4 4.8 %copy.71 = bf16[1536,1024]{1,0:T(8,128)(2,1)} copy(bf16[1536,1024]{0,1:T(8,128)(2,1)} %bitcast.147) | data formatting | bytes 6291456 | tf_op jit(solution)/shard_map/dot_general | solution.py:38
  170.3 5.0 %fusion.12.refs_2_ = f32[8,2,96,768]{3,2,1,0:T(8,128)S(1)} fusion(bf16[8,2,96,1024]{3,2,1,0:T(8,128)(2,1)} %bitcast.148, bf16[1,1024,768]{2,1,0:T(8,128)(2,1)} %param.26), kind=kOutput, calls=%fused_computation.23 | convolution fusion | flops 2415919104 | bytes 9437184 | tf_op jit(solution)/shard_map/dot_general | solution.py:38
  179.4 2.6 fusion.10.refs_0_
  188.8 8.2 %chip_sum.2 = (bf16[8,96,1536]{2,1,0:T(8,128)(2,1)}, f32[96,1536]{1,0:T(8,128)}) custom-call(s32[4]{0:T(128)} %pad_add_fusion.idx, f32[8,2,48,1536]{3,2,1,0:T(8,128)} %copy-done.4, f32[8,48,1536]{2,1,0:T(8,128)} %collective-permute-done.14.refs_1_, f32[8,2,96,768]{3,2,1,0:T(8,128)} %copy-done.3, f32[8,96,768]{2,1,0:T(8,128)} %copy-done.10), custom_call_target="tpu_custom_call" | custom-call | tf_op jit(solution)/shard_map/chip_sum/pallas_call | solution.py:674
  196.9 9.3 %collective-permute-done.16.leave_ref = f32[1,128,1536]{2,1,0:T(8,128)} collective-permute-done((f32[1,128,1536]{2,1,0:T(8,128)}, f32[1,128,1536]{2,1,0:T(8,128)}, u32[]{:S(2)}, u32[]{:S(2)}) %collective-permute-start.16) | collective-permute-done | bytes 786464 | tf_op jit(solution)/shard_map/ppermute | solution.py:862
  206.2 45.3 %third.1 = (bf16[1,1024,1920]{2,1,0:T(8,128)(2,1)}, f32[1,8,1792]{2,1,0:T(8,128)}, f32[1,8,1792]{2,1,0:T(8,128)}, f32[8,1792]{1,0:T(8,128)}) custom-call(f32[1,1024,1792]{2,1,0:T(8,128)} %get-tuple-element.47.pre_ref, bf16[1,1024,1792]{2,1,0:T(8,128)(2,1)} %get-tuple-element.53.mixed_ref, f32[1,1024,128]{2,1,0:T(8,128)} %get-tuple-element.48.z_ref, ...), custom_call_target="tpu_custom_call" | custom-call | tf_op jit(solution)/shard_map/third/pallas_call | solution.py:494
  252.9 5.5 %all-to-all-start = ((bf16[8,96,1536]{2,1,0:T(8,128)(2,1)}), bf16[8,96,1536]{2,1,0:T(8,128)(2,1)}, u32[]{:S(2)}, u32[]{:S(2)}) async-start(bf16[8,96,1536]{2,1,0:T(8,128)(2,1)} %get-tuple-element.69), calls=%async_computation | async-start | bytes 4718592 | tf_op jit(solution)/shard_map/all_to_all | solution.py:873
  262.4 6.0 %fusion.refs_0_ = f32[8,2,48,1920]{3,2,1,0:T(8,128)S(1)} fusion(bf16[8,2,48,1024]{3,2,1,0:T(8,128)(2,1)} %bitcast.152, bf16[1,1024,1920]{2,1,0:T(8,128)(2,1)} %get-tuple-element.64), kind=kOutput, calls=%fused_computation.6 | convolution fusion | flops 3019898880 | bytes 11403264 | tf_op jit(solution)/shard_map/dot_general | solution.py:38
  268.4 2.5 copy-done.2
  277.0 6.6 %fusion.2 = f32[1024,768]{1,0:T(8,128)S(1)} fusion(bf16[768,1920]{1,0:T(8,128)(2,1)} %all-gather.2.cloned.1.call-done.w_ref, bf16[1,1024,1920]{2,1,0:T(8,128)(2,1)} %get-tuple-element.64), kind=kOutput, calls=%fused_computation.8 | convolution fusion | flops 3019898880 | bytes 10027008 | tf_op jit(solution)/shard_map/dot_general | solution.py:38
  283.6 5.3 %fusion.9 = (f32[768]{0:T(1024)S(1)}, f32[1024]{0:T(1024)}, f32[1024,768]{1,0:T(8,128)}) fusion(bf16[1,1024,768]{2,1,0:T(8,128)(2,1)S(1)} %copy-done.1, f32[1024]{0:T(1024)S(1)} %fusion.44, f32[768]{0:T(1024)S(1)} %copy-done.23, f32[1024,768]{1,0:T(8,128)S(1)} %fusion.2, bf16[1024,1536]{1,0:T(8,128)(2,1)S(1)} %copy-done.30, bf16[768,1536]{1,0:T(8,128)(2,1)S(1)} %bitcast.151), kind=kOutput, calls=%fused_computation.16 | convolution fusion | flops 2422208768 | bytes 13383680 | tf_op jit(solution)/shard_map/dot_general | solution.py:38
  289.0 7.1 %chip_sum.3 = (bf16[8,48,1920]{2,1,0:T(8,128)(2,1)}, f32[48,1920]{1,0:T(8,128)}) custom-call(s32[4]{0:T(128)} %pad_add_fusion.idx, f32[8,2,48,1920]{3,2,1,0:T(8,128)} %copy-done.2, f32[8,48,1920]{2,1,0:T(8,128)} %collective-permute-done.18.refs_1_), custom_call_target="tpu_custom_call" | custom-call | tf_op jit(solution)/shard_map/chip_sum/pallas_call | solution.py:674
  296.1 15.7 %all-to-all-done.got_ref = bf16[8,96,1536]{2,1,0:T(8,128)(2,1)} async-done(((bf16[8,96,1536]{2,1,0:T(8,128)(2,1)}), bf16[8,96,1536]{2,1,0:T(8,128)(2,1)}, u32[]{:S(2)}, u32[]{:S(2)}) %all-to-all-start) | async-done | bytes 2359328 | tf_op jit(solution)/shard_map/all_to_all | solution.py:873
  313.1 2.4 collective-permute-start.22
  315.5 4.3 %all-to-all-start.1 = ((bf16[8,48,1920]{2,1,0:T(8,128)(2,1)}), bf16[8,48,1920]{2,1,0:T(8,128)(2,1)}, u32[]{:S(2)}, u32[]{:S(2)}) async-start(bf16[8,48,1920]{2,1,0:T(8,128)(2,1)} %get-tuple-element.73), calls=%async_computation.1 | async-start | bytes 2949120 | tf_op jit(solution)/shard_map/all_to_all | solution.py:907
  322.6 2.3 copy.73
  324.8 2.3 copy.79
  327.1 6.1 %collective-permute-done.23 = f32[96,128]{1,0:T(8,128)S(1)} collective-permute-done((f32[96,128]{1,0:T(8,128)S(1)}, f32[96,128]{1,0:T(8,128)S(1)}, u32[]{:S(2)}, u32[]{:S(2)}) %collective-permute-start.23) | collective-permute-done | bytes 49184 | tf_op jit(solution)/shard_map/ppermute | solution.py:630
  335.5 10.5 %collective-permute-done.24 = f32[96,128]{1,0:T(8,128)S(1)} collective-permute-done((f32[96,128]{1,0:T(8,128)S(1)}, f32[96,128]{1,0:T(8,128)S(1)}, u32[]{:S(2)}, u32[]{:S(2)}) %collective-permute-start.24) | collective-permute-done | bytes 49184 | tf_op jit(solution)/shard_map/ppermute | solution.py:630
  346.0 3.7 collective-permute-start.25
  349.6 5.4 %fusion.5 = f32[1,1024,768]{2,1,0:T(8,128)} fusion(f32[1024,768]{1,0:T(8,128)} %get-tuple-element.143, bf16[1,1024,768]{2,1,0:T(8,128)(2,1)} %u_ref.3, bf16[1,1024,768]{2,1,0:T(8,128)(2,1)} %param.26, f32[1024]{0:T(1024)S(1)} %multiply_multiply_fusion.1, f32[1024]{0:T(1024)} %copy-done.24, f32[768]{0:T(1024)} %param.30), kind=kLoop, calls=%fused_computation.12 | loop fusion | flops 6291456 | bytes 9448448 | tf_op jit(solution)/shard_map/reshape | solution.py:891
  355.0 5.6 %owner_sum.2 = f32[96,1536]{1,0:T(8,128)} custom-call(s32[4]{0:T(128)} %pad_add_fusion.idx, f32[96,1536]{1,0:T(8,128)} %get-tuple-element.65.own_ref, bf16[8,96,1536]{2,1,0:T(8,128)(2,1)} %all-to-all-done.got_ref), custom_call_target="tpu_custom_call" | custom-call | tf_op jit(solution)/shard_map/owner_sum/pallas_call | solution.py:705
  361.6 13.3 %collective-permute-done.19 = f32[96,1536]{1,0:T(8,128)S(1)} collective-permute-done((f32[96,1536]{1,0:T(8,128)}, f32[96,1536]{1,0:T(8,128)S(1)}, u32[]{:S(2)}, u32[]{:S(2)}) %collective-permute-start.19) | collective-permute-done | bytes 589856 | tf_op jit(solution)/shard_map/ppermute | solution.py:566
  380.9 2.9 fusion.20
  383.7 4.0 owner_sum.3
  388.3 2.4 fusion.19
  392.5 3.7 add_multiply_fusion.1
  397.5 2.1 reshape.253
  399.6 7.2 %add_multiply_fusion = f32[2,26,128,128]{3,2,1,0:T(8,128)} fusion(f32[2,26,128,128]{3,2,1,0:T(8,128)} %param.38, f32[2,24,26,128]{3,2,1,0:T(8,128)} %reshape.253), kind=kOutput, calls=%fused_computation.10 | convolution fusion | flops 124387328 | bytes 7454720 | tf_op jit(solution)/shard_map/abji,abjk->abik/dot_general | solution.py:556
  412.4 2.2 copy.83
  (186 shorter events, 74.0 us)
Async XLA Ops:
  7.2 400.5 %copy-start = (f32[2,26,128,128]{3,2,1,0:T(8,128)S(1)}, f32[2,26,128,128]{3,2,1,0:T(8,128)}, u32[]{:S(2)}) copy-start(f32[2,26,128,128]{3,2,1,0:T(8,128)} %param.40) | copy-start | bytes 10223620
  7.2 61.5 %all-gather.2.cloned.1.call-start = ((), (), s32[]{:S(2)}) async-start(), calls=%async_computation.2 | async-start | bytes 3133440 | tf_op jit(solution)/shard_map/all_gather | solution.py:807
  13.4 7.7 %collective-permute-start.6 = (bf16[48,768]{1,0:T(8,128)(2,1)S(1)}, bf16[48,768]{1,0:T(8,128)(2,1)S(1)}, u32[]{:S(2)}, u32[]{:S(2)}) collective-permute-start(bf16[48,768]{1,0:T(8,128)(2,1)S(1)} %fusion.76), channel_id=1, source_target_pairs={{0,16},{8,24},{16,0},{24,8},{1,17},{9,25},{17,1},{25,9},{2,18},{10... | collective-permute-start | bytes 221192 | tf_op jit(solution)/shard_map/ppermute | solution.py:566
  17.5 4.4 %collective-permute-start.7 = (bf16[48,768]{1,0:T(8,128)(2,1)S(1)}, bf16[48,768]{1,0:T(8,128)(2,1)S(1)}, u32[]{:S(2)}, u32[]{:S(2)}) collective-permute-start(bf16[48,768]{1,0:T(8,128)(2,1)S(1)} %fusion.76), channel_id=1, source_target_pairs={{0,24},{8,0},{16,8},{24,16},{1,25},{9,1},{17,9},{25,17},{2,26},{10... | collective-permute-start | bytes 221192 | tf_op jit(solution)/shard_map/ppermute | solution.py:566
  18.9 6.2 %collective-permute-start.5 = (bf16[48,768]{1,0:T(8,128)(2,1)S(1)}, bf16[48,768]{1,0:T(8,128)(2,1)S(1)}, u32[]{:S(2)}, u32[]{:S(2)}) collective-permute-start(bf16[48,768]{1,0:T(8,128)(2,1)S(1)} %fusion.76), channel_id=1, source_target_pairs={{0,8},{8,16},{16,24},{24,0},{1,9},{9,17},{17,25},{25,1},{2,10},{10... | collective-permute-start | bytes 221192 | tf_op jit(solution)/shard_map/ppermute | solution.py:566
  25.1 9.1 %collective-permute-start.8 = (bf16[4,48,768]{2,1,0:T(8,128)(2,1)S(1)}, bf16[4,48,768]{2,1,0:T(8,128)(2,1)S(1)}, u32[]{:S(2)}, u32[]{:S(2)}) collective-permute-start(bf16[4,48,768]{2,1,0:T(8,128)(2,1)S(1)} %get-tuple-element.140), channel_id=1, source_target_pairs={{0,4},{4,0},{1,5},{5,1},{2,6},{6,2},{3,7},{7,3},{8,12},{12,8},{9,1... | collective-permute-start | bytes 884744 | tf_op jit(solution)/shard_map/ppermute | solution.py:566
  26.6 9.1 %collective-permute-start.1 = (bf16[24,1536]{1,0:T(8,128)(2,1)S(1)}, bf16[24,1536]{1,0:T(8,128)(2,1)S(1)}, u32[]{:S(2)}, u32[]{:S(2)}) collective-permute-start(bf16[24,1536]{1,0:T(8,128)(2,1)S(1)} %fusion.77), channel_id=1, source_target_pairs={{0,8},{8,16},{16,24},{24,0},{1,9},{9,17},{17,25},{25,1},{2,10},{10... | collective-permute-start | bytes 221192 | tf_op jit(solution)/shard_map/ppermute | solution.py:566
  26.9 11.5 %collective-permute-start.2 = (bf16[24,1536]{1,0:T(8,128)(2,1)S(1)}, bf16[24,1536]{1,0:T(8,128)(2,1)S(1)}, u32[]{:S(2)}, u32[]{:S(2)}) collective-permute-start(bf16[24,1536]{1,0:T(8,128)(2,1)S(1)} %fusion.77), channel_id=1, source_target_pairs={{0,16},{8,24},{16,0},{24,8},{1,17},{9,25},{17,1},{25,9},{2,18},{10... | collective-permute-start | bytes 221192 | tf_op jit(solution)/shard_map/ppermute | solution.py:566
  29.0 9.3 %collective-permute-start.3 = (bf16[24,1536]{1,0:T(8,128)(2,1)S(1)}, bf16[24,1536]{1,0:T(8,128)(2,1)S(1)}, u32[]{:S(2)}, u32[]{:S(2)}) collective-permute-start(bf16[24,1536]{1,0:T(8,128)(2,1)S(1)} %fusion.77), channel_id=1, source_target_pairs={{0,24},{8,0},{16,8},{24,16},{1,25},{9,1},{17,9},{25,17},{2,26},{10... | collective-permute-start | bytes 221192 | tf_op jit(solution)/shard_map/ppermute | solution.py:566
  34.2 16.3 %collective-permute-start.11 = (bf16[2,4,48,768]{3,2,1,0:T(8,128)(2,1)S(1)}, bf16[2,4,48,768]{3,2,1,0:T(8,128)(2,1)S(1)}, u32[]{:S(2)}, u32[]{:S(2)}) collective-permute-start(bf16[2,4,48,768]{3,2,1,0:T(8,128)(2,1)S(1)} %get-tuple-element.136), channel_id=1, source_target_pairs={{0,1},{1,0},{2,3},{3,2},{4,5},{5,4},{6,7},{7,6},{8,9},{9,8},{10,11... | collective-permute-start | bytes 1769480 | tf_op jit(solution)/shard_map/ppermute | solution.py:566
  38.4 7.6 %collective-permute-start.4 = (bf16[4,24,1536]{2,1,0:T(8,128)(2,1)S(1)}, bf16[4,24,1536]{2,1,0:T(8,128)(2,1)S(1)}, u32[]{:S(2)}, u32[]{:S(2)}) collective-permute-start(bf16[4,24,1536]{2,1,0:T(8,128)(2,1)S(1)} %get-tuple-element.142), channel_id=1, source_target_pairs={{0,4},{4,0},{1,5},{5,1},{2,6},{6,2},{3,7},{7,3},{8,12},{12,8},{9,1... | collective-permute-start | bytes 884744 | tf_op jit(solution)/shard_map/ppermute | solution.py:566
  39.5 29.2 %collective-permute-start = (bf16[1,8,768]{2,1,0:T(8,128)(2,1)S(1)}, bf16[1,8,768]{2,1,0:T(8,128)(2,1)S(1)}, u32[]{:S(2)}, u32[]{:S(2)}) collective-permute-start(bf16[1,8,768]{2,1,0:T(8,128)(2,1)S(1)} %slice.45), channel_id=1, source_target_pairs={{0,1},{2,3},{4,5},{6,7},{8,9},{10,11},{12,13},{14,15},{16,17},{18,... | collective-permute-start | bytes 36872 | tf_op jit(solution)/shard_map/ppermute | solution.py:826
  46.0 16.5 %copy-start.32 = (f32[24]{0:T(128)S(1)}, f32[24]{0:T(128)}, u32[]{:S(2)}) copy-start(f32[24]{0:T(128)} %param.34) | copy-start | bytes 292
  46.0 18.1 %copy-start.28 = (f32[24]{0:T(128)S(1)}, f32[24]{0:T(128)}, u32[]{:S(2)}) copy-start(f32[24]{0:T(128)} %param.35) | copy-start | bytes 292
  46.0 18.2 %copy-start.18 = (f32[4,1792]{1,0:T(4,128)S(1)}, f32[4,1792]{1,0:T(4,128)}, u32[]{:S(2)}) copy-start(f32[4,1792]{1,0:T(4,128)} %param.31) | copy-start | bytes 86020
  46.1 18.8 %copy-start.31 = (f32[24]{0:T(128)S(1)}, f32[24]{0:T(128)}, u32[]{:S(2)}) copy-start(f32[24]{0:T(128)} %param.33) | copy-start | bytes 292
  46.1 15.3 %collective-permute-start.9 = (bf16[2,4,24,1536]{3,2,1,0:T(8,128)(2,1)S(1)}, bf16[2,4,24,1536]{3,2,1,0:T(8,128)(2,1)S(1)}, u32[]{:S(2)}, u32[]{:S(2)}) collective-permute-start(bf16[2,4,24,1536]{3,2,1,0:T(8,128)(2,1)S(1)} %get-tuple-element.138), channel_id=1, source_target_pairs={{0,1},{1,0},{2,3},{3,2},{4,5},{5,4},{6,7},{7,6},{8,9},{9,8},{10,11... | collective-permute-start | bytes 1769480 | tf_op jit(solution)/shard_map/ppermute | solution.py:566
  51.6 13.3 %collective-permute-start.12 = (bf16[2,2,4,48,768]{4,3,2,1,0:T(8,128)(2,1)}, bf16[2,2,4,48,768]{4,3,2,1,0:T(8,128)(2,1)}, u32[]{:S(2)}, u32[]{:S(2)}) collective-permute-start(bf16[2,2,4,48,768]{4,3,2,1,0:T(8,128)(2,1)} %pad_maximum_fusion.1.near_ref), channel_id=1, source_target_pairs={{0,2},{2,0},{1,3},{3,1},{4,6},{6,4},{5,7},{7,5},{8,10},{10,8},{9,1... | collective-permute-start | bytes 3538952 | tf_op jit(solution)/shard_map/ppermute | solution.py:566
  62.5 6.8 %copy-start.27 = (f32[1792]{0:T(1024)S(1)}, f32[1792]{0:T(1024)}, u32[]{:S(2)}) copy-start(f32[1792]{0:T(1024)} %param.32) | copy-start | bytes 21508
  62.5 7.5 %copy-start.23 = (f32[768]{0:T(1024)S(1)}, f32[768]{0:T(1024)}, u32[]{:S(2)}) copy-start(f32[768]{0:T(1024)} %param.30) | copy-start | bytes 9220
  62.5 37.6 %collective-permute-start.10 = (bf16[2,2,4,24,1536]{4,3,2,1,0:T(8,128)(2,1)}, bf16[2,2,4,24,1536]{4,3,2,1,0:T(8,128)(2,1)}, u32[]{:S(2)}, u32[]{:S(2)}) collective-permute-start(bf16[2,2,4,24,1536]{4,3,2,1,0:T(8,128)(2,1)} %pad_maximum_fusion.near_ref), channel_id=1, source_target_pairs={{0,2},{2,0},{1,3},{3,1},{4,6},{6,4},{5,7},{7,5},{8,10},{10,8},{9,1... | collective-permute-start | bytes 3538952 | tf_op jit(solution)/shard_map/ppermute | solution.py:566
  88.0 25.9 %collective-permute-start.13 = (f32[1,128,1536]{2,1,0:T(8,128)}, f32[1,128,1536]{2,1,0:T(8,128)}, u32[]{:S(2)}, u32[]{:S(2)}) collective-permute-start(f32[1,128,1536]{2,1,0:T(8,128)} %get-tuple-element.50), channel_id=1, source_target_pairs={{0,1},{2,3},{4,5},{6,7},{8,9},{10,11},{12,13},{14,15},{16,17},{18,... | collective-permute-start | bytes 2359304 | tf_op jit(solution)/shard_map/ppermute | solution.py:843
  106.5 8.0 %copy-start.26 = (f32[1536]{0:T(1024)S(1)}, f32[1536]{0:T(1024)}, u32[]{:S(2)}) copy-start(f32[1536]{0:T(1024)} %param.36) | copy-start | bytes 18436
  175.3 6.7 %copy-start.3 = (f32[8,2,96,768]{3,2,1,0:T(8,128)}, f32[8,2,96,768]{3,2,1,0:T(8,128)S(1)}, u32[]{:S(2)}) copy-start(f32[8,2,96,768]{3,2,1,0:T(8,128)S(1)} %fusion.12.refs_2_) | copy-start | bytes 14155780
  175.5 10.1 %collective-permute-start.15 = (f32[8,96,768]{2,1,0:T(8,128)S(1)}, f32[8,96,768]{2,1,0:T(8,128)S(1)}, u32[]{:S(2)}, u32[]{:S(2)}) collective-permute-start(f32[8,96,768]{2,1,0:T(8,128)S(1)} %dynamic-slice_bitcast_fusion.1), channel_id=1, source_target_pairs={{0,2},{2,0},{1,3},{3,1},{4,6},{6,4},{5,7},{7,5},{8,10},{10,8},{9,1... | collective-permute-start | bytes 7077896 | tf_op jit(solution)/shard_map/ppermute | solution.py:566
  184.1 4.7 %collective-permute-start.14 = (f32[8,48,1536]{2,1,0:T(8,128)S(1)}, f32[8,48,1536]{2,1,0:T(8,128)}, u32[]{:S(2)}, u32[]{:S(2)}) collective-permute-start(f32[8,48,1536]{2,1,0:T(8,128)S(1)} %dynamic-slice_bitcast_fusion.2), channel_id=1, source_target_pairs={{0,2},{2,0},{1,3},{3,1},{4,6},{6,4},{5,7},{7,5},{8,10},{10,8},{9,1... | collective-permute-start | bytes 7077896 | tf_op jit(solution)/shard_map/ppermute | solution.py:566
  184.3 21.9 %collective-permute-start.16 = (f32[1,128,1536]{2,1,0:T(8,128)}, f32[1,128,1536]{2,1,0:T(8,128)}, u32[]{:S(2)}, u32[]{:S(2)}) collective-permute-start(f32[1,128,1536]{2,1,0:T(8,128)} %get-tuple-element.60), channel_id=1, source_target_pairs={{1,0},{3,2},{5,4},{7,6},{9,8},{11,10},{13,12},{15,14},{17,16},{19,... | collective-permute-start | bytes 2359304 | tf_op jit(solution)/shard_map/ppermute | solution.py:862
  251.6 8.6 %collective-permute-start.17 = (f32[1,8,1792]{2,1,0:T(8,128)}, f32[1,8,1792]{2,1,0:T(8,128)S(1)}, u32[]{:S(2)}, u32[]{:S(2)}) collective-permute-start(f32[1,8,1792]{2,1,0:T(8,128)} %get-tuple-element.63), channel_id=1, source_target_pairs={{1,0},{3,2},{5,4},{7,6},{9,8},{11,10},{13,12},{15,14},{17,16},{19,... | collective-permute-start | bytes 172040 | tf_op jit(solution)/shard_map/ppermute | solution.py:878
  252.9 59.0 %all-to-all-start = ((bf16[8,96,1536]{2,1,0:T(8,128)(2,1)}), bf16[8,96,1536]{2,1,0:T(8,128)(2,1)}, u32[]{:S(2)}, u32[]{:S(2)}) async-start(bf16[8,96,1536]{2,1,0:T(8,128)(2,1)} %get-tuple-element.69), calls=%async_computation | async-start | bytes 4718592 | tf_op jit(solution)/shard_map/all_to_all | solution.py:873
  260.1 12.6 %copy-start.17 = (f32[1024]{0:T(1024)}, f32[1024]{0:T(1024)S(1)}, u32[]{:S(2)}) copy-start(f32[1024]{0:T(1024)S(1)} %fusion.6) | copy-start | bytes 12292
  272.7 16.3 %collective-permute-start.18 = (f32[8,48,1920]{2,1,0:T(8,128)}, f32[8,48,1920]{2,1,0:T(8,128)}, u32[]{:S(2)}, u32[]{:S(2)}) collective-permute-start(f32[8,48,1920]{2,1,0:T(8,128)} %dynamic-slice_bitcast_fusion), channel_id=1, source_target_pairs={{0,2},{2,0},{1,3},{3,1},{4,6},{6,4},{5,7},{7,5},{8,10},{10,8},{9,1... | collective-permute-start | bytes 8847368 | tf_op jit(solution)/shard_map/ppermute | solution.py:566
  272.7 10.9 %copy-start.24 = (f32[1024]{0:T(1024)}, f32[1024]{0:T(1024)S(1)}, u32[]{:S(2)}) copy-start(f32[1024]{0:T(1024)S(1)} %fusion.44) | copy-start | bytes 12292
  276.9 6.7 %copy-start.1 = (bf16[1,1024,768]{2,1,0:T(8,128)(2,1)S(1)}, bf16[1,1024,768]{2,1,0:T(8,128)(2,1)}, u32[]{:S(2)}) copy-start(bf16[1,1024,768]{2,1,0:T(8,128)(2,1)} %u_ref.3) | copy-start | bytes 4718596
  277.0 6.7 %copy-start.9 = (bf16[32,24,1536]{2,1,0:T(8,128)(2,1)S(1)}, bf16[32,24,1536]{2,1,0:T(8,128)(2,1)}, u32[]{:S(2)}) copy-start(bf16[32,24,1536]{2,1,0:T(8,128)(2,1)} %assemble.2) | copy-start | bytes 7077892
  277.0 6.7 %copy-start.30 = (bf16[1024,1536]{1,0:T(8,128)(2,1)S(1)}, bf16[1024,1536]{1,0:T(8,128)(2,1)}, u32[]{:S(2)}) copy-start(bf16[1024,1536]{1,0:T(8,128)(2,1)} %get-tuple-element.52) | copy-start | bytes 9437188
  311.8 1.2 collective-permute-start.21
  313.1 6.7 %collective-permute-start.22 = (f32[96,128]{1,0:T(8,128)S(1)}, f32[96,128]{1,0:T(8,128)}, u32[]{:S(2)}, u32[]{:S(2)}) collective-permute-start(f32[96,128]{1,0:T(8,128)S(1)} %fusion.45), channel_id=1, source_target_pairs={{0,1},{1,0},{2,3},{3,2},{4,5},{5,4},{6,7},{7,6},{8,9},{9,8},{10,11... | collective-permute-start | bytes 147464 | tf_op jit(solution)/shard_map/ppermute | solution.py:630
  315.5 68.2 %all-to-all-start.1 = ((bf16[8,48,1920]{2,1,0:T(8,128)(2,1)}), bf16[8,48,1920]{2,1,0:T(8,128)(2,1)}, u32[]{:S(2)}, u32[]{:S(2)}) async-start(bf16[8,48,1920]{2,1,0:T(8,128)(2,1)} %get-tuple-element.73), calls=%async_computation.1 | async-start | bytes 2949120 | tf_op jit(solution)/shard_map/all_to_all | solution.py:907
  320.6 12.6 %collective-permute-start.23 = (f32[96,128]{1,0:T(8,128)S(1)}, f32[96,128]{1,0:T(8,128)S(1)}, u32[]{:S(2)}, u32[]{:S(2)}) collective-permute-start(f32[96,128]{1,0:T(8,128)S(1)} %fusion.75), channel_id=1, source_target_pairs={{0,4},{4,0},{1,5},{5,1},{2,6},{6,2},{3,7},{7,3},{8,12},{12,8},{9,1... | collective-permute-start | bytes 147464 | tf_op jit(solution)/shard_map/ppermute | solution.py:630
  333.2 12.8 %collective-permute-start.24 = (f32[96,128]{1,0:T(8,128)S(1)}, f32[96,128]{1,0:T(8,128)S(1)}, u32[]{:S(2)}, u32[]{:S(2)}) collective-permute-start(f32[96,128]{1,0:T(8,128)S(1)} %add.142), channel_id=1, source_target_pairs={{0,8},{8,0},{16,24},{24,16},{1,9},{9,1},{17,25},{25,17},{2,10},{10... | collective-permute-start | bytes 147464 | tf_op jit(solution)/shard_map/ppermute | solution.py:630
  346.0 15.0 %collective-permute-start.25 = (f32[96,128]{1,0:T(8,128)S(1)}, f32[96,128]{1,0:T(8,128)S(1)}, u32[]{:S(2)}, u32[]{:S(2)}) collective-permute-start(f32[96,128]{1,0:T(8,128)S(1)} %add.143), channel_id=1, source_target_pairs={{0,16},{8,24},{16,0},{24,8},{1,17},{9,25},{17,1},{25,9},{2,18},{10... | collective-permute-start | bytes 147464 | tf_op jit(solution)/shard_map/ppermute | solution.py:630
  360.7 14.3 %collective-permute-start.19 = (f32[96,1536]{1,0:T(8,128)}, f32[96,1536]{1,0:T(8,128)S(1)}, u32[]{:S(2)}, u32[]{:S(2)}) collective-permute-start(f32[96,1536]{1,0:T(8,128)} %owner_sum.2), channel_id=1, source_target_pairs={{0,1},{1,0},{2,3},{3,2},{4,5},{5,4},{6,7},{7,6},{8,9},{9,8},{10,11... | collective-permute-start | bytes 1769480 | tf_op jit(solution)/shard_map/ppermute | solution.py:566
  387.7 8.8 %copy-start.13 = (f32[48,1920]{1,0:T(8,128)S(1)}, f32[48,1920]{1,0:T(8,128)}, u32[]{:S(2)}) copy-start(f32[48,1920]{1,0:T(8,128)} %owner_sum.3) | copy-start | bytes 1105924
  387.7 8.8 %collective-permute-start.20 = (f32[48,1920]{1,0:T(8,128)}, f32[48,1920]{1,0:T(8,128)S(1)}, u32[]{:S(2)}, u32[]{:S(2)}) collective-permute-start(f32[48,1920]{1,0:T(8,128)} %owner_sum.3), channel_id=1, source_target_pairs={{0,1},{1,0},{2,3},{3,2},{4,5},{5,4},{6,7},{7,6},{8,9},{9,8},{10,11... | collective-permute-start | bytes 1105928 | tf_op jit(solution)/shard_map/ppermute | solution.py:566
  399.6 7.2 %copy-start.5 = (f32[2,24,26,128]{3,2,1,0:T(8,128)S(1)}, f32[2,24,26,128]{3,2,1,0:T(8,128)}, u32[]{:S(2)}) copy-start(f32[2,24,26,128]{3,2,1,0:T(8,128)} %reshape.253) | copy-start | bytes 1916932
  399.6 7.2 %copy-start.7 = (f32[2,26,24,24]{3,2,1,0:T(8,128)S(1)}, f32[2,26,24,24]{3,2,1,0:T(8,128)}, u32[]{:S(2)}) copy-start(f32[2,26,24,24]{3,2,1,0:T(8,128)} %copy.73) | copy-start | bytes 359428
  409.2 7.0 %copy-start.21 = (f32[2,24,24]{2,1,0:T(8,128)S(1)}, f32[2,24,24]{2,1,0:T(8,128)}, u32[]{:S(2)}) copy-start(f32[2,24,24]{2,1,0:T(8,128)} %param.42) | copy-start | bytes 13828
  409.3 7.9 %copy-start.22 = (f32[2,24,24]{2,1,0:T(8,128)S(1)}, f32[2,24,24]{2,1,0:T(8,128)}, u32[]{:S(2)}) copy-start(f32[2,24,24]{2,1,0:T(8,128)} %param.41) | copy-start | bytes 13828
  (15 other events, 48.1 us)
Sparse Core Ops, SparseCore 0:
  12.5 51.1 all-gather.1

commit v4 on v3

--- a/solution.py
+++ b/solution.py
@@ -19,7 +19,6 @@
 
 BL = 128
 PAIRS = HEADS // 2
-ROWS = 16
 
 AXES = ("z", "x", "core")
 
@@ -129,14 +128,17 @@
     mixed = mixed_low.astype(F32)
     z = projected[:, CONVCH:].astype(BF).astype(F32) + dtb_ref[0:1, :]
     z_ref[0] = z
-    full[0:8, :] = tail[...]
-    full[8:, :] = mixed
+    for low in range(0, CONVCH, 256):
+        cols = slice(low, low + 256)
+        own = mixed[:, cols]
+        joined = jnp.concatenate([tail[:, cols], own], axis=0)
+        pre = cb_ref[0:1, cols] + cw_ref[KCONV - 1 : KCONV, cols] * own
+        for tap in range(KCONV - 1):
+            moved = pltpu.roll(joined, KCONV - 1 - tap, 0)[8:, :]
+            pre = pre + cw_ref[tap : tap + 1, cols] * moved
+        pre_ref[0, :, cols] = pre
+        full[:, cols] = pre * sigmoid(pre)
     tail[...] = mixed[tile - 8 :, :]
-    pre = cb_ref[0:1, :] + cw_ref[KCONV - 1 : KCONV, :] * mixed
-    for tap in range(KCONV - 1):
-        pre = pre + cw_ref[tap : tap + 1, :] * full[5 + tap : 5 + tap + tile, :]
-    pre_ref[0] = pre
-    conv = pre * sigmoid(pre)
     step_all = softplus(z)
     rate = rates(alog_ref)
     tri = jnp.where(tri_mask(True), 1.0, 0.0).astype(BF)
@@ -150,21 +152,55 @@
         decay = expand(
             jnp.where(head_lanes((8, 128)), jnp.broadcast_to(jnp.exp(last), (8, 128)), 0.0), emat
         )[0:1, :]
-        inputs_b = conv[rows, DI : DI + DSTATE]
-        fresh = dot3(inputs_b.T, weights * conv[rows, :DI])
+        inputs_b = full[rows, DI : DI + DSTATE]
+        fresh = dot3(inputs_b.T, weights * full[rows, :DI])
         state_ref[0] = state_ref[0] * decay + fresh
         total_ref[0] = total_ref[0] + jnp.broadcast_to(last, (8, 128))
 
 
+def dot_wide(ahl, ah, bh, bl):
+    return dot(ahl, jnp.concatenate([bh, bh], axis=0)) + dot(ah, bl)
+
+
+def dot3_split(a, b, dims):
+    (ah, al), (bh, bl) = a, b
+    return dot(ah, bh, dims) + dot(al, bh, dims) + dot(ah, bl, dims)
+
+
+def wide_split(v):
+    high, low = split2(v)
+    return jnp.concatenate([high, low], axis=1), high
+
+
+def rows8(v):
+    return jnp.sum(v.reshape(v.shape[0] // 8, 8, v.shape[1]), axis=0)
+
+
+def pair_values(pair, cum, cum_t, step, mask, left, transposed):
+    kernels, columns = [], []
+    for h in (2 * pair, 2 * pair + 1):
+        column = jnp.broadcast_to(cum[:, h : h + 1], (BL, BL))
+        row = cum_t[h : h + 1, :]
+        spread = (row - column) if transposed else (column - row)
+        kernels.append(jnp.exp(jnp.where(mask, spread, NEG)))
+        columns.append(column)
+    chosen = jnp.where(left, columns[0], columns[1])
+    steps = jnp.where(left, step[:, 2 * pair : 2 * pair + 1], step[:, 2 * pair + 1 : 2 * pair + 2])
+    return kernels, chosen, steps
+
+
+def lane_sum(v):
+    return jnp.sum(v, axis=1, keepdims=True)
+
+
 def second_kernel(
     pre_ref, z_ref, gate_ref, bgrad_ref, u_ref, enter_ref, wo_ref, skip_ref, ggain_ref, alog_ref,
-    emat_ref, gmat_ref,
+    gmat_ref,
     out_ref, branch_ref, dy_ref, ggrad_ref, state_ref, rdot_ref, dstate_ref, sums_ref,
-    gain_acc, skip_acc, state, running, xs, ys, es,
+    gain_acc, skip_acc, state, running, ys, es,
 ):
     step_index = pl.program_id(1)
     tile = pre_ref.shape[1]
-    parts = tile // BL
 
     @pl.when(step_index == 0)
     def _():
@@ -178,88 +214,97 @@
         skip_acc[...] = jnp.zeros_like(skip_acc)
 
     rate = rates(alog_ref)
-    mask = tri_mask(True)
-    tri = jnp.where(mask, 1.0, 0.0).astype(BF)
-    emat = emat_ref[...]
-    cts = []
-    for part in range(parts):
-        rows = slice(part * BL, (part + 1) * BL)
-        pre = pre_ref[0, rows, :]
+
+    def block(part, carry):
+        rows = pl.ds(pl.multiple_of(part * BL, BL), BL)
+        mask = tri_mask(True)
+        left = lax.broadcasted_iota(jnp.int32, (BL, BL), 1) < HEADDIM
+        tri = jnp.where(mask, 1.0, 0.0).astype(BF)
+        pre = pre_ref[0, rows, DI:]
         conv = pre * sigmoid(pre)
-        x = conv[:, :DI]
-        inputs_b = conv[:, DI : DI + DSTATE]
-        inputs_c = conv[:, DI + DSTATE :]
+        inputs_b, inputs_c = conv[:, :DSTATE], conv[:, DSTATE:]
         step = softplus(z_ref[0, rows, :])
         cum = prefix(tri, step * rate)
         cum_t = cum.T
-        last = cum[BL - 1 : BL, :]
-        lanes = head_lanes(cum.shape)
-        wide = expand(
-            jnp.concatenate(
-                [step, jnp.where(lanes, jnp.exp(cum), 0.0), jnp.exp(last - cum) * step], axis=0
-            ),
-            emat,
-        )
-        grown = wide[BL : 2 * BL]
-        decay = grown[BL - 1 : BL, :]
-        scaled = wide[:BL] * x
         scores = dot3(inputs_c, inputs_b, NT)
-        held = state[...]
-        state_ref[0, part] = held
-        outer = grown * dot3(inputs_c, held)
-        state[...] = held * decay + dot3(inputs_b.T, wide[2 * BL :] * x)
-        for pair in range(PAIRS):
-            cols = slice(pair * 128, (pair + 1) * 128)
-            mixing = []
-            for h in (2 * pair, 2 * pair + 1):
-                spread = jnp.where(mask, cum[:, h : h + 1] - cum_t[h : h + 1, :], NEG)
-                mixing.append(scores * jnp.exp(spread))
-            mh, ml = split2(jnp.concatenate(mixing, axis=1))
-            piece = scaled[:, cols]
-            high = piece.astype(BF).astype(F32)
-            rh, rl = pair_blocks(high), pair_blocks(piece - high)
-            inner = dot(mh, rh) + dot(ml, rh) + dot(mh, rl)
-            ys[rows, cols] = inner + outer[:, cols]
-        xs[rows, :] = x
-        es[rows, :] = grown * running[0:1, :]
-        running[...] = running[...] * decay
-        cts.append(inputs_c.T)
-
-    gain = ggain_ref[0:1, :]
-    skip = skip_ref[0:1, :]
-
-    def rows_step(r, carry):
-        rows = pl.ds(pl.multiple_of(r * ROWS, ROWS), ROWS)
-        x = xs[rows, :]
-        yhat = ys[rows, :]
-        states = (yhat + skip * x).astype(BF).astype(F32)
-        gate = gate_ref[rows, :]
-        sg = sigmoid(gate)
-        sl = gate * sg
-        gated = states * sl
-        inv = lax.rsqrt(jnp.mean(gated * gated, axis=-1, keepdims=True) + EPS)
-        norm = gated * inv
-        branch_ref[rows, :] = (norm * gain).astype(BF)
-        bg = bgrad_ref[rows, :]
-        tg = bg * gain
-        gain_acc[...] += bg * norm
-        dot_row = jnp.mean(tg * norm, axis=-1, keepdims=True)
-        dgated = inv * (tg - norm * dot_row)
-        dy_low = (dgated * sl).astype(BF)
-        dy_ref[rows, :] = dy_low
-        ggrad_ref[rows, :] = (dgated * states * (sg * (1.0 + gate * (1.0 - sg)))).astype(BF)
-        dy = dy_low.astype(F32)
-        skip_acc[...] += dy * x
-        ys[rows, :] = dy * yhat
-        es[rows, :] = es[rows, :] * dy
+        c_wide, c_high = wide_split(inputs_c)
+        bt_wide, bt_high = wide_split(inputs_b.T)
+        ct_wide, ct_high = wide_split(inputs_c.T)
+        squares = jnp.zeros((BL, 128), F32)
+        products = jnp.zeros((BL, 128), F32)
+        for quad in range(PAIRS // 2):
+            cols = slice(quad * 256, (quad + 1) * 256)
+            inner, grown, weighted, xs = [], [], [], []
+            for pair in (2 * quad, 2 * quad + 1):
+                kernels, chosen, steps = pair_values(pair, cum, cum_t, step, mask, left, False)
+                own = pre_ref[0, rows, pair * 128 : (pair + 1) * 128]
+                x = own * sigmoid(own)
+                scaled = steps * x
+                mh, ml = split2(jnp.concatenate([scores * k for k in kernels], axis=1))
+                high = scaled.astype(BF).astype(F32)
+                rh, rl = pair_blocks(high), pair_blocks(scaled - high)
+                inner.append(dot(mh, rh) + dot(ml, rh) + dot(mh, rl))
+                grown.append(jnp.exp(chosen))
+                weighted.append(jnp.exp(chosen[BL - 1 : BL, :] - chosen) * scaled)
+                xs.append(x)
+            inner, grown, weighted, x = (
+                jnp.concatenate(v, axis=1) for v in (inner, grown, weighted, xs)
+            )
+            held = state[:, cols]
+            state_ref[0, part, :, cols] = held
+            yhat = inner + grown * dot_wide(c_wide, c_high, *split2(held))
+            state[:, cols] = held * grown[BL - 1 : BL, :] + dot_wide(
+                bt_wide, bt_high, *split2(weighted)
+            )
+            ys[:, cols] = yhat
+            es[:, cols] = grown
+            states = (yhat + skip_ref[0:1, cols] * x).astype(BF).astype(F32)
+            gate = gate_ref[rows, cols]
+            gated = states * (gate * sigmoid(gate))
+            product = gated * (bgrad_ref[rows, cols] * ggain_ref[0:1, cols])
+            squared = gated * gated
+            squares = squares + squared[:, :128] + squared[:, 128:]
+            products = products + product[:, :128] + product[:, 128:]
+        inv = lax.rsqrt(lane_sum(squares) * (1.0 / DI) + EPS)
+        pull = jnp.broadcast_to(inv * inv * lane_sum(products) * (1.0 / DI), (BL, 128))
+        inv = jnp.broadcast_to(inv, (BL, 128))
+        rdot = jnp.zeros((BL, 128), F32)
+        for quad in range(PAIRS // 2):
+            cols = slice(quad * 256, (quad + 1) * 256)
+            scaled_dy, dot_terms = [], []
+            for pair in (2 * quad, 2 * quad + 1):
+                own_cols = slice(pair * 128, (pair + 1) * 128)
+                own = pre_ref[0, rows, own_cols]
+                x = own * sigmoid(own)
+                yhat = ys[:, own_cols]
+                states = (yhat + skip_ref[0:1, own_cols] * x).astype(BF).astype(F32)
+                gate = gate_ref[rows, own_cols]
+                sg = sigmoid(gate)
+                sl = gate * sg
+                gated = states * sl
+                gain = ggain_ref[0:1, own_cols]
+                upstream = bgrad_ref[rows, own_cols]
+                norm = gated * inv
+                branch_ref[rows, own_cols] = (norm * gain).astype(BF)
+                gain_acc[:, own_cols] += rows8(upstream * norm)
+                dgated = inv * (upstream * gain - gated * pull)
+                dy_low = (dgated * sl).astype(BF)
+                dy_ref[rows, own_cols] = dy_low
+                ggrad_ref[rows, own_cols] = (dgated * states * (sg + sl * (1.0 - sg))).astype(BF)
+                dy = dy_low.astype(F32)
+                skip_acc[:, own_cols] += rows8(dy * x)
+                dot_terms.append(dy * yhat)
+                scaled_dy.append(es[:, own_cols] * running[0:1, own_cols] * dy)
+            rdot = rdot + head_sum(jnp.concatenate(dot_terms, axis=1), gmat_ref[cols, :])
+            dstate_ref[0, :, cols] += dot_wide(
+                ct_wide, ct_high, *split2(jnp.concatenate(scaled_dy, axis=1))
+            )
+            running[:, cols] = running[:, cols] * es[BL - 1 : BL, cols]
+        rdot_ref[0, rows, :] = rdot
         return carry
 
-    lax.fori_loop(0, tile // ROWS, rows_step, 0)
+    lax.fori_loop(0, tile // BL, block, 0)
     out_ref[0] = (u_ref[0].astype(F32) + dot(branch_ref[...], wo_ref[...])).astype(BF)
-    rdot_ref[0] = head_sum(ys[...], gmat_ref[...])
-    for part in range(parts):
-        rows = slice(part * BL, (part + 1) * BL)
-        dstate_ref[0] = dstate_ref[0] + dot3(cts[part], es[rows, :])
 
     @pl.when((step_index == pl.num_programs(1) - 1) & (pl.program_id(0) == pl.num_programs(0) - 1))
     def _():
@@ -269,9 +314,9 @@
 
 def third_kernel(
     pre_ref, mixed_ref, z_ref, dy_ref, state_ref, rdot_ref, leave_ref, cw_ref, skip_ref, alog_ref,
-    emat_ref, gmat_ref,
+    gmat_ref,
     mgrad_ref, last_ref, first_ref, sums_ref,
-    cw_acc, cb_acc, dtb_acc, rate_acc, dstate, tail, full,
+    cw_acc, cb_acc, dtb_acc, rate_acc, dstate, tail,
 ):
     step_index = pl.program_id(1)
 
@@ -287,65 +332,84 @@
 
     rate = rates(alog_ref)
     mask = tri_mask(False)
+    left = lax.broadcasted_iota(jnp.int32, (BL, BL), 1) < HEADDIM
     low_tri = jnp.where(tri_mask(True), 1.0, 0.0).astype(BF)
     high_tri = jnp.where(mask, 1.0, 0.0).astype(BF)
-    emat = emat_ref[...]
-    gmat = gmat_ref[...]
-    skip = skip_ref[0:1, :]
-    pre = pre_ref[0]
-    sg = sigmoid(pre)
-    conv = pre * sg
-    x = conv[:, :DI]
-    inputs_b = conv[:, DI : DI + DSTATE]
-    inputs_c = conv[:, DI + DSTATE :]
+    wide_pre = pre_ref[0, :, DI:]
+    wide_sg = sigmoid(wide_pre)
+    conv = wide_pre * wide_sg
+    inputs_b, inputs_c = conv[:, :DSTATE], conv[:, DSTATE:]
     z = z_ref[0]
     step = softplus(z)
     cum = prefix(low_tri, step * rate)
     cum_t = cum.T
-    last = cum[BL - 1 : BL, :]
     lanes = head_lanes(cum.shape)
-    wide = expand(
-        jnp.concatenate(
-            [
-                step,
-                jnp.where(lanes, jnp.exp(cum), 0.0),
-                jnp.where(lanes, jnp.exp(last - cum), 0.0),
-            ],
-            axis=0,
-        ),
-        emat,
-    )
-    dt_wide, grown, shrink = wide[:BL], wide[BL : 2 * BL], wide[2 * BL :]
-    decay = grown[BL - 1 : BL, :]
-    scaled = dt_wide * x
-    dy = dy_ref[...].astype(F32)
-    held = state_ref[0, 0]
-    ds = dstate[...]
     scores_t = dot3(inputs_b, inputs_c, NT)
-    dscaled_state = shrink * dot3(inputs_b, ds)
+    b_wide, b_high = wide_split(inputs_b)
+    ct_wide, ct_high = wide_split(inputs_c.T)
     dscores_t = jnp.zeros((BL, BL), F32)
-    pieces = []
-    for pair in range(PAIRS):
-        cols = slice(pair * 128, (pair + 1) * 128)
-        kernels = []
-        for h in (2 * pair, 2 * pair + 1):
-            spread = jnp.where(mask, cum_t[h : h + 1, :] - cum[:, h : h + 1], NEG)
-            kernels.append(jnp.exp(spread))
-        mh, ml = split2(jnp.concatenate([scores_t * k for k in kernels], axis=1))
-        dyb = pair_blocks(dy[:, cols])
-        pieces.append(dot(mh, dyb) + dot(ml, dyb))
-        sh, sl = split2(scaled[:, cols])
-        dmix = dot(sh, dyb, NT) + dot(sl, dyb, NT)
-        dscores_t = dscores_t + dmix[:, :BL] * kernels[0] + dmix[:, BL:] * kernels[1]
-    dscaled = jnp.concatenate(pieces, axis=1) + dscaled_state
-    dx = dt_wide * dscaled + skip * dy
-    grown_dy = grown * dy
-    ends = jnp.sum(scaled * dscaled_state, axis=0, keepdims=True) + decay * jnp.sum(
-        held * ds, axis=0, keepdims=True
-    )
-    sums = head_sum(
-        jnp.concatenate([x * dscaled, jnp.broadcast_to(ends, (8, DI))], axis=0), gmat
-    )
+    db = jnp.zeros((BL, DSTATE), F32)
+    dc = jnp.zeros((BL, DSTATE), F32)
+    sums = jnp.zeros((BL + 8, 128), F32)
+
+    def back_conv(cols, dpre):
+        joined = jnp.concatenate([dpre, tail[:, cols]], axis=0)
+        tail[:, cols] = dpre[0:8, :]
+        mixed = mixed_ref[0, :, cols].astype(F32)
+        cb_acc[:, cols] += rows8(dpre)
+        mgrad = cw_ref[KCONV - 1 : KCONV, cols] * dpre
+        cw_acc[KCONV - 1, :, cols] += rows8(dpre * mixed)
+        for tap in range(KCONV - 1):
+            moved = pltpu.roll(joined, BL + 8 - (KCONV - 1 - tap), 0)[:BL, :]
+            mgrad = mgrad + cw_ref[tap : tap + 1, cols] * moved
+            cw_acc[tap, :, cols] += rows8(moved * mixed)
+        mgrad_ref[0, :, cols] = mgrad.astype(BF)
+        last_ref[0, :, cols] = jnp.where(step_index == 0, mgrad[BL - 8 :, :], last_ref[0, :, cols])
+
+    for quad in range(PAIRS // 2):
+        cols = slice(quad * 256, (quad + 1) * 256)
+        inner, grown, shrink, scaled, xs, steps_wide, slopes = [], [], [], [], [], [], []
+        dy = dy_ref[:, cols].astype(F32)
+        for half, pair in enumerate((2 * quad, 2 * quad + 1)):
+            kernels, chosen, steps = pair_values(pair, cum, cum_t, step, mask, left, True)
+            own = pre_ref[0, :, pair * 128 : (pair + 1) * 128]
+            sg = sigmoid(own)
+            x = own * sg
+            slopes.append(sg + x * (1.0 - sg))
+            xd = steps * x
+            mh, ml = split2(jnp.concatenate([scores_t * k for k in kernels], axis=1))
+            dyb = pair_blocks(dy[:, half * 128 : (half + 1) * 128])
+            inner.append(dot(mh, dyb) + dot(ml, dyb))
+            sh, sl = split2(xd)
+            dmix = dot(sh, dyb, NT) + dot(sl, dyb, NT)
+            dscores_t = dscores_t + dmix[:, :BL] * kernels[0] + dmix[:, BL:] * kernels[1]
+            grown.append(jnp.exp(chosen))
+            shrink.append(jnp.exp(chosen[BL - 1 : BL, :] - chosen))
+            scaled.append(xd)
+            xs.append(x)
+            steps_wide.append(steps)
+        inner, grown, shrink, scaled, x, steps_wide, slopes = (
+            jnp.concatenate(v, axis=1) for v in (inner, grown, shrink, scaled, xs, steps_wide, slopes)
+        )
+        held = state_ref[0, 0, :, cols]
+        ds = dstate[:, cols]
+        held_parts, ds_parts = split2(held), split2(ds)
+        decay = grown[BL - 1 : BL, :]
+        dscaled_state = shrink * dot_wide(b_wide, b_high, *ds_parts)
+        dscaled = inner + dscaled_state
+        ends = jnp.sum(scaled * dscaled_state, axis=0, keepdims=True) + decay * jnp.sum(
+            held * ds, axis=0, keepdims=True
+        )
+        sums = sums + head_sum(
+            jnp.concatenate([x * dscaled, jnp.broadcast_to(ends, (8, 256))], axis=0),
+            gmat_ref[cols, :],
+        )
+        grown_parts = split2(grown * dy)
+        dc = dc + dot3_split(grown_parts, held_parts, NT)
+        db = db + dot3_split(split2(shrink * scaled), ds_parts, NT)
+        dstate[:, cols] = decay * ds + dot_wide(ct_wide, ct_high, *grown_parts)
+        back_conv(cols, (steps_wide * dscaled + skip_ref[0:1, cols] * dy) * slopes)
+
     direct = sums[:BL]
     is_last = lax.broadcasted_iota(jnp.int32, (BL, 128), 0) == BL - 1
     dcum = rdot_ref[0] - step * direct + jnp.where(is_last, sums[BL : BL + 1, :], 0.0)
@@ -353,28 +417,15 @@
     drate = prefix(high_tri, dcum)
     dz = (rate * drate + direct) * sigmoid(z)
     mgrad_ref[0, :, CONVCH:] = dz.astype(BF)
-    dtb_acc[...] += jnp.sum(dz.reshape(BL // 8, 8, 128), axis=0)
-    rate_acc[...] += jnp.sum((step * drate).reshape(BL // 8, 8, 128), axis=0)
-    db = dot3(dscores_t, inputs_c) + dot3(shrink * scaled, ds, NT)
-    dc = dot3(dscores_t.T, inputs_b) + dot3(grown_dy, held, NT)
-    dstate[...] = decay * ds + dot3(inputs_c.T, grown_dy)
-    dpre = jnp.concatenate([dx, db, dc], axis=1) * (sg * (1.0 + pre * (1.0 - sg)))
-    full[0:BL, :] = dpre
-    full[BL:, :] = tail[...]
-    tail[...] = dpre[0:8, :]
-    first_ref[0] = dpre[0:8, :]
-    mixed = mixed_ref[0].astype(F32)
-    cb_acc[...] += jnp.sum(dpre.reshape(BL // 8, 8, CONVCH), axis=0)
-    mgrad = jnp.zeros_like(dpre)
-    for tap in range(KCONV):
-        moved = full[KCONV - 1 - tap : KCONV - 1 - tap + BL, :]
-        mgrad = mgrad + cw_ref[tap : tap + 1, :] * moved
-        cw_acc[tap] += jnp.sum((moved * mixed).reshape(BL // 8, 8, CONVCH), axis=0)
-    mgrad_ref[0, :, :CONVCH] = mgrad.astype(BF)
-
-    @pl.when(step_index == 0)
-    def _():
-        last_ref[0] = mgrad[BL - 8 :, :]
+    dtb_acc[...] += rows8(dz)
+    rate_acc[...] += rows8(step * drate)
+    db = db + dot3(dscores_t, inputs_c)
+    dc = dc + dot3(dscores_t.T, inputs_b)
+    back_conv(
+        slice(DI, CONVCH),
+        jnp.concatenate([db, dc], axis=1) * (wide_sg + conv * (1.0 - wide_sg)),
+    )
+    first_ref[0] = tail[...]
 
     @pl.when((step_index == pl.num_programs(1) - 1) & (pl.program_id(0) == pl.num_programs(0) - 1))
     def _():
@@ -436,13 +487,13 @@
             jax.ShapeDtypeStruct((seqs, DSTATE, DI), F32),
             jax.ShapeDtypeStruct((seqs, 8, 128), F32),
         ],
-        scratch_shapes=[pltpu.VMEM((8, CONVCH), F32), pltpu.VMEM((tile + 8, CONVCH), F32)],
+        scratch_shapes=[pltpu.VMEM((8, CONVCH), F32), pltpu.VMEM((tile, CONVCH), F32)],
         compiler_params=pltpu.CompilerParams(**PARAMS),
         name="first",
     )(u, halo, gain, w, cw, cb, dtb, alog, emat)
 
 
-def run_second(pre, z, gate, bgrad, u, enter, wo, skip, ggain, alog, emat, gmat):
+def run_second(pre, z, gate, bgrad, u, enter, wo, skip, ggain, alog, gmat):
     seqs, length, _ = u.shape
     tile = min(256, length)
     steps = length // tile
@@ -457,8 +508,7 @@
         grid=grid,
         in_specs=[
             tok(CONVCH), tok(128), flat(DI), flat(DI), tok(D), per(DSTATE, DI), whole(wo.shape),
-            whole(skip.shape), whole(ggain.shape), whole(alog.shape), whole(emat.shape),
-            whole(gmat.shape),
+            whole(skip.shape), whole(ggain.shape), whole(alog.shape), whole(gmat.shape),
         ],
         out_specs=[
             tok(D), flat(DI), flat(DI), flat(DI),
@@ -476,16 +526,15 @@
             jax.ShapeDtypeStruct((8, DI), F32),
         ],
         scratch_shapes=[
-            pltpu.VMEM((ROWS, DI), F32), pltpu.VMEM((ROWS, DI), F32),
-            pltpu.VMEM((DSTATE, DI), F32), pltpu.VMEM((8, DI), F32), pltpu.VMEM((tile, DI), F32),
-            pltpu.VMEM((tile, DI), F32), pltpu.VMEM((tile, DI), F32),
+            pltpu.VMEM((8, DI), F32), pltpu.VMEM((8, DI), F32), pltpu.VMEM((DSTATE, DI), F32),
+            pltpu.VMEM((8, DI), F32), pltpu.VMEM((BL, DI), F32), pltpu.VMEM((BL, DI), F32),
         ],
         compiler_params=pltpu.CompilerParams(**PARAMS),
         name="second",
-    )(pre, z, gate, bgrad, u, enter, wo, skip, ggain, alog, emat, gmat)
-
-
-def run_third(pre, mixed, z, dy, states, rdot, leave, cw, skip, alog, emat, gmat):
+    )(pre, z, gate, bgrad, u, enter, wo, skip, ggain, alog, gmat)
+
+
+def run_third(pre, mixed, z, dy, states, rdot, leave, cw, skip, alog, gmat):
     seqs, length, _ = pre.shape
     steps = length // BL
     grid = (seqs, steps)
@@ -499,7 +548,7 @@
             pl.BlockSpec((BL, DI), lambda b, i: (b * steps + steps - 1 - i, 0)),
             pl.BlockSpec((1, 1, DSTATE, DI), lambda b, i: (b, steps - 1 - i, 0, 0)),
             tok(128), per(DSTATE, DI), whole(cw.shape), whole(skip.shape), whole(alog.shape),
-            whole(emat.shape), whole(gmat.shape),
+            whole(gmat.shape),
         ],
         out_specs=[
             tok(WIDE), per(8, CONVCH), per(8, CONVCH), whole((8, CONVCH)),
@@ -514,11 +563,10 @@
             pltpu.VMEM((KCONV, 8, CONVCH), F32), pltpu.VMEM((8, CONVCH), F32),
             pltpu.VMEM((8, 128), F32), pltpu.VMEM((8, 128), F32),
             pltpu.VMEM((DSTATE, DI), F32), pltpu.VMEM((8, CONVCH), F32),
-            pltpu.VMEM((BL + 8, CONVCH), F32),
         ],
         compiler_params=pltpu.CompilerParams(**PARAMS),
         name="third",
-    )(pre, mixed, z, dy, states, rdot, leave, cw, skip, alog, emat, gmat)
+    )(pre, mixed, z, dy, states, rdot, leave, cw, skip, alog, gmat)
 
 
 def run_patch(mgrad, mixed, last8, near, cw):
@@ -632,31 +680,30 @@
     return v
 
 
+STEP_OWNERS = 4
+
+
 def chip_kernel(idx, *refs):
     send_ref, own_ref = refs[-2:]
-    pieces = []
-    for part_ref, got_ref in zip(refs[:-2:2], refs[1:-2:2]):
-        total = part_ref[0, 0] + got_ref[0]
-        width = own_ref.shape[1]
-        rows = total.shape[0] * total.shape[1] // width
-        pieces += [
-            total[i * rows : (i + 1) * rows] for i in range(total.shape[0] // rows)
-        ]
-    mine = pl.program_id(0) == idx[0] * 2 + idx[1]
-    row = 0
-    col = 0
-    for piece in pieces:
-        rows, cols = piece.shape
-        at = (slice(row, row + rows), slice(col, col + cols))
-        send_ref[(0,) + at] = piece.astype(BF)
-
-        @pl.when(mine)
-        def _(at=at, piece=piece):
-            own_ref[at] = piece
-
-        col += cols
-        if col == own_ref.shape[1]:
-            row, col = row + rows, 0
+    width = own_ref.shape[1]
+    for owner in range(STEP_OWNERS):
+        mine = pl.program_id(0) * STEP_OWNERS + owner == idx[0] * 2 + idx[1]
+        row, col = 0, 0
+        for part_ref, got_ref in zip(refs[:-2:2], refs[1:-2:2]):
+            total = part_ref[owner, 0] + got_ref[owner]
+            rows = total.shape[0] * total.shape[1] // width
+            for low in range(0, total.shape[0], rows):
+                piece = total[low : low + rows]
+                at = (slice(row, row + rows), slice(col, col + piece.shape[1]))
+                send_ref[(owner,) + at] = piece.astype(BF)
+
+                @pl.when(mine)
+                def _(at=at, piece=piece):
+                    own_ref[at] = piece
+
+                col += piece.shape[1]
+                if col == width:
+                    row, col = row + rows, 0
 
 
 def chip_sum(idx, pairs):
@@ -667,18 +714,18 @@
         total += rows * cols
         ins += [blocks, got]
         in_specs += [
-            pl.BlockSpec((1, 1, rows, cols), lambda i, idx: (i, idx[2], 0, 0)),
-            pl.BlockSpec((1, rows, cols), lambda i, idx: (i, 0, 0)),
+            pl.BlockSpec((STEP_OWNERS, 1, rows, cols), lambda i, idx: (i, idx[2], 0, 0)),
+            pl.BlockSpec((STEP_OWNERS, rows, cols), lambda i, idx: (i, 0, 0)),
         ]
     rows = total // width
     return pl.pallas_call(
         chip_kernel,
         grid_spec=pltpu.PrefetchScalarGridSpec(
             num_scalar_prefetch=1,
-            grid=(8,),
+            grid=(8 // STEP_OWNERS,),
             in_specs=in_specs,
             out_specs=[
-                pl.BlockSpec((1, rows, width), lambda i, idx: (i, 0, 0)),
+                pl.BlockSpec((STEP_OWNERS, rows, width), lambda i, idx: (i, 0, 0)),
                 pl.BlockSpec((rows, width), lambda i, idx: (0, 0)),
             ],
         ),
@@ -701,7 +748,7 @@
 
 def owner_sum(idx, own, got):
     rows, width = own.shape
-    tile = 16
+    tile = 48
     return pl.pallas_call(
         owner_kernel,
         grid_spec=pltpu.PrefetchScalarGridSpec(
@@ -730,35 +777,36 @@
     return jnp.stack([v] + [swapped(v, axis, size, offset) for offset in range(1, size)])
 
 
-def assemble_kernel(idx, near_ref, far_ref, out_ref, *, order):
-    sizes = {"z": 4, "x": 2, "seq": 2}
-    here = {"z": idx[0], "x": idx[1], "core": idx[2], "seq": idx[3]}
-    for a in range(near_ref.shape[0]):
-        for b in range(near_ref.shape[1]):
-            for c in range(near_ref.shape[2]):
+def assemble_kernel(idx, *refs, order):
+    out_ref = refs[-1]
+    sizes = {"z": 4, "x": 2}
+    here = {"z": idx[0], "x": idx[1]}
+    spots = ((idx[2], idx[3]), (idx[2], 1 - idx[3]), (1 - idx[2], idx[3]), (1 - idx[2], 1 - idx[3]))
+    for ref, (core, seq) in zip(refs[:-1], spots):
+        for a in range(ref.shape[0]):
+            for b in range(ref.shape[1]):
                 at = dict(
                     (axis, lax.rem(here[axis] - back + sizes[axis], sizes[axis]))
-                    for axis, back in zip(order[::-1], (a, b, c))
+                    for axis, back in zip(order[::-1], (a, b))
                 )
-                for ref, core in ((near_ref, here["core"]), (far_ref, 1 - here["core"])):
-                    block = ((at["z"] * 2 + at["x"]) * 2 + core) * 2 + at["seq"]
-                    out_ref[block] = ref[a, b, c]
-
-
-def assemble(idx, near, far, order):
-    rows, cols = near.shape[-2:]
+                out_ref[((at["z"] * 2 + at["x"]) * 2 + core) * 2 + seq] = ref[a, b]
+
+
+def assemble(idx, pieces, order):
+    shape = pieces[0].shape
+    rows, cols = shape[-2:]
     out = pl.pallas_call(
         functools.partial(assemble_kernel, order=order),
         grid_spec=pltpu.PrefetchScalarGridSpec(
             num_scalar_prefetch=1,
             grid=(1,),
-            in_specs=[pl.BlockSpec(near.shape, lambda i, idx: (0,) * 5)] * 2,
+            in_specs=[pl.BlockSpec(shape, lambda i, idx: (0,) * 4)] * 4,
             out_specs=pl.BlockSpec((32, rows, cols), lambda i, idx: (0, 0, 0)),
         ),
-        out_shape=jax.ShapeDtypeStruct((32, rows, cols), near.dtype),
+        out_shape=jax.ShapeDtypeStruct((32, rows, cols), pieces[0].dtype),
         compiler_params=pltpu.CompilerParams(**PARAMS),
         name="assemble",
-    )(idx, near, far)
+    )(idx, *pieces)
     return out.reshape(32 * rows, cols)
 
 
@@ -807,24 +855,6 @@
     main = lax.all_gather(
         jnp.concatenate([in_low[:, DI:], dt_low], axis=1), AXES, axis=0, tiled=True
     )
-    torus_sizes = tuple(lax.axis_size(a) for a in ("z", "x", "core", "seq"))
-    direct = torus_sizes == (4, 2, 2, 2)
-    idx = jnp.stack([lax.axis_index(a) for a in ("z", "x", "core", "seq")]).astype(jnp.int32)
-    gate_low, out_low = in_low[:, :DI], out_weight.astype(BF)
-    if direct:
-        order = ("z", "x", "seq")
-        gate_near = pick(gate_low.reshape(2, -1, DI), idx[3])
-        out_near = pick(out_low.reshape(2, -1, D), idx[3])
-        gate_near = around(around(gate_near, "z"), "x")
-        out_near = around(around(out_near, "z"), "x")
-        main, _, _ = lax.optimization_barrier((main, gate_near, out_near))
-        gate_near = around(gate_near, "seq")
-        out_near = around(out_near, "seq")
-    else:
-        wg = lax.all_gather(gate_low, AXES, axis=0, tiled=True)
-        wo = lax.all_gather(out_low, AXES, axis=0, tiled=True)
-    halo = lax.ppermute(block_input[:, local_len - 8 :, :], "seq", up)
-
     part = jnp.arange(128)
     channel = jnp.arange(DI)
     emat = (
@@ -835,9 +865,31 @@
     alog = row8(decay_log, 128)
     dtb = row8(jnp.concatenate([dt_bias, jnp.full((128 - HEADS,), -1e4, F32)]))
     cw8 = jnp.pad(conv_weight, ((0, 4), (0, 0)))
+    gain8, cb8 = row8(norm_gain), row8(conv_bias)
+    ggain8 = row8(gate_gain)
+    tables = (emat, gmat, skip_wide, alog, dtb, cw8, gain8, cb8, ggain8)
+    torus_sizes = tuple(lax.axis_size(a) for a in ("z", "x", "core", "seq"))
+    direct = torus_sizes == (4, 2, 2, 2)
+    idx = jnp.stack([lax.axis_index(a) for a in ("z", "x", "core", "seq")]).astype(jnp.int32)
+    gate_low, out_low = in_low[:, :DI], out_weight.astype(BF)
+    if direct:
+        order = ("z", "x")
+        gate_near = pick(gate_low.reshape(2, -1, DI), idx[3])
+        out_near = pick(out_low.reshape(2, -1, D), idx[3])
+        gate_near = around(around(gate_near, "z"), "x")
+        out_near = around(around(out_near, "z"), "x")
+        main = lax.optimization_barrier((main, gate_near, out_near) + tables)[0]
+        gate_got = swapped(gate_near, "seq", 2, 1)
+        out_got = swapped(out_near, "seq", 2, 1)
+        gate_far = swapped(gate_near, "core", 2, 1)
+        out_far = swapped(out_near, "core", 2, 1)
+    else:
+        wg = lax.all_gather(gate_low, AXES, axis=0, tiled=True)
+        wo = lax.all_gather(out_low, AXES, axis=0, tiled=True)
+    halo = lax.ppermute(block_input[:, local_len - 8 :, :], "seq", up)
 
     normed, mixed, pre, z, local_state, total = run_first(
-        block_input, halo, row8(norm_gain), main, cw8, row8(conv_bias), dtb, alog, emat
+        block_input, halo, gain8, main, cw8, cb8, dtb, alog, emat
     )
     span = jnp.repeat(jnp.exp(total[:, 0:1, :HEADS]), HEADDIM, axis=2)
     enter = lax.ppermute(local_state, "seq", up)
@@ -845,10 +897,10 @@
         enter = lax.ppermute(local_state + span * enter, "seq", up)
 
     if direct:
-        out_far = swapped(out_near, "core", 2, 1)
-        gate_far = swapped(gate_near, "core", 2, 1)
-        wo = assemble(idx, out_near, out_far, order)
-        wg = assemble(idx, gate_near, gate_far, order)
+        out_far_got = swapped(out_got, "core", 2, 1)
+        gate_far_got = swapped(gate_got, "core", 2, 1)
+        wo = assemble(idx, (out_near, out_got, out_far, out_far_got), order)
+        wg = assemble(idx, (gate_near, gate_got, gate_far, gate_far_got), order)
     normed_rows = normed.reshape(row_count, D)
     upstream = cotangent.reshape(row_count, D)
     gate_part = dot(normed_rows, wg)
@@ -856,8 +908,8 @@
     (
         block_output, branch, states_grad, gate_grad, states, rdot, local_dstate, row_sums,
     ) = run_second(
-        pre, z, gate_part, branch_grad, block_input, enter, wo, skip_wide, row8(gate_gain), alog,
-        emat, gmat,
+        pre, z, gate_part, branch_grad, block_input, enter, wo, skip_wide, ggain8, alog,
+        gmat,
     )
     leave = lax.ppermute(local_dstate, "seq", down)
     for _ in range(seq_devices - 2):
@@ -866,14 +918,14 @@
     out_partial = dot(branch, upstream, TN)
     gate_partial = dot(normed_rows, gate_grad, TN)
     if direct:
-        early, early_own = chip_sum(
-            idx, [core_exchange(gate_partial, idx[2]), core_exchange(out_partial, idx[2])]
-        )
+        gate_pair = core_exchange(gate_partial, idx[2])
+        out_pair = core_exchange(out_partial, idx[2])
+        early, early_own = chip_sum(idx, [gate_pair, out_pair])
         states_grad, early = lax.optimization_barrier((states_grad, early))
         early = lax.all_to_all(early, ("z", "x"), split_axis=0, concat_axis=0, tiled=True)
 
     mgrad, last8, first8, column_sums = run_third(
-        pre, mixed, z, states_grad, states, rdot, leave, cw8, skip_wide, alog, emat, gmat
+        pre, mixed, z, states_grad, states, rdot, leave, cw8, skip_wide, alog, gmat
     )
     near = lax.ppermute(first8, "seq", down)
     mgrad, extra = run_patch(mgrad, mixed, last8, near, cw8)
@@ -918,6 +970,8 @@
         mixed_sum = reduce_plain(core_sum(mixed_local))
     vector_rows = jnp.pad(vector_local, (0, -vector_local.shape[0] % 1024)).reshape(-1, 128)
     for axis in ("core", "seq", "x", "z"):
+        if direct and axis == "x":
+            vector_rows = lax.optimization_barrier((late, vector_rows))[1]
         vector_rows = xor_sum(vector_rows, axis)
     vector_grad = vector_rows.reshape(-1)[: vector_local.shape[0]]
 

time: 432 us -> 406 us (0.940)
  Pallas kernels: 147 us -> 125 us
    pallas_call x1, Pallas kernels: 50.2 us -> 41.2 us  [run_second(): pl.pallas_call(second_kernel, grid=grid, in_specs=[tok(CONVCH), tok(128),...]
    ppermute x5, waiting for transfers between devices: 17.8 us -> 10.5 us  [xor_sum(): v = v + lax.ppermute(v, axis, [(i, i ^ bit) for i in range(size)])]
    pallas_call x1, Pallas kernels: 45.3 us -> 40.5 us  [run_third(): pl.pallas_call(third_kernel, grid=grid, in_specs=[tok(CONVCH), tok(CONVCH...]
    pallas_call x2, Pallas kernels: 15.3 us -> 10.9 us  [chip_sum(): pl.pallas_call(chip_kernel, grid_spec=pltpu.PrefetchScalarGridSpec(num_sc...]
    ppermute x17 -> x19, starting transfers between devices: 17.8 us -> 19 us  [swapped(): lax.ppermute(v, axis, [(i, (i + offset) % size) for i in range(size)])]
    ppermute x17 -> x19, waiting for transfers between devices: 39.3 us -> 40.3 us  [swapped(): lax.ppermute(v, axis, [(i, (i + offset) % size) for i in range(size)])]
    unnamed x73 -> x81, local copies, waits for them, and re-layouts: 21.8 us -> 22.5 us
  transfers between devices with their start and end apart: 29 -> 31, of which waited for: 16 -> 11; matrix products, arithmetic and copies ran while one was open for 20% -> 21% of each run, Pallas kernels for 11% -> 11%
where the time goes in v4:
time: 406 us; the launch traced here: 399 us
  Pallas kernels  125 us (31%)
  waiting for transfers between devices  80.4 us (20%)
  matrix products  62.3 us (15%)
  local copies, waits for them, and re-layouts  47.3 us (12%)
  starting transfers between devices  43.8 us (11%)
  other arithmetic  24.3 us (6%)
  between operations  15 us (4%)
    pallas_call x1, Pallas kernels, run_second(): pl.pallas_call(second_kernel, grid=grid, in_specs=[tok(CONVCH), tok(128),...  41.2 us
    pallas_call x1, Pallas kernels, run_third(): pl.pallas_call(third_kernel, grid=grid, in_specs=[tok(CONVCH), tok(CONVCH...  40.5 us
    ppermute x19, waiting for transfers between devices, swapped(): lax.ppermute(v, axis, [(i, (i + offset) % size) for i in range(size)])  40.3 us
    dot_general x7, matrix products, dot(): return lax.dot_general(a, b, dims, preferred_element_type=F32)  40.2 us
    unnamed x81, local copies, waits for them, and re-layouts  22.5 us
    ppermute x19, starting transfers between devices, swapped(): lax.ppermute(v, axis, [(i, (i + offset) % size) for i in range(size)])  19 us
    all_to_all x1, waiting for transfers between devices, body(): lax.all_to_all(early, ('z', 'x'), split_axis=0, concat_axis=0, tiled=True)  18.5 us
    pallas_call x1, Pallas kernels, run_first(): pl.pallas_call(first_kernel, grid=grid, in_specs=[tok(D), per(8, D), whol...  16.8 us
  transfers between devices with their start and end apart: 31, of which 11 were waited for; matrix products, arithmetic and copies ran while one was open for 21% of the time, Pallas kernels for 11%

profile of v4, /device:TPU:0, one launch (start us, length us, event | category | flops | bytes accessed | tf_op | source)
XLA Modules:
  0.0 398.6 jit_solution(11088230710329327042)
XLA Ops:
  13.3 3.1 collective-permute-start.1
  16.4 2.6 collective-permute-start.2
  20.4 2.1 collective-permute-start.7
  23.9 6.5 %collective-permute-done.6 = bf16[48,768]{1,0:T(8,128)(2,1)S(1)} collective-permute-done((bf16[48,768]{1,0:T(8,128)(2,1)S(1)}, bf16[48,768]{1,0:T(8,128)(2,1)S(1)}, u32[]{:S(2)}, u32[]{:S(2)}) %collective-permute-start.6) | collective-permute-done | bytes 73760 | tf_op jit(solution)/shard_map/ppermute | solution.py:614
  30.5 3.5 collective-permute-start.3
  34.0 3.8 collective-permute-start
  40.0 8.6 %collective-permute-done.8 = bf16[4,48,768]{2,1,0:T(8,128)(2,1)S(1)} collective-permute-done((bf16[4,48,768]{2,1,0:T(8,128)(2,1)S(1)}, bf16[4,48,768]{2,1,0:T(8,128)(2,1)S(1)}, u32[]{:S(2)}, u32[]{:S(2)}) %collective-permute-start.8) | collective-permute-done | bytes 294944 | tf_op jit(solution)/shard_map/ppermute | solution.py:614
  50.5 7.0 %collective-permute-done.4 = bf16[4,24,1536]{2,1,0:T(8,128)(2,1)S(1)} collective-permute-done((bf16[4,24,1536]{2,1,0:T(8,128)(2,1)S(1)}, bf16[4,24,1536]{2,1,0:T(8,128)(2,1)S(1)}, u32[]{:S(2)}, u32[]{:S(2)}) %collective-permute-start.4) | collective-permute-done | bytes 294944 | tf_op jit(solution)/shard_map/ppermute | solution.py:614
  58.4 5.9 %collective-permute-done.12.refs_1_ = bf16[2,4,48,768]{3,2,1,0:T(8,128)(2,1)} collective-permute-done((bf16[2,4,48,768]{3,2,1,0:T(8,128)(2,1)}, bf16[2,4,48,768]{3,2,1,0:T(8,128)(2,1)}, u32[]{:S(2)}, u32[]{:S(2)}) %collective-permute-start.12) | collective-permute-done | bytes 589856 | tf_op jit(solution)/shard_map/ppermute | solution.py:614
  67.8 4.5 %collective-permute-done.9.refs_1_ = bf16[2,4,24,1536]{3,2,1,0:T(8,128)(2,1)} collective-permute-done((bf16[2,4,24,1536]{3,2,1,0:T(8,128)(2,1)}, bf16[2,4,24,1536]{3,2,1,0:T(8,128)(2,1)}, u32[]{:S(2)}, u32[]{:S(2)}) %collective-permute-start.9) | collective-permute-done | bytes 589856 | tf_op jit(solution)/shard_map/ppermute | solution.py:614
  72.4 3.8 assemble.3
  80.4 16.8 %first.1 = (bf16[1,1024,768]{2,1,0:T(8,128)(2,1)}, bf16[1,1024,1792]{2,1,0:T(8,128)(2,1)}, f32[1,1024,1792]{2,1,0:T(8,128)}, f32[1,1024,128]{2,1,0:T(8,128)}, f3...) custom-call(bf16[1,1024,768]{2,1,0:T(8,128)(2,1)} %u_ref.3, bf16[1,8,768]{2,1,0:T(8,128)(2,1)} %copy-done.28, ...), custom_call_target="tpu_custom_call" | custom-call | tf_op jit(solution)/shard_map/first/pallas_call | solution.py:472
  97.3 2.8 collective-permute-start.15
  100.1 7.3 %convolution_bitcast_fusion.bgrad_ref = f32[1024,1536]{1,0:T(8,128)} fusion(bf16[1536,768]{1,0:T(8,128)(2,1)} %bitcast.139, bf16[1,1024,768]{2,1,0:T(8,128)(2,1)} %param.26), kind=kOutput, calls=%fused_computation.5 | convolution fusion | flops 2415919104 | bytes 10223616 | tf_op jit(solution)/shard_map/dot_general | solution.py:37
  107.4 3.8 assemble.2
  111.3 3.0 copy.70
  114.3 7.4 %fusion.15.gate_ref = f32[1024,1536]{1,0:T(8,128)} fusion(bf16[768,1536]{1,0:T(8,128)(2,1)} %bitcast.144, bf16[1,1024,768]{2,1,0:T(8,128)(2,1)} %get-tuple-element.50), kind=kOutput, calls=%fused_computation.26 | convolution fusion | flops 2415919104 | bytes 10223616 | tf_op jit(solution)/shard_map/dot_general | solution.py:37
  121.7 41.2 %second.1 = (bf16[1,1024,768]{2,1,0:T(8,128)(2,1)}, bf16[1024,1536]{1,0:T(8,128)(2,1)}, bf16[1024,1536]{1,0:T(8,128)(2,1)}, bf16[1024,1536]{1,0:T(8,128)(2,1)}, ...) custom-call(f32[1,1024,1792]{2,1,0:T(8,128)} %get-tuple-element.48.pre_ref, ...), custom_call_target="tpu_custom_call" | custom-call | tf_op jit(solution)/shard_map/second/pallas_call | solution.py:506
  162.9 4.7 %copy.71 = bf16[1536,1024]{1,0:T(8,128)(2,1)} copy(bf16[1536,1024]{0,1:T(8,128)(2,1)} %bitcast.141) | data formatting | bytes 6291456 | tf_op jit(solution)/shard_map/dot_general | solution.py:37
  167.6 5.0 %fusion.12.refs_2_ = f32[8,2,96,768]{3,2,1,0:T(8,128)S(1)} fusion(bf16[8,2,96,1024]{3,2,1,0:T(8,128)(2,1)} %bitcast.142, bf16[1,1024,768]{2,1,0:T(8,128)(2,1)} %param.26), kind=kOutput, calls=%fused_computation.23 | convolution fusion | flops 2415919104 | bytes 9437184 | tf_op jit(solution)/shard_map/dot_general | solution.py:37
  173.1 2.1 copy-done.14
  176.7 2.6 fusion.10.refs_0_
  186.1 6.3 %chip_sum.2 = (bf16[8,96,1536]{2,1,0:T(8,128)(2,1)}, f32[96,1536]{1,0:T(8,128)}) custom-call(s32[4]{0:T(128)} %pad_add_fusion.idx, f32[8,2,48,1536]{3,2,1,0:T(8,128)} %copy-done.4, f32[8,48,1536]{2,1,0:T(8,128)} %collective-permute-done.16.refs_1_, f32[8,2,96,768]{3,2,1,0:T(8,128)} %copy-done.3, f32[8,96,768]{2,1,0:T(8,128)} %copy-done.12), custom_call_target="tpu_custom_call" | custom-call | tf_op jit(solution)/shard_map/chip_sum/pallas_call | solution.py:721
  192.5 11.1 %collective-permute-done.18.leave_ref = f32[1,128,1536]{2,1,0:T(8,128)} collective-permute-done((f32[1,128,1536]{2,1,0:T(8,128)}, f32[1,128,1536]{2,1,0:T(8,128)}, u32[]{:S(2)}, u32[]{:S(2)}) %collective-permute-start.18) | collective-permute-done | bytes 786464 | tf_op jit(solution)/shard_map/ppermute | solution.py:914
  203.6 40.5 %third.1 = (bf16[1,1024,1920]{2,1,0:T(8,128)(2,1)}, f32[1,8,1792]{2,1,0:T(8,128)}, f32[1,8,1792]{2,1,0:T(8,128)}, f32[8,1792]{1,0:T(8,128)}) custom-call(f32[1,1024,1792]{2,1,0:T(8,128)} %get-tuple-element.48.pre_ref, bf16[1,1024,1792]{2,1,0:T(8,128)(2,1)} %get-tuple-element.54.mixed_ref, f32[1,1024,128]{2,1,0:T(8,128)} %get-tuple-element.49.z_ref, ...), custom_call_target="tpu_custom_call" | custom-call | tf_op jit(solution)/shard_map/third/pallas_call | solution.py:543
  245.4 4.4 %all-to-all-start = ((bf16[8,96,1536]{2,1,0:T(8,128)(2,1)}), bf16[8,96,1536]{2,1,0:T(8,128)(2,1)}, u32[]{:S(2)}, u32[]{:S(2)}) async-start(bf16[8,96,1536]{2,1,0:T(8,128)(2,1)} %get-tuple-element.70), calls=%async_computation | async-start | bytes 4718592 | tf_op jit(solution)/shard_map/all_to_all | solution.py:925
  253.8 6.0 %fusion.refs_0_ = f32[8,2,48,1920]{3,2,1,0:T(8,128)S(1)} fusion(bf16[8,2,48,1024]{3,2,1,0:T(8,128)(2,1)} %bitcast.146, bf16[1,1024,1920]{2,1,0:T(8,128)(2,1)} %get-tuple-element.65), kind=kOutput, calls=%fused_computation.6 | convolution fusion | flops 3019898880 | bytes 11403264 | tf_op jit(solution)/shard_map/dot_general | solution.py:37
  259.9 2.5 copy-done.2
  268.4 6.6 %fusion.2 = f32[1024,768]{1,0:T(8,128)S(1)} fusion(bf16[768,1920]{1,0:T(8,128)(2,1)} %all-gather.2.cloned.1.call-done.w_ref, bf16[1,1024,1920]{2,1,0:T(8,128)(2,1)} %get-tuple-element.65), kind=kOutput, calls=%fused_computation.8 | convolution fusion | flops 3019898880 | bytes 10027008 | tf_op jit(solution)/shard_map/dot_general | solution.py:37
  275.1 5.3 %fusion.9 = (f32[768]{0:T(1024)S(1)}, f32[1024]{0:T(1024)}, f32[1024,768]{1,0:T(8,128)}) fusion(bf16[1,1024,768]{2,1,0:T(8,128)(2,1)S(1)} %copy-done.1, f32[1024]{0:T(1024)S(1)} %fusion.44, f32[768]{0:T(1024)S(1)} %copy-done.26, f32[1024,768]{1,0:T(8,128)S(1)} %fusion.2, bf16[1024,1536]{1,0:T(8,128)(2,1)S(1)} %copy-done.33, bf16[768,1536]{1,0:T(8,128)(2,1)S(1)} %bitcast.145), kind=kOutput, calls=%fused_computation.16 | convolution fusion | flops 2422208768 | bytes 13383680 | tf_op jit(solution)/shard_map/dot_general | solution.py:37
  280.5 4.6 %chip_sum.3 = (bf16[8,48,1920]{2,1,0:T(8,128)(2,1)}, f32[48,1920]{1,0:T(8,128)}) custom-call(s32[4]{0:T(128)} %pad_add_fusion.idx, f32[8,2,48,1920]{3,2,1,0:T(8,128)} %copy-done.2, f32[8,48,1920]{2,1,0:T(8,128)} %collective-permute-done.20.refs_1_), custom_call_target="tpu_custom_call" | custom-call | tf_op jit(solution)/shard_map/chip_sum/pallas_call | solution.py:721
  285.0 18.5 %all-to-all-done.got_ref = bf16[8,96,1536]{2,1,0:T(8,128)(2,1)} async-done(((bf16[8,96,1536]{2,1,0:T(8,128)(2,1)}), bf16[8,96,1536]{2,1,0:T(8,128)(2,1)}, u32[]{:S(2)}, u32[]{:S(2)}) %all-to-all-start) | async-done | bytes 2359328 | tf_op jit(solution)/shard_map/all_to_all | solution.py:925
  303.5 4.3 %all-to-all-start.1 = ((bf16[8,48,1920]{2,1,0:T(8,128)(2,1)}), bf16[8,48,1920]{2,1,0:T(8,128)(2,1)}, u32[]{:S(2)}, u32[]{:S(2)}) async-start(bf16[8,48,1920]{2,1,0:T(8,128)(2,1)} %get-tuple-element.74), calls=%async_computation.1 | async-start | bytes 2949120 | tf_op jit(solution)/shard_map/all_to_all | solution.py:959
  307.8 2.3 copy.73
  310.1 2.3 copy.79
  313.7 3.6 owner_sum.2
  317.3 2.4 collective-permute-start.21
  319.9 5.4 %fusion.5 = f32[1,1024,768]{2,1,0:T(8,128)} fusion(f32[1024,768]{1,0:T(8,128)} %get-tuple-element.141, bf16[1,1024,768]{2,1,0:T(8,128)(2,1)} %u_ref.3, bf16[1,1024,768]{2,1,0:T(8,128)(2,1)} %param.26, f32[1024]{0:T(1024)} %multiply_multiply_fusion.1, f32[1024]{0:T(1024)} %copy-done.27, f32[768]{0:T(1024)} %param.30), kind=kLoop, calls=%fused_computation.12 | loop fusion | flops 6291456 | bytes 9448448 | tf_op jit(solution)/shard_map/reshape | solution.py:943
  325.3 9.7 %collective-permute-done.24 = f32[96,128]{1,0:T(8,128)S(1)} collective-permute-done((f32[96,128]{1,0:T(8,128)S(1)}, f32[96,128]{1,0:T(8,128)S(1)}, u32[]{:S(2)}, u32[]{:S(2)}) %collective-permute-start.24) | collective-permute-done | bytes 49184 | tf_op jit(solution)/shard_map/ppermute | solution.py:678
  338.4 4.2 %add_multiply_fusion.1 = f32[4,6,128,128]{3,2,1,0:T(8,128)} fusion(f32[4,6,128,128]{3,2,1,0:T(8,128)} %param.46, f32[4,24,6,128]{3,2,1,0:T(8,128)} %reshape.256), kind=kOutput, calls=%fused_computation.28 | convolution fusion | flops 57409536 | bytes 3440640 | tf_op jit(solution)/shard_map/abji,abjk->abik/dot_general | solution.py:604
  346.8 2.0 collective-permute-start.26
  348.8 2.1 fusion.20
  351.0 2.9 collective-permute-start.27
  356.6 3.2 owner_sum.3
  362.2 6.0 %collective-permute-done.22 = f32[48,1920]{1,0:T(8,128)S(1)} collective-permute-done((f32[48,1920]{1,0:T(8,128)}, f32[48,1920]{1,0:T(8,128)S(1)}, u32[]{:S(2)}, u32[]{:S(2)}) %collective-permute-start.22) | collective-permute-done | bytes 368672 | tf_op jit(solution)/shard_map/ppermute | solution.py:614
  371.1 2.1 reshape.253
  373.3 7.2 %add_multiply_fusion = f32[2,26,128,128]{3,2,1,0:T(8,128)} fusion(f32[2,26,128,128]{3,2,1,0:T(8,128)} %param.38, f32[2,24,26,128]{3,2,1,0:T(8,128)} %reshape.253), kind=kOutput, calls=%fused_computation.10 | convolution fusion | flops 124387328 | bytes 7454720 | tf_op jit(solution)/shard_map/abji,abjk->abik/dot_general | solution.py:604
  386.0 2.2 copy.83
  (195 shorter events, 67.7 us)
Async XLA Ops:
  7.2 374.2 %copy-start = (f32[2,26,128,128]{3,2,1,0:T(8,128)S(1)}, f32[2,26,128,128]{3,2,1,0:T(8,128)}, u32[]{:S(2)}) copy-start(f32[2,26,128,128]{3,2,1,0:T(8,128)} %param.40) | copy-start | bytes 10223620
  7.2 68.9 %all-gather.2.cloned.1.call-start = ((), (), s32[]{:S(2)}) async-start(), calls=%async_computation.2 | async-start | bytes 3133440 | tf_op jit(solution)/shard_map/all_gather | solution.py:855
  13.3 51.0 %copy-start.35 = (f32[24]{0:T(128)S(1)}, f32[24]{0:T(128)}, u32[]{:S(2)}) copy-start(f32[24]{0:T(128)} %param.34) | copy-start | bytes 292
  13.3 26.1 %collective-permute-start.1 = (bf16[24,1536]{1,0:T(8,128)(2,1)S(1)}, bf16[24,1536]{1,0:T(8,128)(2,1)S(1)}, u32[]{:S(2)}, u32[]{:S(2)}) collective-permute-start(bf16[24,1536]{1,0:T(8,128)(2,1)S(1)} %fusion.75), channel_id=1, source_target_pairs={{0,8},{8,16},{16,24},{24,0},{1,9},{9,17},{17,25},{25,1},{2,10},{10... | collective-permute-start | bytes 221192 | tf_op jit(solution)/shard_map/ppermute | solution.py:614
  16.4 22.9 %collective-permute-start.2 = (bf16[24,1536]{1,0:T(8,128)(2,1)S(1)}, bf16[24,1536]{1,0:T(8,128)(2,1)S(1)}, u32[]{:S(2)}, u32[]{:S(2)}) collective-permute-start(bf16[24,1536]{1,0:T(8,128)(2,1)S(1)} %fusion.75), channel_id=1, source_target_pairs={{0,16},{8,24},{16,0},{24,8},{1,17},{9,25},{17,1},{25,9},{2,18},{10... | collective-permute-start | bytes 221192 | tf_op jit(solution)/shard_map/ppermute | solution.py:614
  20.0 10.4 %collective-permute-start.6 = (bf16[48,768]{1,0:T(8,128)(2,1)S(1)}, bf16[48,768]{1,0:T(8,128)(2,1)S(1)}, u32[]{:S(2)}, u32[]{:S(2)}) collective-permute-start(bf16[48,768]{1,0:T(8,128)(2,1)S(1)} %fusion.74), channel_id=1, source_target_pairs={{0,16},{8,24},{16,0},{24,8},{1,17},{9,25},{17,1},{25,9},{2,18},{10... | collective-permute-start | bytes 221192 | tf_op jit(solution)/shard_map/ppermute | solution.py:614
  20.4 13.5 %collective-permute-start.7 = (bf16[48,768]{1,0:T(8,128)(2,1)S(1)}, bf16[48,768]{1,0:T(8,128)(2,1)S(1)}, u32[]{:S(2)}, u32[]{:S(2)}) collective-permute-start(bf16[48,768]{1,0:T(8,128)(2,1)S(1)} %fusion.74), channel_id=1, source_target_pairs={{0,24},{8,0},{16,8},{24,16},{1,25},{9,1},{17,9},{25,17},{2,26},{10... | collective-permute-start | bytes 221192 | tf_op jit(solution)/shard_map/ppermute | solution.py:614
  22.5 15.2 %collective-permute-start.5 = (bf16[48,768]{1,0:T(8,128)(2,1)S(1)}, bf16[48,768]{1,0:T(8,128)(2,1)S(1)}, u32[]{:S(2)}, u32[]{:S(2)}) collective-permute-start(bf16[48,768]{1,0:T(8,128)(2,1)S(1)} %fusion.74), channel_id=1, source_target_pairs={{0,8},{8,16},{16,24},{24,0},{1,9},{9,17},{17,25},{25,1},{2,10},{10... | collective-permute-start | bytes 221192 | tf_op jit(solution)/shard_map/ppermute | solution.py:614
  23.9 34.5 %copy-start.17 = (s32[1536]{0:T(1024)}, s32[1536]{0:T(1024)S(1)}, u32[]{:S(2)}) copy-start(s32[1536]{0:T(1024)S(1)} %add_select_fusion) | copy-start | bytes 18436
  23.9 42.7 %copy-start.31 = (f32[24]{0:T(128)S(1)}, f32[24]{0:T(128)}, u32[]{:S(2)}) copy-start(f32[24]{0:T(128)} %param.35) | copy-start | bytes 292
  23.9 42.8 %copy-start.21 = (f32[4,1792]{1,0:T(4,128)S(1)}, f32[4,1792]{1,0:T(4,128)}, u32[]{:S(2)}) copy-start(f32[4,1792]{1,0:T(4,128)} %param.31) | copy-start | bytes 86020
  23.9 43.4 %copy-start.34 = (f32[24]{0:T(128)S(1)}, f32[24]{0:T(128)}, u32[]{:S(2)}) copy-start(f32[24]{0:T(128)} %param.33) | copy-start | bytes 292
  30.5 8.9 %collective-permute-start.3 = (bf16[24,1536]{1,0:T(8,128)(2,1)S(1)}, bf16[24,1536]{1,0:T(8,128)(2,1)S(1)}, u32[]{:S(2)}, u32[]{:S(2)}) collective-permute-start(bf16[24,1536]{1,0:T(8,128)(2,1)S(1)} %fusion.75), channel_id=1, source_target_pairs={{0,24},{8,0},{16,8},{24,16},{1,25},{9,1},{17,9},{25,17},{2,26},{10... | collective-permute-start | bytes 221192 | tf_op jit(solution)/shard_map/ppermute | solution.py:614
  34.0 45.9 %collective-permute-start = (bf16[1,8,768]{2,1,0:T(8,128)(2,1)}, bf16[1,8,768]{2,1,0:T(8,128)(2,1)S(1)}, u32[]{:S(2)}, u32[]{:S(2)}) collective-permute-start(bf16[1,8,768]{2,1,0:T(8,128)(2,1)} %slice.45), channel_id=1, source_target_pairs={{0,1},{2,3},{4,5},{6,7},{8,9},{10,11},{12,13},{14,15},{16,17},{18,... | collective-permute-start | bytes 36872 | tf_op jit(solution)/shard_map/ppermute | solution.py:889
  37.8 10.9 %collective-permute-start.8 = (bf16[4,48,768]{2,1,0:T(8,128)(2,1)S(1)}, bf16[4,48,768]{2,1,0:T(8,128)(2,1)S(1)}, u32[]{:S(2)}, u32[]{:S(2)}) collective-permute-start(bf16[4,48,768]{2,1,0:T(8,128)(2,1)S(1)} %get-tuple-element.138), channel_id=1, source_target_pairs={{0,4},{4,0},{1,5},{5,1},{2,6},{6,2},{3,7},{7,3},{8,12},{12,8},{9,1... | collective-permute-start | bytes 884744 | tf_op jit(solution)/shard_map/ppermute | solution.py:614
  39.5 18.0 %collective-permute-start.4 = (bf16[4,24,1536]{2,1,0:T(8,128)(2,1)S(1)}, bf16[4,24,1536]{2,1,0:T(8,128)(2,1)S(1)}, u32[]{:S(2)}, u32[]{:S(2)}) collective-permute-start(bf16[4,24,1536]{2,1,0:T(8,128)(2,1)S(1)} %get-tuple-element.140), channel_id=1, source_target_pairs={{0,4},{4,0},{1,5},{5,1},{2,6},{6,2},{3,7},{7,3},{8,12},{12,8},{9,1... | collective-permute-start | bytes 884744 | tf_op jit(solution)/shard_map/ppermute | solution.py:614
  49.5 14.8 %collective-permute-start.12 = (bf16[2,4,48,768]{3,2,1,0:T(8,128)(2,1)}, bf16[2,4,48,768]{3,2,1,0:T(8,128)(2,1)}, u32[]{:S(2)}, u32[]{:S(2)}) collective-permute-start(bf16[2,4,48,768]{3,2,1,0:T(8,128)(2,1)} %pad_maximum_fusion.2.refs_0_), channel_id=1, source_target_pairs={{0,1},{1,0},{2,3},{3,2},{4,5},{5,4},{6,7},{7,6},{8,9},{9,8},{10,11... | collective-permute-start | bytes 1769480 | tf_op jit(solution)/shard_map/ppermute | solution.py:614
  50.5 21.8 %collective-permute-start.13 = (bf16[2,4,48,768]{3,2,1,0:T(8,128)(2,1)}, bf16[2,4,48,768]{3,2,1,0:T(8,128)(2,1)}, u32[]{:S(2)}, u32[]{:S(2)}) collective-permute-start(bf16[2,4,48,768]{3,2,1,0:T(8,128)(2,1)} %pad_maximum_fusion.2.refs_0_), channel_id=1, source_target_pairs={{0,2},{2,0},{1,3},{3,1},{4,6},{6,4},{5,7},{7,5},{8,10},{10,8},{9,1... | collective-permute-start | bytes 1769480 | tf_op jit(solution)/shard_map/ppermute | solution.py:614
  57.5 19.9 %copy-start.30 = (f32[1792]{0:T(1024)S(1)}, f32[1792]{0:T(1024)}, u32[]{:S(2)}) copy-start(f32[1792]{0:T(1024)} %param.32) | copy-start | bytes 21508
  57.5 20.5 %copy-start.29 = (f32[1536]{0:T(1024)S(1)}, f32[1536]{0:T(1024)}, u32[]{:S(2)}) copy-start(f32[1536]{0:T(1024)} %param.36) | copy-start | bytes 18436
  57.5 21.1 %copy-start.26 = (f32[768]{0:T(1024)S(1)}, f32[768]{0:T(1024)}, u32[]{:S(2)}) copy-start(f32[768]{0:T(1024)} %param.30) | copy-start | bytes 9220
  58.4 14.0 %collective-permute-start.9 = (bf16[2,4,24,1536]{3,2,1,0:T(8,128)(2,1)}, bf16[2,4,24,1536]{3,2,1,0:T(8,128)(2,1)}, u32[]{:S(2)}, u32[]{:S(2)}) collective-permute-start(bf16[2,4,24,1536]{3,2,1,0:T(8,128)(2,1)} %pad_maximum_fusion.1.refs_0_), channel_id=1, source_target_pairs={{0,1},{1,0},{2,3},{3,2},{4,5},{5,4},{6,7},{7,6},{8,9},{9,8},{10,11... | collective-permute-start | bytes 1769480 | tf_op jit(solution)/shard_map/ppermute | solution.py:614
  64.3 8.1 %collective-permute-start.14 = (bf16[2,4,48,768]{3,2,1,0:T(8,128)(2,1)}, bf16[2,4,48,768]{3,2,1,0:T(8,128)(2,1)}, u32[]{:S(2)}, u32[]{:S(2)}) collective-permute-start(bf16[2,4,48,768]{3,2,1,0:T(8,128)(2,1)} %collective-permute-done.12.refs_1_), channel_id=1, source_target_pairs={{0,2},{2,0},{1,3},{3,1},{4,6},{6,4},{5,7},{7,5},{8,10},{10,8},{9,1... | collective-permute-start | bytes 1769480 | tf_op jit(solution)/shard_map/ppermute | solution.py:614
  67.3 40.1 %collective-permute-start.10 = (bf16[2,4,24,1536]{3,2,1,0:T(8,128)(2,1)}, bf16[2,4,24,1536]{3,2,1,0:T(8,128)(2,1)}, u32[]{:S(2)}, u32[]{:S(2)}) collective-permute-start(bf16[2,4,24,1536]{3,2,1,0:T(8,128)(2,1)} %pad_maximum_fusion.1.refs_0_), channel_id=1, source_target_pairs={{0,2},{2,0},{1,3},{3,1},{4,6},{6,4},{5,7},{7,5},{8,10},{10,8},{9,1... | collective-permute-start | bytes 1769480 | tf_op jit(solution)/shard_map/ppermute | solution.py:614
  72.3 35.1 %collective-permute-start.11 = (bf16[2,4,24,1536]{3,2,1,0:T(8,128)(2,1)}, bf16[2,4,24,1536]{3,2,1,0:T(8,128)(2,1)}, u32[]{:S(2)}, u32[]{:S(2)}) collective-permute-start(bf16[2,4,24,1536]{3,2,1,0:T(8,128)(2,1)} %collective-permute-done.9.refs_1_), channel_id=1, source_target_pairs={{0,2},{2,0},{1,3},{3,1},{4,6},{6,4},{5,7},{7,5},{8,10},{10,8},{9,1... | collective-permute-start | bytes 1769480 | tf_op jit(solution)/shard_map/ppermute | solution.py:614
  97.3 24.4 %collective-permute-start.15 = (f32[1,128,1536]{2,1,0:T(8,128)}, f32[1,128,1536]{2,1,0:T(8,128)}, u32[]{:S(2)}, u32[]{:S(2)}) collective-permute-start(f32[1,128,1536]{2,1,0:T(8,128)} %get-tuple-element.51), channel_id=1, source_target_pairs={{0,1},{2,3},{4,5},{6,7},{8,9},{10,11},{12,13},{14,15},{16,17},{18,... | collective-permute-start | bytes 2359304 | tf_op jit(solution)/shard_map/ppermute | solution.py:895
  172.8 10.1 %collective-permute-start.17 = (f32[8,96,768]{2,1,0:T(8,128)S(1)}, f32[8,96,768]{2,1,0:T(8,128)S(1)}, u32[]{:S(2)}, u32[]{:S(2)}) collective-permute-start(f32[8,96,768]{2,1,0:T(8,128)S(1)} %dynamic-slice_bitcast_fusion.1), channel_id=1, source_target_pairs={{0,2},{2,0},{1,3},{3,1},{4,6},{6,4},{5,7},{7,5},{8,10},{10,8},{9,1... | collective-permute-start | bytes 7077896 | tf_op jit(solution)/shard_map/ppermute | solution.py:614
  181.4 4.7 %collective-permute-start.16 = (f32[8,48,1536]{2,1,0:T(8,128)S(1)}, f32[8,48,1536]{2,1,0:T(8,128)}, u32[]{:S(2)}, u32[]{:S(2)}) collective-permute-start(f32[8,48,1536]{2,1,0:T(8,128)S(1)} %dynamic-slice_bitcast_fusion.2), channel_id=1, source_target_pairs={{0,2},{2,0},{1,3},{3,1},{4,6},{6,4},{5,7},{7,5},{8,10},{10,8},{9,1... | collective-permute-start | bytes 7077896 | tf_op jit(solution)/shard_map/ppermute | solution.py:614
  181.7 21.9 %collective-permute-start.18 = (f32[1,128,1536]{2,1,0:T(8,128)}, f32[1,128,1536]{2,1,0:T(8,128)}, u32[]{:S(2)}, u32[]{:S(2)}) collective-permute-start(f32[1,128,1536]{2,1,0:T(8,128)} %get-tuple-element.61), channel_id=1, source_target_pairs={{1,0},{3,2},{5,4},{7,6},{9,8},{11,10},{13,12},{15,14},{17,16},{19,... | collective-permute-start | bytes 2359304 | tf_op jit(solution)/shard_map/ppermute | solution.py:914
  244.1 7.5 %collective-permute-start.19 = (f32[1,8,1792]{2,1,0:T(8,128)}, f32[1,8,1792]{2,1,0:T(8,128)S(1)}, u32[]{:S(2)}, u32[]{:S(2)}) collective-permute-start(f32[1,8,1792]{2,1,0:T(8,128)} %get-tuple-element.64), channel_id=1, source_target_pairs={{1,0},{3,2},{5,4},{7,6},{9,8},{11,10},{13,12},{15,14},{17,16},{19,... | collective-permute-start | bytes 172040 | tf_op jit(solution)/shard_map/ppermute | solution.py:930
  245.4 58.1 %all-to-all-start = ((bf16[8,96,1536]{2,1,0:T(8,128)(2,1)}), bf16[8,96,1536]{2,1,0:T(8,128)(2,1)}, u32[]{:S(2)}, u32[]{:S(2)}) async-start(bf16[8,96,1536]{2,1,0:T(8,128)(2,1)} %get-tuple-element.70), calls=%async_computation | async-start | bytes 4718592 | tf_op jit(solution)/shard_map/all_to_all | solution.py:925
  251.6 12.6 %copy-start.20 = (f32[1024]{0:T(1024)}, f32[1024]{0:T(1024)S(1)}, u32[]{:S(2)}) copy-start(f32[1024]{0:T(1024)S(1)} %fusion.6) | copy-start | bytes 12292
  264.2 16.3 %collective-permute-start.20 = (f32[8,48,1920]{2,1,0:T(8,128)}, f32[8,48,1920]{2,1,0:T(8,128)}, u32[]{:S(2)}, u32[]{:S(2)}) collective-permute-start(f32[8,48,1920]{2,1,0:T(8,128)} %dynamic-slice_bitcast_fusion), channel_id=1, source_target_pairs={{0,2},{2,0},{1,3},{3,1},{4,6},{6,4},{5,7},{7,5},{8,10},{10,8},{9,1... | collective-permute-start | bytes 8847368 | tf_op jit(solution)/shard_map/ppermute | solution.py:614
  264.2 10.9 %copy-start.27 = (f32[1024]{0:T(1024)}, f32[1024]{0:T(1024)S(1)}, u32[]{:S(2)}) copy-start(f32[1024]{0:T(1024)S(1)} %fusion.44) | copy-start | bytes 12292
  303.5 39.1 %all-to-all-start.1 = ((bf16[8,48,1920]{2,1,0:T(8,128)(2,1)}), bf16[8,48,1920]{2,1,0:T(8,128)(2,1)}, u32[]{:S(2)}, u32[]{:S(2)}) async-start(bf16[8,48,1920]{2,1,0:T(8,128)(2,1)} %get-tuple-element.74), calls=%async_computation.1 | async-start | bytes 2949120 | tf_op jit(solution)/shard_map/all_to_all | solution.py:959
  312.4 7.4 %collective-permute-start.23 = (f32[96,128]{1,0:T(8,128)S(1)}, f32[96,128]{1,0:T(8,128)S(1)}, u32[]{:S(2)}, u32[]{:S(2)}) collective-permute-start(f32[96,128]{1,0:T(8,128)S(1)} %pad_bitcast_fusion), channel_id=1, source_target_pairs={{0,2},{2,0},{1,3},{3,1},{4,6},{6,4},{5,7},{7,5},{8,10},{10,8},{9,1... | collective-permute-start | bytes 147464 | tf_op jit(solution)/shard_map/ppermute | solution.py:678
  317.3 17.7 %collective-permute-start.21 = (f32[96,1536]{1,0:T(8,128)}, f32[96,1536]{1,0:T(8,128)S(1)}, u32[]{:S(2)}, u32[]{:S(2)}) collective-permute-start(f32[96,1536]{1,0:T(8,128)} %owner_sum.2), channel_id=1, source_target_pairs={{0,1},{1,0},{2,3},{3,2},{4,5},{5,4},{6,7},{7,6},{8,9},{9,8},{10,11... | collective-permute-start | bytes 1769480 | tf_op jit(solution)/shard_map/ppermute | solution.py:614
  319.8 15.2 %collective-permute-start.24 = (f32[96,128]{1,0:T(8,128)S(1)}, f32[96,128]{1,0:T(8,128)S(1)}, u32[]{:S(2)}, u32[]{:S(2)}) collective-permute-start(f32[96,128]{1,0:T(8,128)S(1)} %fusion.45), channel_id=1, source_target_pairs={{0,1},{1,0},{2,3},{3,2},{4,5},{5,4},{6,7},{7,6},{8,9},{9,8},{10,11... | collective-permute-start | bytes 147464 | tf_op jit(solution)/shard_map/ppermute | solution.py:678
  319.9 15.2 %copy-start.13 = (f32[96,1536]{1,0:T(8,128)S(1)}, f32[96,1536]{1,0:T(8,128)}, u32[]{:S(2)}) copy-start(f32[96,1536]{1,0:T(8,128)} %owner_sum.2) | copy-start | bytes 1769476
  342.7 11.2 %copy-start.6 = (f32[4,24,6,128]{3,2,1,0:T(8,128)S(1)}, f32[4,24,6,128]{3,2,1,0:T(8,128)}, u32[]{:S(2)}) copy-start(f32[4,24,6,128]{3,2,1,0:T(8,128)} %reshape.256) | copy-start | bytes 884740
  342.7 11.2 %copy-start.16 = (f32[4,6,24,24]{3,2,1,0:T(8,128)S(1)}, f32[4,6,24,24]{3,2,1,0:T(8,128)}, u32[]{:S(2)}) copy-start(f32[4,6,24,24]{3,2,1,0:T(8,128)} %param.45) | copy-start | bytes 165892
  342.7 12.3 %copy-start.10 = (f32[96,1536]{1,0:T(8,128)S(1)}, f32[96,1536]{1,0:T(8,128)}, u32[]{:S(2)}) copy-start(f32[96,1536]{1,0:T(8,128)} %copy-done.9) | copy-start | bytes 1769476
  342.7 4.2 %collective-permute-start.25 = (f32[96,128]{1,0:T(8,128)S(1)}, f32[96,128]{1,0:T(8,128)S(1)}, u32[]{:S(2)}, u32[]{:S(2)}) collective-permute-start(f32[96,128]{1,0:T(8,128)S(1)} %fusion.73), channel_id=1, source_target_pairs={{0,4},{4,0},{1,5},{5,1},{2,6},{6,2},{3,7},{7,3},{8,12},{12,8},{9,1... | collective-permute-start | bytes 147464 | tf_op jit(solution)/shard_map/ppermute | solution.py:678
  346.8 4.2 %collective-permute-start.26 = (f32[96,128]{1,0:T(8,128)S(1)}, f32[96,128]{1,0:T(8,128)S(1)}, u32[]{:S(2)}, u32[]{:S(2)}) collective-permute-start(f32[96,128]{1,0:T(8,128)S(1)} %add.140), channel_id=1, source_target_pairs={{0,8},{8,0},{16,24},{24,16},{1,9},{9,1},{17,25},{25,17},{2,10},{10... | collective-permute-start | bytes 147464 | tf_op jit(solution)/shard_map/ppermute | solution.py:678
  350.9 10.6 %copy-start.19 = (f32[11336]{0:T(1024)S(1)}, f32[11336]{0:T(1024)}, u32[]{:S(2)}) copy-start(f32[11336]{0:T(1024)} %param.49) | copy-start | bytes 136036
  351.0 10.5 %collective-permute-start.27 = (f32[96,128]{1,0:T(8,128)S(1)}, f32[96,128]{1,0:T(8,128)S(1)}, u32[]{:S(2)}, u32[]{:S(2)}) collective-permute-start(f32[96,128]{1,0:T(8,128)S(1)} %add.141), channel_id=1, source_target_pairs={{0,16},{8,24},{16,0},{24,8},{1,17},{9,25},{17,1},{25,9},{2,18},{10... | collective-permute-start | bytes 147464 | tf_op jit(solution)/shard_map/ppermute | solution.py:678
  359.7 8.5 %collective-permute-start.22 = (f32[48,1920]{1,0:T(8,128)}, f32[48,1920]{1,0:T(8,128)S(1)}, u32[]{:S(2)}, u32[]{:S(2)}) collective-permute-start(f32[48,1920]{1,0:T(8,128)} %owner_sum.3), channel_id=1, source_target_pairs={{0,1},{1,0},{2,3},{3,2},{4,5},{5,4},{6,7},{7,6},{8,9},{9,8},{10,11... | collective-permute-start | bytes 1105928 | tf_op jit(solution)/shard_map/ppermute | solution.py:614
  382.9 7.8 %copy-start.25 = (f32[2,24,24]{2,1,0:T(8,128)S(1)}, f32[2,24,24]{2,1,0:T(8,128)}, u32[]{:S(2)}) copy-start(f32[2,24,24]{2,1,0:T(8,128)} %param.41) | copy-start | bytes 13828
  (20 other events, 83.1 us)
Sparse Core Ops, SparseCore 0:
  12.5 54.4 all-gather.1

commit v5 on v4

--- a/solution.py
+++ b/solution.py
@@ -16,6 +16,8 @@
 DI = 1536
 CONVCH = 1792
 WIDE = CONVCH + 128
+ROW_BLOCK = 24
+COL_BLOCK = 128
 
 BL = 128
 PAIRS = HEADS // 2
@@ -26,6 +28,7 @@
 LR = 0.25
 LR_VEC = 0.02
 NEG = -1e30
+LOG2E = 1.4426950408889634
 BF = jnp.bfloat16
 F32 = jnp.float32
 NN = (((1,), (0,)), ((), ()))
@@ -86,7 +89,18 @@
 
 
 def sigmoid(v):
-    return 1.0 / (1.0 + jnp.exp(-v))
+    return 0.5 * jnp.tanh(0.5 * v) + 0.5
+
+
+def silu(v):
+    half = 0.5 * v
+    return half * jnp.tanh(half) + half
+
+
+def silu_parts(v):
+    half = 0.5 * v
+    curve = jnp.tanh(half)
+    return half * curve + half, 0.5 * curve + 0.5
 
 
 def rates(alog_ref):
@@ -94,9 +108,14 @@
     return jnp.where(head_lanes(rate.shape), rate, 0.0)
 
 
-def pair_blocks(v):
-    left = lax.broadcasted_iota(jnp.int32, v.shape, 1) < HEADDIM
-    return jnp.concatenate([jnp.where(left, v, 0.0), jnp.where(left, 0.0, v)], axis=0).astype(BF)
+def pair_masks():
+    left = lax.broadcasted_iota(jnp.int32, (BL, BL), 1) < HEADDIM
+    first = jnp.where(left, 1.0, 0.0)
+    return first.astype(BF), (1.0 - first).astype(BF)
+
+
+def pair_blocks(v, masks):
+    return jnp.concatenate([v * masks[0], v * masks[1]], axis=0)
 
 
 def norm_rows(u, gain):
@@ -137,25 +156,27 @@
             moved = pltpu.roll(joined, KCONV - 1 - tap, 0)[8:, :]
             pre = pre + cw_ref[tap : tap + 1, cols] * moved
         pre_ref[0, :, cols] = pre
-        full[:, cols] = pre * sigmoid(pre)
+        full[:, cols] = silu(pre)
     tail[...] = mixed[tile - 8 :, :]
-    step_all = softplus(z)
     rate = rates(alog_ref)
-    tri = jnp.where(tri_mask(True), 1.0, 0.0).astype(BF)
-    emat = emat_ref[...]
-    for part in range(tile // BL):
-        rows = slice(part * BL, (part + 1) * BL)
-        step = step_all[rows]
+
+    def block(part, carry):
+        rows = pl.ds(pl.multiple_of(part * BL, BL), BL)
+        tri = jnp.where(tri_mask(True), 1.0, 0.0).astype(BF)
+        step = softplus(z_ref[0, rows, :])
         cum = prefix(tri, step * rate)
         last = cum[BL - 1 : BL, :]
-        weights = expand(jnp.exp(last - cum) * step, emat)
+        weights = expand(jnp.exp(last - cum) * step, emat_ref[...])
         decay = expand(
-            jnp.where(head_lanes((8, 128)), jnp.broadcast_to(jnp.exp(last), (8, 128)), 0.0), emat
+            jnp.where(head_lanes((8, 128)), jnp.broadcast_to(jnp.exp(last), (8, 128)), 0.0),
+            emat_ref[...],
         )[0:1, :]
-        inputs_b = full[rows, DI : DI + DSTATE]
-        fresh = dot3(inputs_b.T, weights * full[rows, :DI])
+        fresh = dot3(full[rows, DI : DI + DSTATE].T, weights * full[rows, :DI])
         state_ref[0] = state_ref[0] * decay + fresh
         total_ref[0] = total_ref[0] + jnp.broadcast_to(last, (8, 128))
+        return carry
+
+    lax.fori_loop(0, tile // BL, block, 0)
 
 
 def dot_wide(ahl, ah, bh, bl):
@@ -182,7 +203,7 @@
         column = jnp.broadcast_to(cum[:, h : h + 1], (BL, BL))
         row = cum_t[h : h + 1, :]
         spread = (row - column) if transposed else (column - row)
-        kernels.append(jnp.exp(jnp.where(mask, spread, NEG)))
+        kernels.append(jnp.exp2(jnp.where(mask, spread, NEG)))
         columns.append(column)
     chosen = jnp.where(left, columns[0], columns[1])
     steps = jnp.where(left, step[:, 2 * pair : 2 * pair + 1], step[:, 2 * pair + 1 : 2 * pair + 2])
@@ -194,10 +215,10 @@
 
 
 def second_kernel(
-    pre_ref, z_ref, gate_ref, bgrad_ref, u_ref, enter_ref, wo_ref, skip_ref, ggain_ref, alog_ref,
+    pre_ref, z_ref, normed_ref, up_ref, u_ref, enter_ref, wg_ref, wo_ref, skip_ref, ggain_ref, alog_ref,
     gmat_ref,
     out_ref, branch_ref, dy_ref, ggrad_ref, state_ref, rdot_ref, dstate_ref, sums_ref,
-    gain_acc, skip_acc, state, running, ys, es,
+    gain_acc, skip_acc, state, running, ys, es, xs_ref, ss_ref, sl_ref, sg_ref, up_scratch,
 ):
     step_index = pl.program_id(1)
     tile = pre_ref.shape[1]
@@ -219,12 +240,12 @@
         rows = pl.ds(pl.multiple_of(part * BL, BL), BL)
         mask = tri_mask(True)
         left = lax.broadcasted_iota(jnp.int32, (BL, BL), 1) < HEADDIM
+        masks = pair_masks()
         tri = jnp.where(mask, 1.0, 0.0).astype(BF)
-        pre = pre_ref[0, rows, DI:]
-        conv = pre * sigmoid(pre)
+        conv = silu(pre_ref[0, rows, DI:])
         inputs_b, inputs_c = conv[:, :DSTATE], conv[:, DSTATE:]
         step = softplus(z_ref[0, rows, :])
-        cum = prefix(tri, step * rate)
+        cum = prefix(tri, step * (rate * LOG2E))
         cum_t = cum.T
         scores = dot3(inputs_c, inputs_b, NT)
         c_wide, c_high = wide_split(inputs_c)
@@ -237,15 +258,13 @@
             inner, grown, weighted, xs = [], [], [], []
             for pair in (2 * quad, 2 * quad + 1):
                 kernels, chosen, steps = pair_values(pair, cum, cum_t, step, mask, left, False)
-                own = pre_ref[0, rows, pair * 128 : (pair + 1) * 128]
-                x = own * sigmoid(own)
+                x = silu(pre_ref[0, rows, pair * 128 : (pair + 1) * 128])
                 scaled = steps * x
                 mh, ml = split2(jnp.concatenate([scores * k for k in kernels], axis=1))
-                high = scaled.astype(BF).astype(F32)
-                rh, rl = pair_blocks(high), pair_blocks(scaled - high)
+                rh, rl = (pair_blocks(v, masks) for v in split2(scaled))
                 inner.append(dot(mh, rh) + dot(ml, rh) + dot(mh, rl))
-                grown.append(jnp.exp(chosen))
-                weighted.append(jnp.exp(chosen[BL - 1 : BL, :] - chosen) * scaled)
+                grown.append(jnp.exp2(chosen))
+                weighted.append(jnp.exp2(chosen[BL - 1 : BL, :] - chosen) * scaled)
                 xs.append(x)
             inner, grown, weighted, x = (
                 jnp.concatenate(v, axis=1) for v in (inner, grown, weighted, xs)
@@ -259,9 +278,15 @@
             ys[:, cols] = yhat
             es[:, cols] = grown
             states = (yhat + skip_ref[0:1, cols] * x).astype(BF).astype(F32)
-            gate = gate_ref[rows, cols]
-            gated = states * (gate * sigmoid(gate))
-            product = gated * (bgrad_ref[rows, cols] * ggain_ref[0:1, cols])
+            sl, sg = silu_parts(dot(normed_ref[0, rows, :], wg_ref[:, cols]))
+            upstream = dot(up_ref[rows, :], wo_ref[cols, :], NT)
+            up_scratch[:, cols] = upstream
+            gated = states * sl
+            xs_ref[:, cols] = x
+            ss_ref[:, cols] = states
+            sl_ref[:, cols] = sl
+            sg_ref[:, cols] = sg
+            product = gated * (upstream * ggain_ref[0:1, cols])
             squared = gated * gated
             squares = squares + squared[:, :128] + squared[:, 128:]
             products = products + product[:, :128] + product[:, 128:]
@@ -274,16 +299,13 @@
             scaled_dy, dot_terms = [], []
             for pair in (2 * quad, 2 * quad + 1):
                 own_cols = slice(pair * 128, (pair + 1) * 128)
-                own = pre_ref[0, rows, own_cols]
-                x = own * sigmoid(own)
+                x = xs_ref[:, own_cols]
                 yhat = ys[:, own_cols]
-                states = (yhat + skip_ref[0:1, own_cols] * x).astype(BF).astype(F32)
-                gate = gate_ref[rows, own_cols]
-                sg = sigmoid(gate)
-                sl = gate * sg
+                states = ss_ref[:, own_cols]
+                sl, sg = sl_ref[:, own_cols], sg_ref[:, own_cols]
                 gated = states * sl
                 gain = ggain_ref[0:1, own_cols]
-                upstream = bgrad_ref[rows, own_cols]
+                upstream = up_scratch[:, own_cols]
                 norm = gated * inv
                 branch_ref[rows, own_cols] = (norm * gain).astype(BF)
                 gain_acc[:, own_cols] += rows8(upstream * norm)
@@ -333,15 +355,15 @@
     rate = rates(alog_ref)
     mask = tri_mask(False)
     left = lax.broadcasted_iota(jnp.int32, (BL, BL), 1) < HEADDIM
+    masks = pair_masks()
     low_tri = jnp.where(tri_mask(True), 1.0, 0.0).astype(BF)
     high_tri = jnp.where(mask, 1.0, 0.0).astype(BF)
     wide_pre = pre_ref[0, :, DI:]
-    wide_sg = sigmoid(wide_pre)
-    conv = wide_pre * wide_sg
+    conv, wide_sg = silu_parts(wide_pre)
     inputs_b, inputs_c = conv[:, :DSTATE], conv[:, DSTATE:]
     z = z_ref[0]
     step = softplus(z)
-    cum = prefix(low_tri, step * rate)
+    cum = prefix(low_tri, step * (rate * LOG2E))
     cum_t = cum.T
     lanes = head_lanes(cum.shape)
     scores_t = dot3(inputs_b, inputs_c, NT)
@@ -370,21 +392,20 @@
         cols = slice(quad * 256, (quad + 1) * 256)
         inner, grown, shrink, scaled, xs, steps_wide, slopes = [], [], [], [], [], [], []
         dy = dy_ref[:, cols].astype(F32)
-        for half, pair in enumerate((2 * quad, 2 * quad + 1)):
+        for pair in (2 * quad, 2 * quad + 1):
             kernels, chosen, steps = pair_values(pair, cum, cum_t, step, mask, left, True)
             own = pre_ref[0, :, pair * 128 : (pair + 1) * 128]
-            sg = sigmoid(own)
-            x = own * sg
+            x, sg = silu_parts(own)
             slopes.append(sg + x * (1.0 - sg))
             xd = steps * x
             mh, ml = split2(jnp.concatenate([scores_t * k for k in kernels], axis=1))
-            dyb = pair_blocks(dy[:, half * 128 : (half + 1) * 128])
+            dyb = pair_blocks(dy_ref[:, pair * 128 : (pair + 1) * 128], masks)
             inner.append(dot(mh, dyb) + dot(ml, dyb))
             sh, sl = split2(xd)
             dmix = dot(sh, dyb, NT) + dot(sl, dyb, NT)
             dscores_t = dscores_t + dmix[:, :BL] * kernels[0] + dmix[:, BL:] * kernels[1]
-            grown.append(jnp.exp(chosen))
-            shrink.append(jnp.exp(chosen[BL - 1 : BL, :] - chosen))
+            grown.append(jnp.exp2(chosen))
+            shrink.append(jnp.exp2(chosen[BL - 1 : BL, :] - chosen))
             scaled.append(xd)
             xs.append(x)
             steps_wide.append(steps)
@@ -493,7 +514,7 @@
     )(u, halo, gain, w, cw, cb, dtb, alog, emat)
 
 
-def run_second(pre, z, gate, bgrad, u, enter, wo, skip, ggain, alog, gmat):
+def run_second(pre, z, normed, up, u, enter, wg, wo, skip, ggain, alog, gmat):
     seqs, length, _ = u.shape
     tile = min(256, length)
     steps = length // tile
@@ -507,7 +528,8 @@
         second_kernel,
         grid=grid,
         in_specs=[
-            tok(CONVCH), tok(128), flat(DI), flat(DI), tok(D), per(DSTATE, DI), whole(wo.shape),
+            tok(CONVCH), tok(128), tok(D), flat(D), tok(D), per(DSTATE, DI), whole(wg.shape),
+            whole(wo.shape),
             whole(skip.shape), whole(ggain.shape), whole(alog.shape), whole(gmat.shape),
         ],
         out_specs=[
@@ -527,11 +549,11 @@
         ],
         scratch_shapes=[
             pltpu.VMEM((8, DI), F32), pltpu.VMEM((8, DI), F32), pltpu.VMEM((DSTATE, DI), F32),
-            pltpu.VMEM((8, DI), F32), pltpu.VMEM((BL, DI), F32), pltpu.VMEM((BL, DI), F32),
+            pltpu.VMEM((8, DI), F32), *[pltpu.VMEM((BL, DI), F32)] * 7,
         ],
         compiler_params=pltpu.CompilerParams(**PARAMS),
         name="second",
-    )(pre, z, gate, bgrad, u, enter, wo, skip, ggain, alog, gmat)
+    )(pre, z, normed, up, u, enter, wg, wo, skip, ggain, alog, gmat)
 
 
 def run_third(pre, mixed, z, dy, states, rdot, leave, cw, skip, alog, gmat):
@@ -589,11 +611,6 @@
     )(mgrad, mixed, last8, near, cw)
 
 
-def norm_piece(incoming, norm_gain):
-    inv_rms = lax.rsqrt(jnp.mean(incoming * incoming, axis=-1, keepdims=True) + EPS)
-    return incoming * inv_rms * norm_gain
-
-
 def kron_update(gradient, left_stat, right_stat, left_root, right_root):
     row_tiles, col_tiles = (left_stat.shape[0], left_stat.shape[1])
     row_size, col_size = (left_stat.shape[-1], right_stat.shape[-1])
@@ -608,6 +625,90 @@
     shaped = jnp.einsum("abij,abjk->abik", shaped, right_root, precision=lax.Precision.HIGH)
     update = (-LR * shaped).transpose(0, 2, 1, 3).reshape(gradient.shape)
     return (update, left_new, right_new)
+
+
+def kron_kernel(*refs):
+    grad_ref, left_ref, right_ref, left_root_ref, right_root_ref = refs[:5]
+    update_ref, left_new_ref, right_new_ref = refs[-3:]
+    for r in range(left_ref.shape[0]):
+        rows = slice(r * ROW_BLOCK, (r + 1) * ROW_BLOCK)
+        for c in range(left_ref.shape[1]):
+            cols = slice(c * COL_BLOCK, (c + 1) * COL_BLOCK)
+            grad = grad_ref[rows, cols]
+            left_new_ref[r, c] = 0.5 * left_ref[r, c] + 0.5 * dot3(grad, grad, NT)
+            right_new_ref[r, c] = 0.5 * right_ref[r, c] + 0.5 * dot3(grad.T, grad)
+            shaped = dot3(dot3(left_root_ref[r, c], grad), right_root_ref[r, c])
+            update_ref[rows, cols] = -LR * shaped
+
+
+def kron_tiles(grad, left, right, left_root, right_root, first, step, earlier=None):
+    row_tiles = left.shape[0]
+    rows, cols = grad.shape
+    base = first // step
+    stat = lambda size: pl.BlockSpec(
+        (row_tiles, step, size, size), lambda i: (0, base + i, 0, 0)
+    )
+    wide = step * COL_BLOCK
+    ins = [grad, left, right, left_root, right_root]
+    in_specs = [pl.BlockSpec((rows, wide), lambda i: (0, i))] + [stat(ROW_BLOCK), stat(COL_BLOCK)] * 2
+    aliases = {}
+    if earlier is not None:
+        ins += list(earlier)
+        in_specs += [pl.BlockSpec(memory_space=pl.ANY)] * 3
+        aliases = {5: 0, 6: 1, 7: 2}
+    total = left.shape[1] * COL_BLOCK
+    return pl.pallas_call(
+        kron_kernel,
+        grid=(cols // wide,),
+        in_specs=in_specs,
+        out_specs=[
+            pl.BlockSpec((rows, wide), lambda i: (0, base + i)), stat(ROW_BLOCK), stat(COL_BLOCK),
+        ],
+        out_shape=[
+            jax.ShapeDtypeStruct((rows, total), F32),
+            jax.ShapeDtypeStruct(left.shape, F32),
+            jax.ShapeDtypeStruct(right.shape, F32),
+        ],
+        input_output_aliases=aliases,
+        compiler_params=pltpu.CompilerParams(**PARAMS),
+        name="kron",
+    )(*ins)
+
+
+def back_kernel(
+    ggrad_ref, mgrad_ref, wg_ref, main_ref, u_ref, up_ref, gain_ref, out_ref, gain_grad_ref
+):
+    @pl.when(pl.program_id(0) == 0)
+    def _():
+        gain_grad_ref[...] = jnp.zeros_like(gain_grad_ref)
+
+    grad = dot(ggrad_ref[...], wg_ref[...], NT) + dot(mgrad_ref[...], main_ref[...], NT)
+    u = u_ref[...].astype(F32)
+    inv = lax.rsqrt(jnp.mean(u * u, axis=-1, keepdims=True) + EPS)
+    norm = u * inv
+    gain_grad_ref[...] += rows8(grad * norm)
+    scaled = grad * gain_ref[0:1, :]
+    pull = jnp.mean(scaled * norm, axis=-1, keepdims=True)
+    out_ref[...] = up_ref[...].astype(F32) + inv * (scaled - norm * pull)
+
+
+def run_back(ggrad, mgrad, wg, main, u, up, gain):
+    rows = u.shape[0]
+    tile = min(256, rows)
+    tok = lambda width: pl.BlockSpec((tile, width), lambda i: (i, 0))
+    return pl.pallas_call(
+        back_kernel,
+        grid=(rows // tile,),
+        in_specs=[
+            tok(DI), tok(WIDE), pl.BlockSpec(wg.shape, lambda i: (0, 0)),
+            pl.BlockSpec(main.shape, lambda i: (0, 0)), tok(D), tok(D),
+            pl.BlockSpec(gain.shape, lambda i: (0, 0)),
+        ],
+        out_specs=[tok(D), pl.BlockSpec((8, D), lambda i: (0, 0))],
+        out_shape=[jax.ShapeDtypeStruct((rows, D), F32), jax.ShapeDtypeStruct((8, D), F32)],
+        compiler_params=pltpu.CompilerParams(**PARAMS),
+        name="back",
+    )(ggrad, mgrad, wg, main, u, up, gain)
 
 
 def swapped(v, axis, size, offset):
@@ -903,12 +1004,10 @@
         wg = assemble(idx, (gate_near, gate_got, gate_far, gate_far_got), order)
     normed_rows = normed.reshape(row_count, D)
     upstream = cotangent.reshape(row_count, D)
-    gate_part = dot(normed_rows, wg)
-    branch_grad = dot(upstream, wo, NT)
     (
         block_output, branch, states_grad, gate_grad, states, rdot, local_dstate, row_sums,
     ) = run_second(
-        pre, z, gate_part, branch_grad, block_input, enter, wo, skip_wide, ggain8, alog,
+        pre, z, normed, upstream, block_input, enter, wg, wo, skip_wide, ggain8, alog,
         gmat,
     )
     leave = lax.ppermute(local_dstate, "seq", down)
@@ -934,17 +1033,14 @@
 
     mgrad_rows = mgrad.reshape(row_count, WIDE)
     mixed_local = dot(normed_rows, mgrad_rows, TN)
-    normed_grad = (
-        dot(gate_grad, wg, NT) + dot(mgrad_rows, main, NT)
-    )
-    incoming = block_input.reshape(row_count, D).astype(F32)
-    _, norm_back = jax.vjp(norm_piece, incoming, norm_gain)
-    input_part, norm_gain_grad = norm_back(normed_grad)
-    input_grad = (input_part + upstream.astype(F32)).reshape(block_input.shape)
+    input_grad, gain_rows = run_back(
+        gate_grad, mgrad_rows, wg, main, block_input.reshape(row_count, D), upstream, gain8
+    )
+    input_grad = input_grad.reshape(block_input.shape)
 
     vector_local = jnp.concatenate(
         [
-            norm_gain_grad,
+            gain_rows.sum(0),
             row_sums[0],
             conv_weight_grad.reshape(-1),
             conv_bias_grad,
@@ -954,8 +1050,8 @@
         ]
     )
     if direct:
-        late, late_own = chip_sum(idx, [core_exchange(mixed_local, idx[2])])
-        vector_local, early, late = lax.optimization_barrier((vector_local, early, late))
+        mixed_pair = core_exchange(mixed_local, idx[2])
+        late, late_own = chip_sum(idx, [mixed_pair])
         late = lax.all_to_all(late, ("z", "x"), split_axis=0, concat_axis=0, tiled=True)
         early_own = owner_sum(idx, early_own, early)
         early_own = early_own + swapped(early_own, "seq", 2, 1)
@@ -978,14 +1074,16 @@
     in_grad = jnp.concatenate([gate_sum, mixed_sum[:, :CONVCH]], axis=1)
     dt_grad = mixed_sum[:, CONVCH : CONVCH + HEADS]
 
-    in_update, in_left_new, in_right_new = kron_update(
-        in_grad, in_left, in_right, in_left_root, in_right_root
+    gate_tiles = kron_tiles(gate_sum, in_left, in_right, in_left_root, in_right_root, 0, 2)
+    in_update, in_left_new, in_right_new = kron_tiles(
+        mixed_sum[:, :CONVCH], in_left, in_right, in_left_root, in_right_root, DI // COL_BLOCK, 2,
+        gate_tiles,
     )
     dt_update, dt_left_wide, dt_right_wide = kron_update(
         dt_grad, dt_left[:, None], dt_right[:, None], dt_left_root[:, None], dt_right_root[:, None]
     )
-    out_update, out_left_new, out_right_new = kron_update(
-        out_grad, out_left, out_right, out_left_root, out_right_root
+    out_update, out_left_new, out_right_new = kron_tiles(
+        out_grad, out_left, out_right, out_left_root, out_right_root, 0, 1
     )
     vector_moment_new = 0.5 * vector_moment + 0.5 * vector_grad * vector_grad
     vector_update = -LR_VEC * vector_grad * lax.rsqrt(vector_moment_new)

time: 406 us -> 365 us (0.90); the launches traced: 399 us -> 363 us
  matrix products: 62.3 us -> 16.9 us
  Pallas kernels: 125 us -> 168 us
  local copies, waits for them, and re-layouts: 47.3 us -> 32 us
  other arithmetic: 24.3 us -> 10.8 us
  waiting for transfers between devices: 80.4 us -> 76.2 us
    pallas_call x0 -> x4, Pallas kernels: none -> 35 us  [the longest x3 23.2 us: kron_tiles(): pl.pallas_call(kron_kernel, grid=(cols // wide,), in_specs=in_specs, out_...]
    dot_general x7 -> x3, matrix products: 40.2 us -> 15 us  [dot(): return lax.dot_general(a, b, dims, preferred_element_type=F32)]
    all_to_all x1, waiting for transfers between devices: 18.5 us -> 0.01 us  [body(): lax.all_to_all(early, ('z', 'x'), split_axis=0, concat_axis=0, tiled=True)]
    all_gather x1, waiting for transfers between devices: 0.01 us -> 15.1 us  [body(): lax.all_gather(jnp.concatenate([in_low[:, DI:], dt_low], axis=1), AXES, a...]
    ppermute x19, waiting for transfers between devices: 40.3 us -> 27.4 us  [swapped(): lax.ppermute(v, axis, [(i, (i + offset) % size) for i in range(size)])]
    dot_general x3 -> x1, matrix products: 12.2 us -> 0.82 us  [kron_update(): jnp.einsum('abji,abjk->abik', grad_tiles, grad_tiles, precision=lax.Preci...]
    ppermute x5, waiting for transfers between devices: 10.5 us -> 17.8 us  [xor_sum(): v = v + lax.ppermute(v, axis, [(i, i ^ bit) for i in range(size)])]
    unnamed x81 -> x75, local copies, waits for them, and re-layouts: 22.5 us -> 16.4 us
  transfers between devices with their start and end apart: 31 -> 31, of which waited for: 11 -> 16; matrix products, arithmetic and copies ran while one was open for 21% -> 9% of each run, Pallas kernels for 11% -> 32%
where the time goes in v5:
time: 365 us; the launch traced here: 363 us
  Pallas kernels  168 us (46%)
  waiting for transfers between devices  76.2 us (21%)
  starting transfers between devices  44.2 us (12%)
  local copies, waits for them, and re-layouts  32 us (9%)
  matrix products  16.9 us (5%)
  between operations  14.6 us (4%)
  other arithmetic  10.8 us (3%)
    pallas_call x1, Pallas kernels, run_second(): pl.pallas_call(second_kernel, grid=grid, in_specs=[tok(CONVCH), tok(128),...  44.6 us
    pallas_call x1, Pallas kernels, run_third(): pl.pallas_call(third_kernel, grid=grid, in_specs=[tok(CONVCH), tok(CONVCH...  40.5 us
    ppermute x19, waiting for transfers between devices, swapped(): lax.ppermute(v, axis, [(i, (i + offset) % size) for i in range(size)])  27.4 us
    pallas_call x3, Pallas kernels, kron_tiles(): pl.pallas_call(kron_kernel, grid=(cols // wide,), in_specs=in_specs, out_...  23.2 us
    pallas_call x1, Pallas kernels, run_first(): pl.pallas_call(first_kernel, grid=grid, in_specs=[tok(D), per(8, D), whol...  21.5 us
    ppermute x19, starting transfers between devices, swapped(): lax.ppermute(v, axis, [(i, (i + offset) % size) for i in range(size)])  18.6 us
    ppermute x5, waiting for transfers between devices, xor_sum(): v = v + lax.ppermute(v, axis, [(i, i ^ bit) for i in range(size)])  17.8 us
    unnamed x75, local copies, waits for them, and re-layouts  16.4 us
  transfers between devices with their start and end apart: 31, of which 16 were waited for; matrix products, arithmetic and copies ran while one was open for 9% of the time, Pallas kernels for 32%

profile of v5, /device:TPU:0, one launch (start us, length us, event | category | flops | bytes accessed | tf_op | source)
XLA Modules:
  0.0 363.2 jit_solution(7181337552858096222)
XLA Ops:
  10.0 5.1 %collective-permute-start.3 = (bf16[24,1536]{1,0:T(8,128)(2,1)S(1)}, bf16[24,1536]{1,0:T(8,128)(2,1)S(1)}, u32[]{:S(2)}, u32[]{:S(2)}) collective-permute-start(bf16[24,1536]{1,0:T(8,128)(2,1)S(1)} %fusion.34), channel_id=1, source_target_pairs={{0,24},{8,0},{16,8},{24,16},{1,25},{9,1},{17,9},{25,17},{2,26},{10... | collective-permute-start | bytes 221192 | tf_op jit(solution)/shard_map/ppermute | solution.py:715
  17.2 2.9 collective-permute-start.7
  22.8 3.4 collective-permute-start
  26.3 1.6 collective-permute-start.4
  27.9 5.1 %collective-permute-done.6 = bf16[48,768]{1,0:T(8,128)(2,1)S(1)} collective-permute-done((bf16[48,768]{1,0:T(8,128)(2,1)S(1)}, bf16[48,768]{1,0:T(8,128)(2,1)S(1)}, u32[]{:S(2)}, u32[]{:S(2)}) %collective-permute-start.6) | collective-permute-done | bytes 73760 | tf_op jit(solution)/shard_map/ppermute | solution.py:715
  33.0 1.9 collective-permute-start.8
  35.9 1.6 collective-permute-start.10
  37.5 4.3 %collective-permute-done.8 = bf16[4,48,768]{2,1,0:T(8,128)(2,1)S(1)} collective-permute-done((bf16[4,48,768]{2,1,0:T(8,128)(2,1)S(1)}, bf16[4,48,768]{2,1,0:T(8,128)(2,1)S(1)}, u32[]{:S(2)}, u32[]{:S(2)}) %collective-permute-start.8) | collective-permute-done | bytes 294944 | tf_op jit(solution)/shard_map/ppermute | solution.py:715
  41.8 1.5 collective-permute-start.13
  45.1 15.1 %all-gather.2.cloned.1.call-done.w_ref.main_ref = bf16[768,1920]{1,0:T(8,128)(2,1)} async-done(((bf16[48,1920]{1,0:T(8,128)(2,1)}), bf16[768,1920]{1,0:T(8,128)(2,1)}) %all-gather.2.cloned.1.call-update) | async-done | bytes 2949136 | tf_op jit(solution)/shard_map/all_gather | solution.py:956
  64.5 21.5 %first.1 = (bf16[1,1024,768]{2,1,0:T(8,128)(2,1)}, bf16[1,1024,1792]{2,1,0:T(8,128)(2,1)}, f32[1,1024,1792]{2,1,0:T(8,128)}, f32[1,1024,128]{2,1,0:T(8,128)}, f3...) custom-call(bf16[1,1024,768]{2,1,0:T(8,128)(2,1)} %u_ref.3, bf16[1,8,768]{2,1,0:T(8,128)(2,1)} %copy-done.28, ...), custom_call_target="tpu_custom_call" | custom-call | tf_op jit(solution)/shard_map/first/pallas_call | solution.py:493
  86.0 4.3 %collective-permute-start.9 = (f32[1,128,1536]{2,1,0:T(8,128)}, f32[1,128,1536]{2,1,0:T(8,128)}, u32[]{:S(2)}, u32[]{:S(2)}) collective-permute-start(f32[1,128,1536]{2,1,0:T(8,128)} %get-tuple-element.59), channel_id=1, source_target_pairs={{0,1},{2,3},{4,5},{6,7},{8,9},{10,11},{12,13},{14,15},{16,17},{18,... | collective-permute-start | bytes 2359304 | tf_op jit(solution)/shard_map/ppermute | solution.py:996
  93.3 3.8 %assemble.2 = bf16[32,24,1536]{2,1,0:T(8,128)(2,1)} custom-call(s32[4]{0:T(128)} %pad_add_fusion.idx, bf16[2,4,24,1536]{3,2,1,0:T(8,128)(2,1)} %copy-done.9, bf16[2,4,24,1536]{3,2,1,0:T(8,128)(2,1)} %copy-done.15, bf16[2,4,24,1536]{3,2,1,0:T(8,128)(2,1)} %copy-done.17, bf16[2,4,24,1536]{3,2,1,0:T(8,128)(2,1)} %collective-permute-done.12.refs_3_), custom_call_target="tpu_custom_call" | custom-call | tf_op jit(solution)/shard_map/assemble/pallas_call | solution.py:899
  97.2 3.9 %assemble.3 = bf16[32,48,768]{2,1,0:T(8,128)(2,1)} custom-call(s32[4]{0:T(128)} %pad_add_fusion.idx, bf16[2,4,48,768]{3,2,1,0:T(8,128)(2,1)} %copy-done.10, bf16[2,4,48,768]{3,2,1,0:T(8,128)(2,1)} %copy-done.16, bf16[2,4,48,768]{3,2,1,0:T(8,128)(2,1)} %collective-permute-done.14.refs_2_, bf16[2,4,48,768]{3,2,1,0:T(8,128)(2,1)} %collective-permute-done.15.refs_3_), custom_call_target="tpu_custom_call" | custom-call | tf_op jit(solution)/shard_map/assemble/pallas_call | solution.py:899
  101.1 1.7 copy.70
  102.8 4.1 %collective-permute-done.9.enter_ref = f32[1,128,1536]{2,1,0:T(8,128)} collective-permute-done((f32[1,128,1536]{2,1,0:T(8,128)}, f32[1,128,1536]{2,1,0:T(8,128)}, u32[]{:S(2)}, u32[]{:S(2)}) %collective-permute-start.9) | collective-permute-done | bytes 786464 | tf_op jit(solution)/shard_map/ppermute | solution.py:996
  106.9 44.6 %second.1 = (bf16[1,1024,768]{2,1,0:T(8,128)(2,1)}, bf16[1024,1536]{1,0:T(8,128)(2,1)}, bf16[1024,1536]{1,0:T(8,128)(2,1)}, bf16[1024,1536]{1,0:T(8,128)(2,1)}, ...) custom-call(f32[1,1024,1792]{2,1,0:T(8,128)} %get-tuple-element.56.pre_ref, ...), custom_call_target="tpu_custom_call" | custom-call | tf_op jit(solution)/shard_map/second/pallas_call | solution.py:527
  151.5 4.5 %fusion.2.refs_0_ = f32[8,2,48,1536]{3,2,1,0:T(8,128)S(1)} fusion(bf16[8,2,48,1024]{3,2,1,0:T(8,128)(2,1)S(1)} %bitcast.96, bf16[1024,1536]{1,0:T(8,128)(2,1)} %get-tuple-element.61.ggrad_ref), kind=kOutput, calls=%fused_computation.2 | convolution fusion | flops 2415919104 | bytes 9437184 | tf_op jit(solution)/shard_map/dot_general | solution.py:40
  156.0 2.1 copy-done.2
  158.1 1.6 dynamic-slice_bitcast_fusion.2
  159.7 4.8 %copy.71 = bf16[1536,1024]{1,0:T(8,128)(2,1)} copy(bf16[1536,1024]{0,1:T(8,128)(2,1)} %bitcast.93) | data formatting | bytes 6291456 | tf_op jit(solution)/shard_map/dot_general | solution.py:40
  164.5 4.5 %fusion.4.refs_2_ = f32[8,2,96,768]{3,2,1,0:T(8,128)S(1)} fusion(bf16[8,2,96,1024]{3,2,1,0:T(8,128)(2,1)} %bitcast.94, bf16[1,1024,768]{2,1,0:T(8,128)(2,1)S(1)} %copy-done.5), kind=kOutput, calls=%fused_computation.7 | convolution fusion | flops 2415919104 | bytes 9437184 | tf_op jit(solution)/shard_map/dot_general | solution.py:40
  169.1 2.2 copy-done.3
  173.3 2.9 collective-permute-done.17.refs_3_
  177.5 6.2 %chip_sum.2 = (bf16[8,96,1536]{2,1,0:T(8,128)(2,1)}, f32[96,1536]{1,0:T(8,128)}) custom-call(s32[4]{0:T(128)} %pad_add_fusion.idx, f32[8,2,48,1536]{3,2,1,0:T(8,128)} %copy-done.2, f32[8,48,1536]{2,1,0:T(8,128)} %collective-permute-done.16.refs_1_, f32[8,2,96,768]{3,2,1,0:T(8,128)} %copy-done.3, f32[8,96,768]{2,1,0:T(8,128)} %copy-done.11), custom_call_target="tpu_custom_call" | custom-call | tf_op jit(solution)/shard_map/chip_sum/pallas_call | solution.py:822
  183.7 3.8 %all-to-all-start = ((bf16[8,96,1536]{2,1,0:T(8,128)(2,1)}), bf16[8,96,1536]{2,1,0:T(8,128)(2,1)S(1)}, u32[]{:S(2)}, u32[]{:S(2)}) async-start(bf16[8,96,1536]{2,1,0:T(8,128)(2,1)} %get-tuple-element.76), calls=%async_computation | async-start | bytes 4718592 | tf_op jit(solution)/shard_map/all_to_all | solution.py:1024
  187.5 6.1 %collective-permute-done.18.leave_ref = f32[1,128,1536]{2,1,0:T(8,128)S(1)} collective-permute-done((f32[1,128,1536]{2,1,0:T(8,128)}, f32[1,128,1536]{2,1,0:T(8,128)S(1)}, u32[]{:S(2)}, u32[]{:S(2)}) %collective-permute-start.18) | collective-permute-done | bytes 786464 | tf_op jit(solution)/shard_map/ppermute | solution.py:1013
  194.5 40.5 %third.1 = (bf16[1,1024,1920]{2,1,0:T(8,128)(2,1)}, f32[1,8,1792]{2,1,0:T(8,128)}, f32[1,8,1792]{2,1,0:T(8,128)}, f32[8,1792]{1,0:T(8,128)}) custom-call(f32[1,1024,1792]{2,1,0:T(8,128)} %get-tuple-element.56.pre_ref, bf16[1,1024,1792]{2,1,0:T(8,128)(2,1)} %get-tuple-element.62.mixed_ref, f32[1,1024,128]{2,1,0:T(8,128)} %get-tuple-element.57.z_ref, ...), custom_call_target="tpu_custom_call" | custom-call | tf_op jit(solution)/shard_map/third/pallas_call | solution.py:565
  236.3 5.0 %collective-permute-done.19.near_ref = f32[1,8,1792]{2,1,0:T(8,128)S(1)} collective-permute-done((f32[1,8,1792]{2,1,0:T(8,128)}, f32[1,8,1792]{2,1,0:T(8,128)S(1)}, u32[]{:S(2)}, u32[]{:S(2)}) %collective-permute-start.19) | collective-permute-done | bytes 57376 | tf_op jit(solution)/shard_map/ppermute | solution.py:1029
  241.9 1.6 patch.1
  243.5 6.0 %fusion.refs_0_ = f32[8,2,48,1920]{3,2,1,0:T(8,128)S(1)} fusion(bf16[8,2,48,1024]{3,2,1,0:T(8,128)(2,1)} %bitcast.95, bf16[1,1024,1920]{2,1,0:T(8,128)(2,1)} %get-tuple-element.73), kind=kOutput, calls=%fused_computation | convolution fusion | flops 3019898880 | bytes 11403264 | tf_op jit(solution)/shard_map/dot_general | solution.py:40
  249.8 2.4 copy-done.1
  252.1 5.5 %collective-permute-done.21.refs_1_ = f32[8,48,1920]{2,1,0:T(8,128)} collective-permute-done((f32[8,48,1920]{2,1,0:T(8,128)S(1)}, f32[8,48,1920]{2,1,0:T(8,128)}, u32[]{:S(2)}, u32[]{:S(2)}) %collective-permute-start.21) | collective-permute-done | bytes 2949152 | tf_op jit(solution)/shard_map/ppermute | solution.py:715
  257.6 4.5 %chip_sum.3 = (bf16[8,48,1920]{2,1,0:T(8,128)(2,1)}, f32[48,1920]{1,0:T(8,128)}) custom-call(s32[4]{0:T(128)} %pad_add_fusion.idx, f32[8,2,48,1920]{3,2,1,0:T(8,128)} %copy-done.1, f32[8,48,1920]{2,1,0:T(8,128)} %collective-permute-done.21.refs_1_), custom_call_target="tpu_custom_call" | custom-call | tf_op jit(solution)/shard_map/chip_sum/pallas_call | solution.py:822
  262.2 4.6 %all-to-all-start.1 = ((bf16[8,48,1920]{2,1,0:T(8,128)(2,1)}), bf16[8,48,1920]{2,1,0:T(8,128)(2,1)}, u32[]{:S(2)}, u32[]{:S(2)}) async-start(bf16[8,48,1920]{2,1,0:T(8,128)(2,1)} %get-tuple-element.78), calls=%async_computation.1 | async-start | bytes 2949120 | tf_op jit(solution)/shard_map/all_to_all | solution.py:1055
  267.9 11.9 %back.1 = (f32[1024,768]{1,0:T(8,128)}, f32[8,768]{1,0:T(8,128)}) custom-call(bf16[1024,1536]{1,0:T(8,128)(2,1)} %get-tuple-element.61.ggrad_ref, bf16[1024,1920]{1,0:T(8,128)(2,1)} %bitcast.87, bf16[768,1536]{1,0:T(8,128)(2,1)} %bitcast.86, bf16[768,1920]{1,0:T(8,128)(2,1)} %all-gather.2.cloned.1.call-done.w_ref.main_ref, bf16[1024,768]{1,0:T(8,128)(2,1)} %bitcast.88, ...), custom_call_target="tpu_custom_call" | custom-call | tf_op jit(solution)/shard_map/back/pallas_call | solution.py:699
  281.0 3.4 owner_sum.2
  284.5 2.1 collective-permute-start.24
  286.5 14.8 %collective-permute-done.24 = f32[96,128]{1,0:T(8,128)S(1)} collective-permute-done((f32[96,128]{1,0:T(8,128)S(1)}, f32[96,128]{1,0:T(8,128)S(1)}, u32[]{:S(2)}, u32[]{:S(2)}) %collective-permute-start.24) | collective-permute-done | bytes 49184 | tf_op jit(solution)/shard_map/ppermute | solution.py:779
  302.0 1.5 collective-permute-start.25
  307.2 3.0 collective-permute-done.26
  310.2 2.0 collective-permute-start.27
  313.8 7.3 %kron.3 = (f32[48,3328]{1,0:T(8,128)}, f32[2,26,24,24]{3,2,1,0:T(8,128)}, f32[2,26,128,128]{3,2,1,0:T(8,128)}) custom-call(f32[48,1536]{1,0:T(8,128)} %slice.63.refs_0_, f32[2,26,24,24]{3,2,1,0:T(8,128)} %copy.74.refs_1_, f32[2,26,128,128]{3,2,1,0:T(8,128)} %refs_2_.4, f32[2,26,24,24]{3,2,1,0:T(8,128)} %copy.75.refs_3_, f32[2,26,128,128]{3,2,1,0:T(8,128)} %refs_4_.4), custom_call_target="tpu_custom_call" | custom-call | tf_op jit(solution)/shard_map/kron/pallas_call | solution.py:660
  321.1 7.3 %kron.5 = (f32[96,768]{1,0:T(8,128)}, f32[4,6,24,24]{3,2,1,0:T(8,128)}, f32[4,6,128,128]{3,2,1,0:T(8,128)}) custom-call(f32[96,768]{1,0:T(8,128)} %pad_maximum_fusion.5.refs_0_, f32[4,6,24,24]{3,2,1,0:T(8,128)} %refs_1_.3, f32[4,6,128,128]{3,2,1,0:T(8,128)} %refs_2_.5, f32[4,6,24,24]{3,2,1,0:T(8,128)} %refs_3_.3, f32[4,6,128,128]{3,2,1,0:T(8,128)} %refs_4_.5), custom_call_target="tpu_custom_call" | custom-call | tf_op jit(solution)/shard_map/kron/pallas_call | solution.py:660
  328.4 3.3 owner_sum.3
  332.8 7.6 %collective-permute-done.22 = f32[48,1920]{1,0:T(8,128)S(1)} collective-permute-done((f32[48,1920]{1,0:T(8,128)}, f32[48,1920]{1,0:T(8,128)S(1)}, u32[]{:S(2)}, u32[]{:S(2)}) %collective-permute-start.22) | collective-permute-done | bytes 368672 | tf_op jit(solution)/shard_map/ppermute | solution.py:715
  344.1 8.5 %kron.4 = (f32[48,3328]{1,0:T(8,128)}, f32[2,26,24,24]{3,2,1,0:T(8,128)}, f32[2,26,128,128]{3,2,1,0:T(8,128)}) custom-call(f32[48,1792]{1,0:T(8,128)} %copy-done.7, f32[2,26,24,24]{3,2,1,0:T(8,128)} %copy.74.refs_1_, f32[2,26,128,128]{3,2,1,0:T(8,128)} %refs_2_.4, ...), custom_call_target="tpu_custom_call", output_to_operand_aliasing={{0}: (5, {}), {1}: (6, {}), {2}: (7, {})} | custom-call | tf_op jit(solution)/shard_map/kron/pallas_call | solution.py:660
  352.5 2.2 copy.81
  (174 shorter events, 38.6 us)
Async XLA Ops:
  7.2 335.9 %copy-start = (f32[2,24,24]{2,1,0:T(8,128)S(1)}, f32[2,24,24]{2,1,0:T(8,128)}, u32[]{:S(2)}) copy-start(f32[2,24,24]{2,1,0:T(8,128)} %param.43) | copy-start | bytes 13828
  7.2 53.0 %all-gather.2.cloned.1.call-start = ((), (), s32[]{:S(2)}) async-start(), calls=%async_computation.2 | async-start | bytes 3133440 | tf_op jit(solution)/shard_map/all_gather | solution.py:956
  10.0 34.4 %copy-start.34 = (f32[24]{0:T(128)S(1)}, f32[24]{0:T(128)}, u32[]{:S(2)}) copy-start(f32[24]{0:T(128)} %param.34) | copy-start | bytes 292
  10.0 34.4 %copy-start.32 = (f32[24]{0:T(128)S(1)}, f32[24]{0:T(128)}, u32[]{:S(2)}) copy-start(f32[24]{0:T(128)} %param.35) | copy-start | bytes 292
  10.0 34.5 %copy-start.33 = (f32[24]{0:T(128)S(1)}, f32[24]{0:T(128)}, u32[]{:S(2)}) copy-start(f32[24]{0:T(128)} %param.33) | copy-start | bytes 292
  10.0 34.5 %copy-start.22 = (f32[4,1792]{1,0:T(4,128)S(1)}, f32[4,1792]{1,0:T(4,128)}, u32[]{:S(2)}) copy-start(f32[4,1792]{1,0:T(4,128)} %param.31) | copy-start | bytes 86020
  10.0 50.2 %copy-start.31 = (f32[768]{0:T(1024)S(1)}, f32[768]{0:T(1024)}, u32[]{:S(2)}) copy-start(f32[768]{0:T(1024)} %param.30) | copy-start | bytes 9220
  10.0 52.6 %copy-start.30 = (f32[1792]{0:T(1024)S(1)}, f32[1792]{0:T(1024)}, u32[]{:S(2)}) copy-start(f32[1792]{0:T(1024)} %param.32) | copy-start | bytes 21508
  10.0 11.9 %collective-permute-start.3 = (bf16[24,1536]{1,0:T(8,128)(2,1)S(1)}, bf16[24,1536]{1,0:T(8,128)(2,1)S(1)}, u32[]{:S(2)}, u32[]{:S(2)}) collective-permute-start(bf16[24,1536]{1,0:T(8,128)(2,1)S(1)} %fusion.34), channel_id=1, source_target_pairs={{0,24},{8,0},{16,8},{24,16},{1,25},{9,1},{17,9},{25,17},{2,26},{10... | collective-permute-start | bytes 221192 | tf_op jit(solution)/shard_map/ppermute | solution.py:715
  15.2 7.7 %collective-permute-start.2 = (bf16[24,1536]{1,0:T(8,128)(2,1)S(1)}, bf16[24,1536]{1,0:T(8,128)(2,1)S(1)}, u32[]{:S(2)}, u32[]{:S(2)}) collective-permute-start(bf16[24,1536]{1,0:T(8,128)(2,1)S(1)} %fusion.34), channel_id=1, source_target_pairs={{0,16},{8,24},{16,0},{24,8},{1,17},{9,25},{17,1},{25,9},{2,18},{10... | collective-permute-start | bytes 221192 | tf_op jit(solution)/shard_map/ppermute | solution.py:715
  15.2 11.1 %collective-permute-start.1 = (bf16[24,1536]{1,0:T(8,128)(2,1)S(1)}, bf16[24,1536]{1,0:T(8,128)(2,1)S(1)}, u32[]{:S(2)}, u32[]{:S(2)}) collective-permute-start(bf16[24,1536]{1,0:T(8,128)(2,1)S(1)} %fusion.34), channel_id=1, source_target_pairs={{0,8},{8,16},{16,24},{24,0},{1,9},{9,17},{17,25},{25,1},{2,10},{10... | collective-permute-start | bytes 221192 | tf_op jit(solution)/shard_map/ppermute | solution.py:715
  17.2 46.1 %copy-start.29 = (f32[1536]{0:T(1024)S(1)}, f32[1536]{0:T(1024)}, u32[]{:S(2)}) copy-start(f32[1536]{0:T(1024)} %param.36) | copy-start | bytes 18436
  17.2 10.7 %collective-permute-start.7 = (bf16[48,768]{1,0:T(8,128)(2,1)S(1)}, bf16[48,768]{1,0:T(8,128)(2,1)S(1)}, u32[]{:S(2)}, u32[]{:S(2)}) collective-permute-start(bf16[48,768]{1,0:T(8,128)(2,1)S(1)} %fusion.33), channel_id=1, source_target_pairs={{0,24},{8,0},{16,8},{24,16},{1,25},{9,1},{17,9},{25,17},{2,26},{10... | collective-permute-start | bytes 221192 | tf_op jit(solution)/shard_map/ppermute | solution.py:715
  20.1 12.9 %collective-permute-start.6 = (bf16[48,768]{1,0:T(8,128)(2,1)S(1)}, bf16[48,768]{1,0:T(8,128)(2,1)S(1)}, u32[]{:S(2)}, u32[]{:S(2)}) collective-permute-start(bf16[48,768]{1,0:T(8,128)(2,1)S(1)} %fusion.33), channel_id=1, source_target_pairs={{0,16},{8,24},{16,0},{24,8},{1,17},{9,25},{17,1},{25,9},{2,18},{10... | collective-permute-start | bytes 221192 | tf_op jit(solution)/shard_map/ppermute | solution.py:715
  22.0 11.0 %collective-permute-start.5 = (bf16[48,768]{1,0:T(8,128)(2,1)S(1)}, bf16[48,768]{1,0:T(8,128)(2,1)S(1)}, u32[]{:S(2)}, u32[]{:S(2)}) collective-permute-start(bf16[48,768]{1,0:T(8,128)(2,1)S(1)} %fusion.33), channel_id=1, source_target_pairs={{0,8},{8,16},{16,24},{24,0},{1,9},{9,17},{17,25},{25,1},{2,10},{10... | collective-permute-start | bytes 221192 | tf_op jit(solution)/shard_map/ppermute | solution.py:715
  22.8 41.1 %collective-permute-start = (bf16[1,8,768]{2,1,0:T(8,128)(2,1)S(1)}, bf16[1,8,768]{2,1,0:T(8,128)(2,1)S(1)}, u32[]{:S(2)}, u32[]{:S(2)}) collective-permute-start(bf16[1,8,768]{2,1,0:T(8,128)(2,1)S(1)} %slice.46), channel_id=1, source_target_pairs={{0,1},{2,3},{4,5},{6,7},{8,9},{10,11},{12,13},{14,15},{16,17},{18,... | collective-permute-start | bytes 36872 | tf_op jit(solution)/shard_map/ppermute | solution.py:990
  26.3 9.5 %collective-permute-start.4 = (bf16[4,24,1536]{2,1,0:T(8,128)(2,1)S(1)}, bf16[4,24,1536]{2,1,0:T(8,128)(2,1)S(1)}, u32[]{:S(2)}, u32[]{:S(2)}) collective-permute-start(bf16[4,24,1536]{2,1,0:T(8,128)(2,1)S(1)} %get-tuple-element.154), channel_id=1, source_target_pairs={{0,4},{4,0},{1,5},{5,1},{2,6},{6,2},{3,7},{7,3},{8,12},{12,8},{9,1... | collective-permute-start | bytes 884744 | tf_op jit(solution)/shard_map/ppermute | solution.py:715
  33.0 8.8 %collective-permute-start.8 = (bf16[4,48,768]{2,1,0:T(8,128)(2,1)S(1)}, bf16[4,48,768]{2,1,0:T(8,128)(2,1)S(1)}, u32[]{:S(2)}, u32[]{:S(2)}) collective-permute-start(bf16[4,48,768]{2,1,0:T(8,128)(2,1)S(1)} %get-tuple-element.152), channel_id=1, source_target_pairs={{0,4},{4,0},{1,5},{5,1},{2,6},{6,2},{3,7},{7,3},{8,12},{12,8},{9,1... | collective-permute-start | bytes 884744 | tf_op jit(solution)/shard_map/ppermute | solution.py:715
  35.9 54.4 %copy-start.9 = (bf16[2,4,24,1536]{3,2,1,0:T(8,128)(2,1)}, bf16[2,4,24,1536]{3,2,1,0:T(8,128)(2,1)S(1)}, u32[]{:S(2)}) copy-start(bf16[2,4,24,1536]{3,2,1,0:T(8,128)(2,1)S(1)} %pad_maximum_fusion.1.refs_0_) | copy-start | bytes 1769476
  35.9 54.4 %collective-permute-start.10 = (bf16[2,4,24,1536]{3,2,1,0:T(8,128)(2,1)S(1)}, bf16[2,4,24,1536]{3,2,1,0:T(8,128)(2,1)S(1)}, u32[]{:S(2)}, u32[]{:S(2)}) collective-permute-start(bf16[2,4,24,1536]{3,2,1,0:T(8,128)(2,1)S(1)} %pad_maximum_fusion.1.refs_0_), channel_id=1, source_target_pairs={{0,1},{1,0},{2,3},{3,2},{4,5},{5,4},{6,7},{7,6},{8,9},{9,8},{10,11... | collective-permute-start | bytes 1769480 | tf_op jit(solution)/shard_map/ppermute | solution.py:715
  41.8 55.3 %copy-start.10 = (bf16[2,4,48,768]{3,2,1,0:T(8,128)(2,1)}, bf16[2,4,48,768]{3,2,1,0:T(8,128)(2,1)S(1)}, u32[]{:S(2)}) copy-start(bf16[2,4,48,768]{3,2,1,0:T(8,128)(2,1)S(1)} %pad_maximum_fusion.2.refs_0_) | copy-start | bytes 1769476
  41.8 49.1 %collective-permute-start.13 = (bf16[2,4,48,768]{3,2,1,0:T(8,128)(2,1)S(1)}, bf16[2,4,48,768]{3,2,1,0:T(8,128)(2,1)S(1)}, u32[]{:S(2)}, u32[]{:S(2)}) collective-permute-start(bf16[2,4,48,768]{3,2,1,0:T(8,128)(2,1)S(1)} %pad_maximum_fusion.2.refs_0_), channel_id=1, source_target_pairs={{0,1},{1,0},{2,3},{3,2},{4,5},{5,4},{6,7},{7,6},{8,9},{9,8},{10,11... | collective-permute-start | bytes 1769480 | tf_op jit(solution)/shard_map/ppermute | solution.py:715
  86.0 20.9 %collective-permute-start.9 = (f32[1,128,1536]{2,1,0:T(8,128)}, f32[1,128,1536]{2,1,0:T(8,128)}, u32[]{:S(2)}, u32[]{:S(2)}) collective-permute-start(f32[1,128,1536]{2,1,0:T(8,128)} %get-tuple-element.59), channel_id=1, source_target_pairs={{0,1},{2,3},{4,5},{6,7},{8,9},{10,11},{12,13},{14,15},{16,17},{18,... | collective-permute-start | bytes 2359304 | tf_op jit(solution)/shard_map/ppermute | solution.py:996
  90.3 2.0 collective-permute-start.11
  90.3 3.0 collective-permute-start.12
  90.8 6.3 %collective-permute-start.14 = (bf16[2,4,48,768]{3,2,1,0:T(8,128)(2,1)S(1)}, bf16[2,4,48,768]{3,2,1,0:T(8,128)(2,1)}, u32[]{:S(2)}, u32[]{:S(2)}) collective-permute-start(bf16[2,4,48,768]{3,2,1,0:T(8,128)(2,1)S(1)} %pad_maximum_fusion.2.refs_0_), channel_id=1, source_target_pairs={{0,2},{2,0},{1,3},{3,1},{4,6},{6,4},{5,7},{7,5},{8,10},{10,8},{9,1... | collective-permute-start | bytes 1769480 | tf_op jit(solution)/shard_map/ppermute | solution.py:715
  90.9 6.2 %collective-permute-start.15 = (bf16[2,4,48,768]{3,2,1,0:T(8,128)(2,1)S(1)}, bf16[2,4,48,768]{3,2,1,0:T(8,128)(2,1)}, u32[]{:S(2)}, u32[]{:S(2)}) collective-permute-start(bf16[2,4,48,768]{3,2,1,0:T(8,128)(2,1)S(1)} %collective-permute-done.13.refs_1_), channel_id=1, source_target_pairs={{0,2},{2,0},{1,3},{3,1},{4,6},{6,4},{5,7},{7,5},{8,10},{10,8},{9,1... | collective-permute-start | bytes 1769480 | tf_op jit(solution)/shard_map/ppermute | solution.py:715
  106.9 44.6 %copy-start.13 = (bf16[768,1024]{1,0:T(8,128)(2,1)S(1)}, bf16[768,1024]{1,0:T(8,128)(2,1)}, u32[]{:S(2)}) copy-start(bf16[768,1024]{1,0:T(8,128)(2,1)} %copy.70) | copy-start | bytes 4718596
  159.7 13.5 %collective-permute-start.16 = (f32[8,48,1536]{2,1,0:T(8,128)}, f32[8,48,1536]{2,1,0:T(8,128)}, u32[]{:S(2)}, u32[]{:S(2)}) collective-permute-start(f32[8,48,1536]{2,1,0:T(8,128)} %dynamic-slice_bitcast_fusion.2), channel_id=1, source_target_pairs={{0,2},{2,0},{1,3},{3,1},{4,6},{6,4},{5,7},{7,5},{8,10},{10,8},{9,1... | collective-permute-start | bytes 7077896 | tf_op jit(solution)/shard_map/ppermute | solution.py:715
  171.4 4.7 %collective-permute-start.17 = (f32[8,96,768]{2,1,0:T(8,128)S(1)}, f32[8,96,768]{2,1,0:T(8,128)S(1)}, u32[]{:S(2)}, u32[]{:S(2)}) collective-permute-start(f32[8,96,768]{2,1,0:T(8,128)S(1)} %dynamic-slice_bitcast_fusion.1), channel_id=1, source_target_pairs={{0,2},{2,0},{1,3},{3,1},{4,6},{6,4},{5,7},{7,5},{8,10},{10,8},{9,1... | collective-permute-start | bytes 7077896 | tf_op jit(solution)/shard_map/ppermute | solution.py:715
  172.0 21.7 %collective-permute-start.18 = (f32[1,128,1536]{2,1,0:T(8,128)}, f32[1,128,1536]{2,1,0:T(8,128)S(1)}, u32[]{:S(2)}, u32[]{:S(2)}) collective-permute-start(f32[1,128,1536]{2,1,0:T(8,128)} %get-tuple-element.69), channel_id=1, source_target_pairs={{1,0},{3,2},{5,4},{7,6},{9,8},{11,10},{13,12},{15,14},{17,16},{19,... | collective-permute-start | bytes 2359304 | tf_op jit(solution)/shard_map/ppermute | solution.py:1013
  183.7 78.5 %all-to-all-start = ((bf16[8,96,1536]{2,1,0:T(8,128)(2,1)}), bf16[8,96,1536]{2,1,0:T(8,128)(2,1)S(1)}, u32[]{:S(2)}, u32[]{:S(2)}) async-start(bf16[8,96,1536]{2,1,0:T(8,128)(2,1)} %get-tuple-element.76), calls=%async_computation | async-start | bytes 4718592 | tf_op jit(solution)/shard_map/all_to_all | solution.py:1024
  235.0 6.3 %collective-permute-start.19 = (f32[1,8,1792]{2,1,0:T(8,128)}, f32[1,8,1792]{2,1,0:T(8,128)S(1)}, u32[]{:S(2)}, u32[]{:S(2)}) collective-permute-start(f32[1,8,1792]{2,1,0:T(8,128)} %get-tuple-element.72), channel_id=1, source_target_pairs={{1,0},{3,2},{5,4},{7,6},{9,8},{11,10},{13,12},{15,14},{17,16},{19,... | collective-permute-start | bytes 172040 | tf_op jit(solution)/shard_map/ppermute | solution.py:1029
  252.1 5.5 %collective-permute-start.21 = (f32[8,48,1920]{2,1,0:T(8,128)S(1)}, f32[8,48,1920]{2,1,0:T(8,128)}, u32[]{:S(2)}, u32[]{:S(2)}) collective-permute-start(f32[8,48,1920]{2,1,0:T(8,128)S(1)} %dynamic-slice_bitcast_fusion), channel_id=1, source_target_pairs={{0,2},{2,0},{1,3},{3,1},{4,6},{6,4},{5,7},{7,5},{8,10},{10,8},{9,1... | collective-permute-start | bytes 8847368 | tf_op jit(solution)/shard_map/ppermute | solution.py:715
  262.2 17.6 %copy-start.4 = (bf16[8,96,1536]{2,1,0:T(8,128)(2,1)}, bf16[8,96,1536]{2,1,0:T(8,128)(2,1)S(1)}, u32[]{:S(2)}) copy-start(bf16[8,96,1536]{2,1,0:T(8,128)(2,1)S(1)} %all-to-all-done.got_ref) | copy-start | bytes 7077892
  262.2 39.8 %all-to-all-start.1 = ((bf16[8,48,1920]{2,1,0:T(8,128)(2,1)}), bf16[8,48,1920]{2,1,0:T(8,128)(2,1)}, u32[]{:S(2)}, u32[]{:S(2)}) async-start(bf16[8,48,1920]{2,1,0:T(8,128)(2,1)} %get-tuple-element.78), calls=%async_computation.1 | async-start | bytes 2949120 | tf_op jit(solution)/shard_map/all_to_all | solution.py:1055
  279.8 23.6 %copy-start.18 = (f32[2,26,24,24]{1,3,2,0:T(8,128)S(1)}, f32[2,26,24,24]{1,3,2,0:T(8,128)}, u32[]{:S(2)}) copy-start(f32[2,26,24,24]{1,3,2,0:T(8,128)} %param.37) | copy-start | bytes 359428
  279.8 24.9 %copy-start.19 = (f32[2,26,24,24]{1,3,2,0:T(8,128)S(1)}, f32[2,26,24,24]{1,3,2,0:T(8,128)}, u32[]{:S(2)}) copy-start(f32[2,26,24,24]{1,3,2,0:T(8,128)} %param.39) | copy-start | bytes 359428
  280.8 3.6 collective-permute-start.23
  284.4 21.5 %copy-start.12 = (f32[96,1536]{1,0:T(8,128)S(1)}, f32[96,1536]{1,0:T(8,128)}, u32[]{:S(2)}) copy-start(f32[96,1536]{1,0:T(8,128)} %owner_sum.2) | copy-start | bytes 1769476
  284.4 21.5 %collective-permute-start.20 = (f32[96,1536]{1,0:T(8,128)}, f32[96,1536]{1,0:T(8,128)S(1)}, u32[]{:S(2)}, u32[]{:S(2)}) collective-permute-start(f32[96,1536]{1,0:T(8,128)} %owner_sum.2), channel_id=1, source_target_pairs={{0,1},{1,0},{2,3},{3,2},{4,5},{5,4},{6,7},{7,6},{8,9},{9,8},{10,11... | collective-permute-start | bytes 1769480 | tf_op jit(solution)/shard_map/ppermute | solution.py:715
  284.5 16.9 %collective-permute-start.24 = (f32[96,128]{1,0:T(8,128)S(1)}, f32[96,128]{1,0:T(8,128)S(1)}, u32[]{:S(2)}, u32[]{:S(2)}) collective-permute-start(f32[96,128]{1,0:T(8,128)S(1)} %fusion.15), channel_id=1, source_target_pairs={{0,1},{1,0},{2,3},{3,2},{4,5},{5,4},{6,7},{7,6},{8,9},{9,8},{10,11... | collective-permute-start | bytes 147464 | tf_op jit(solution)/shard_map/ppermute | solution.py:779
  302.0 4.1 %collective-permute-start.25 = (f32[96,128]{1,0:T(8,128)S(1)}, f32[96,128]{1,0:T(8,128)S(1)}, u32[]{:S(2)}, u32[]{:S(2)}) collective-permute-start(f32[96,128]{1,0:T(8,128)S(1)} %fusion.32), channel_id=1, source_target_pairs={{0,4},{4,0},{1,5},{5,1},{2,6},{6,2},{3,7},{7,3},{8,12},{12,8},{9,1... | collective-permute-start | bytes 147464 | tf_op jit(solution)/shard_map/ppermute | solution.py:779
  306.1 4.2 %collective-permute-start.26 = (f32[96,128]{1,0:T(8,128)S(1)}, f32[96,128]{1,0:T(8,128)S(1)}, u32[]{:S(2)}, u32[]{:S(2)}) collective-permute-start(f32[96,128]{1,0:T(8,128)S(1)} %add.97), channel_id=1, source_target_pairs={{0,8},{8,0},{16,24},{24,16},{1,9},{9,1},{17,25},{25,17},{2,10},{10... | collective-permute-start | bytes 147464 | tf_op jit(solution)/shard_map/ppermute | solution.py:779
  310.2 21.9 %collective-permute-start.27 = (f32[96,128]{1,0:T(8,128)S(1)}, f32[96,128]{1,0:T(8,128)S(1)}, u32[]{:S(2)}, u32[]{:S(2)}) collective-permute-start(f32[96,128]{1,0:T(8,128)S(1)} %add.98), channel_id=1, source_target_pairs={{0,16},{8,24},{16,0},{24,8},{1,17},{9,25},{17,1},{25,9},{2,18},{10... | collective-permute-start | bytes 147464 | tf_op jit(solution)/shard_map/ppermute | solution.py:779
  328.4 13.0 %copy-start.8 = (f32[48,1536]{1,0:T(8,128)S(1)}, f32[48,1536]{1,0:T(8,128)}, u32[]{:S(2)}) copy-start(f32[48,1536]{1,0:T(8,128)} %slice.63.refs_0_) | copy-start | bytes 884740
  328.4 14.8 %copy-start.23 = (f32[2,24,24]{2,1,0:T(8,128)S(1)}, f32[2,24,24]{2,1,0:T(8,128)}, u32[]{:S(2)}) copy-start(f32[2,24,24]{2,1,0:T(8,128)} %param.44) | copy-start | bytes 13828
  331.8 8.6 %collective-permute-start.22 = (f32[48,1920]{1,0:T(8,128)}, f32[48,1920]{1,0:T(8,128)S(1)}, u32[]{:S(2)}, u32[]{:S(2)}) collective-permute-start(f32[48,1920]{1,0:T(8,128)} %owner_sum.3), channel_id=1, source_target_pairs={{0,1},{1,0},{2,3},{3,2},{4,5},{5,4},{6,7},{7,6},{8,9},{9,8},{10,11... | collective-permute-start | bytes 1105928 | tf_op jit(solution)/shard_map/ppermute | solution.py:715
  (18 other events, 83.7 us)
Sparse Core Ops, SparseCore 0:
  10.8 49.4 all-gather.1

commit v6 on v5

--- a/solution.py
+++ b/solution.py
@@ -160,23 +160,21 @@
     tail[...] = mixed[tile - 8 :, :]
     rate = rates(alog_ref)
 
-    def block(part, carry):
-        rows = pl.ds(pl.multiple_of(part * BL, BL), BL)
-        tri = jnp.where(tri_mask(True), 1.0, 0.0).astype(BF)
-        step = softplus(z_ref[0, rows, :])
+    step_all = softplus(z)
+    tri = jnp.where(tri_mask(True), 1.0, 0.0).astype(BF)
+    emat = emat_ref[...]
+    for part in range(tile // BL):
+        rows = slice(part * BL, (part + 1) * BL)
+        step = step_all[rows]
         cum = prefix(tri, step * rate)
         last = cum[BL - 1 : BL, :]
-        weights = expand(jnp.exp(last - cum) * step, emat_ref[...])
+        weights = expand(jnp.exp(last - cum) * step, emat)
         decay = expand(
-            jnp.where(head_lanes((8, 128)), jnp.broadcast_to(jnp.exp(last), (8, 128)), 0.0),
-            emat_ref[...],
+            jnp.where(head_lanes((8, 128)), jnp.broadcast_to(jnp.exp(last), (8, 128)), 0.0), emat
         )[0:1, :]
         fresh = dot3(full[rows, DI : DI + DSTATE].T, weights * full[rows, :DI])
         state_ref[0] = state_ref[0] * decay + fresh
         total_ref[0] = total_ref[0] + jnp.broadcast_to(last, (8, 128))
-        return carry
-
-    lax.fori_loop(0, tile // BL, block, 0)
 
 
 def dot_wide(ahl, ah, bh, bl):
@@ -597,10 +595,11 @@
     tok = lambda width: pl.BlockSpec((1, 16, width), lambda b: (b, end, 0))
     per = pl.BlockSpec((1, 8, CONVCH), lambda b: (b, 0, 0))
     row = pl.BlockSpec((8, CONVCH), lambda b: (0, 0))
+    taps = pl.BlockSpec(cw.shape, lambda b: (0, 0))
     return pl.pallas_call(
         patch_kernel,
         grid=(seqs,),
-        in_specs=[tok(WIDE), tok(CONVCH), per, per, row],
+        in_specs=[tok(WIDE), tok(CONVCH), per, per, taps],
         out_specs=[tok(WIDE), row],
         out_shape=[
             jax.ShapeDtypeStruct(mgrad.shape, BF),
@@ -625,6 +624,11 @@
     shaped = jnp.einsum("abij,abjk->abik", shaped, right_root, precision=lax.Precision.HIGH)
     update = (-LR * shaped).transpose(0, 2, 1, 3).reshape(gradient.shape)
     return (update, left_new, right_new)
+
+
+def float_parts(v):
+    high = v.astype(BF).astype(F32)
+    return high, v - high
 
 
 def kron_kernel(*refs):
@@ -635,9 +639,20 @@
         for c in range(left_ref.shape[1]):
             cols = slice(c * COL_BLOCK, (c + 1) * COL_BLOCK)
             grad = grad_ref[rows, cols]
-            left_new_ref[r, c] = 0.5 * left_ref[r, c] + 0.5 * dot3(grad, grad, NT)
-            right_new_ref[r, c] = 0.5 * right_ref[r, c] + 0.5 * dot3(grad.T, grad)
-            shaped = dot3(dot3(left_root_ref[r, c], grad), right_root_ref[r, c])
+            high, low = float_parts(grad)
+            root_high, root_low = float_parts(left_root_ref[r, c])
+            below = jnp.concatenate([high, high, low], axis=0).astype(BF)
+            right = dot(jnp.concatenate([high, low, high], axis=0).astype(BF), below, TN)
+            rooted = dot(
+                jnp.concatenate([root_high, root_low, root_high], axis=0).astype(BF), below, TN
+            )
+            high, low = high.astype(BF), low.astype(BF)
+            left = dot(
+                jnp.concatenate([high, low], axis=1), jnp.concatenate([high, high], axis=1), NT
+            ) + dot(high, low, NT)
+            left_new_ref[r, c] = 0.5 * left_ref[r, c] + 0.5 * left
+            right_new_ref[r, c] = 0.5 * right_ref[r, c] + 0.5 * right
+            shaped = dot_wide(*wide_split(rooted), *split2(right_root_ref[r, c]))
             update_ref[rows, cols] = -LR * shaped
 
 
@@ -909,13 +924,6 @@
         name="assemble",
     )(idx, *pieces)
     return out.reshape(32 * rows, cols)
-
-
-def row8(v, width=None):
-    v = v.reshape(1, -1)
-    if width is not None:
-        v = jnp.pad(v, ((0, 0), (0, width - v.shape[1])))
-    return jnp.broadcast_to(v, (8, v.shape[1]))
 
 
 def body(
@@ -962,12 +970,12 @@
         ((part[:, None] % 32) == (channel[None, :] // HEADDIM)) & (part[:, None] < 96)
     ).astype(BF)
     gmat = ((channel[:, None] // HEADDIM) == part[None, :]).astype(BF)
-    skip_wide = row8(jnp.repeat(skip_gain, HEADDIM))
-    alog = row8(decay_log, 128)
-    dtb = row8(jnp.concatenate([dt_bias, jnp.full((128 - HEADS,), -1e4, F32)]))
-    cw8 = jnp.pad(conv_weight, ((0, 4), (0, 0)))
-    gain8, cb8 = row8(norm_gain), row8(conv_bias)
-    ggain8 = row8(gate_gain)
+    skip_wide = jnp.repeat(skip_gain, HEADDIM).reshape(1, DI)
+    alog = jnp.pad(decay_log, (0, 128 - HEADS)).reshape(1, 128)
+    dtb = jnp.pad(dt_bias, (0, 128 - HEADS), constant_values=-1e4).reshape(1, 128)
+    cw8 = conv_weight
+    gain8, cb8 = norm_gain.reshape(1, D), conv_bias.reshape(1, CONVCH)
+    ggain8 = gate_gain.reshape(1, DI)
     tables = (emat, gmat, skip_wide, alog, dtb, cw8, gain8, cb8, ggain8)
     torus_sizes = tuple(lax.axis_size(a) for a in ("z", "x", "core", "seq"))
     direct = torus_sizes == (4, 2, 2, 2)

time: 365 us -> 357 us (0.978)
  Pallas kernels: 168 us -> 164 us
    pallas_call x1, Pallas kernels: 21.5 us -> 17 us  [run_first(): pl.pallas_call(first_kernel, grid=grid, in_specs=[tok(D), per(8, D), whol...]
    broadcast_in_dim x9 -> x1, local copies, waits for them, and re-layouts: 3.82 us -> 0.07 us  [body(): skip_wide = jnp.repeat(skip_gain, HEADDIM).reshape(1, DI)]
    unnamed x75 -> x73, local copies, waits for them, and re-layouts: 16.4 us -> 16.3 us
  transfers between devices with their start and end apart: 31 -> 31, of which waited for: 16 -> 16; matrix products, arithmetic and copies ran while one was open for 9% -> 9% of each run, Pallas kernels for 32% -> 31%
where the time goes in v6:
time: 357 us; the launch traced here: 355 us
  Pallas kernels  164 us (46%)
  waiting for transfers between devices  73.4 us (21%)
  starting transfers between devices  44.3 us (12%)
  local copies, waits for them, and re-layouts  31.1 us (9%)
  matrix products  16.9 us (5%)
  between operations  14.6 us (4%)
  other arithmetic  10.7 us (3%)
    pallas_call x1, Pallas kernels, run_second(): pl.pallas_call(second_kernel, grid=grid, in_specs=[tok(CONVCH), tok(128),...  44.6 us
    pallas_call x1, Pallas kernels, run_third(): pl.pallas_call(third_kernel, grid=grid, in_specs=[tok(CONVCH), tok(CONVCH...  40.6 us
    ppermute x19, waiting for transfers between devices, swapped(): lax.ppermute(v, axis, [(i, (i + offset) % size) for i in range(size)])  27.4 us
    pallas_call x3, Pallas kernels, kron_tiles(): pl.pallas_call(kron_kernel, grid=(cols // wide,), in_specs=in_specs, out_...  23.1 us
    ppermute x19, starting transfers between devices, swapped(): lax.ppermute(v, axis, [(i, (i + offset) % size) for i in range(size)])  18.6 us
    ppermute x5, waiting for transfers between devices, xor_sum(): v = v + lax.ppermute(v, axis, [(i, i ^ bit) for i in range(size)])  17.8 us
    pallas_call x1, Pallas kernels, run_first(): pl.pallas_call(first_kernel, grid=grid, in_specs=[tok(D), per(8, D), whol...  17 us
    unnamed x73, local copies, waits for them, and re-layouts  16.3 us
  transfers between devices with their start and end apart: 31, of which 16 were waited for; matrix products, arithmetic and copies ran while one was open for 9% of the time, Pallas kernels for 31%

profile of v6, /device:TPU:0, one launch (start us, length us, event | category | flops | bytes accessed | tf_op | source)
XLA Modules:
  0.0 355.0 jit_solution(17577818091900794002)
XLA Ops:
  10.0 5.1 %collective-permute-start.3 = (bf16[24,1536]{1,0:T(8,128)(2,1)S(1)}, bf16[24,1536]{1,0:T(8,128)(2,1)S(1)}, u32[]{:S(2)}, u32[]{:S(2)}) collective-permute-start(bf16[24,1536]{1,0:T(8,128)(2,1)S(1)} %fusion.34), channel_id=1, source_target_pairs={{0,24},{8,0},{16,8},{24,16},{1,25},{9,1},{17,9},{25,17},{2,26},{10... | collective-permute-start | bytes 221192 | tf_op jit(solution)/shard_map/ppermute | solution.py:730
  17.2 2.9 collective-permute-start.7
  22.8 3.4 collective-permute-start
  26.3 1.6 collective-permute-start.4
  27.9 5.1 %collective-permute-done.6 = bf16[48,768]{1,0:T(8,128)(2,1)S(1)} collective-permute-done((bf16[48,768]{1,0:T(8,128)(2,1)S(1)}, bf16[48,768]{1,0:T(8,128)(2,1)S(1)}, u32[]{:S(2)}, u32[]{:S(2)}) %collective-permute-start.6) | collective-permute-done | bytes 73760 | tf_op jit(solution)/shard_map/ppermute | solution.py:730
  33.0 1.9 collective-permute-start.8
  35.9 1.6 collective-permute-start.10
  37.5 4.3 %collective-permute-done.8 = bf16[4,48,768]{2,1,0:T(8,128)(2,1)S(1)} collective-permute-done((bf16[4,48,768]{2,1,0:T(8,128)(2,1)S(1)}, bf16[4,48,768]{2,1,0:T(8,128)(2,1)S(1)}, u32[]{:S(2)}, u32[]{:S(2)}) %collective-permute-start.8) | collective-permute-done | bytes 294944 | tf_op jit(solution)/shard_map/ppermute | solution.py:730
  41.8 1.5 collective-permute-start.13
  47.9 12.2 %all-gather.2.cloned.1.call-done.w_ref.main_ref = bf16[768,1920]{1,0:T(8,128)(2,1)} async-done(((bf16[48,1920]{1,0:T(8,128)(2,1)}), bf16[768,1920]{1,0:T(8,128)(2,1)}) %all-gather.2.cloned.1.call-update) | async-done | bytes 2949136 | tf_op jit(solution)/shard_map/all_gather | solution.py:964
  60.7 17.0 %first.1 = (bf16[1,1024,768]{2,1,0:T(8,128)(2,1)}, bf16[1,1024,1792]{2,1,0:T(8,128)(2,1)}, f32[1,1024,1792]{2,1,0:T(8,128)}, f32[1,1024,128]{2,1,0:T(8,128)}, f3...) custom-call(bf16[1,1024,768]{2,1,0:T(8,128)(2,1)} %u_ref.3, bf16[1,8,768]{2,1,0:T(8,128)(2,1)} %copy-done.27, ...), custom_call_target="tpu_custom_call" | custom-call | tf_op jit(solution)/shard_map/first/pallas_call | solution.py:491
  77.8 4.3 %collective-permute-start.9 = (f32[1,128,1536]{2,1,0:T(8,128)}, f32[1,128,1536]{2,1,0:T(8,128)}, u32[]{:S(2)}, u32[]{:S(2)}) collective-permute-start(f32[1,128,1536]{2,1,0:T(8,128)} %get-tuple-element.59), channel_id=1, source_target_pairs={{0,1},{2,3},{4,5},{6,7},{8,9},{10,11},{12,13},{14,15},{16,17},{18,... | collective-permute-start | bytes 2359304 | tf_op jit(solution)/shard_map/ppermute | solution.py:1004
  85.0 3.8 %assemble.2 = bf16[32,24,1536]{2,1,0:T(8,128)(2,1)} custom-call(s32[4]{0:T(128)} %pad_add_fusion.idx, bf16[2,4,24,1536]{3,2,1,0:T(8,128)(2,1)} %copy-done.9, bf16[2,4,24,1536]{3,2,1,0:T(8,128)(2,1)} %copy-done.15, bf16[2,4,24,1536]{3,2,1,0:T(8,128)(2,1)} %copy-done.17, bf16[2,4,24,1536]{3,2,1,0:T(8,128)(2,1)} %collective-permute-done.12.refs_3_), custom_call_target="tpu_custom_call" | custom-call | tf_op jit(solution)/shard_map/assemble/pallas_call | solution.py:914
  88.9 4.0 %assemble.3 = bf16[32,48,768]{2,1,0:T(8,128)(2,1)} custom-call(s32[4]{0:T(128)} %pad_add_fusion.idx, bf16[2,4,48,768]{3,2,1,0:T(8,128)(2,1)} %copy-done.10, bf16[2,4,48,768]{3,2,1,0:T(8,128)(2,1)} %copy-done.16, bf16[2,4,48,768]{3,2,1,0:T(8,128)(2,1)} %collective-permute-done.14.refs_2_, bf16[2,4,48,768]{3,2,1,0:T(8,128)(2,1)} %collective-permute-done.15.refs_3_), custom_call_target="tpu_custom_call" | custom-call | tf_op jit(solution)/shard_map/assemble/pallas_call | solution.py:914
  92.8 1.7 copy.70
  94.5 4.1 %collective-permute-done.9.enter_ref = f32[1,128,1536]{2,1,0:T(8,128)} collective-permute-done((f32[1,128,1536]{2,1,0:T(8,128)}, f32[1,128,1536]{2,1,0:T(8,128)}, u32[]{:S(2)}, u32[]{:S(2)}) %collective-permute-start.9) | collective-permute-done | bytes 786464 | tf_op jit(solution)/shard_map/ppermute | solution.py:1004
  98.6 44.6 %second.1 = (bf16[1,1024,768]{2,1,0:T(8,128)(2,1)}, bf16[1024,1536]{1,0:T(8,128)(2,1)}, bf16[1024,1536]{1,0:T(8,128)(2,1)}, bf16[1024,1536]{1,0:T(8,128)(2,1)}, ...) custom-call(f32[1,1024,1792]{2,1,0:T(8,128)} %get-tuple-element.56.pre_ref, ...), custom_call_target="tpu_custom_call" | custom-call | tf_op jit(solution)/shard_map/second/pallas_call | solution.py:525
  143.3 4.5 %fusion.2.refs_0_ = f32[8,2,48,1536]{3,2,1,0:T(8,128)S(1)} fusion(bf16[8,2,48,1024]{3,2,1,0:T(8,128)(2,1)S(1)} %bitcast.97, bf16[1024,1536]{1,0:T(8,128)(2,1)} %get-tuple-element.61.ggrad_ref), kind=kOutput, calls=%fused_computation.2 | convolution fusion | flops 2415919104 | bytes 9437184 | tf_op jit(solution)/shard_map/dot_general | solution.py:40
  147.8 2.1 copy-done.2
  149.9 1.6 dynamic-slice_bitcast_fusion.2
  151.5 4.8 %copy.71 = bf16[1536,1024]{1,0:T(8,128)(2,1)} copy(bf16[1536,1024]{0,1:T(8,128)(2,1)} %bitcast.94) | data formatting | bytes 6291456 | tf_op jit(solution)/shard_map/dot_general | solution.py:40
  156.3 4.5 %fusion.4.refs_2_ = f32[8,2,96,768]{3,2,1,0:T(8,128)S(1)} fusion(bf16[8,2,96,1024]{3,2,1,0:T(8,128)(2,1)} %bitcast.95, bf16[1,1024,768]{2,1,0:T(8,128)(2,1)S(1)} %copy-done.5), kind=kOutput, calls=%fused_computation.7 | convolution fusion | flops 2415919104 | bytes 9437184 | tf_op jit(solution)/shard_map/dot_general | solution.py:40
  160.9 2.1 copy-done.3
  165.0 2.9 collective-permute-done.17.refs_3_
  169.3 6.2 %chip_sum.2 = (bf16[8,96,1536]{2,1,0:T(8,128)(2,1)}, f32[96,1536]{1,0:T(8,128)}) custom-call(s32[4]{0:T(128)} %pad_add_fusion.idx, f32[8,2,48,1536]{3,2,1,0:T(8,128)} %copy-done.2, f32[8,48,1536]{2,1,0:T(8,128)} %collective-permute-done.16.refs_1_, f32[8,2,96,768]{3,2,1,0:T(8,128)} %copy-done.3, f32[8,96,768]{2,1,0:T(8,128)} %copy-done.11), custom_call_target="tpu_custom_call" | custom-call | tf_op jit(solution)/shard_map/chip_sum/pallas_call | solution.py:837
  175.5 3.8 %all-to-all-start = ((bf16[8,96,1536]{2,1,0:T(8,128)(2,1)}), bf16[8,96,1536]{2,1,0:T(8,128)(2,1)S(1)}, u32[]{:S(2)}, u32[]{:S(2)}) async-start(bf16[8,96,1536]{2,1,0:T(8,128)(2,1)} %get-tuple-element.76), calls=%async_computation | async-start | bytes 4718592 | tf_op jit(solution)/shard_map/all_to_all | solution.py:1032
  179.3 6.1 %collective-permute-done.18.leave_ref = f32[1,128,1536]{2,1,0:T(8,128)S(1)} collective-permute-done((f32[1,128,1536]{2,1,0:T(8,128)}, f32[1,128,1536]{2,1,0:T(8,128)S(1)}, u32[]{:S(2)}, u32[]{:S(2)}) %collective-permute-start.18) | collective-permute-done | bytes 786464 | tf_op jit(solution)/shard_map/ppermute | solution.py:1021
  186.3 40.6 %third.1 = (bf16[1,1024,1920]{2,1,0:T(8,128)(2,1)}, f32[1,8,1792]{2,1,0:T(8,128)}, f32[1,8,1792]{2,1,0:T(8,128)}, f32[8,1792]{1,0:T(8,128)}) custom-call(f32[1,1024,1792]{2,1,0:T(8,128)} %get-tuple-element.56.pre_ref, bf16[1,1024,1792]{2,1,0:T(8,128)(2,1)} %get-tuple-element.62.mixed_ref, f32[1,1024,128]{2,1,0:T(8,128)} %get-tuple-element.57.z_ref, ...), custom_call_target="tpu_custom_call" | custom-call | tf_op jit(solution)/shard_map/third/pallas_call | solution.py:563
  228.2 5.0 %collective-permute-done.19.near_ref = f32[1,8,1792]{2,1,0:T(8,128)S(1)} collective-permute-done((f32[1,8,1792]{2,1,0:T(8,128)}, f32[1,8,1792]{2,1,0:T(8,128)S(1)}, u32[]{:S(2)}, u32[]{:S(2)}) %collective-permute-start.19) | collective-permute-done | bytes 57376 | tf_op jit(solution)/shard_map/ppermute | solution.py:1037
  233.8 1.6 patch.1
  235.4 6.0 %fusion.refs_0_ = f32[8,2,48,1920]{3,2,1,0:T(8,128)S(1)} fusion(bf16[8,2,48,1024]{3,2,1,0:T(8,128)(2,1)} %bitcast.96, bf16[1,1024,1920]{2,1,0:T(8,128)(2,1)} %get-tuple-element.73), kind=kOutput, calls=%fused_computation | convolution fusion | flops 3019898880 | bytes 11403264 | tf_op jit(solution)/shard_map/dot_general | solution.py:40
  241.6 2.3 copy-done.1
  244.0 5.5 %collective-permute-done.21.refs_1_ = f32[8,48,1920]{2,1,0:T(8,128)} collective-permute-done((f32[8,48,1920]{2,1,0:T(8,128)S(1)}, f32[8,48,1920]{2,1,0:T(8,128)}, u32[]{:S(2)}, u32[]{:S(2)}) %collective-permute-start.21) | collective-permute-done | bytes 2949152 | tf_op jit(solution)/shard_map/ppermute | solution.py:730
  249.5 4.5 %chip_sum.3 = (bf16[8,48,1920]{2,1,0:T(8,128)(2,1)}, f32[48,1920]{1,0:T(8,128)}) custom-call(s32[4]{0:T(128)} %pad_add_fusion.idx, f32[8,2,48,1920]{3,2,1,0:T(8,128)} %copy-done.1, f32[8,48,1920]{2,1,0:T(8,128)} %collective-permute-done.21.refs_1_), custom_call_target="tpu_custom_call" | custom-call | tf_op jit(solution)/shard_map/chip_sum/pallas_call | solution.py:837
  254.0 4.6 %all-to-all-start.1 = ((bf16[8,48,1920]{2,1,0:T(8,128)(2,1)}), bf16[8,48,1920]{2,1,0:T(8,128)(2,1)}, u32[]{:S(2)}, u32[]{:S(2)}) async-start(bf16[8,48,1920]{2,1,0:T(8,128)(2,1)} %get-tuple-element.78), calls=%async_computation.1 | async-start | bytes 2949120 | tf_op jit(solution)/shard_map/all_to_all | solution.py:1063
  259.8 11.9 %back.1 = (f32[1024,768]{1,0:T(8,128)}, f32[8,768]{1,0:T(8,128)}) custom-call(bf16[1024,1536]{1,0:T(8,128)(2,1)} %get-tuple-element.61.ggrad_ref, bf16[1024,1920]{1,0:T(8,128)(2,1)} %bitcast.88, bf16[768,1536]{1,0:T(8,128)(2,1)} %bitcast.87, bf16[768,1920]{1,0:T(8,128)(2,1)} %all-gather.2.cloned.1.call-done.w_ref.main_ref, bf16[1024,768]{1,0:T(8,128)(2,1)} %bitcast.89, ...), custom_call_target="tpu_custom_call" | custom-call | tf_op jit(solution)/shard_map/back/pallas_call | solution.py:714
  272.9 3.4 owner_sum.2
  276.3 2.1 collective-permute-start.24
  278.4 14.8 %collective-permute-done.24 = f32[96,128]{1,0:T(8,128)S(1)} collective-permute-done((f32[96,128]{1,0:T(8,128)S(1)}, f32[96,128]{1,0:T(8,128)S(1)}, u32[]{:S(2)}, u32[]{:S(2)}) %collective-permute-start.24) | collective-permute-done | bytes 49184 | tf_op jit(solution)/shard_map/ppermute | solution.py:794
  293.8 1.5 collective-permute-start.25
  299.1 3.0 collective-permute-done.26
  302.1 2.1 collective-permute-start.27
  305.6 7.3 %kron.3 = (f32[48,3328]{1,0:T(8,128)}, f32[2,26,24,24]{3,2,1,0:T(8,128)}, f32[2,26,128,128]{3,2,1,0:T(8,128)}) custom-call(f32[48,1536]{1,0:T(8,128)} %slice.63.refs_0_, f32[2,26,24,24]{3,2,1,0:T(8,128)} %copy.74.refs_1_, f32[2,26,128,128]{3,2,1,0:T(8,128)} %refs_2_.4, f32[2,26,24,24]{3,2,1,0:T(8,128)} %copy.75.refs_3_, f32[2,26,128,128]{3,2,1,0:T(8,128)} %refs_4_.4), custom_call_target="tpu_custom_call" | custom-call | tf_op jit(solution)/shard_map/kron/pallas_call | solution.py:675
  312.9 7.3 %kron.5 = (f32[96,768]{1,0:T(8,128)}, f32[4,6,24,24]{3,2,1,0:T(8,128)}, f32[4,6,128,128]{3,2,1,0:T(8,128)}) custom-call(f32[96,768]{1,0:T(8,128)} %pad_maximum_fusion.5.refs_0_, f32[4,6,24,24]{3,2,1,0:T(8,128)} %refs_1_.3, f32[4,6,128,128]{3,2,1,0:T(8,128)} %refs_2_.5, f32[4,6,24,24]{3,2,1,0:T(8,128)} %refs_3_.3, f32[4,6,128,128]{3,2,1,0:T(8,128)} %refs_4_.5), custom_call_target="tpu_custom_call" | custom-call | tf_op jit(solution)/shard_map/kron/pallas_call | solution.py:675
  320.2 3.3 owner_sum.3
  324.6 7.5 %collective-permute-done.22 = f32[48,1920]{1,0:T(8,128)S(1)} collective-permute-done((f32[48,1920]{1,0:T(8,128)}, f32[48,1920]{1,0:T(8,128)S(1)}, u32[]{:S(2)}, u32[]{:S(2)}) %collective-permute-start.22) | collective-permute-done | bytes 368672 | tf_op jit(solution)/shard_map/ppermute | solution.py:730
  335.8 8.5 %kron.4 = (f32[48,3328]{1,0:T(8,128)}, f32[2,26,24,24]{3,2,1,0:T(8,128)}, f32[2,26,128,128]{3,2,1,0:T(8,128)}) custom-call(f32[48,1792]{1,0:T(8,128)} %copy-done.7, f32[2,26,24,24]{3,2,1,0:T(8,128)} %copy.74.refs_1_, f32[2,26,128,128]{3,2,1,0:T(8,128)} %refs_2_.4, ...), custom_call_target="tpu_custom_call", output_to_operand_aliasing={{0}: (5, {}), {1}: (6, {}), {2}: (7, {})} | custom-call | tf_op jit(solution)/shard_map/kron/pallas_call | solution.py:675
  344.3 2.2 copy.81
  (168 shorter events, 37.8 us)
Async XLA Ops:
  7.2 327.7 %copy-start = (f32[2,24,24]{2,1,0:T(8,128)S(1)}, f32[2,24,24]{2,1,0:T(8,128)}, u32[]{:S(2)}) copy-start(f32[2,24,24]{2,1,0:T(8,128)} %param.43) | copy-start | bytes 13828
  7.2 52.9 %all-gather.2.cloned.1.call-start = ((), (), s32[]{:S(2)}) async-start(), calls=%async_computation.2 | async-start | bytes 3133440 | tf_op jit(solution)/shard_map/all_gather | solution.py:964
  10.0 34.4 %copy-start.33 = (f32[24]{0:T(128)S(1)}, f32[24]{0:T(128)}, u32[]{:S(2)}) copy-start(f32[24]{0:T(128)} %param.34) | copy-start | bytes 292
  10.0 34.9 %copy-start.32 = (f32[24]{0:T(128)S(1)}, f32[24]{0:T(128)}, u32[]{:S(2)}) copy-start(f32[24]{0:T(128)} %param.33) | copy-start | bytes 292
  10.0 35.4 %copy-start.30 = (f32[768]{0:T(1024)S(1)}, f32[768]{0:T(1024)}, u32[]{:S(2)}) copy-start(f32[768]{0:T(1024)} %param.30) | copy-start | bytes 9220
  10.0 36.0 %copy-start.31 = (f32[24]{0:T(128)S(1)}, f32[24]{0:T(128)}, u32[]{:S(2)}) copy-start(f32[24]{0:T(128)} %param.35) | copy-start | bytes 292
  10.0 36.7 %copy-start.29 = (f32[1792]{0:T(1024)S(1)}, f32[1792]{0:T(1024)}, u32[]{:S(2)}) copy-start(f32[1792]{0:T(1024)} %param.32) | copy-start | bytes 21508
  10.0 37.3 %copy-start.28 = (f32[1536]{0:T(1024)S(1)}, f32[1536]{0:T(1024)}, u32[]{:S(2)}) copy-start(f32[1536]{0:T(1024)} %param.36) | copy-start | bytes 18436
  10.0 11.9 %collective-permute-start.3 = (bf16[24,1536]{1,0:T(8,128)(2,1)S(1)}, bf16[24,1536]{1,0:T(8,128)(2,1)S(1)}, u32[]{:S(2)}, u32[]{:S(2)}) collective-permute-start(bf16[24,1536]{1,0:T(8,128)(2,1)S(1)} %fusion.34), channel_id=1, source_target_pairs={{0,24},{8,0},{16,8},{24,16},{1,25},{9,1},{17,9},{25,17},{2,26},{10... | collective-permute-start | bytes 221192 | tf_op jit(solution)/shard_map/ppermute | solution.py:730
  15.2 7.7 %collective-permute-start.2 = (bf16[24,1536]{1,0:T(8,128)(2,1)S(1)}, bf16[24,1536]{1,0:T(8,128)(2,1)S(1)}, u32[]{:S(2)}, u32[]{:S(2)}) collective-permute-start(bf16[24,1536]{1,0:T(8,128)(2,1)S(1)} %fusion.34), channel_id=1, source_target_pairs={{0,16},{8,24},{16,0},{24,8},{1,17},{9,25},{17,1},{25,9},{2,18},{10... | collective-permute-start | bytes 221192 | tf_op jit(solution)/shard_map/ppermute | solution.py:730
  15.2 11.1 %collective-permute-start.1 = (bf16[24,1536]{1,0:T(8,128)(2,1)S(1)}, bf16[24,1536]{1,0:T(8,128)(2,1)S(1)}, u32[]{:S(2)}, u32[]{:S(2)}) collective-permute-start(bf16[24,1536]{1,0:T(8,128)(2,1)S(1)} %fusion.34), channel_id=1, source_target_pairs={{0,8},{8,16},{16,24},{24,0},{1,9},{9,17},{17,25},{25,1},{2,10},{10... | collective-permute-start | bytes 221192 | tf_op jit(solution)/shard_map/ppermute | solution.py:730
  17.2 10.7 %collective-permute-start.7 = (bf16[48,768]{1,0:T(8,128)(2,1)S(1)}, bf16[48,768]{1,0:T(8,128)(2,1)S(1)}, u32[]{:S(2)}, u32[]{:S(2)}) collective-permute-start(bf16[48,768]{1,0:T(8,128)(2,1)S(1)} %fusion.33), channel_id=1, source_target_pairs={{0,24},{8,0},{16,8},{24,16},{1,25},{9,1},{17,9},{25,17},{2,26},{10... | collective-permute-start | bytes 221192 | tf_op jit(solution)/shard_map/ppermute | solution.py:730
  20.0 12.9 %collective-permute-start.6 = (bf16[48,768]{1,0:T(8,128)(2,1)S(1)}, bf16[48,768]{1,0:T(8,128)(2,1)S(1)}, u32[]{:S(2)}, u32[]{:S(2)}) collective-permute-start(bf16[48,768]{1,0:T(8,128)(2,1)S(1)} %fusion.33), channel_id=1, source_target_pairs={{0,16},{8,24},{16,0},{24,8},{1,17},{9,25},{17,1},{25,9},{2,18},{10... | collective-permute-start | bytes 221192 | tf_op jit(solution)/shard_map/ppermute | solution.py:730
  21.9 11.0 %collective-permute-start.5 = (bf16[48,768]{1,0:T(8,128)(2,1)S(1)}, bf16[48,768]{1,0:T(8,128)(2,1)S(1)}, u32[]{:S(2)}, u32[]{:S(2)}) collective-permute-start(bf16[48,768]{1,0:T(8,128)(2,1)S(1)} %fusion.33), channel_id=1, source_target_pairs={{0,8},{8,16},{16,24},{24,0},{1,9},{9,17},{17,25},{25,1},{2,10},{10... | collective-permute-start | bytes 221192 | tf_op jit(solution)/shard_map/ppermute | solution.py:730
  22.8 37.3 %collective-permute-start = (bf16[1,8,768]{2,1,0:T(8,128)(2,1)S(1)}, bf16[1,8,768]{2,1,0:T(8,128)(2,1)S(1)}, u32[]{:S(2)}, u32[]{:S(2)}) collective-permute-start(bf16[1,8,768]{2,1,0:T(8,128)(2,1)S(1)} %slice.46), channel_id=1, source_target_pairs={{0,1},{2,3},{4,5},{6,7},{8,9},{10,11},{12,13},{14,15},{16,17},{18,... | collective-permute-start | bytes 36872 | tf_op jit(solution)/shard_map/ppermute | solution.py:998
  26.3 9.5 %collective-permute-start.4 = (bf16[4,24,1536]{2,1,0:T(8,128)(2,1)S(1)}, bf16[4,24,1536]{2,1,0:T(8,128)(2,1)S(1)}, u32[]{:S(2)}, u32[]{:S(2)}) collective-permute-start(bf16[4,24,1536]{2,1,0:T(8,128)(2,1)S(1)} %get-tuple-element.154), channel_id=1, source_target_pairs={{0,4},{4,0},{1,5},{5,1},{2,6},{6,2},{3,7},{7,3},{8,12},{12,8},{9,1... | collective-permute-start | bytes 884744 | tf_op jit(solution)/shard_map/ppermute | solution.py:730
  33.0 8.8 %collective-permute-start.8 = (bf16[4,48,768]{2,1,0:T(8,128)(2,1)S(1)}, bf16[4,48,768]{2,1,0:T(8,128)(2,1)S(1)}, u32[]{:S(2)}, u32[]{:S(2)}) collective-permute-start(bf16[4,48,768]{2,1,0:T(8,128)(2,1)S(1)} %get-tuple-element.152), channel_id=1, source_target_pairs={{0,4},{4,0},{1,5},{5,1},{2,6},{6,2},{3,7},{7,3},{8,12},{12,8},{9,1... | collective-permute-start | bytes 884744 | tf_op jit(solution)/shard_map/ppermute | solution.py:730
  35.9 46.1 %copy-start.9 = (bf16[2,4,24,1536]{3,2,1,0:T(8,128)(2,1)}, bf16[2,4,24,1536]{3,2,1,0:T(8,128)(2,1)S(1)}, u32[]{:S(2)}) copy-start(bf16[2,4,24,1536]{3,2,1,0:T(8,128)(2,1)S(1)} %pad_maximum_fusion.1.refs_0_) | copy-start | bytes 1769476
  35.9 46.1 %collective-permute-start.10 = (bf16[2,4,24,1536]{3,2,1,0:T(8,128)(2,1)S(1)}, bf16[2,4,24,1536]{3,2,1,0:T(8,128)(2,1)S(1)}, u32[]{:S(2)}, u32[]{:S(2)}) collective-permute-start(bf16[2,4,24,1536]{3,2,1,0:T(8,128)(2,1)S(1)} %pad_maximum_fusion.1.refs_0_), channel_id=1, source_target_pairs={{0,1},{1,0},{2,3},{3,2},{4,5},{5,4},{6,7},{7,6},{8,9},{9,8},{10,11... | collective-permute-start | bytes 1769480 | tf_op jit(solution)/shard_map/ppermute | solution.py:730
  41.8 47.0 %copy-start.10 = (bf16[2,4,48,768]{3,2,1,0:T(8,128)(2,1)}, bf16[2,4,48,768]{3,2,1,0:T(8,128)(2,1)S(1)}, u32[]{:S(2)}) copy-start(bf16[2,4,48,768]{3,2,1,0:T(8,128)(2,1)S(1)} %pad_maximum_fusion.2.refs_0_) | copy-start | bytes 1769476
  41.8 40.8 %collective-permute-start.13 = (bf16[2,4,48,768]{3,2,1,0:T(8,128)(2,1)S(1)}, bf16[2,4,48,768]{3,2,1,0:T(8,128)(2,1)S(1)}, u32[]{:S(2)}, u32[]{:S(2)}) collective-permute-start(bf16[2,4,48,768]{3,2,1,0:T(8,128)(2,1)S(1)} %pad_maximum_fusion.2.refs_0_), channel_id=1, source_target_pairs={{0,1},{1,0},{2,3},{3,2},{4,5},{5,4},{6,7},{7,6},{8,9},{9,8},{10,11... | collective-permute-start | bytes 1769480 | tf_op jit(solution)/shard_map/ppermute | solution.py:730
  77.8 20.9 %collective-permute-start.9 = (f32[1,128,1536]{2,1,0:T(8,128)}, f32[1,128,1536]{2,1,0:T(8,128)}, u32[]{:S(2)}, u32[]{:S(2)}) collective-permute-start(f32[1,128,1536]{2,1,0:T(8,128)} %get-tuple-element.59), channel_id=1, source_target_pairs={{0,1},{2,3},{4,5},{6,7},{8,9},{10,11},{12,13},{14,15},{16,17},{18,... | collective-permute-start | bytes 2359304 | tf_op jit(solution)/shard_map/ppermute | solution.py:1004
  82.0 2.0 collective-permute-start.11
  82.1 3.0 collective-permute-start.12
  82.5 6.3 %collective-permute-start.14 = (bf16[2,4,48,768]{3,2,1,0:T(8,128)(2,1)S(1)}, bf16[2,4,48,768]{3,2,1,0:T(8,128)(2,1)}, u32[]{:S(2)}, u32[]{:S(2)}) collective-permute-start(bf16[2,4,48,768]{3,2,1,0:T(8,128)(2,1)S(1)} %pad_maximum_fusion.2.refs_0_), channel_id=1, source_target_pairs={{0,2},{2,0},{1,3},{3,1},{4,6},{6,4},{5,7},{7,5},{8,10},{10,8},{9,1... | collective-permute-start | bytes 1769480 | tf_op jit(solution)/shard_map/ppermute | solution.py:730
  82.6 6.2 %collective-permute-start.15 = (bf16[2,4,48,768]{3,2,1,0:T(8,128)(2,1)S(1)}, bf16[2,4,48,768]{3,2,1,0:T(8,128)(2,1)}, u32[]{:S(2)}, u32[]{:S(2)}) collective-permute-start(bf16[2,4,48,768]{3,2,1,0:T(8,128)(2,1)S(1)} %collective-permute-done.13.refs_1_), channel_id=1, source_target_pairs={{0,2},{2,0},{1,3},{3,1},{4,6},{6,4},{5,7},{7,5},{8,10},{10,8},{9,1... | collective-permute-start | bytes 1769480 | tf_op jit(solution)/shard_map/ppermute | solution.py:730
  98.6 44.6 %copy-start.13 = (bf16[768,1024]{1,0:T(8,128)(2,1)S(1)}, bf16[768,1024]{1,0:T(8,128)(2,1)}, u32[]{:S(2)}) copy-start(bf16[768,1024]{1,0:T(8,128)(2,1)} %copy.70) | copy-start | bytes 4718596
  151.5 13.5 %collective-permute-start.16 = (f32[8,48,1536]{2,1,0:T(8,128)}, f32[8,48,1536]{2,1,0:T(8,128)}, u32[]{:S(2)}, u32[]{:S(2)}) collective-permute-start(f32[8,48,1536]{2,1,0:T(8,128)} %dynamic-slice_bitcast_fusion.2), channel_id=1, source_target_pairs={{0,2},{2,0},{1,3},{3,1},{4,6},{6,4},{5,7},{7,5},{8,10},{10,8},{9,1... | collective-permute-start | bytes 7077896 | tf_op jit(solution)/shard_map/ppermute | solution.py:730
  163.2 4.7 %collective-permute-start.17 = (f32[8,96,768]{2,1,0:T(8,128)S(1)}, f32[8,96,768]{2,1,0:T(8,128)S(1)}, u32[]{:S(2)}, u32[]{:S(2)}) collective-permute-start(f32[8,96,768]{2,1,0:T(8,128)S(1)} %dynamic-slice_bitcast_fusion.1), channel_id=1, source_target_pairs={{0,2},{2,0},{1,3},{3,1},{4,6},{6,4},{5,7},{7,5},{8,10},{10,8},{9,1... | collective-permute-start | bytes 7077896 | tf_op jit(solution)/shard_map/ppermute | solution.py:730
  163.7 21.7 %collective-permute-start.18 = (f32[1,128,1536]{2,1,0:T(8,128)}, f32[1,128,1536]{2,1,0:T(8,128)S(1)}, u32[]{:S(2)}, u32[]{:S(2)}) collective-permute-start(f32[1,128,1536]{2,1,0:T(8,128)} %get-tuple-element.69), channel_id=1, source_target_pairs={{1,0},{3,2},{5,4},{7,6},{9,8},{11,10},{13,12},{15,14},{17,16},{19,... | collective-permute-start | bytes 2359304 | tf_op jit(solution)/shard_map/ppermute | solution.py:1021
  175.5 78.5 %all-to-all-start = ((bf16[8,96,1536]{2,1,0:T(8,128)(2,1)}), bf16[8,96,1536]{2,1,0:T(8,128)(2,1)S(1)}, u32[]{:S(2)}, u32[]{:S(2)}) async-start(bf16[8,96,1536]{2,1,0:T(8,128)(2,1)} %get-tuple-element.76), calls=%async_computation | async-start | bytes 4718592 | tf_op jit(solution)/shard_map/all_to_all | solution.py:1032
  226.9 6.3 %collective-permute-start.19 = (f32[1,8,1792]{2,1,0:T(8,128)}, f32[1,8,1792]{2,1,0:T(8,128)S(1)}, u32[]{:S(2)}, u32[]{:S(2)}) collective-permute-start(f32[1,8,1792]{2,1,0:T(8,128)} %get-tuple-element.72), channel_id=1, source_target_pairs={{1,0},{3,2},{5,4},{7,6},{9,8},{11,10},{13,12},{15,14},{17,16},{19,... | collective-permute-start | bytes 172040 | tf_op jit(solution)/shard_map/ppermute | solution.py:1037
  244.0 5.5 %collective-permute-start.21 = (f32[8,48,1920]{2,1,0:T(8,128)S(1)}, f32[8,48,1920]{2,1,0:T(8,128)}, u32[]{:S(2)}, u32[]{:S(2)}) collective-permute-start(f32[8,48,1920]{2,1,0:T(8,128)S(1)} %dynamic-slice_bitcast_fusion), channel_id=1, source_target_pairs={{0,2},{2,0},{1,3},{3,1},{4,6},{6,4},{5,7},{7,5},{8,10},{10,8},{9,1... | collective-permute-start | bytes 8847368 | tf_op jit(solution)/shard_map/ppermute | solution.py:730
  254.0 17.6 %copy-start.4 = (bf16[8,96,1536]{2,1,0:T(8,128)(2,1)}, bf16[8,96,1536]{2,1,0:T(8,128)(2,1)S(1)}, u32[]{:S(2)}) copy-start(bf16[8,96,1536]{2,1,0:T(8,128)(2,1)S(1)} %all-to-all-done.got_ref) | copy-start | bytes 7077892
  254.0 39.8 %all-to-all-start.1 = ((bf16[8,48,1920]{2,1,0:T(8,128)(2,1)}), bf16[8,48,1920]{2,1,0:T(8,128)(2,1)}, u32[]{:S(2)}, u32[]{:S(2)}) async-start(bf16[8,48,1920]{2,1,0:T(8,128)(2,1)} %get-tuple-element.78), calls=%async_computation.1 | async-start | bytes 2949120 | tf_op jit(solution)/shard_map/all_to_all | solution.py:1063
  259.8 12.8 %copy-start.26 = (f32[8,1792]{1,0:T(8,128)S(1)}, f32[8,1792]{1,0:T(8,128)}, u32[]{:S(2)}) copy-start(f32[8,1792]{1,0:T(8,128)} %get-tuple-element.91) | copy-start | bytes 172036
  271.7 23.6 %copy-start.18 = (f32[2,26,24,24]{1,3,2,0:T(8,128)S(1)}, f32[2,26,24,24]{1,3,2,0:T(8,128)}, u32[]{:S(2)}) copy-start(f32[2,26,24,24]{1,3,2,0:T(8,128)} %param.37) | copy-start | bytes 359428
  271.7 24.9 %copy-start.19 = (f32[2,26,24,24]{1,3,2,0:T(8,128)S(1)}, f32[2,26,24,24]{1,3,2,0:T(8,128)}, u32[]{:S(2)}) copy-start(f32[2,26,24,24]{1,3,2,0:T(8,128)} %param.39) | copy-start | bytes 359428
  272.7 3.6 %collective-permute-start.23 = (f32[96,128]{1,0:T(8,128)S(1)}, f32[96,128]{1,0:T(8,128)S(1)}, u32[]{:S(2)}, u32[]{:S(2)}) collective-permute-start(f32[96,128]{1,0:T(8,128)S(1)} %pad_bitcast_fusion), channel_id=1, source_target_pairs={{0,2},{2,0},{1,3},{3,1},{4,6},{6,4},{5,7},{7,5},{8,10},{10,8},{9,1... | collective-permute-start | bytes 147464 | tf_op jit(solution)/shard_map/ppermute | solution.py:794
  276.3 21.5 %copy-start.12 = (f32[96,1536]{1,0:T(8,128)S(1)}, f32[96,1536]{1,0:T(8,128)}, u32[]{:S(2)}) copy-start(f32[96,1536]{1,0:T(8,128)} %owner_sum.2) | copy-start | bytes 1769476
  276.3 21.5 %collective-permute-start.20 = (f32[96,1536]{1,0:T(8,128)}, f32[96,1536]{1,0:T(8,128)S(1)}, u32[]{:S(2)}, u32[]{:S(2)}) collective-permute-start(f32[96,1536]{1,0:T(8,128)} %owner_sum.2), channel_id=1, source_target_pairs={{0,1},{1,0},{2,3},{3,2},{4,5},{5,4},{6,7},{7,6},{8,9},{9,8},{10,11... | collective-permute-start | bytes 1769480 | tf_op jit(solution)/shard_map/ppermute | solution.py:730
  276.3 16.8 %collective-permute-start.24 = (f32[96,128]{1,0:T(8,128)S(1)}, f32[96,128]{1,0:T(8,128)S(1)}, u32[]{:S(2)}, u32[]{:S(2)}) collective-permute-start(f32[96,128]{1,0:T(8,128)S(1)} %fusion.15), channel_id=1, source_target_pairs={{0,1},{1,0},{2,3},{3,2},{4,5},{5,4},{6,7},{7,6},{8,9},{9,8},{10,11... | collective-permute-start | bytes 147464 | tf_op jit(solution)/shard_map/ppermute | solution.py:794
  293.8 4.1 %collective-permute-start.25 = (f32[96,128]{1,0:T(8,128)S(1)}, f32[96,128]{1,0:T(8,128)S(1)}, u32[]{:S(2)}, u32[]{:S(2)}) collective-permute-start(f32[96,128]{1,0:T(8,128)S(1)} %fusion.32), channel_id=1, source_target_pairs={{0,4},{4,0},{1,5},{5,1},{2,6},{6,2},{3,7},{7,3},{8,12},{12,8},{9,1... | collective-permute-start | bytes 147464 | tf_op jit(solution)/shard_map/ppermute | solution.py:794
  297.9 4.2 %collective-permute-start.26 = (f32[96,128]{1,0:T(8,128)S(1)}, f32[96,128]{1,0:T(8,128)S(1)}, u32[]{:S(2)}, u32[]{:S(2)}) collective-permute-start(f32[96,128]{1,0:T(8,128)S(1)} %add.95), channel_id=1, source_target_pairs={{0,8},{8,0},{16,24},{24,16},{1,9},{9,1},{17,25},{25,17},{2,10},{10... | collective-permute-start | bytes 147464 | tf_op jit(solution)/shard_map/ppermute | solution.py:794
  302.1 21.8 %collective-permute-start.27 = (f32[96,128]{1,0:T(8,128)S(1)}, f32[96,128]{1,0:T(8,128)S(1)}, u32[]{:S(2)}, u32[]{:S(2)}) collective-permute-start(f32[96,128]{1,0:T(8,128)S(1)} %add.96), channel_id=1, source_target_pairs={{0,16},{8,24},{16,0},{24,8},{1,17},{9,25},{17,1},{25,9},{2,18},{10... | collective-permute-start | bytes 147464 | tf_op jit(solution)/shard_map/ppermute | solution.py:794
  320.2 13.0 %copy-start.8 = (f32[48,1536]{1,0:T(8,128)S(1)}, f32[48,1536]{1,0:T(8,128)}, u32[]{:S(2)}) copy-start(f32[48,1536]{1,0:T(8,128)} %slice.63.refs_0_) | copy-start | bytes 884740
  320.2 14.8 %copy-start.22 = (f32[2,24,24]{2,1,0:T(8,128)S(1)}, f32[2,24,24]{2,1,0:T(8,128)}, u32[]{:S(2)}) copy-start(f32[2,24,24]{2,1,0:T(8,128)} %param.44) | copy-start | bytes 13828
  323.6 8.6 %collective-permute-start.22 = (f32[48,1920]{1,0:T(8,128)}, f32[48,1920]{1,0:T(8,128)S(1)}, u32[]{:S(2)}, u32[]{:S(2)}) collective-permute-start(f32[48,1920]{1,0:T(8,128)} %owner_sum.3), channel_id=1, source_target_pairs={{0,1},{1,0},{2,3},{3,2},{4,5},{5,4},{6,7},{7,6},{8,9},{9,8},{10,11... | collective-permute-start | bytes 1105928 | tf_op jit(solution)/shard_map/ppermute | solution.py:730
  (17 other events, 70.9 us)
Sparse Core Ops, SparseCore 0:
  10.8 49.3 all-gather.1

commit v7 on v6

--- a/solution.py
+++ b/solution.py
@@ -124,7 +124,7 @@
 
 
 def first_kernel(
-    u_ref, halo_ref, gain_ref, w_ref, cw_ref, cb_ref, dtb_ref, alog_ref, emat_ref,
+    u_ref, halo_ref, gain_ref, w_ref, side_ref, cw_ref, cb_ref, dtb_ref, alog_ref, emat_ref,
     normed_ref, mixed_ref, pre_ref, z_ref, state_ref, total_ref,
     tail, full,
 ):
@@ -135,21 +135,24 @@
     @pl.when(step_index == 0)
     def _():
         near = norm_rows(halo_ref[0].astype(F32), gain).astype(BF)
-        tail[...] = dot(near, w_ref[:, :CONVCH]).astype(BF).astype(F32)
+        tail[:, :DI] = dot(near, w_ref[...]).astype(BF).astype(F32)
+        tail[:, DI:] = dot(near, side_ref[...])[:, : CONVCH - DI].astype(BF).astype(F32)
         state_ref[...] = jnp.zeros_like(state_ref)
         total_ref[...] = jnp.zeros_like(total_ref)
 
     normed = norm_rows(u_ref[0].astype(F32), gain).astype(BF)
     normed_ref[0] = normed
-    projected = dot(normed, w_ref[...])
-    mixed_low = projected[:, :CONVCH].astype(BF)
+    side = dot(normed, side_ref[...])
+    mixed_low = jnp.concatenate(
+        [dot(normed, w_ref[...]).astype(BF), side[:, : CONVCH - DI].astype(BF)], axis=1
+    )
     mixed_ref[0] = mixed_low
-    mixed = mixed_low.astype(F32)
-    z = projected[:, CONVCH:].astype(BF).astype(F32) + dtb_ref[0:1, :]
+    z = side[:, CONVCH - DI :].astype(BF).astype(F32) + dtb_ref[0:1, :]
     z_ref[0] = z
-    for low in range(0, CONVCH, 256):
-        cols = slice(low, low + 256)
-        own = mixed[:, cols]
+
+    def conv_columns(i, carry):
+        cols = pl.ds(pl.multiple_of(i * 256, 256), 256)
+        own = mixed_ref[0, :, cols].astype(F32)
         joined = jnp.concatenate([tail[:, cols], own], axis=0)
         pre = cb_ref[0:1, cols] + cw_ref[KCONV - 1 : KCONV, cols] * own
         for tap in range(KCONV - 1):
@@ -157,7 +160,10 @@
             pre = pre + cw_ref[tap : tap + 1, cols] * moved
         pre_ref[0, :, cols] = pre
         full[:, cols] = silu(pre)
-    tail[...] = mixed[tile - 8 :, :]
+        return carry
+
+    lax.fori_loop(0, CONVCH // 256, conv_columns, 0)
+    tail[...] = mixed_low[tile - 8 :, :].astype(F32)
     rate = rates(alog_ref)
 
     step_all = softplus(z)
@@ -482,7 +488,7 @@
     return pl.BlockSpec(shape, lambda b, i: zeros)
 
 
-def run_first(u, halo, gain, w, cw, cb, dtb, alog, emat):
+def run_first(u, halo, gain, w, side, cw, cb, dtb, alog, emat):
     seqs, length, _ = u.shape
     tile = min(256, length)
     grid = (seqs, length // tile)
@@ -493,6 +499,7 @@
         grid=grid,
         in_specs=[
             tok(D), per(8, D), whole(gain.shape), whole(w.shape),
+            whole(side.shape),
             whole(cw.shape), whole(cb.shape), whole(dtb.shape), whole(alog.shape), whole(emat.shape),
         ],
         out_specs=[
@@ -509,7 +516,7 @@
         scratch_shapes=[pltpu.VMEM((8, CONVCH), F32), pltpu.VMEM((tile, CONVCH), F32)],
         compiler_params=pltpu.CompilerParams(**PARAMS),
         name="first",
-    )(u, halo, gain, w, cw, cb, dtb, alog, emat)
+    )(u, halo, gain, w, side, cw, cb, dtb, alog, emat)
 
 
 def run_second(pre, z, normed, up, u, enter, wg, wo, skip, ggain, alog, gmat):
@@ -631,13 +638,14 @@
     return high, v - high
 
 
-def kron_kernel(*refs):
+def kron_kernel(*refs, unroll):
     grad_ref, left_ref, right_ref, left_root_ref, right_root_ref = refs[:5]
     update_ref, left_new_ref, right_new_ref = refs[-3:]
-    for r in range(left_ref.shape[0]):
-        rows = slice(r * ROW_BLOCK, (r + 1) * ROW_BLOCK)
-        for c in range(left_ref.shape[1]):
-            cols = slice(c * COL_BLOCK, (c + 1) * COL_BLOCK)
+
+    def column(c, carry):
+        cols = pl.ds(pl.multiple_of(c * COL_BLOCK, COL_BLOCK), COL_BLOCK)
+        for r in range(left_ref.shape[0]):
+            rows = slice(r * ROW_BLOCK, (r + 1) * ROW_BLOCK)
             grad = grad_ref[rows, cols]
             high, low = float_parts(grad)
             root_high, root_low = float_parts(left_root_ref[r, c])
@@ -654,14 +662,17 @@
             right_new_ref[r, c] = 0.5 * right_ref[r, c] + 0.5 * right
             shaped = dot_wide(*wide_split(rooted), *split2(right_root_ref[r, c]))
             update_ref[rows, cols] = -LR * shaped
+        return carry
+
+    lax.fori_loop(0, left_ref.shape[1], column, 0, unroll=unroll)
 
 
 def kron_tiles(grad, left, right, left_root, right_root, first, step, earlier=None):
     row_tiles = left.shape[0]
     rows, cols = grad.shape
-    base = first // step
     stat = lambda size: pl.BlockSpec(
-        (row_tiles, step, size, size), lambda i: (0, base + i, 0, 0)
+        tuple(pl.Element(n) for n in (row_tiles, step, size, size)),
+        lambda i: (0, first + step * i, 0, 0),
     )
     wide = step * COL_BLOCK
     ins = [grad, left, right, left_root, right_root]
@@ -673,11 +684,15 @@
         aliases = {5: 0, 6: 1, 7: 2}
     total = left.shape[1] * COL_BLOCK
     return pl.pallas_call(
-        kron_kernel,
+        functools.partial(kron_kernel, unroll=max(1, 4 // row_tiles)),
         grid=(cols // wide,),
         in_specs=in_specs,
         out_specs=[
-            pl.BlockSpec((rows, wide), lambda i: (0, base + i)), stat(ROW_BLOCK), stat(COL_BLOCK),
+            pl.BlockSpec(
+                (pl.Element(rows), pl.Element(wide)),
+                lambda i: (0, pl.multiple_of(first * COL_BLOCK + wide * i, COL_BLOCK)),
+            ),
+            stat(ROW_BLOCK), stat(COL_BLOCK),
         ],
         out_shape=[
             jax.ShapeDtypeStruct((rows, total), F32),
@@ -691,13 +706,17 @@
 
 
 def back_kernel(
-    ggrad_ref, mgrad_ref, wg_ref, main_ref, u_ref, up_ref, gain_ref, out_ref, gain_grad_ref
+    ggrad_ref, mgrad_ref, wg_ref, main_ref, side_ref, u_ref, up_ref, gain_ref, out_ref, gain_grad_ref
 ):
     @pl.when(pl.program_id(0) == 0)
     def _():
         gain_grad_ref[...] = jnp.zeros_like(gain_grad_ref)
 
-    grad = dot(ggrad_ref[...], wg_ref[...], NT) + dot(mgrad_ref[...], main_ref[...], NT)
+    grad = (
+        dot(ggrad_ref[...], wg_ref[...], NT)
+        + dot(mgrad_ref[:, :DI], main_ref[...], NT)
+        + dot(mgrad_ref[:, DI:], side_ref[...], NT)
+    )
     u = u_ref[...].astype(F32)
     inv = lax.rsqrt(jnp.mean(u * u, axis=-1, keepdims=True) + EPS)
     norm = u * inv
@@ -707,7 +726,7 @@
     out_ref[...] = up_ref[...].astype(F32) + inv * (scaled - norm * pull)
 
 
-def run_back(ggrad, mgrad, wg, main, u, up, gain):
+def run_back(ggrad, mgrad, wg, main, side, u, up, gain):
     rows = u.shape[0]
     tile = min(256, rows)
     tok = lambda width: pl.BlockSpec((tile, width), lambda i: (i, 0))
@@ -716,14 +735,15 @@
         grid=(rows // tile,),
         in_specs=[
             tok(DI), tok(WIDE), pl.BlockSpec(wg.shape, lambda i: (0, 0)),
-            pl.BlockSpec(main.shape, lambda i: (0, 0)), tok(D), tok(D),
+            pl.BlockSpec(main.shape, lambda i: (0, 0)), pl.BlockSpec(side.shape, lambda i: (0, 0)),
+            tok(D), tok(D),
             pl.BlockSpec(gain.shape, lambda i: (0, 0)),
         ],
         out_specs=[tok(D), pl.BlockSpec((8, D), lambda i: (0, 0))],
         out_shape=[jax.ShapeDtypeStruct((rows, D), F32), jax.ShapeDtypeStruct((8, D), F32)],
         compiler_params=pltpu.CompilerParams(**PARAMS),
         name="back",
-    )(ggrad, mgrad, wg, main, u, up, gain)
+    )(ggrad, mgrad, wg, main, side, u, up, gain)
 
 
 def swapped(v, axis, size, offset):
@@ -802,7 +822,8 @@
 def chip_kernel(idx, *refs):
     send_ref, own_ref = refs[-2:]
     width = own_ref.shape[1]
-    for owner in range(STEP_OWNERS):
+
+    def one_owner(owner, carry):
         mine = pl.program_id(0) * STEP_OWNERS + owner == idx[0] * 2 + idx[1]
         row, col = 0, 0
         for part_ref, got_ref in zip(refs[:-2:2], refs[1:-2:2]):
@@ -820,6 +841,9 @@
                 col += piece.shape[1]
                 if col == width:
                     row, col = row + rows, 0
+        return carry
+
+    lax.fori_loop(0, STEP_OWNERS, one_owner, 0)
 
 
 def chip_sum(idx, pairs):
@@ -961,9 +985,8 @@
 
     in_low = in_weight.astype(BF)
     dt_low = jnp.pad(dt_weight.astype(BF), ((0, 0), (0, 128 - HEADS)))
-    main = lax.all_gather(
-        jnp.concatenate([in_low[:, DI:], dt_low], axis=1), AXES, axis=0, tiled=True
-    )
+    main = lax.all_gather(in_low[:, DI : 2 * DI], AXES, axis=0, tiled=True)
+    side_low = jnp.concatenate([in_low[:, 2 * DI :], dt_low], axis=1)
     part = jnp.arange(128)
     channel = jnp.arange(DI)
     emat = (
@@ -983,22 +1006,30 @@
     gate_low, out_low = in_low[:, :DI], out_weight.astype(BF)
     if direct:
         order = ("z", "x")
+        side_near = pick(side_low.reshape(2, -1, WIDE - DI), idx[3])
+        side_near = around(around(side_near, "z"), "x")
+        side_far = swapped(side_near, "core", 2, 1)
+        side_got = swapped(side_near, "seq", 2, 1)
+        side = assemble(
+            idx, (side_near, side_got, side_far, swapped(side_got, "core", 2, 1)), order
+        )
         gate_near = pick(gate_low.reshape(2, -1, DI), idx[3])
         out_near = pick(out_low.reshape(2, -1, D), idx[3])
         gate_near = around(around(gate_near, "z"), "x")
         out_near = around(around(out_near, "z"), "x")
-        main = lax.optimization_barrier((main, gate_near, out_near) + tables)[0]
+        main = lax.optimization_barrier((main, side, gate_near, out_near) + tables)[0]
         gate_got = swapped(gate_near, "seq", 2, 1)
         out_got = swapped(out_near, "seq", 2, 1)
         gate_far = swapped(gate_near, "core", 2, 1)
         out_far = swapped(out_near, "core", 2, 1)
     else:
+        side = lax.all_gather(side_low, AXES, axis=0, tiled=True)
         wg = lax.all_gather(gate_low, AXES, axis=0, tiled=True)
         wo = lax.all_gather(out_low, AXES, axis=0, tiled=True)
     halo = lax.ppermute(block_input[:, local_len - 8 :, :], "seq", up)
 
     normed, mixed, pre, z, local_state, total = run_first(
-        block_input, halo, gain8, main, cw8, cb8, dtb, alog, emat
+        block_input, halo, gain8, main, side, cw8, cb8, dtb, alog, emat
     )
     span = jnp.repeat(jnp.exp(total[:, 0:1, :HEADS]), HEADDIM, axis=2)
     enter = lax.ppermute(local_state, "seq", up)
@@ -1042,7 +1073,7 @@
     mgrad_rows = mgrad.reshape(row_count, WIDE)
     mixed_local = dot(normed_rows, mgrad_rows, TN)
     input_grad, gain_rows = run_back(
-        gate_grad, mgrad_rows, wg, main, block_input.reshape(row_count, D), upstream, gain8
+        gate_grad, mgrad_rows, wg, main, side, block_input.reshape(row_count, D), upstream, gain8
     )
     input_grad = input_grad.reshape(block_input.shape)
 
@@ -1082,16 +1113,16 @@
     in_grad = jnp.concatenate([gate_sum, mixed_sum[:, :CONVCH]], axis=1)
     dt_grad = mixed_sum[:, CONVCH : CONVCH + HEADS]
 
-    gate_tiles = kron_tiles(gate_sum, in_left, in_right, in_left_root, in_right_root, 0, 2)
+    gate_tiles = kron_tiles(gate_sum, in_left, in_right, in_left_root, in_right_root, 0, 6)
     in_update, in_left_new, in_right_new = kron_tiles(
-        mixed_sum[:, :CONVCH], in_left, in_right, in_left_root, in_right_root, DI // COL_BLOCK, 2,
+        mixed_sum[:, :CONVCH], in_left, in_right, in_left_root, in_right_root, DI // COL_BLOCK, 7,
         gate_tiles,
     )
     dt_update, dt_left_wide, dt_right_wide = kron_update(
         dt_grad, dt_left[:, None], dt_right[:, None], dt_left_root[:, None], dt_right_root[:, None]
     )
     out_update, out_left_new, out_right_new = kron_tiles(
-        out_grad, out_left, out_right, out_left_root, out_right_root, 0, 1
+        out_grad, out_left, out_right, out_left_root, out_right_root, 0, 3
     )
     vector_moment_new = 0.5 * vector_moment + 0.5 * vector_grad * vector_grad
     vector_update = -LR_VEC * vector_grad * lax.rsqrt(vector_moment_new)

time: 357 us -> 361 us (1.011)
  waiting for transfers between devices: 73.4 us -> 60.3 us
  starting transfers between devices: 44.3 us -> 55.3 us
  Pallas kernels: 164 us -> 169 us
    all_gather x1, waiting for transfers between devices: 12.2 us -> 0.43 us  [body(): main = lax.all_gather(in_low[:, DI:2 * DI], AXES, axis=0, tiled=True)]
    ppermute x19 -> x26, starting transfers between devices: 18.6 us -> 22.7 us  [swapped(): lax.ppermute(v, axis, [(i, (i + offset) % size) for i in range(size)])]
    pallas_call x1, Pallas kernels: 17 us -> 20.9 us  [run_first(): pl.pallas_call(first_kernel, grid=grid, in_specs=[tok(D), per(8, D), whol...]
    all_to_all x1, starting transfers between devices: 3.84 us -> 7.73 us  [body(): lax.all_to_all(early, ('z', 'x'), split_axis=0, concat_axis=0, tiled=True)]
    ppermute x1, waiting for transfers between devices: 6.12 us -> 2.24 us  [body(): leave = lax.ppermute(local_dstate, 'seq', down)]
    ppermute x19 -> x26, waiting for transfers between devices: 27.4 us -> 30.6 us  [swapped(): lax.ppermute(v, axis, [(i, (i + offset) % size) for i in range(size)])]
    pallas_call x2 -> x3, Pallas kernels: 7.79 us -> 10.4 us  [assemble(): pl.pallas_call(functools.partial(assemble_kernel, order=order), grid_spec...]
    unnamed x73 -> x81, local copies, waits for them, and re-layouts: 16.3 us -> 17.6 us
  transfers between devices with their start and end apart: 31 -> 38, of which waited for: 16 -> 17; matrix products, arithmetic and copies ran while one was open for 9% -> 9% of each run, Pallas kernels for 31% -> 32%
where the time goes in v7:
time: 361 us; the launch traced here: 360 us
  Pallas kernels  169 us (47%)
  waiting for transfers between devices  60.3 us (17%)
  starting transfers between devices  55.3 us (15%)
  local copies, waits for them, and re-layouts  33 us (9%)
  matrix products  16.9 us (5%)
  between operations  14.7 us (4%)
  other arithmetic  10.1 us (3%)
    pallas_call x1, Pallas kernels, run_second(): pl.pallas_call(second_kernel, grid=grid, in_specs=[tok(CONVCH), tok(128),...  44.6 us
    pallas_call x1, Pallas kernels, run_third(): pl.pallas_call(third_kernel, grid=grid, in_specs=[tok(CONVCH), tok(CONVCH...  40.6 us
    ppermute x26, waiting for transfers between devices, swapped(): lax.ppermute(v, axis, [(i, (i + offset) % size) for i in range(size)])  30.6 us
    ppermute x26, starting transfers between devices, swapped(): lax.ppermute(v, axis, [(i, (i + offset) % size) for i in range(size)])  22.7 us
    pallas_call x3, Pallas kernels, kron_tiles(): pl.pallas_call(functools.partial(kron_kernel, unroll=max(1, 4 // row_tile...  21.6 us
    pallas_call x1, Pallas kernels, run_first(): pl.pallas_call(first_kernel, grid=grid, in_specs=[tok(D), per(8, D), whol...  20.9 us
    unnamed x81, local copies, waits for them, and re-layouts  17.6 us
    ppermute x5, waiting for transfers between devices, xor_sum(): v = v + lax.ppermute(v, axis, [(i, i ^ bit) for i in range(size)])  17.3 us
  transfers between devices with their start and end apart: 38, of which 17 were waited for; matrix products, arithmetic and copies ran while one was open for 9% of the time, Pallas kernels for 32%

profile of v7, /device:TPU:0, one launch (start us, length us, event | category | flops | bytes accessed | tf_op | source)
XLA Modules:
  0.0 359.6 jit_solution(9010545966891331986)
XLA Ops:
  9.9 5.1 %collective-permute-start.3 = (bf16[24,384]{1,0:T(8,128)(2,1)S(1)}, bf16[24,384]{1,0:T(8,128)(2,1)S(1)}, u32[]{:S(2)}, u32[]{:S(2)}) collective-permute-start(bf16[24,384]{1,0:T(8,128)(2,1)S(1)} %fusion.37), channel_id=1, source_target_pairs={{0,24},{8,0},{16,8},{24,16},{1,25},{9,1},{17,9},{25,17},{2,26},{10... | collective-permute-start | bytes 55304 | tf_op jit(solution)/shard_map/ppermute | solution.py:750
  15.6 2.5 collective-permute-start.9
  18.1 2.0 collective-permute-start.8
  22.9 2.2 collective-permute-done.9
  25.1 1.6 collective-permute-start.14
  27.4 3.5 collective-permute-start
  31.0 1.6 collective-permute-start.11
  33.9 2.5 collective-permute-done.13
  41.2 7.1 %collective-permute-done.15 = bf16[4,48,768]{2,1,0:T(8,128)(2,1)S(1)} collective-permute-done((bf16[4,48,768]{2,1,0:T(8,128)(2,1)S(1)}, bf16[4,48,768]{2,1,0:T(8,128)(2,1)S(1)}, u32[]{:S(2)}, u32[]{:S(2)}) %collective-permute-start.15) | collective-permute-done | bytes 294944 | tf_op jit(solution)/shard_map/ppermute | solution.py:750
  56.8 2.7 assemble.3
  60.5 20.9 %first.1 = (bf16[1,1024,768]{2,1,0:T(8,128)(2,1)}, bf16[1,1024,1792]{2,1,0:T(8,128)(2,1)}, f32[1,1024,1792]{2,1,0:T(8,128)}, f32[1,1024,128]{2,1,0:T(8,128)}, f3...) custom-call(bf16[1,1024,768]{2,1,0:T(8,128)(2,1)} %u_ref.3, bf16[1,8,768]{2,1,0:T(8,128)(2,1)} %copy-done.31, ...), custom_call_target="tpu_custom_call" | custom-call | tf_op jit(solution)/shard_map/first/pallas_call | solution.py:497
  81.5 3.1 collective-permute-start.16
  87.6 3.8 %assemble.4 = bf16[32,24,1536]{2,1,0:T(8,128)(2,1)} custom-call(s32[4]{0:T(128)} %pad_add_fusion.idx, bf16[2,4,24,1536]{3,2,1,0:T(8,128)(2,1)} %copy-done.9, bf16[2,4,24,1536]{3,2,1,0:T(8,128)(2,1)} %copy-done.15, bf16[2,4,24,1536]{3,2,1,0:T(8,128)(2,1)} %copy-done.17, bf16[2,4,24,1536]{3,2,1,0:T(8,128)(2,1)} %collective-permute-done.19.refs_3_), custom_call_target="tpu_custom_call" | custom-call | tf_op jit(solution)/shard_map/assemble/pallas_call | solution.py:938
  91.4 3.9 %assemble.5 = bf16[32,48,768]{2,1,0:T(8,128)(2,1)} custom-call(s32[4]{0:T(128)} %pad_add_fusion.idx, bf16[2,4,48,768]{3,2,1,0:T(8,128)(2,1)} %copy-done.10, bf16[2,4,48,768]{3,2,1,0:T(8,128)(2,1)} %copy-done.16, bf16[2,4,48,768]{3,2,1,0:T(8,128)(2,1)} %collective-permute-done.21.refs_2_, bf16[2,4,48,768]{3,2,1,0:T(8,128)(2,1)} %collective-permute-done.22.refs_3_), custom_call_target="tpu_custom_call" | custom-call | tf_op jit(solution)/shard_map/assemble/pallas_call | solution.py:938
  95.3 1.7 copy.70
  97.0 4.1 %collective-permute-done.16.enter_ref = f32[1,128,1536]{2,1,0:T(8,128)} collective-permute-done((f32[1,128,1536]{2,1,0:T(8,128)}, f32[1,128,1536]{2,1,0:T(8,128)}, u32[]{:S(2)}, u32[]{:S(2)}) %collective-permute-start.16) | collective-permute-done | bytes 786464 | tf_op jit(solution)/shard_map/ppermute | solution.py:1035
  101.1 44.6 %second.1 = (bf16[1,1024,768]{2,1,0:T(8,128)(2,1)}, bf16[1024,1536]{1,0:T(8,128)(2,1)}, bf16[1024,1536]{1,0:T(8,128)(2,1)}, bf16[1024,1536]{1,0:T(8,128)(2,1)}, ...) custom-call(f32[1,1024,1792]{2,1,0:T(8,128)} %get-tuple-element.56.pre_ref, ...), custom_call_target="tpu_custom_call" | custom-call | tf_op jit(solution)/shard_map/second/pallas_call | solution.py:532
  145.8 4.5 %fusion.2.refs_0_ = f32[8,2,48,1536]{3,2,1,0:T(8,128)S(1)} fusion(bf16[8,2,48,1024]{3,2,1,0:T(8,128)(2,1)S(1)} %bitcast.109, bf16[1024,1536]{1,0:T(8,128)(2,1)} %get-tuple-element.61.ggrad_ref), kind=kOutput, calls=%fused_computation.2 | convolution fusion | flops 2415919104 | bytes 9437184 | tf_op jit(solution)/shard_map/dot_general | solution.py:40
  150.3 2.1 copy-done.2
  152.4 1.6 dynamic-slice_bitcast_fusion.2
  154.0 4.8 %copy.71 = bf16[1536,1024]{1,0:T(8,128)(2,1)} copy(bf16[1536,1024]{0,1:T(8,128)(2,1)} %bitcast.106) | data formatting | bytes 6291456 | tf_op jit(solution)/shard_map/dot_general | solution.py:40
  158.8 4.5 %fusion.4.refs_2_ = f32[8,2,96,768]{3,2,1,0:T(8,128)S(1)} fusion(bf16[8,2,96,1024]{3,2,1,0:T(8,128)(2,1)} %bitcast.107, bf16[1,1024,768]{2,1,0:T(8,128)(2,1)S(1)} %copy-done.5), kind=kOutput, calls=%fused_computation.7 | convolution fusion | flops 2415919104 | bytes 9437184 | tf_op jit(solution)/shard_map/dot_general | solution.py:40
  163.4 2.1 copy-done.3
  167.5 2.9 collective-permute-done.24.refs_3_
  171.8 6.1 %chip_sum.2 = (bf16[8,96,1536]{2,1,0:T(8,128)(2,1)}, f32[96,1536]{1,0:T(8,128)}) custom-call(s32[4]{0:T(128)} %pad_add_fusion.idx, f32[8,2,48,1536]{3,2,1,0:T(8,128)} %copy-done.2, f32[8,48,1536]{2,1,0:T(8,128)} %collective-permute-done.23.refs_1_, f32[8,2,96,768]{3,2,1,0:T(8,128)} %copy-done.3, f32[8,96,768]{2,1,0:T(8,128)} %copy-done.11), custom_call_target="tpu_custom_call" | custom-call | tf_op jit(solution)/shard_map/chip_sum/pallas_call | solution.py:861
  177.9 7.7 %all-to-all-start = ((bf16[8,96,1536]{2,1,0:T(8,128)(2,1)}), bf16[8,96,1536]{2,1,0:T(8,128)(2,1)S(1)}, u32[]{:S(2)}, u32[]{:S(2)}) async-start(bf16[8,96,1536]{2,1,0:T(8,128)(2,1)} %get-tuple-element.76), calls=%async_computation | async-start | bytes 4718592 | tf_op jit(solution)/shard_map/all_to_all | solution.py:1063
  185.7 2.2 collective-permute-done.25.leave_ref
  188.8 40.6 %third.1 = (bf16[1,1024,1920]{2,1,0:T(8,128)(2,1)}, f32[1,8,1792]{2,1,0:T(8,128)}, f32[1,8,1792]{2,1,0:T(8,128)}, f32[8,1792]{1,0:T(8,128)}) custom-call(f32[1,1024,1792]{2,1,0:T(8,128)} %get-tuple-element.56.pre_ref, bf16[1,1024,1792]{2,1,0:T(8,128)(2,1)} %get-tuple-element.62.mixed_ref, f32[1,1024,128]{2,1,0:T(8,128)} %get-tuple-element.57.z_ref, ...), custom_call_target="tpu_custom_call" | custom-call | tf_op jit(solution)/shard_map/third/pallas_call | solution.py:570
  230.7 5.0 %collective-permute-done.26.near_ref = f32[1,8,1792]{2,1,0:T(8,128)S(1)} collective-permute-done((f32[1,8,1792]{2,1,0:T(8,128)}, f32[1,8,1792]{2,1,0:T(8,128)S(1)}, u32[]{:S(2)}, u32[]{:S(2)}) %collective-permute-start.26) | collective-permute-done | bytes 57376 | tf_op jit(solution)/shard_map/ppermute | solution.py:1068
  236.3 1.6 patch.1
  237.9 6.0 %fusion.refs_0_ = f32[8,2,48,1920]{3,2,1,0:T(8,128)S(1)} fusion(bf16[8,2,48,1024]{3,2,1,0:T(8,128)(2,1)} %bitcast.108, bf16[1,1024,1920]{2,1,0:T(8,128)(2,1)} %get-tuple-element.73), kind=kOutput, calls=%fused_computation | convolution fusion | flops 3019898880 | bytes 11403264 | tf_op jit(solution)/shard_map/dot_general | solution.py:40
  244.1 2.3 copy-done.1
  246.5 5.5 %collective-permute-done.28.refs_1_ = f32[8,48,1920]{2,1,0:T(8,128)} collective-permute-done((f32[8,48,1920]{2,1,0:T(8,128)S(1)}, f32[8,48,1920]{2,1,0:T(8,128)}, u32[]{:S(2)}, u32[]{:S(2)}) %collective-permute-start.28) | collective-permute-done | bytes 2949152 | tf_op jit(solution)/shard_map/ppermute | solution.py:750
  252.0 4.6 %chip_sum.3 = (bf16[8,48,1920]{2,1,0:T(8,128)(2,1)}, f32[48,1920]{1,0:T(8,128)}) custom-call(s32[4]{0:T(128)} %pad_add_fusion.idx, f32[8,2,48,1920]{3,2,1,0:T(8,128)} %copy-done.1, f32[8,48,1920]{2,1,0:T(8,128)} %collective-permute-done.28.refs_1_), custom_call_target="tpu_custom_call" | custom-call | tf_op jit(solution)/shard_map/chip_sum/pallas_call | solution.py:861
  256.6 7.7 %all-to-all-start.1 = ((bf16[8,48,1920]{2,1,0:T(8,128)(2,1)}), bf16[8,48,1920]{2,1,0:T(8,128)(2,1)}, u32[]{:S(2)}, u32[]{:S(2)}) async-start(bf16[8,48,1920]{2,1,0:T(8,128)(2,1)} %get-tuple-element.78), calls=%async_computation.1 | async-start | bytes 2949120 | tf_op jit(solution)/shard_map/all_to_all | solution.py:1094
  265.5 12.0 %back.1 = (f32[1024,768]{1,0:T(8,128)}, f32[8,768]{1,0:T(8,128)}) custom-call(bf16[1024,1536]{1,0:T(8,128)(2,1)} %get-tuple-element.61.ggrad_ref, bf16[1024,1920]{1,0:T(8,128)(2,1)} %bitcast.98, bf16[768,1536]{1,0:T(8,128)(2,1)} %bitcast.97, bf16[768,1536]{1,0:T(8,128)(2,1)} %all-gather.2.cloned.1.call-done.w_ref.main_ref, bf16[768,384]{1,0:T(8,128)(2,1)} %bitcast.105, ...), custom_call_target="tpu_custom_call" | custom-call | tf_op jit(solution)/shard_map/back/pallas_call | solution.py:733
  278.5 3.4 owner_sum.2
  282.0 2.1 collective-permute-start.31
  284.1 14.9 %collective-permute-done.31 = f32[96,128]{1,0:T(8,128)S(1)} collective-permute-done((f32[96,128]{1,0:T(8,128)S(1)}, f32[96,128]{1,0:T(8,128)S(1)}, u32[]{:S(2)}, u32[]{:S(2)}) %collective-permute-start.31) | collective-permute-done | bytes 49184 | tf_op jit(solution)/shard_map/ppermute | solution.py:814
  303.7 1.8 collective-permute-start.33
  305.6 2.3 collective-permute-done.33
  307.9 2.4 collective-permute-start.34
  311.8 6.9 %kron.3 = (f32[48,3328]{1,0:T(8,128)}, f32[2,26,24,24]{3,2,1,0:T(8,128)}, f32[2,26,128,128]{3,2,1,0:T(8,128)}) custom-call(f32[48,1536]{1,0:T(8,128)} %slice.68.refs_0_, f32[2,26,24,24]{3,2,1,0:T(8,128)} %copy.74.refs_1_, f32[2,26,128,128]{3,2,1,0:T(8,128)} %refs_2_.4, f32[2,26,24,24]{3,2,1,0:T(8,128)} %copy.75.refs_3_, f32[2,26,128,128]{3,2,1,0:T(8,128)} %refs_4_.4), custom_call_target="tpu_custom_call" | custom-call | tf_op jit(solution)/shard_map/kron/pallas_call | solution.py:686
  318.7 6.9 %kron.5 = (f32[96,768]{1,0:T(8,128)}, f32[4,6,24,24]{3,2,1,0:T(8,128)}, f32[4,6,128,128]{3,2,1,0:T(8,128)}) custom-call(f32[96,768]{1,0:T(8,128)} %pad_maximum_fusion.5.refs_0_, f32[4,6,24,24]{3,2,1,0:T(8,128)} %refs_1_.3, f32[4,6,128,128]{3,2,1,0:T(8,128)} %refs_2_.5, f32[4,6,24,24]{3,2,1,0:T(8,128)} %refs_3_.3, f32[4,6,128,128]{3,2,1,0:T(8,128)} %refs_4_.5), custom_call_target="tpu_custom_call" | custom-call | tf_op jit(solution)/shard_map/kron/pallas_call | solution.py:686
  325.5 3.3 owner_sum.3
  329.9 7.5 %collective-permute-done.29 = f32[48,1920]{1,0:T(8,128)S(1)} collective-permute-done((f32[48,1920]{1,0:T(8,128)}, f32[48,1920]{1,0:T(8,128)S(1)}, u32[]{:S(2)}, u32[]{:S(2)}) %collective-permute-start.29) | collective-permute-done | bytes 368672 | tf_op jit(solution)/shard_map/ppermute | solution.py:750
  341.1 7.8 %kron.4 = (f32[48,3328]{1,0:T(8,128)}, f32[2,26,24,24]{3,2,1,0:T(8,128)}, f32[2,26,128,128]{3,2,1,0:T(8,128)}) custom-call(f32[48,1792]{1,0:T(8,128)} %copy-done.7, f32[2,26,24,24]{3,2,1,0:T(8,128)} %copy.74.refs_1_, f32[2,26,128,128]{3,2,1,0:T(8,128)} %refs_2_.4, ...), custom_call_target="tpu_custom_call", output_to_operand_aliasing={{0}: (5, {}), {1}: (6, {}), {2}: (7, {})} | custom-call | tf_op jit(solution)/shard_map/kron/pallas_call | solution.py:686
  348.9 2.2 copy.81
  (195 shorter events, 46.2 us)
Async XLA Ops:
  7.2 332.9 %copy-start = (f32[2,24,24]{2,1,0:T(8,128)S(1)}, f32[2,24,24]{2,1,0:T(8,128)}, u32[]{:S(2)}) copy-start(f32[2,24,24]{2,1,0:T(8,128)} %param.43) | copy-start | bytes 13828
  7.2 52.7 %all-gather.2.cloned.1.call-start = ((), (), s32[]{:S(2)}) async-start(), calls=%async_computation.2 | async-start | bytes 2506752 | tf_op jit(solution)/shard_map/all_gather | solution.py:988
  9.9 17.3 %collective-permute-start.3 = (bf16[24,384]{1,0:T(8,128)(2,1)S(1)}, bf16[24,384]{1,0:T(8,128)(2,1)S(1)}, u32[]{:S(2)}, u32[]{:S(2)}) collective-permute-start(bf16[24,384]{1,0:T(8,128)(2,1)S(1)} %fusion.37), channel_id=1, source_target_pairs={{0,24},{8,0},{16,8},{24,16},{1,25},{9,1},{17,9},{25,17},{2,26},{10... | collective-permute-start | bytes 55304 | tf_op jit(solution)/shard_map/ppermute | solution.py:750
  15.1 12.4 %collective-permute-start.2 = (bf16[24,384]{1,0:T(8,128)(2,1)S(1)}, bf16[24,384]{1,0:T(8,128)(2,1)S(1)}, u32[]{:S(2)}, u32[]{:S(2)}) collective-permute-start(bf16[24,384]{1,0:T(8,128)(2,1)S(1)} %fusion.37), channel_id=1, source_target_pairs={{0,16},{8,24},{16,0},{24,8},{1,17},{9,25},{17,1},{25,9},{2,18},{10... | collective-permute-start | bytes 55304 | tf_op jit(solution)/shard_map/ppermute | solution.py:750
  15.1 7.8 %collective-permute-start.10 = (bf16[24,1536]{1,0:T(8,128)(2,1)S(1)}, bf16[24,1536]{1,0:T(8,128)(2,1)S(1)}, u32[]{:S(2)}, u32[]{:S(2)}) collective-permute-start(bf16[24,1536]{1,0:T(8,128)(2,1)S(1)} %fusion.36), channel_id=1, source_target_pairs={{0,24},{8,0},{16,8},{24,16},{1,25},{9,1},{17,9},{25,17},{2,26},{10... | collective-permute-start | bytes 221192 | tf_op jit(solution)/shard_map/ppermute | solution.py:750
  15.6 9.5 %collective-permute-start.9 = (bf16[24,1536]{1,0:T(8,128)(2,1)S(1)}, bf16[24,1536]{1,0:T(8,128)(2,1)S(1)}, u32[]{:S(2)}, u32[]{:S(2)}) collective-permute-start(bf16[24,1536]{1,0:T(8,128)(2,1)S(1)} %fusion.36), channel_id=1, source_target_pairs={{0,16},{8,24},{16,0},{24,8},{1,17},{9,25},{17,1},{25,9},{2,18},{10... | collective-permute-start | bytes 221192 | tf_op jit(solution)/shard_map/ppermute | solution.py:750
  18.1 8.6 %collective-permute-start.8 = (bf16[24,1536]{1,0:T(8,128)(2,1)S(1)}, bf16[24,1536]{1,0:T(8,128)(2,1)S(1)}, u32[]{:S(2)}, u32[]{:S(2)}) collective-permute-start(bf16[24,1536]{1,0:T(8,128)(2,1)S(1)} %fusion.36), channel_id=1, source_target_pairs={{0,8},{8,16},{16,24},{24,0},{1,9},{9,17},{17,25},{25,1},{2,10},{10... | collective-permute-start | bytes 221192 | tf_op jit(solution)/shard_map/ppermute | solution.py:750
  21.8 29.0 %copy-start.37 = (f32[24]{0:T(128)S(1)}, f32[24]{0:T(128)}, u32[]{:S(2)}) copy-start(f32[24]{0:T(128)} %param.34) | copy-start | bytes 292
  21.8 30.0 %copy-start.36 = (f32[24]{0:T(128)S(1)}, f32[24]{0:T(128)}, u32[]{:S(2)}) copy-start(f32[24]{0:T(128)} %param.33) | copy-start | bytes 292
  21.8 31.1 %copy-start.34 = (f32[768]{0:T(1024)S(1)}, f32[768]{0:T(1024)}, u32[]{:S(2)}) copy-start(f32[768]{0:T(1024)} %param.30) | copy-start | bytes 9220
  21.8 31.7 %copy-start.35 = (f32[24]{0:T(128)S(1)}, f32[24]{0:T(128)}, u32[]{:S(2)}) copy-start(f32[24]{0:T(128)} %param.35) | copy-start | bytes 292
  21.8 32.4 %copy-start.33 = (f32[1792]{0:T(1024)S(1)}, f32[1792]{0:T(1024)}, u32[]{:S(2)}) copy-start(f32[1792]{0:T(1024)} %param.32) | copy-start | bytes 21508
  21.8 33.0 %copy-start.32 = (f32[1536]{0:T(1024)S(1)}, f32[1536]{0:T(1024)}, u32[]{:S(2)}) copy-start(f32[1536]{0:T(1024)} %param.36) | copy-start | bytes 18436
  22.9 8.1 %collective-permute-start.1 = (bf16[24,384]{1,0:T(8,128)(2,1)S(1)}, bf16[24,384]{1,0:T(8,128)(2,1)S(1)}, u32[]{:S(2)}, u32[]{:S(2)}) collective-permute-start(bf16[24,384]{1,0:T(8,128)(2,1)S(1)} %fusion.37), channel_id=1, source_target_pairs={{0,8},{8,16},{16,24},{24,0},{1,9},{9,17},{17,25},{25,1},{2,10},{10... | collective-permute-start | bytes 55304 | tf_op jit(solution)/shard_map/ppermute | solution.py:750
  25.1 7.5 %collective-permute-start.14 = (bf16[48,768]{1,0:T(8,128)(2,1)S(1)}, bf16[48,768]{1,0:T(8,128)(2,1)S(1)}, u32[]{:S(2)}, u32[]{:S(2)}) collective-permute-start(bf16[48,768]{1,0:T(8,128)(2,1)S(1)} %fusion.35), channel_id=1, source_target_pairs={{0,24},{8,0},{16,8},{24,16},{1,25},{9,1},{17,9},{25,17},{2,26},{10... | collective-permute-start | bytes 221192 | tf_op jit(solution)/shard_map/ppermute | solution.py:750
  26.7 9.7 %collective-permute-start.13 = (bf16[48,768]{1,0:T(8,128)(2,1)S(1)}, bf16[48,768]{1,0:T(8,128)(2,1)S(1)}, u32[]{:S(2)}, u32[]{:S(2)}) collective-permute-start(bf16[48,768]{1,0:T(8,128)(2,1)S(1)} %fusion.35), channel_id=1, source_target_pairs={{0,16},{8,24},{16,0},{24,8},{1,17},{9,25},{17,1},{25,9},{2,18},{10... | collective-permute-start | bytes 221192 | tf_op jit(solution)/shard_map/ppermute | solution.py:750
  27.3 9.1 %collective-permute-start.12 = (bf16[48,768]{1,0:T(8,128)(2,1)S(1)}, bf16[48,768]{1,0:T(8,128)(2,1)S(1)}, u32[]{:S(2)}, u32[]{:S(2)}) collective-permute-start(bf16[48,768]{1,0:T(8,128)(2,1)S(1)} %fusion.35), channel_id=1, source_target_pairs={{0,8},{8,16},{16,24},{24,0},{1,9},{9,17},{17,25},{25,1},{2,10},{10... | collective-permute-start | bytes 221192 | tf_op jit(solution)/shard_map/ppermute | solution.py:750
  27.4 32.5 %collective-permute-start = (bf16[1,8,768]{2,1,0:T(8,128)(2,1)S(1)}, bf16[1,8,768]{2,1,0:T(8,128)(2,1)S(1)}, u32[]{:S(2)}, u32[]{:S(2)}) collective-permute-start(bf16[1,8,768]{2,1,0:T(8,128)(2,1)S(1)} %slice.49), channel_id=1, source_target_pairs={{0,1},{2,3},{4,5},{6,7},{8,9},{10,11},{12,13},{14,15},{16,17},{18,... | collective-permute-start | bytes 36872 | tf_op jit(solution)/shard_map/ppermute | solution.py:1029
  31.0 8.6 %collective-permute-start.11 = (bf16[4,24,1536]{2,1,0:T(8,128)(2,1)S(1)}, bf16[4,24,1536]{2,1,0:T(8,128)(2,1)S(1)}, u32[]{:S(2)}, u32[]{:S(2)}) collective-permute-start(bf16[4,24,1536]{2,1,0:T(8,128)(2,1)S(1)} %get-tuple-element.156), channel_id=1, source_target_pairs={{0,4},{4,0},{1,5},{5,1},{2,6},{6,2},{3,7},{7,3},{8,12},{12,8},{9,1... | collective-permute-start | bytes 884744 | tf_op jit(solution)/shard_map/ppermute | solution.py:750
  32.6 6.3 %collective-permute-start.4 = (bf16[4,24,384]{2,1,0:T(8,128)(2,1)S(1)}, bf16[4,24,384]{2,1,0:T(8,128)(2,1)S(1)}, u32[]{:S(2)}, u32[]{:S(2)}) collective-permute-start(bf16[4,24,384]{2,1,0:T(8,128)(2,1)S(1)} %get-tuple-element.158), channel_id=1, source_target_pairs={{0,4},{4,0},{1,5},{5,1},{2,6},{6,2},{3,7},{7,3},{8,12},{12,8},{9,1... | collective-permute-start | bytes 221192 | tf_op jit(solution)/shard_map/ppermute | solution.py:750
  36.5 11.8 %collective-permute-start.15 = (bf16[4,48,768]{2,1,0:T(8,128)(2,1)S(1)}, bf16[4,48,768]{2,1,0:T(8,128)(2,1)S(1)}, u32[]{:S(2)}, u32[]{:S(2)}) collective-permute-start(bf16[4,48,768]{2,1,0:T(8,128)(2,1)S(1)} %get-tuple-element.154), channel_id=1, source_target_pairs={{0,4},{4,0},{1,5},{5,1},{2,6},{6,2},{3,7},{7,3},{8,12},{12,8},{9,1... | collective-permute-start | bytes 884744 | tf_op jit(solution)/shard_map/ppermute | solution.py:750
  38.9 12.4 %collective-permute-start.5 = (bf16[2,4,24,384]{3,2,1,0:T(8,128)(2,1)S(1)}, bf16[2,4,24,384]{3,2,1,0:T(8,128)(2,1)S(1)}, u32[]{:S(2)}, u32[]{:S(2)}) collective-permute-start(bf16[2,4,24,384]{3,2,1,0:T(8,128)(2,1)S(1)} %pad_maximum_fusion.6.refs_0_), channel_id=1, source_target_pairs={{0,1},{1,0},{2,3},{3,2},{4,5},{5,4},{6,7},{7,6},{8,9},{9,8},{10,11... | collective-permute-start | bytes 442376 | tf_op jit(solution)/shard_map/ppermute | solution.py:750
  39.7 44.9 %copy-start.9 = (bf16[2,4,24,1536]{3,2,1,0:T(8,128)(2,1)}, bf16[2,4,24,1536]{3,2,1,0:T(8,128)(2,1)S(1)}, u32[]{:S(2)}) copy-start(bf16[2,4,24,1536]{3,2,1,0:T(8,128)(2,1)S(1)} %pad_maximum_fusion.1.refs_0_) | copy-start | bytes 1769476
  39.7 44.9 %collective-permute-start.17 = (bf16[2,4,24,1536]{3,2,1,0:T(8,128)(2,1)S(1)}, bf16[2,4,24,1536]{3,2,1,0:T(8,128)(2,1)S(1)}, u32[]{:S(2)}, u32[]{:S(2)}) collective-permute-start(bf16[2,4,24,1536]{3,2,1,0:T(8,128)(2,1)S(1)} %pad_maximum_fusion.1.refs_0_), channel_id=1, source_target_pairs={{0,1},{1,0},{2,3},{3,2},{4,5},{5,4},{6,7},{7,6},{8,9},{9,8},{10,11... | collective-permute-start | bytes 1769480 | tf_op jit(solution)/shard_map/ppermute | solution.py:750
  48.4 36.7 %copy-start.10 = (bf16[2,4,48,768]{3,2,1,0:T(8,128)(2,1)}, bf16[2,4,48,768]{3,2,1,0:T(8,128)(2,1)S(1)}, u32[]{:S(2)}) copy-start(bf16[2,4,48,768]{3,2,1,0:T(8,128)(2,1)S(1)} %pad_maximum_fusion.2.refs_0_) | copy-start | bytes 1769476
  48.4 36.8 %collective-permute-start.20 = (bf16[2,4,48,768]{3,2,1,0:T(8,128)(2,1)S(1)}, bf16[2,4,48,768]{3,2,1,0:T(8,128)(2,1)S(1)}, u32[]{:S(2)}, u32[]{:S(2)}) collective-permute-start(bf16[2,4,48,768]{3,2,1,0:T(8,128)(2,1)S(1)} %pad_maximum_fusion.2.refs_0_), channel_id=1, source_target_pairs={{0,1},{1,0},{2,3},{3,2},{4,5},{5,4},{6,7},{7,6},{8,9},{9,8},{10,11... | collective-permute-start | bytes 1769480 | tf_op jit(solution)/shard_map/ppermute | solution.py:750
  51.3 4.2 %collective-permute-start.6 = (bf16[2,4,24,384]{3,2,1,0:T(8,128)(2,1)S(1)}, bf16[2,4,24,384]{3,2,1,0:T(8,128)(2,1)S(1)}, u32[]{:S(2)}, u32[]{:S(2)}) collective-permute-start(bf16[2,4,24,384]{3,2,1,0:T(8,128)(2,1)S(1)} %pad_maximum_fusion.6.refs_0_), channel_id=1, source_target_pairs={{0,2},{2,0},{1,3},{3,1},{4,6},{6,4},{5,7},{7,5},{8,10},{10,8},{9,1... | collective-permute-start | bytes 442376 | tf_op jit(solution)/shard_map/ppermute | solution.py:750
  51.3 4.2 %collective-permute-start.7 = (bf16[2,4,24,384]{3,2,1,0:T(8,128)(2,1)S(1)}, bf16[2,4,24,384]{3,2,1,0:T(8,128)(2,1)S(1)}, u32[]{:S(2)}, u32[]{:S(2)}) collective-permute-start(bf16[2,4,24,384]{3,2,1,0:T(8,128)(2,1)S(1)} %collective-permute-done.5.refs_1_), channel_id=1, source_target_pairs={{0,2},{2,0},{1,3},{3,1},{4,6},{6,4},{5,7},{7,5},{8,10},{10,8},{9,1... | collective-permute-start | bytes 442376 | tf_op jit(solution)/shard_map/ppermute | solution.py:750
  81.5 19.7 %collective-permute-start.16 = (f32[1,128,1536]{2,1,0:T(8,128)}, f32[1,128,1536]{2,1,0:T(8,128)}, u32[]{:S(2)}, u32[]{:S(2)}) collective-permute-start(f32[1,128,1536]{2,1,0:T(8,128)} %get-tuple-element.59), channel_id=1, source_target_pairs={{0,1},{2,3},{4,5},{6,7},{8,9},{10,11},{12,13},{14,15},{16,17},{18,... | collective-permute-start | bytes 2359304 | tf_op jit(solution)/shard_map/ppermute | solution.py:1035
  84.6 2.0 collective-permute-start.18
  84.6 3.0 collective-permute-start.19
  85.1 6.3 %collective-permute-start.21 = (bf16[2,4,48,768]{3,2,1,0:T(8,128)(2,1)S(1)}, bf16[2,4,48,768]{3,2,1,0:T(8,128)(2,1)}, u32[]{:S(2)}, u32[]{:S(2)}) collective-permute-start(bf16[2,4,48,768]{3,2,1,0:T(8,128)(2,1)S(1)} %pad_maximum_fusion.2.refs_0_), channel_id=1, source_target_pairs={{0,2},{2,0},{1,3},{3,1},{4,6},{6,4},{5,7},{7,5},{8,10},{10,8},{9,1... | collective-permute-start | bytes 1769480 | tf_op jit(solution)/shard_map/ppermute | solution.py:750
  85.2 6.2 %collective-permute-start.22 = (bf16[2,4,48,768]{3,2,1,0:T(8,128)(2,1)S(1)}, bf16[2,4,48,768]{3,2,1,0:T(8,128)(2,1)}, u32[]{:S(2)}, u32[]{:S(2)}) collective-permute-start(bf16[2,4,48,768]{3,2,1,0:T(8,128)(2,1)S(1)} %collective-permute-done.20.refs_1_), channel_id=1, source_target_pairs={{0,2},{2,0},{1,3},{3,1},{4,6},{6,4},{5,7},{7,5},{8,10},{10,8},{9,1... | collective-permute-start | bytes 1769480 | tf_op jit(solution)/shard_map/ppermute | solution.py:750
  101.1 44.7 %copy-start.13 = (bf16[768,1024]{1,0:T(8,128)(2,1)S(1)}, bf16[768,1024]{1,0:T(8,128)(2,1)}, u32[]{:S(2)}) copy-start(bf16[768,1024]{1,0:T(8,128)(2,1)} %copy.70) | copy-start | bytes 4718596
  154.0 13.5 %collective-permute-start.23 = (f32[8,48,1536]{2,1,0:T(8,128)}, f32[8,48,1536]{2,1,0:T(8,128)}, u32[]{:S(2)}, u32[]{:S(2)}) collective-permute-start(f32[8,48,1536]{2,1,0:T(8,128)} %dynamic-slice_bitcast_fusion.2), channel_id=1, source_target_pairs={{0,2},{2,0},{1,3},{3,1},{4,6},{6,4},{5,7},{7,5},{8,10},{10,8},{9,1... | collective-permute-start | bytes 7077896 | tf_op jit(solution)/shard_map/ppermute | solution.py:750
  165.7 4.7 %collective-permute-start.24 = (f32[8,96,768]{2,1,0:T(8,128)S(1)}, f32[8,96,768]{2,1,0:T(8,128)S(1)}, u32[]{:S(2)}, u32[]{:S(2)}) collective-permute-start(f32[8,96,768]{2,1,0:T(8,128)S(1)} %dynamic-slice_bitcast_fusion.1), channel_id=1, source_target_pairs={{0,2},{2,0},{1,3},{3,1},{4,6},{6,4},{5,7},{7,5},{8,10},{10,8},{9,1... | collective-permute-start | bytes 7077896 | tf_op jit(solution)/shard_map/ppermute | solution.py:750
  166.2 21.7 %collective-permute-start.25 = (f32[1,128,1536]{2,1,0:T(8,128)}, f32[1,128,1536]{2,1,0:T(8,128)S(1)}, u32[]{:S(2)}, u32[]{:S(2)}) collective-permute-start(f32[1,128,1536]{2,1,0:T(8,128)} %get-tuple-element.69), channel_id=1, source_target_pairs={{1,0},{3,2},{5,4},{7,6},{9,8},{11,10},{13,12},{15,14},{17,16},{19,... | collective-permute-start | bytes 2359304 | tf_op jit(solution)/shard_map/ppermute | solution.py:1052
  177.9 78.6 %all-to-all-start = ((bf16[8,96,1536]{2,1,0:T(8,128)(2,1)}), bf16[8,96,1536]{2,1,0:T(8,128)(2,1)S(1)}, u32[]{:S(2)}, u32[]{:S(2)}) async-start(bf16[8,96,1536]{2,1,0:T(8,128)(2,1)} %get-tuple-element.76), calls=%async_computation | async-start | bytes 4718592 | tf_op jit(solution)/shard_map/all_to_all | solution.py:1063
  229.4 6.3 %collective-permute-start.26 = (f32[1,8,1792]{2,1,0:T(8,128)}, f32[1,8,1792]{2,1,0:T(8,128)S(1)}, u32[]{:S(2)}, u32[]{:S(2)}) collective-permute-start(f32[1,8,1792]{2,1,0:T(8,128)} %get-tuple-element.72), channel_id=1, source_target_pairs={{1,0},{3,2},{5,4},{7,6},{9,8},{11,10},{13,12},{15,14},{17,16},{19,... | collective-permute-start | bytes 172040 | tf_op jit(solution)/shard_map/ppermute | solution.py:1068
  246.5 5.5 %collective-permute-start.28 = (f32[8,48,1920]{2,1,0:T(8,128)S(1)}, f32[8,48,1920]{2,1,0:T(8,128)}, u32[]{:S(2)}, u32[]{:S(2)}) collective-permute-start(f32[8,48,1920]{2,1,0:T(8,128)S(1)} %dynamic-slice_bitcast_fusion), channel_id=1, source_target_pairs={{0,2},{2,0},{1,3},{3,1},{4,6},{6,4},{5,7},{7,5},{8,10},{10,8},{9,1... | collective-permute-start | bytes 8847368 | tf_op jit(solution)/shard_map/ppermute | solution.py:750
  256.6 43.0 %all-to-all-start.1 = ((bf16[8,48,1920]{2,1,0:T(8,128)(2,1)}), bf16[8,48,1920]{2,1,0:T(8,128)(2,1)}, u32[]{:S(2)}, u32[]{:S(2)}) async-start(bf16[8,48,1920]{2,1,0:T(8,128)(2,1)} %get-tuple-element.78), calls=%async_computation.1 | async-start | bytes 2949120 | tf_op jit(solution)/shard_map/all_to_all | solution.py:1094
  278.5 3.5 collective-permute-start.30
  282.0 21.6 %collective-permute-start.27 = (f32[96,1536]{1,0:T(8,128)}, f32[96,1536]{1,0:T(8,128)S(1)}, u32[]{:S(2)}, u32[]{:S(2)}) collective-permute-start(f32[96,1536]{1,0:T(8,128)} %owner_sum.2), channel_id=1, source_target_pairs={{0,1},{1,0},{2,3},{3,2},{4,5},{5,4},{6,7},{7,6},{8,9},{9,8},{10,11... | collective-permute-start | bytes 1769480 | tf_op jit(solution)/shard_map/ppermute | solution.py:750
  282.0 17.0 %collective-permute-start.31 = (f32[96,128]{1,0:T(8,128)S(1)}, f32[96,128]{1,0:T(8,128)S(1)}, u32[]{:S(2)}, u32[]{:S(2)}) collective-permute-start(f32[96,128]{1,0:T(8,128)S(1)} %fusion.15), channel_id=1, source_target_pairs={{0,1},{1,0},{2,3},{3,2},{4,5},{5,4},{6,7},{7,6},{8,9},{9,8},{10,11... | collective-permute-start | bytes 147464 | tf_op jit(solution)/shard_map/ppermute | solution.py:814
  299.6 4.1 %collective-permute-start.32 = (f32[96,128]{1,0:T(8,128)S(1)}, f32[96,128]{1,0:T(8,128)S(1)}, u32[]{:S(2)}, u32[]{:S(2)}) collective-permute-start(f32[96,128]{1,0:T(8,128)S(1)} %fusion.34), channel_id=1, source_target_pairs={{0,4},{4,0},{1,5},{5,1},{2,6},{6,2},{3,7},{7,3},{8,12},{12,8},{9,1... | collective-permute-start | bytes 147464 | tf_op jit(solution)/shard_map/ppermute | solution.py:814
  303.7 4.2 %collective-permute-start.33 = (f32[96,128]{1,0:T(8,128)S(1)}, f32[96,128]{1,0:T(8,128)S(1)}, u32[]{:S(2)}, u32[]{:S(2)}) collective-permute-start(f32[96,128]{1,0:T(8,128)S(1)} %add.97), channel_id=1, source_target_pairs={{0,8},{8,0},{16,24},{24,16},{1,9},{9,1},{17,25},{25,17},{2,10},{10... | collective-permute-start | bytes 147464 | tf_op jit(solution)/shard_map/ppermute | solution.py:814
  307.9 21.3 %collective-permute-start.34 = (f32[96,128]{1,0:T(8,128)S(1)}, f32[96,128]{1,0:T(8,128)S(1)}, u32[]{:S(2)}, u32[]{:S(2)}) collective-permute-start(f32[96,128]{1,0:T(8,128)S(1)} %add.98), channel_id=1, source_target_pairs={{0,16},{8,24},{16,0},{24,8},{1,17},{9,25},{17,1},{25,9},{2,18},{10... | collective-permute-start | bytes 147464 | tf_op jit(solution)/shard_map/ppermute | solution.py:814
  328.9 8.6 %collective-permute-start.29 = (f32[48,1920]{1,0:T(8,128)}, f32[48,1920]{1,0:T(8,128)S(1)}, u32[]{:S(2)}, u32[]{:S(2)}) collective-permute-start(f32[48,1920]{1,0:T(8,128)} %owner_sum.3), channel_id=1, source_target_pairs={{0,1},{1,0},{2,3},{3,2},{4,5},{5,4},{6,7},{7,6},{8,9},{9,8},{10,11... | collective-permute-start | bytes 1105928 | tf_op jit(solution)/shard_map/ppermute | solution.py:750
  (28 other events, 225.9 us)
Sparse Core Ops, SparseCore 0:
  10.9 49.0 all-gather.1

commit v8 on v6

--- a/solution.py
+++ b/solution.py
@@ -631,13 +631,14 @@
     return high, v - high
 
 
-def kron_kernel(*refs):
+def kron_kernel(*refs, unroll):
     grad_ref, left_ref, right_ref, left_root_ref, right_root_ref = refs[:5]
     update_ref, left_new_ref, right_new_ref = refs[-3:]
-    for r in range(left_ref.shape[0]):
-        rows = slice(r * ROW_BLOCK, (r + 1) * ROW_BLOCK)
-        for c in range(left_ref.shape[1]):
-            cols = slice(c * COL_BLOCK, (c + 1) * COL_BLOCK)
+
+    def column(c, carry):
+        cols = pl.ds(pl.multiple_of(c * COL_BLOCK, COL_BLOCK), COL_BLOCK)
+        for r in range(left_ref.shape[0]):
+            rows = slice(r * ROW_BLOCK, (r + 1) * ROW_BLOCK)
             grad = grad_ref[rows, cols]
             high, low = float_parts(grad)
             root_high, root_low = float_parts(left_root_ref[r, c])
@@ -654,14 +655,17 @@
             right_new_ref[r, c] = 0.5 * right_ref[r, c] + 0.5 * right
             shaped = dot_wide(*wide_split(rooted), *split2(right_root_ref[r, c]))
             update_ref[rows, cols] = -LR * shaped
+        return carry
+
+    lax.fori_loop(0, left_ref.shape[1], column, 0, unroll=unroll)
 
 
 def kron_tiles(grad, left, right, left_root, right_root, first, step, earlier=None):
     row_tiles = left.shape[0]
     rows, cols = grad.shape
-    base = first // step
     stat = lambda size: pl.BlockSpec(
-        (row_tiles, step, size, size), lambda i: (0, base + i, 0, 0)
+        tuple(pl.Element(n) for n in (row_tiles, step, size, size)),
+        lambda i: (0, first + step * i, 0, 0),
     )
     wide = step * COL_BLOCK
     ins = [grad, left, right, left_root, right_root]
@@ -673,11 +677,15 @@
         aliases = {5: 0, 6: 1, 7: 2}
     total = left.shape[1] * COL_BLOCK
     return pl.pallas_call(
-        kron_kernel,
+        functools.partial(kron_kernel, unroll=max(1, 4 // row_tiles)),
         grid=(cols // wide,),
         in_specs=in_specs,
         out_specs=[
-            pl.BlockSpec((rows, wide), lambda i: (0, base + i)), stat(ROW_BLOCK), stat(COL_BLOCK),
+            pl.BlockSpec(
+                (pl.Element(rows), pl.Element(wide)),
+                lambda i: (0, pl.multiple_of(first * COL_BLOCK + wide * i, COL_BLOCK)),
+            ),
+            stat(ROW_BLOCK), stat(COL_BLOCK),
         ],
         out_shape=[
             jax.ShapeDtypeStruct((rows, total), F32),
@@ -802,7 +810,8 @@
 def chip_kernel(idx, *refs):
     send_ref, own_ref = refs[-2:]
     width = own_ref.shape[1]
-    for owner in range(STEP_OWNERS):
+
+    def one_owner(owner, carry):
         mine = pl.program_id(0) * STEP_OWNERS + owner == idx[0] * 2 + idx[1]
         row, col = 0, 0
         for part_ref, got_ref in zip(refs[:-2:2], refs[1:-2:2]):
@@ -820,6 +829,9 @@
                 col += piece.shape[1]
                 if col == width:
                     row, col = row + rows, 0
+        return carry
+
+    lax.fori_loop(0, STEP_OWNERS, one_owner, 0)
 
 
 def chip_sum(idx, pairs):
@@ -1082,16 +1094,16 @@
     in_grad = jnp.concatenate([gate_sum, mixed_sum[:, :CONVCH]], axis=1)
     dt_grad = mixed_sum[:, CONVCH : CONVCH + HEADS]
 
-    gate_tiles = kron_tiles(gate_sum, in_left, in_right, in_left_root, in_right_root, 0, 2)
+    gate_tiles = kron_tiles(gate_sum, in_left, in_right, in_left_root, in_right_root, 0, 6)
     in_update, in_left_new, in_right_new = kron_tiles(
-        mixed_sum[:, :CONVCH], in_left, in_right, in_left_root, in_right_root, DI // COL_BLOCK, 2,
+        mixed_sum[:, :CONVCH], in_left, in_right, in_left_root, in_right_root, DI // COL_BLOCK, 7,
         gate_tiles,
     )
     dt_update, dt_left_wide, dt_right_wide = kron_update(
         dt_grad, dt_left[:, None], dt_right[:, None], dt_left_root[:, None], dt_right_root[:, None]
     )
     out_update, out_left_new, out_right_new = kron_tiles(
-        out_grad, out_left, out_right, out_left_root, out_right_root, 0, 1
+        out_grad, out_left, out_right, out_left_root, out_right_root, 0, 3
     )
     vector_moment_new = 0.5 * vector_moment + 0.5 * vector_grad * vector_grad
     vector_update = -LR_VEC * vector_grad * lax.rsqrt(vector_moment_new)

time: 357 us -> 355 us (level)
  no operation moved by 1% of the time
where the time goes in v8:
time: 355 us; the launch traced here: 354 us
  Pallas kernels  163 us (46%)
  waiting for transfers between devices  73.4 us (21%)
  starting transfers between devices  44.2 us (12%)
  local copies, waits for them, and re-layouts  31.1 us (9%)
  matrix products  16.9 us (5%)
  between operations  14.6 us (4%)
  other arithmetic  10.7 us (3%)
    pallas_call x1, Pallas kernels, run_second(): pl.pallas_call(second_kernel, grid=grid, in_specs=[tok(CONVCH), tok(128),...  44.6 us
    pallas_call x1, Pallas kernels, run_third(): pl.pallas_call(third_kernel, grid=grid, in_specs=[tok(CONVCH), tok(CONVCH...  40.6 us
    ppermute x19, waiting for transfers between devices, swapped(): lax.ppermute(v, axis, [(i, (i + offset) % size) for i in range(size)])  27.4 us
    pallas_call x3, Pallas kernels, kron_tiles(): pl.pallas_call(functools.partial(kron_kernel, unroll=max(1, 4 // row_tile...  21.6 us
    ppermute x19, starting transfers between devices, swapped(): lax.ppermute(v, axis, [(i, (i + offset) % size) for i in range(size)])  18.6 us
    ppermute x5, waiting for transfers between devices, xor_sum(): v = v + lax.ppermute(v, axis, [(i, i ^ bit) for i in range(size)])  17.8 us
    pallas_call x1, Pallas kernels, run_first(): pl.pallas_call(first_kernel, grid=grid, in_specs=[tok(D), per(8, D), whol...  17 us
    unnamed x73, local copies, waits for them, and re-layouts  16.3 us
  transfers between devices with their start and end apart: 31, of which 16 were waited for; matrix products, arithmetic and copies ran while one was open for 9% of the time, Pallas kernels for 31%

profile of v8, /device:TPU:0, one launch (start us, length us, event | category | flops | bytes accessed | tf_op | source)
XLA Modules:
  0.0 353.5 jit_solution(16737192795800935235)
XLA Ops:
  10.0 5.1 %collective-permute-start.3 = (bf16[24,1536]{1,0:T(8,128)(2,1)S(1)}, bf16[24,1536]{1,0:T(8,128)(2,1)S(1)}, u32[]{:S(2)}, u32[]{:S(2)}) collective-permute-start(bf16[24,1536]{1,0:T(8,128)(2,1)S(1)} %fusion.34), channel_id=1, source_target_pairs={{0,24},{8,0},{16,8},{24,16},{1,25},{9,1},{17,9},{25,17},{2,26},{10... | collective-permute-start | bytes 221192 | tf_op jit(solution)/shard_map/ppermute | solution.py:738
  17.2 2.9 collective-permute-start.7
  22.8 3.4 collective-permute-start
  26.3 1.6 collective-permute-start.4
  27.9 5.1 %collective-permute-done.6 = bf16[48,768]{1,0:T(8,128)(2,1)S(1)} collective-permute-done((bf16[48,768]{1,0:T(8,128)(2,1)S(1)}, bf16[48,768]{1,0:T(8,128)(2,1)S(1)}, u32[]{:S(2)}, u32[]{:S(2)}) %collective-permute-start.6) | collective-permute-done | bytes 73760 | tf_op jit(solution)/shard_map/ppermute | solution.py:738
  33.0 1.9 collective-permute-start.8
  35.9 1.6 collective-permute-start.10
  37.5 4.3 %collective-permute-done.8 = bf16[4,48,768]{2,1,0:T(8,128)(2,1)S(1)} collective-permute-done((bf16[4,48,768]{2,1,0:T(8,128)(2,1)S(1)}, bf16[4,48,768]{2,1,0:T(8,128)(2,1)S(1)}, u32[]{:S(2)}, u32[]{:S(2)}) %collective-permute-start.8) | collective-permute-done | bytes 294944 | tf_op jit(solution)/shard_map/ppermute | solution.py:738
  41.8 1.5 collective-permute-start.13
  47.9 12.2 %all-gather.2.cloned.1.call-done.w_ref.main_ref = bf16[768,1920]{1,0:T(8,128)(2,1)} async-done(((bf16[48,1920]{1,0:T(8,128)(2,1)}), bf16[768,1920]{1,0:T(8,128)(2,1)}) %all-gather.2.cloned.1.call-update) | async-done | bytes 2949136 | tf_op jit(solution)/shard_map/all_gather | solution.py:976
  60.7 17.0 %first.1 = (bf16[1,1024,768]{2,1,0:T(8,128)(2,1)}, bf16[1,1024,1792]{2,1,0:T(8,128)(2,1)}, f32[1,1024,1792]{2,1,0:T(8,128)}, f32[1,1024,128]{2,1,0:T(8,128)}, f3...) custom-call(bf16[1,1024,768]{2,1,0:T(8,128)(2,1)} %u_ref.3, bf16[1,8,768]{2,1,0:T(8,128)(2,1)} %copy-done.27, ...), custom_call_target="tpu_custom_call" | custom-call | tf_op jit(solution)/shard_map/first/pallas_call | solution.py:491
  77.8 4.3 %collective-permute-start.9 = (f32[1,128,1536]{2,1,0:T(8,128)}, f32[1,128,1536]{2,1,0:T(8,128)}, u32[]{:S(2)}, u32[]{:S(2)}) collective-permute-start(f32[1,128,1536]{2,1,0:T(8,128)} %get-tuple-element.59), channel_id=1, source_target_pairs={{0,1},{2,3},{4,5},{6,7},{8,9},{10,11},{12,13},{14,15},{16,17},{18,... | collective-permute-start | bytes 2359304 | tf_op jit(solution)/shard_map/ppermute | solution.py:1016
  85.0 3.8 %assemble.2 = bf16[32,24,1536]{2,1,0:T(8,128)(2,1)} custom-call(s32[4]{0:T(128)} %pad_add_fusion.idx, bf16[2,4,24,1536]{3,2,1,0:T(8,128)(2,1)} %copy-done.9, bf16[2,4,24,1536]{3,2,1,0:T(8,128)(2,1)} %copy-done.15, bf16[2,4,24,1536]{3,2,1,0:T(8,128)(2,1)} %copy-done.17, bf16[2,4,24,1536]{3,2,1,0:T(8,128)(2,1)} %collective-permute-done.12.refs_3_), custom_call_target="tpu_custom_call" | custom-call | tf_op jit(solution)/shard_map/assemble/pallas_call | solution.py:926
  88.9 4.0 %assemble.3 = bf16[32,48,768]{2,1,0:T(8,128)(2,1)} custom-call(s32[4]{0:T(128)} %pad_add_fusion.idx, bf16[2,4,48,768]{3,2,1,0:T(8,128)(2,1)} %copy-done.10, bf16[2,4,48,768]{3,2,1,0:T(8,128)(2,1)} %copy-done.16, bf16[2,4,48,768]{3,2,1,0:T(8,128)(2,1)} %collective-permute-done.14.refs_2_, bf16[2,4,48,768]{3,2,1,0:T(8,128)(2,1)} %collective-permute-done.15.refs_3_), custom_call_target="tpu_custom_call" | custom-call | tf_op jit(solution)/shard_map/assemble/pallas_call | solution.py:926
  92.8 1.7 copy.70
  94.5 4.1 %collective-permute-done.9.enter_ref = f32[1,128,1536]{2,1,0:T(8,128)} collective-permute-done((f32[1,128,1536]{2,1,0:T(8,128)}, f32[1,128,1536]{2,1,0:T(8,128)}, u32[]{:S(2)}, u32[]{:S(2)}) %collective-permute-start.9) | collective-permute-done | bytes 786464 | tf_op jit(solution)/shard_map/ppermute | solution.py:1016
  98.6 44.6 %second.1 = (bf16[1,1024,768]{2,1,0:T(8,128)(2,1)}, bf16[1024,1536]{1,0:T(8,128)(2,1)}, bf16[1024,1536]{1,0:T(8,128)(2,1)}, bf16[1024,1536]{1,0:T(8,128)(2,1)}, ...) custom-call(f32[1,1024,1792]{2,1,0:T(8,128)} %get-tuple-element.56.pre_ref, ...), custom_call_target="tpu_custom_call" | custom-call | tf_op jit(solution)/shard_map/second/pallas_call | solution.py:525
  143.3 4.5 %fusion.2.refs_0_ = f32[8,2,48,1536]{3,2,1,0:T(8,128)S(1)} fusion(bf16[8,2,48,1024]{3,2,1,0:T(8,128)(2,1)S(1)} %bitcast.97, bf16[1024,1536]{1,0:T(8,128)(2,1)} %get-tuple-element.61.ggrad_ref), kind=kOutput, calls=%fused_computation.2 | convolution fusion | flops 2415919104 | bytes 9437184 | tf_op jit(solution)/shard_map/dot_general | solution.py:40
  147.8 2.1 copy-done.2
  149.9 1.6 dynamic-slice_bitcast_fusion.2
  151.5 4.8 %copy.71 = bf16[1536,1024]{1,0:T(8,128)(2,1)} copy(bf16[1536,1024]{0,1:T(8,128)(2,1)} %bitcast.94) | data formatting | bytes 6291456 | tf_op jit(solution)/shard_map/dot_general | solution.py:40
  156.3 4.5 %fusion.4.refs_2_ = f32[8,2,96,768]{3,2,1,0:T(8,128)S(1)} fusion(bf16[8,2,96,1024]{3,2,1,0:T(8,128)(2,1)} %bitcast.95, bf16[1,1024,768]{2,1,0:T(8,128)(2,1)S(1)} %copy-done.5), kind=kOutput, calls=%fused_computation.7 | convolution fusion | flops 2415919104 | bytes 9437184 | tf_op jit(solution)/shard_map/dot_general | solution.py:40
  160.9 2.1 copy-done.3
  165.0 2.9 collective-permute-done.17.refs_3_
  169.3 6.1 %chip_sum.2 = (bf16[8,96,1536]{2,1,0:T(8,128)(2,1)}, f32[96,1536]{1,0:T(8,128)}) custom-call(s32[4]{0:T(128)} %pad_add_fusion.idx, f32[8,2,48,1536]{3,2,1,0:T(8,128)} %copy-done.2, f32[8,48,1536]{2,1,0:T(8,128)} %collective-permute-done.16.refs_1_, f32[8,2,96,768]{3,2,1,0:T(8,128)} %copy-done.3, f32[8,96,768]{2,1,0:T(8,128)} %copy-done.11), custom_call_target="tpu_custom_call" | custom-call | tf_op jit(solution)/shard_map/chip_sum/pallas_call | solution.py:849
  175.4 3.8 %all-to-all-start = ((bf16[8,96,1536]{2,1,0:T(8,128)(2,1)}), bf16[8,96,1536]{2,1,0:T(8,128)(2,1)S(1)}, u32[]{:S(2)}, u32[]{:S(2)}) async-start(bf16[8,96,1536]{2,1,0:T(8,128)(2,1)} %get-tuple-element.76), calls=%async_computation | async-start | bytes 4718592 | tf_op jit(solution)/shard_map/all_to_all | solution.py:1044
  179.3 6.2 %collective-permute-done.18.leave_ref = f32[1,128,1536]{2,1,0:T(8,128)S(1)} collective-permute-done((f32[1,128,1536]{2,1,0:T(8,128)}, f32[1,128,1536]{2,1,0:T(8,128)S(1)}, u32[]{:S(2)}, u32[]{:S(2)}) %collective-permute-start.18) | collective-permute-done | bytes 786464 | tf_op jit(solution)/shard_map/ppermute | solution.py:1033
  186.3 40.6 %third.1 = (bf16[1,1024,1920]{2,1,0:T(8,128)(2,1)}, f32[1,8,1792]{2,1,0:T(8,128)}, f32[1,8,1792]{2,1,0:T(8,128)}, f32[8,1792]{1,0:T(8,128)}) custom-call(f32[1,1024,1792]{2,1,0:T(8,128)} %get-tuple-element.56.pre_ref, bf16[1,1024,1792]{2,1,0:T(8,128)(2,1)} %get-tuple-element.62.mixed_ref, f32[1,1024,128]{2,1,0:T(8,128)} %get-tuple-element.57.z_ref, ...), custom_call_target="tpu_custom_call" | custom-call | tf_op jit(solution)/shard_map/third/pallas_call | solution.py:563
  228.2 5.0 %collective-permute-done.19.near_ref = f32[1,8,1792]{2,1,0:T(8,128)S(1)} collective-permute-done((f32[1,8,1792]{2,1,0:T(8,128)}, f32[1,8,1792]{2,1,0:T(8,128)S(1)}, u32[]{:S(2)}, u32[]{:S(2)}) %collective-permute-start.19) | collective-permute-done | bytes 57376 | tf_op jit(solution)/shard_map/ppermute | solution.py:1049
  233.8 1.6 patch.1
  235.4 6.0 %fusion.refs_0_ = f32[8,2,48,1920]{3,2,1,0:T(8,128)S(1)} fusion(bf16[8,2,48,1024]{3,2,1,0:T(8,128)(2,1)} %bitcast.96, bf16[1,1024,1920]{2,1,0:T(8,128)(2,1)} %get-tuple-element.73), kind=kOutput, calls=%fused_computation | convolution fusion | flops 3019898880 | bytes 11403264 | tf_op jit(solution)/shard_map/dot_general | solution.py:40
  241.6 2.3 copy-done.1
  244.0 5.5 %collective-permute-done.21.refs_1_ = f32[8,48,1920]{2,1,0:T(8,128)} collective-permute-done((f32[8,48,1920]{2,1,0:T(8,128)S(1)}, f32[8,48,1920]{2,1,0:T(8,128)}, u32[]{:S(2)}, u32[]{:S(2)}) %collective-permute-start.21) | collective-permute-done | bytes 2949152 | tf_op jit(solution)/shard_map/ppermute | solution.py:738
  249.5 4.6 %chip_sum.3 = (bf16[8,48,1920]{2,1,0:T(8,128)(2,1)}, f32[48,1920]{1,0:T(8,128)}) custom-call(s32[4]{0:T(128)} %pad_add_fusion.idx, f32[8,2,48,1920]{3,2,1,0:T(8,128)} %copy-done.1, f32[8,48,1920]{2,1,0:T(8,128)} %collective-permute-done.21.refs_1_), custom_call_target="tpu_custom_call" | custom-call | tf_op jit(solution)/shard_map/chip_sum/pallas_call | solution.py:849
  254.1 4.6 %all-to-all-start.1 = ((bf16[8,48,1920]{2,1,0:T(8,128)(2,1)}), bf16[8,48,1920]{2,1,0:T(8,128)(2,1)}, u32[]{:S(2)}, u32[]{:S(2)}) async-start(bf16[8,48,1920]{2,1,0:T(8,128)(2,1)} %get-tuple-element.78), calls=%async_computation.1 | async-start | bytes 2949120 | tf_op jit(solution)/shard_map/all_to_all | solution.py:1075
  259.8 11.9 %back.1 = (f32[1024,768]{1,0:T(8,128)}, f32[8,768]{1,0:T(8,128)}) custom-call(bf16[1024,1536]{1,0:T(8,128)(2,1)} %get-tuple-element.61.ggrad_ref, bf16[1024,1920]{1,0:T(8,128)(2,1)} %bitcast.88, bf16[768,1536]{1,0:T(8,128)(2,1)} %bitcast.87, bf16[768,1920]{1,0:T(8,128)(2,1)} %all-gather.2.cloned.1.call-done.w_ref.main_ref, bf16[1024,768]{1,0:T(8,128)(2,1)} %bitcast.89, ...), custom_call_target="tpu_custom_call" | custom-call | tf_op jit(solution)/shard_map/back/pallas_call | solution.py:722
  272.9 3.4 owner_sum.2
  276.3 2.1 collective-permute-start.24
  278.4 14.8 %collective-permute-done.24 = f32[96,128]{1,0:T(8,128)S(1)} collective-permute-done((f32[96,128]{1,0:T(8,128)S(1)}, f32[96,128]{1,0:T(8,128)S(1)}, u32[]{:S(2)}, u32[]{:S(2)}) %collective-permute-start.24) | collective-permute-done | bytes 49184 | tf_op jit(solution)/shard_map/ppermute | solution.py:802
  293.9 1.5 collective-permute-start.25
  299.1 3.0 collective-permute-done.26
  302.1 2.0 collective-permute-start.27
  305.7 6.9 %kron.3 = (f32[48,3328]{1,0:T(8,128)}, f32[2,26,24,24]{3,2,1,0:T(8,128)}, f32[2,26,128,128]{3,2,1,0:T(8,128)}) custom-call(f32[48,1536]{1,0:T(8,128)} %slice.63.refs_0_, f32[2,26,24,24]{3,2,1,0:T(8,128)} %copy.74.refs_1_, f32[2,26,128,128]{3,2,1,0:T(8,128)} %refs_2_.4, f32[2,26,24,24]{3,2,1,0:T(8,128)} %copy.75.refs_3_, f32[2,26,128,128]{3,2,1,0:T(8,128)} %refs_4_.4), custom_call_target="tpu_custom_call" | custom-call | tf_op jit(solution)/shard_map/kron/pallas_call | solution.py:679
  312.5 6.9 %kron.5 = (f32[96,768]{1,0:T(8,128)}, f32[4,6,24,24]{3,2,1,0:T(8,128)}, f32[4,6,128,128]{3,2,1,0:T(8,128)}) custom-call(f32[96,768]{1,0:T(8,128)} %pad_maximum_fusion.5.refs_0_, f32[4,6,24,24]{3,2,1,0:T(8,128)} %refs_1_.3, f32[4,6,128,128]{3,2,1,0:T(8,128)} %refs_2_.5, f32[4,6,24,24]{3,2,1,0:T(8,128)} %refs_3_.3, f32[4,6,128,128]{3,2,1,0:T(8,128)} %refs_4_.5), custom_call_target="tpu_custom_call" | custom-call | tf_op jit(solution)/shard_map/kron/pallas_call | solution.py:679
  319.4 3.3 owner_sum.3
  323.8 7.5 %collective-permute-done.22 = f32[48,1920]{1,0:T(8,128)S(1)} collective-permute-done((f32[48,1920]{1,0:T(8,128)}, f32[48,1920]{1,0:T(8,128)S(1)}, u32[]{:S(2)}, u32[]{:S(2)}) %collective-permute-start.22) | collective-permute-done | bytes 368672 | tf_op jit(solution)/shard_map/ppermute | solution.py:738
  335.0 7.8 %kron.4 = (f32[48,3328]{1,0:T(8,128)}, f32[2,26,24,24]{3,2,1,0:T(8,128)}, f32[2,26,128,128]{3,2,1,0:T(8,128)}) custom-call(f32[48,1792]{1,0:T(8,128)} %copy-done.7, f32[2,26,24,24]{3,2,1,0:T(8,128)} %copy.74.refs_1_, f32[2,26,128,128]{3,2,1,0:T(8,128)} %refs_2_.4, ...), custom_call_target="tpu_custom_call", output_to_operand_aliasing={{0}: (5, {}), {1}: (6, {}), {2}: (7, {})} | custom-call | tf_op jit(solution)/shard_map/kron/pallas_call | solution.py:679
  342.8 2.2 copy.81
  (168 shorter events, 37.7 us)
Async XLA Ops:
  7.2 326.8 %copy-start = (f32[2,24,24]{2,1,0:T(8,128)S(1)}, f32[2,24,24]{2,1,0:T(8,128)}, u32[]{:S(2)}) copy-start(f32[2,24,24]{2,1,0:T(8,128)} %param.43) | copy-start | bytes 13828
  7.2 52.9 %all-gather.2.cloned.1.call-start = ((), (), s32[]{:S(2)}) async-start(), calls=%async_computation.2 | async-start | bytes 3133440 | tf_op jit(solution)/shard_map/all_gather | solution.py:976
  10.0 34.4 %copy-start.33 = (f32[24]{0:T(128)S(1)}, f32[24]{0:T(128)}, u32[]{:S(2)}) copy-start(f32[24]{0:T(128)} %param.34) | copy-start | bytes 292
  10.0 34.9 %copy-start.32 = (f32[24]{0:T(128)S(1)}, f32[24]{0:T(128)}, u32[]{:S(2)}) copy-start(f32[24]{0:T(128)} %param.33) | copy-start | bytes 292
  10.0 35.4 %copy-start.30 = (f32[768]{0:T(1024)S(1)}, f32[768]{0:T(1024)}, u32[]{:S(2)}) copy-start(f32[768]{0:T(1024)} %param.30) | copy-start | bytes 9220
  10.0 36.0 %copy-start.31 = (f32[24]{0:T(128)S(1)}, f32[24]{0:T(128)}, u32[]{:S(2)}) copy-start(f32[24]{0:T(128)} %param.35) | copy-start | bytes 292
  10.0 36.7 %copy-start.29 = (f32[1792]{0:T(1024)S(1)}, f32[1792]{0:T(1024)}, u32[]{:S(2)}) copy-start(f32[1792]{0:T(1024)} %param.32) | copy-start | bytes 21508
  10.0 37.3 %copy-start.28 = (f32[1536]{0:T(1024)S(1)}, f32[1536]{0:T(1024)}, u32[]{:S(2)}) copy-start(f32[1536]{0:T(1024)} %param.36) | copy-start | bytes 18436
  10.0 11.9 %collective-permute-start.3 = (bf16[24,1536]{1,0:T(8,128)(2,1)S(1)}, bf16[24,1536]{1,0:T(8,128)(2,1)S(1)}, u32[]{:S(2)}, u32[]{:S(2)}) collective-permute-start(bf16[24,1536]{1,0:T(8,128)(2,1)S(1)} %fusion.34), channel_id=1, source_target_pairs={{0,24},{8,0},{16,8},{24,16},{1,25},{9,1},{17,9},{25,17},{2,26},{10... | collective-permute-start | bytes 221192 | tf_op jit(solution)/shard_map/ppermute | solution.py:738
  15.2 7.7 %collective-permute-start.2 = (bf16[24,1536]{1,0:T(8,128)(2,1)S(1)}, bf16[24,1536]{1,0:T(8,128)(2,1)S(1)}, u32[]{:S(2)}, u32[]{:S(2)}) collective-permute-start(bf16[24,1536]{1,0:T(8,128)(2,1)S(1)} %fusion.34), channel_id=1, source_target_pairs={{0,16},{8,24},{16,0},{24,8},{1,17},{9,25},{17,1},{25,9},{2,18},{10... | collective-permute-start | bytes 221192 | tf_op jit(solution)/shard_map/ppermute | solution.py:738
  15.2 11.1 %collective-permute-start.1 = (bf16[24,1536]{1,0:T(8,128)(2,1)S(1)}, bf16[24,1536]{1,0:T(8,128)(2,1)S(1)}, u32[]{:S(2)}, u32[]{:S(2)}) collective-permute-start(bf16[24,1536]{1,0:T(8,128)(2,1)S(1)} %fusion.34), channel_id=1, source_target_pairs={{0,8},{8,16},{16,24},{24,0},{1,9},{9,17},{17,25},{25,1},{2,10},{10... | collective-permute-start | bytes 221192 | tf_op jit(solution)/shard_map/ppermute | solution.py:738
  17.2 10.7 %collective-permute-start.7 = (bf16[48,768]{1,0:T(8,128)(2,1)S(1)}, bf16[48,768]{1,0:T(8,128)(2,1)S(1)}, u32[]{:S(2)}, u32[]{:S(2)}) collective-permute-start(bf16[48,768]{1,0:T(8,128)(2,1)S(1)} %fusion.33), channel_id=1, source_target_pairs={{0,24},{8,0},{16,8},{24,16},{1,25},{9,1},{17,9},{25,17},{2,26},{10... | collective-permute-start | bytes 221192 | tf_op jit(solution)/shard_map/ppermute | solution.py:738
  20.0 12.9 %collective-permute-start.6 = (bf16[48,768]{1,0:T(8,128)(2,1)S(1)}, bf16[48,768]{1,0:T(8,128)(2,1)S(1)}, u32[]{:S(2)}, u32[]{:S(2)}) collective-permute-start(bf16[48,768]{1,0:T(8,128)(2,1)S(1)} %fusion.33), channel_id=1, source_target_pairs={{0,16},{8,24},{16,0},{24,8},{1,17},{9,25},{17,1},{25,9},{2,18},{10... | collective-permute-start | bytes 221192 | tf_op jit(solution)/shard_map/ppermute | solution.py:738
  21.9 11.0 %collective-permute-start.5 = (bf16[48,768]{1,0:T(8,128)(2,1)S(1)}, bf16[48,768]{1,0:T(8,128)(2,1)S(1)}, u32[]{:S(2)}, u32[]{:S(2)}) collective-permute-start(bf16[48,768]{1,0:T(8,128)(2,1)S(1)} %fusion.33), channel_id=1, source_target_pairs={{0,8},{8,16},{16,24},{24,0},{1,9},{9,17},{17,25},{25,1},{2,10},{10... | collective-permute-start | bytes 221192 | tf_op jit(solution)/shard_map/ppermute | solution.py:738
  22.8 37.3 %collective-permute-start = (bf16[1,8,768]{2,1,0:T(8,128)(2,1)S(1)}, bf16[1,8,768]{2,1,0:T(8,128)(2,1)S(1)}, u32[]{:S(2)}, u32[]{:S(2)}) collective-permute-start(bf16[1,8,768]{2,1,0:T(8,128)(2,1)S(1)} %slice.46), channel_id=1, source_target_pairs={{0,1},{2,3},{4,5},{6,7},{8,9},{10,11},{12,13},{14,15},{16,17},{18,... | collective-permute-start | bytes 36872 | tf_op jit(solution)/shard_map/ppermute | solution.py:1010
  26.3 9.5 %collective-permute-start.4 = (bf16[4,24,1536]{2,1,0:T(8,128)(2,1)S(1)}, bf16[4,24,1536]{2,1,0:T(8,128)(2,1)S(1)}, u32[]{:S(2)}, u32[]{:S(2)}) collective-permute-start(bf16[4,24,1536]{2,1,0:T(8,128)(2,1)S(1)} %get-tuple-element.154), channel_id=1, source_target_pairs={{0,4},{4,0},{1,5},{5,1},{2,6},{6,2},{3,7},{7,3},{8,12},{12,8},{9,1... | collective-permute-start | bytes 884744 | tf_op jit(solution)/shard_map/ppermute | solution.py:738
  33.0 8.8 %collective-permute-start.8 = (bf16[4,48,768]{2,1,0:T(8,128)(2,1)S(1)}, bf16[4,48,768]{2,1,0:T(8,128)(2,1)S(1)}, u32[]{:S(2)}, u32[]{:S(2)}) collective-permute-start(bf16[4,48,768]{2,1,0:T(8,128)(2,1)S(1)} %get-tuple-element.152), channel_id=1, source_target_pairs={{0,4},{4,0},{1,5},{5,1},{2,6},{6,2},{3,7},{7,3},{8,12},{12,8},{9,1... | collective-permute-start | bytes 884744 | tf_op jit(solution)/shard_map/ppermute | solution.py:738
  35.9 46.1 %copy-start.9 = (bf16[2,4,24,1536]{3,2,1,0:T(8,128)(2,1)}, bf16[2,4,24,1536]{3,2,1,0:T(8,128)(2,1)S(1)}, u32[]{:S(2)}) copy-start(bf16[2,4,24,1536]{3,2,1,0:T(8,128)(2,1)S(1)} %pad_maximum_fusion.1.refs_0_) | copy-start | bytes 1769476
  35.9 46.1 %collective-permute-start.10 = (bf16[2,4,24,1536]{3,2,1,0:T(8,128)(2,1)S(1)}, bf16[2,4,24,1536]{3,2,1,0:T(8,128)(2,1)S(1)}, u32[]{:S(2)}, u32[]{:S(2)}) collective-permute-start(bf16[2,4,24,1536]{3,2,1,0:T(8,128)(2,1)S(1)} %pad_maximum_fusion.1.refs_0_), channel_id=1, source_target_pairs={{0,1},{1,0},{2,3},{3,2},{4,5},{5,4},{6,7},{7,6},{8,9},{9,8},{10,11... | collective-permute-start | bytes 1769480 | tf_op jit(solution)/shard_map/ppermute | solution.py:738
  41.8 47.0 %copy-start.10 = (bf16[2,4,48,768]{3,2,1,0:T(8,128)(2,1)}, bf16[2,4,48,768]{3,2,1,0:T(8,128)(2,1)S(1)}, u32[]{:S(2)}) copy-start(bf16[2,4,48,768]{3,2,1,0:T(8,128)(2,1)S(1)} %pad_maximum_fusion.2.refs_0_) | copy-start | bytes 1769476
  41.8 40.8 %collective-permute-start.13 = (bf16[2,4,48,768]{3,2,1,0:T(8,128)(2,1)S(1)}, bf16[2,4,48,768]{3,2,1,0:T(8,128)(2,1)S(1)}, u32[]{:S(2)}, u32[]{:S(2)}) collective-permute-start(bf16[2,4,48,768]{3,2,1,0:T(8,128)(2,1)S(1)} %pad_maximum_fusion.2.refs_0_), channel_id=1, source_target_pairs={{0,1},{1,0},{2,3},{3,2},{4,5},{5,4},{6,7},{7,6},{8,9},{9,8},{10,11... | collective-permute-start | bytes 1769480 | tf_op jit(solution)/shard_map/ppermute | solution.py:738
  77.8 20.9 %collective-permute-start.9 = (f32[1,128,1536]{2,1,0:T(8,128)}, f32[1,128,1536]{2,1,0:T(8,128)}, u32[]{:S(2)}, u32[]{:S(2)}) collective-permute-start(f32[1,128,1536]{2,1,0:T(8,128)} %get-tuple-element.59), channel_id=1, source_target_pairs={{0,1},{2,3},{4,5},{6,7},{8,9},{10,11},{12,13},{14,15},{16,17},{18,... | collective-permute-start | bytes 2359304 | tf_op jit(solution)/shard_map/ppermute | solution.py:1016
  82.0 2.0 collective-permute-start.11
  82.1 3.0 collective-permute-start.12
  82.5 6.3 %collective-permute-start.14 = (bf16[2,4,48,768]{3,2,1,0:T(8,128)(2,1)S(1)}, bf16[2,4,48,768]{3,2,1,0:T(8,128)(2,1)}, u32[]{:S(2)}, u32[]{:S(2)}) collective-permute-start(bf16[2,4,48,768]{3,2,1,0:T(8,128)(2,1)S(1)} %pad_maximum_fusion.2.refs_0_), channel_id=1, source_target_pairs={{0,2},{2,0},{1,3},{3,1},{4,6},{6,4},{5,7},{7,5},{8,10},{10,8},{9,1... | collective-permute-start | bytes 1769480 | tf_op jit(solution)/shard_map/ppermute | solution.py:738
  82.6 6.2 %collective-permute-start.15 = (bf16[2,4,48,768]{3,2,1,0:T(8,128)(2,1)S(1)}, bf16[2,4,48,768]{3,2,1,0:T(8,128)(2,1)}, u32[]{:S(2)}, u32[]{:S(2)}) collective-permute-start(bf16[2,4,48,768]{3,2,1,0:T(8,128)(2,1)S(1)} %collective-permute-done.13.refs_1_), channel_id=1, source_target_pairs={{0,2},{2,0},{1,3},{3,1},{4,6},{6,4},{5,7},{7,5},{8,10},{10,8},{9,1... | collective-permute-start | bytes 1769480 | tf_op jit(solution)/shard_map/ppermute | solution.py:738
  98.6 44.6 %copy-start.13 = (bf16[768,1024]{1,0:T(8,128)(2,1)S(1)}, bf16[768,1024]{1,0:T(8,128)(2,1)}, u32[]{:S(2)}) copy-start(bf16[768,1024]{1,0:T(8,128)(2,1)} %copy.70) | copy-start | bytes 4718596
  151.5 13.5 %collective-permute-start.16 = (f32[8,48,1536]{2,1,0:T(8,128)}, f32[8,48,1536]{2,1,0:T(8,128)}, u32[]{:S(2)}, u32[]{:S(2)}) collective-permute-start(f32[8,48,1536]{2,1,0:T(8,128)} %dynamic-slice_bitcast_fusion.2), channel_id=1, source_target_pairs={{0,2},{2,0},{1,3},{3,1},{4,6},{6,4},{5,7},{7,5},{8,10},{10,8},{9,1... | collective-permute-start | bytes 7077896 | tf_op jit(solution)/shard_map/ppermute | solution.py:738
  163.2 4.7 %collective-permute-start.17 = (f32[8,96,768]{2,1,0:T(8,128)S(1)}, f32[8,96,768]{2,1,0:T(8,128)S(1)}, u32[]{:S(2)}, u32[]{:S(2)}) collective-permute-start(f32[8,96,768]{2,1,0:T(8,128)S(1)} %dynamic-slice_bitcast_fusion.1), channel_id=1, source_target_pairs={{0,2},{2,0},{1,3},{3,1},{4,6},{6,4},{5,7},{7,5},{8,10},{10,8},{9,1... | collective-permute-start | bytes 7077896 | tf_op jit(solution)/shard_map/ppermute | solution.py:738
  163.7 21.7 %collective-permute-start.18 = (f32[1,128,1536]{2,1,0:T(8,128)}, f32[1,128,1536]{2,1,0:T(8,128)S(1)}, u32[]{:S(2)}, u32[]{:S(2)}) collective-permute-start(f32[1,128,1536]{2,1,0:T(8,128)} %get-tuple-element.69), channel_id=1, source_target_pairs={{1,0},{3,2},{5,4},{7,6},{9,8},{11,10},{13,12},{15,14},{17,16},{19,... | collective-permute-start | bytes 2359304 | tf_op jit(solution)/shard_map/ppermute | solution.py:1033
  175.4 78.6 %all-to-all-start = ((bf16[8,96,1536]{2,1,0:T(8,128)(2,1)}), bf16[8,96,1536]{2,1,0:T(8,128)(2,1)S(1)}, u32[]{:S(2)}, u32[]{:S(2)}) async-start(bf16[8,96,1536]{2,1,0:T(8,128)(2,1)} %get-tuple-element.76), calls=%async_computation | async-start | bytes 4718592 | tf_op jit(solution)/shard_map/all_to_all | solution.py:1044
  226.9 6.3 %collective-permute-start.19 = (f32[1,8,1792]{2,1,0:T(8,128)}, f32[1,8,1792]{2,1,0:T(8,128)S(1)}, u32[]{:S(2)}, u32[]{:S(2)}) collective-permute-start(f32[1,8,1792]{2,1,0:T(8,128)} %get-tuple-element.72), channel_id=1, source_target_pairs={{1,0},{3,2},{5,4},{7,6},{9,8},{11,10},{13,12},{15,14},{17,16},{19,... | collective-permute-start | bytes 172040 | tf_op jit(solution)/shard_map/ppermute | solution.py:1049
  244.0 5.5 %collective-permute-start.21 = (f32[8,48,1920]{2,1,0:T(8,128)S(1)}, f32[8,48,1920]{2,1,0:T(8,128)}, u32[]{:S(2)}, u32[]{:S(2)}) collective-permute-start(f32[8,48,1920]{2,1,0:T(8,128)S(1)} %dynamic-slice_bitcast_fusion), channel_id=1, source_target_pairs={{0,2},{2,0},{1,3},{3,1},{4,6},{6,4},{5,7},{7,5},{8,10},{10,8},{9,1... | collective-permute-start | bytes 8847368 | tf_op jit(solution)/shard_map/ppermute | solution.py:738
  254.1 17.6 %copy-start.4 = (bf16[8,96,1536]{2,1,0:T(8,128)(2,1)}, bf16[8,96,1536]{2,1,0:T(8,128)(2,1)S(1)}, u32[]{:S(2)}) copy-start(bf16[8,96,1536]{2,1,0:T(8,128)(2,1)S(1)} %all-to-all-done.got_ref) | copy-start | bytes 7077892
  254.1 39.8 %all-to-all-start.1 = ((bf16[8,48,1920]{2,1,0:T(8,128)(2,1)}), bf16[8,48,1920]{2,1,0:T(8,128)(2,1)}, u32[]{:S(2)}, u32[]{:S(2)}) async-start(bf16[8,48,1920]{2,1,0:T(8,128)(2,1)} %get-tuple-element.78), calls=%async_computation.1 | async-start | bytes 2949120 | tf_op jit(solution)/shard_map/all_to_all | solution.py:1075
  259.8 12.8 %copy-start.26 = (f32[8,1792]{1,0:T(8,128)S(1)}, f32[8,1792]{1,0:T(8,128)}, u32[]{:S(2)}) copy-start(f32[8,1792]{1,0:T(8,128)} %get-tuple-element.91) | copy-start | bytes 172036
  271.7 23.6 %copy-start.18 = (f32[2,26,24,24]{1,3,2,0:T(8,128)S(1)}, f32[2,26,24,24]{1,3,2,0:T(8,128)}, u32[]{:S(2)}) copy-start(f32[2,26,24,24]{1,3,2,0:T(8,128)} %param.37) | copy-start | bytes 359428
  271.7 24.9 %copy-start.19 = (f32[2,26,24,24]{1,3,2,0:T(8,128)S(1)}, f32[2,26,24,24]{1,3,2,0:T(8,128)}, u32[]{:S(2)}) copy-start(f32[2,26,24,24]{1,3,2,0:T(8,128)} %param.39) | copy-start | bytes 359428
  272.7 3.6 %collective-permute-start.23 = (f32[96,128]{1,0:T(8,128)S(1)}, f32[96,128]{1,0:T(8,128)S(1)}, u32[]{:S(2)}, u32[]{:S(2)}) collective-permute-start(f32[96,128]{1,0:T(8,128)S(1)} %pad_bitcast_fusion), channel_id=1, source_target_pairs={{0,2},{2,0},{1,3},{3,1},{4,6},{6,4},{5,7},{7,5},{8,10},{10,8},{9,1... | collective-permute-start | bytes 147464 | tf_op jit(solution)/shard_map/ppermute | solution.py:802
  276.3 21.5 %copy-start.12 = (f32[96,1536]{1,0:T(8,128)S(1)}, f32[96,1536]{1,0:T(8,128)}, u32[]{:S(2)}) copy-start(f32[96,1536]{1,0:T(8,128)} %owner_sum.2) | copy-start | bytes 1769476
  276.3 21.5 %collective-permute-start.20 = (f32[96,1536]{1,0:T(8,128)}, f32[96,1536]{1,0:T(8,128)S(1)}, u32[]{:S(2)}, u32[]{:S(2)}) collective-permute-start(f32[96,1536]{1,0:T(8,128)} %owner_sum.2), channel_id=1, source_target_pairs={{0,1},{1,0},{2,3},{3,2},{4,5},{5,4},{6,7},{7,6},{8,9},{9,8},{10,11... | collective-permute-start | bytes 1769480 | tf_op jit(solution)/shard_map/ppermute | solution.py:738
  276.3 16.9 %collective-permute-start.24 = (f32[96,128]{1,0:T(8,128)S(1)}, f32[96,128]{1,0:T(8,128)S(1)}, u32[]{:S(2)}, u32[]{:S(2)}) collective-permute-start(f32[96,128]{1,0:T(8,128)S(1)} %fusion.15), channel_id=1, source_target_pairs={{0,1},{1,0},{2,3},{3,2},{4,5},{5,4},{6,7},{7,6},{8,9},{9,8},{10,11... | collective-permute-start | bytes 147464 | tf_op jit(solution)/shard_map/ppermute | solution.py:802
  293.9 4.1 %collective-permute-start.25 = (f32[96,128]{1,0:T(8,128)S(1)}, f32[96,128]{1,0:T(8,128)S(1)}, u32[]{:S(2)}, u32[]{:S(2)}) collective-permute-start(f32[96,128]{1,0:T(8,128)S(1)} %fusion.32), channel_id=1, source_target_pairs={{0,4},{4,0},{1,5},{5,1},{2,6},{6,2},{3,7},{7,3},{8,12},{12,8},{9,1... | collective-permute-start | bytes 147464 | tf_op jit(solution)/shard_map/ppermute | solution.py:802
  298.0 4.2 %collective-permute-start.26 = (f32[96,128]{1,0:T(8,128)S(1)}, f32[96,128]{1,0:T(8,128)S(1)}, u32[]{:S(2)}, u32[]{:S(2)}) collective-permute-start(f32[96,128]{1,0:T(8,128)S(1)} %add.95), channel_id=1, source_target_pairs={{0,8},{8,0},{16,24},{24,16},{1,9},{9,1},{17,25},{25,17},{2,10},{10... | collective-permute-start | bytes 147464 | tf_op jit(solution)/shard_map/ppermute | solution.py:802
  302.1 21.0 %collective-permute-start.27 = (f32[96,128]{1,0:T(8,128)S(1)}, f32[96,128]{1,0:T(8,128)S(1)}, u32[]{:S(2)}, u32[]{:S(2)}) collective-permute-start(f32[96,128]{1,0:T(8,128)S(1)} %add.96), channel_id=1, source_target_pairs={{0,16},{8,24},{16,0},{24,8},{1,17},{9,25},{17,1},{25,9},{2,18},{10... | collective-permute-start | bytes 147464 | tf_op jit(solution)/shard_map/ppermute | solution.py:802
  319.4 13.0 %copy-start.8 = (f32[48,1536]{1,0:T(8,128)S(1)}, f32[48,1536]{1,0:T(8,128)}, u32[]{:S(2)}) copy-start(f32[48,1536]{1,0:T(8,128)} %slice.63.refs_0_) | copy-start | bytes 884740
  319.4 14.8 %copy-start.22 = (f32[2,24,24]{2,1,0:T(8,128)S(1)}, f32[2,24,24]{2,1,0:T(8,128)}, u32[]{:S(2)}) copy-start(f32[2,24,24]{2,1,0:T(8,128)} %param.44) | copy-start | bytes 13828
  322.7 8.6 %collective-permute-start.22 = (f32[48,1920]{1,0:T(8,128)}, f32[48,1920]{1,0:T(8,128)S(1)}, u32[]{:S(2)}, u32[]{:S(2)}) collective-permute-start(f32[48,1920]{1,0:T(8,128)} %owner_sum.3), channel_id=1, source_target_pairs={{0,1},{1,0},{2,3},{3,2},{4,5},{5,4},{6,7},{7,6},{8,9},{9,8},{10,11... | collective-permute-start | bytes 1105928 | tf_op jit(solution)/shard_map/ppermute | solution.py:738
  (17 other events, 69.1 us)
Sparse Core Ops, SparseCore 0:
  10.8 49.3 all-gather.1
